TPU v7x, 128 devices: a whole 4x4x4 slice. The times are simulated.
128 devices in a mesh: grp: 4 (over z_lo, core), tp: 32 (over z_hi, x, y).
Axes of the slice: x: 4, y: 4, z: 4 (z_hi: 2, z_lo: 2; z = z_hi * 2 + z_lo), core: 2. Of those that a mesh axis runs over, the one named last changes fastest.
Arguments:
- teacher_hidden: bfloat16 [384, 8192], P(('grp', 'tp')), may hold values from -150 to 150
- teacher_head: bfloat16 [8192, 98304], P(None, ('grp', 'tp')), may hold values from -0.0625 to 0.0625
- student_hidden: bfloat16 [384, 3584], P(('grp', 'tp')), may hold values from -150 to 150
- student_head: bfloat16 [3584, 98304], P(None, ('grp', 'tp')), may hold values from -0.09375 to 0.09375
- labels: int32 [384], replicated, may hold values from 0 to 98303
- owner_map: int32 [384], replicated, may hold values from 0 to 383, each once
Outputs:
- token_loss: float32 [384], P(('grp', 'tp'))
- grad_head: bfloat16 [3584, 98304], P(None, ('grp', 'tp'))
- grad_hidden: bfloat16 [384, 3584], P(('grp', 'tp'))
Inputs may be any that keep to these rules, and one draw needn't show every extreme that they name: owner_map holds each of 0 to 383 once.
All inputs are finite; a program needn't handle non-finite values.
Results may differ from a plain program's by a relative error of at most 0.0085.
Values may be sent and summed in bfloat16 or wider, within the bound.
No kernel may reach another device: no remote copies, remote signals or barrier semaphores. Data moves between devices by JAX's collectives and lax.ppermute only.
A program may use at most 128 MiB of HBM per device.

v0:
```python
import math

import jax
import jax.numpy as jnp
from jax import lax
from jax.sharding import PartitionSpec as P

VOCABULARY = 98304
TOKENS = 384


def row_terms(teacher_rows, student_rows, teacher_lse, student_lse, weight, reverse, hits):
    log_teacher = teacher_rows - teacher_lse[:, None]
    log_student = student_rows - student_lse[:, None]
    teacher_prob = jnp.exp(log_teacher)
    student_prob = jnp.exp(log_student)
    mixed = weight[:, None] * (student_prob - teacher_prob)
    mixed = mixed + (1.0 - weight)[:, None] * student_prob * (
        log_student - log_teacher - reverse[:, None]
    )
    mixed = mixed + student_prob - hits.astype(jnp.float32)
    return (mixed / TOKENS).astype(jnp.bfloat16)


def whole_rows(teacher_rows, student_rows, hits):
    teacher_top = jnp.max(teacher_rows, axis=1)
    student_top = jnp.max(student_rows, axis=1)
    teacher_lse = teacher_top + jnp.log(
        jnp.sum(jnp.exp(teacher_rows - teacher_top[:, None]), axis=1)
    )
    student_lse = student_top + jnp.log(
        jnp.sum(jnp.exp(student_rows - student_top[:, None]), axis=1)
    )
    log_teacher = teacher_rows - teacher_lse[:, None]
    log_student = student_rows - student_lse[:, None]
    teacher_prob = jnp.exp(log_teacher)
    student_prob = jnp.exp(log_student)
    entropy = -jnp.sum(teacher_prob * log_teacher, axis=1)
    weight = entropy / math.log(VOCABULARY)
    forward = jnp.sum(teacher_prob * (log_teacher - log_student), axis=1)
    reverse = jnp.sum(student_prob * (log_student - log_teacher), axis=1)
    cross = student_lse - jnp.sum(jnp.where(hits, student_rows, 0.0), axis=1)
    loss = weight * forward + (1.0 - weight) * reverse + cross
    return (
        loss,
        row_terms(teacher_rows, student_rows, teacher_lse, student_lse, weight, reverse, hits),
    )


def shards(teacher_hidden, teacher_head, student_hidden, student_head, labels, owner_map):
    rows = student_hidden.shape[0]
    position = lax.axis_index(("grp", "tp"))
    teacher_logits = jnp.dot(
        lax.all_gather(teacher_hidden, ("grp", "tp"), axis=0, tiled=True),
        teacher_head,
        preferred_element_type=jnp.float32,
    )
    student_full = lax.all_gather(student_hidden, ("grp", "tp"), axis=0, tiled=True)
    teacher_logits = jnp.take(teacher_logits, owner_map, axis=0)
    student_logits = jnp.dot(student_full, student_head, preferred_element_type=jnp.float32)
    owned_teacher, owned_student = (
        lax.all_to_all(teacher_logits, ("grp", "tp"), split_axis=0, concat_axis=1, tiled=True),
        lax.all_to_all(student_logits, ("grp", "tp"), split_axis=0, concat_axis=1, tiled=True),
    )
    own_labels = lax.dynamic_slice_in_dim(labels, position * rows, rows)
    owned_hits = own_labels[:, None] == lax.iota(jnp.int32, owned_teacher.shape[1])[None, :]
    token_loss, owned_grad = whole_rows(owned_teacher, owned_student, owned_hits)
    grad_logits = lax.all_to_all(owned_grad, ("grp", "tp"), split_axis=1, concat_axis=0, tiled=True)
    grad_head = lax.dot_general(
        student_full, grad_logits, (((0,), (0,)), ((), ())), preferred_element_type=jnp.float32
    ).astype(jnp.bfloat16)
    grad_hidden = lax.psum_scatter(
        lax.dot_general(
            grad_logits, student_head, (((1,), (1,)), ((), ())), preferred_element_type=jnp.float32
        ),
        ("grp", "tp"),
        scatter_dimension=0,
        tiled=True,
    )
    return (token_loss, grad_head, grad_hidden.astype(jnp.bfloat16))


def solution(mesh):
    in_specs = (
        P(("grp", "tp"), None),
        P(None, ("grp", "tp")),
        P(("grp", "tp"), None),
        P(None, ("grp", "tp")),
        P(),
        P(),
    )
    out_specs = (P(("grp", "tp")), P(None, ("grp", "tp")), P(("grp", "tp"), None))
    return jax.shard_map(shards, mesh=mesh, in_specs=in_specs, out_specs=out_specs, check_vma=False)
```

profile of v0, /device:TPU:0, one launch (start us, length us, event | category | flops | bytes accessed | tf_op | source)
XLA Modules:
  0.0 866.5 jit_solution(14327685298822195751)
XLA Ops:
  7.2 0.0 all-gather.7.cloned.1.call-start
  7.2 0.7 all-gather.7.cloned.1.call-update
  7.9 0.0 all-gather.5.cloned.1.call-start
  7.9 0.7 all-gather.5.cloned.1.call-update
  8.6 0.7 compare_and_fusion
  9.3 0.2 broadcast_in_dim.18
  9.6 0.7 compare_select_fusion.1
  10.3 304.7 %all-gather.7.cloned.1.call-done = bf16[128,3,3584]{2,1,0:T(4,128)(2,1)} async-done(((bf16[1,3,3584]{2,1,0:T(4,128)(2,1)}), bf16[128,3,3584]{2,1,0:T(4,128)(2,1)}) %all-gather.7.cloned.1.call-update) | async-done | bytes 2752528 | tf_op jit(solution)/shard_map/all_gather | solution.py:58
  315.0 5.6 reshape.142
  320.6 0.0 copy-start
  320.6 7.0 fusion.13
  327.6 0.0 copy-done
  327.6 2.5 all_to_all.33
  330.1 10.5 %all-to-all-start.1 = ((f32[128,3,768]{2,1,0:T(4,128)}), f32[128,3,768]{2,1,0:T(4,128)S(1)}, u32[]{:S(2)}, u32[]{:S(2)}) async-start(f32[128,3,768]{2,1,0:T(4,128)} %all_to_all.33), calls=%async_computation.1 | async-start | bytes 3145728 | tf_op jit(solution)/shard_map/all_to_all | solution.py:63
  340.6 295.8 %all-gather.5.cloned.1.call-done = bf16[128,3,8192]{2,1,0:T(4,128)(2,1)} async-done(((bf16[1,3,8192]{2,1,0:T(4,128)(2,1)}), bf16[128,3,8192]{2,1,0:T(4,128)(2,1)}) %all-gather.5.cloned.1.call-update) | async-done | bytes 6291472 | tf_op jit(solution)/shard_map/all_gather | solution.py:54
  636.4 13.8 %reshape.140 = bf16[384,8192]{1,0:T(8,128)(2,1)} reshape(bf16[128,3,8192]{2,1,0:T(4,128)(2,1)} %all-gather.5.cloned.1.call-done) | data formatting | bytes 12582912
  650.1 9.9 %fusion.12 = f32[384,768]{1,0:T(8,128)S(1)} fusion(bf16[384,8192]{1,0:T(8,128)(2,1)} %reshape.140, bf16[8192,768]{1,0:T(8,128)(2,1)} %param.7), kind=kOutput, calls=%fused_computation.36 | convolution fusion | flops 4831838208 | bytes 20054016 | tf_op jit(solution)/shard_map/dot_general | solution.py:53
  660.1 2.5 gather_fusion
  662.5 1.6 gather.7
  664.1 1.6 broadcast_select_fusion
  665.7 0.0 all-to-all-done.1
  665.7 9.0 %all-to-all-start = ((f32[128,3,768]{2,1,0:T(4,128)}), f32[128,3,768]{2,1,0:T(4,128)}, u32[]{:S(2)}, u32[]{:S(2)}) async-start(f32[128,3,768]{2,1,0:T(4,128)} %broadcast_select_fusion), calls=%async_computation | async-start | bytes 3145728 | tf_op jit(solution)/shard_map/all_to_all | solution.py:62
  674.7 0.8 dynamic_slice.3
  675.5 0.9 reduce_max.19
  676.4 1.0 fusion.11
  677.4 20.3 %all-to-all-done = f32[128,3,768]{2,1,0:T(4,128)} async-done(((f32[128,3,768]{2,1,0:T(4,128)}), f32[128,3,768]{2,1,0:T(4,128)}, u32[]{:S(2)}, u32[]{:S(2)}) %all-to-all-start) | async-done | bytes 1179680 | tf_op jit(solution)/shard_map/all_to_all | solution.py:62
  697.7 2.3 reduce_max.18
  700.0 2.4 exponential_reduce_fusion
  702.5 3.6 fusion.6
  706.0 0.5 negate_multiply_fusion
  706.6 4.0 fusion.4
  710.5 0.0 copy-start.1
  710.5 5.4 all-to-all-start.2
  716.0 15.1 %all-to-all-done.2 = bf16[3,128,768]{2,0,1:T(4,128)(2,1)S(1)} async-done(((bf16[3,128,768]{2,0,1:T(4,128)(2,1)}), bf16[3,128,768]{2,0,1:T(4,128)(2,1)S(1)}, u32[]{:S(2)}, u32[]{:S(2)}) %all-to-all-start.2) | async-done | bytes 589856 | tf_op jit(solution)/shard_map/all_to_all | solution.py:68
  731.1 1.2 all_to_all.38
  732.3 0.0 copy-done.1
  732.3 0.0 copy-start.2
  732.3 6.0 fusion
  738.3 0.0 copy-done.2
  738.3 7.4 fusion.14
  745.6 8.3 copy.11
  753.9 105.1 %all-reduce.2 = bf16[384,3584]{1,0:T(8,128)(2,1)S(1)} all-reduce(f32[384,3584]{1,0:T(8,128)} %fusion.14), channel_id=2, replica_groups=mesh['grp'=4,'tp'=32] {'grp','tp'}, use_global_device_ids=true, to_apply=%region_8.9.clone | all-reduce | flops 1376256 | bytes 8257536
  859.0 0.6 dynamic-slice_convert_fusion
  (4 shorter events, 0.1 us)
Async XLA Ops:
  7.2 307.8 %all-gather.7.cloned.1.call-start = ((), (), s32[]{:S(2)}) async-start(), calls=%async_computation.4 | async-start | bytes 3698688 | tf_op jit(solution)/shard_map/all_gather | solution.py:58
  7.9 628.5 %all-gather.5.cloned.1.call-start = ((), (), s32[]{:S(2)}) async-start(), calls=%async_computation.3 | async-start | bytes 8454144 | tf_op jit(solution)/shard_map/all_gather | solution.py:54
  320.6 7.0 copy-start
  330.1 335.6 %all-to-all-start.1 = ((f32[128,3,768]{2,1,0:T(4,128)}), f32[128,3,768]{2,1,0:T(4,128)S(1)}, u32[]{:S(2)}, u32[]{:S(2)}) async-start(f32[128,3,768]{2,1,0:T(4,128)} %all_to_all.33), calls=%async_computation.1 | async-start | bytes 3145728 | tf_op jit(solution)/shard_map/all_to_all | solution.py:63
  665.7 32.0 %all-to-all-start = ((f32[128,3,768]{2,1,0:T(4,128)}), f32[128,3,768]{2,1,0:T(4,128)}, u32[]{:S(2)}, u32[]{:S(2)}) async-start(f32[128,3,768]{2,1,0:T(4,128)} %broadcast_select_fusion), calls=%async_computation | async-start | bytes 3145728 | tf_op jit(solution)/shard_map/all_to_all | solution.py:62
  710.5 21.8 %copy-start.1 = (bf16[384,3584]{1,0:T(8,128)(2,1)S(1)}, bf16[384,3584]{1,0:T(8,128)(2,1)}, u32[]{:S(2)}) copy-start(bf16[384,3584]{1,0:T(8,128)(2,1)} %copy-done) | copy-start | bytes 8257540
  710.5 20.5 %all-to-all-start.2 = ((bf16[3,128,768]{2,0,1:T(4,128)(2,1)}), bf16[3,128,768]{2,0,1:T(4,128)(2,1)S(1)}, u32[]{:S(2)}, u32[]{:S(2)}) async-start(bf16[3,128,768]{2,0,1:T(4,128)(2,1)} %fusion.4), calls=%async_computation.2 | async-start | bytes 1572864 | tf_op jit(solution)/shard_map/all_to_all | solution.py:68
  732.3 6.0 copy-start.2
Sparse Core Ops, SparseCore 0:
  9.7 305.2 all-gather.6
  316.7 319.6 all-gather.4
where the time goes:
time: 868 us; the launch traced here: 866 us
  waiting for transfers between devices  637 us (73%)
  blocking collectives  105 us (12%)
  local copies, waits for them, and re-layouts  37.1 us (4%)
  matrix products  30.2 us (3%)
  starting transfers between devices  25 us (3%)
  other arithmetic  17.8 us (2%)
  between operations  14.1 us (2%)
    all_gather x1, waiting for transfers between devices, shards(): lax.all_gather(student_hidden, ('grp', 'tp'), axis=0, tiled=True)  305 us
    all_gather x1, waiting for transfers between devices, shards(): lax.all_gather(teacher_hidden, ('grp', 'tp'), axis=0, tiled=True)  296 us
    unnamed x1, blocking collectives  105 us
    unnamed x9, local copies, waits for them, and re-layouts  27.7 us
    all_to_all x1, waiting for transfers between devices, shards(): lax.all_to_all(teacher_logits, ('grp', 'tp'), split_axis=0, concat_axis=1...  20.3 us
  transfers between devices with their start and end apart: 5, of which 4 were waited for; matrix products, arithmetic and copies ran while one was open for 5% of the time, Pallas kernels for 0%

commit v1 on v0

v1 whole, which is shorter than its diff:
```python
import functools
import math

import jax
import jax.numpy as jnp
from jax import lax
from jax.experimental import pallas as pl
from jax.experimental.pallas import tpu as pltpu
from jax.sharding import PartitionSpec as P


AXES = ("grp", "tp")
DEVICES = 128
TOKENS = 384
ROWS = 3
HALF = TOKENS // 2
BF16 = jnp.bfloat16
F32 = jnp.float32
VMEM = pl.BlockSpec(memory_space=pltpu.VMEM)
SMEM = pl.BlockSpec(memory_space=pltpu.SMEM)
HBM = pl.BlockSpec(memory_space=pltpu.HBM)
STAGES = (("y", "x", "z"), ("z", "y", "x"))


def coords(d):
    return {"zl": d // 64, "c": d // 32 % 2, "zh": d // 16 % 2, "x": d // 4 % 4, "y": d % 4, "z": d // 16 % 2 * 2 + d // 64}


def device(c, x, y, z):
    return ((z % 2 * 2 + c) * 2 + z // 2) * 16 + x * 4 + y


def moved(d, dim, k):
    at = coords(d)
    at[dim] = (at[dim] + k) % 4
    return device(at["c"], at["x"], at["y"], at["z"])


def swap(value):
    return lax.ppermute(value, AXES, [(d, d ^ 32) for d in range(DEVICES)])


def shift(value, stage, k):
    pairs = [(d, moved(d, STAGES[coords(d)["c"]][stage], k)) for d in range(DEVICES)]
    return lax.ppermute(value, AXES, pairs)


def token_order(me):
    j = lax.iota(jnp.int32, TOKENS)
    r = j % HALF
    steps = (r // 3 % 4, r // 12 % 4, r // 48)
    tokens = []
    for core in range(2):
        at = {dim: (me[dim] - step) % 4 for dim, step in zip(STAGES[core], steps)}
        tokens.append(device(core, at["x"], at["y"], at["z"]) * ROWS + r % ROWS)
    first = (j < HALF) == (me["c"] == 0)
    return jnp.where(first, tokens[0], tokens[1])[None, :]


def split3(v):
    high = v.astype(BF16)
    rest = v - high.astype(F32)
    middle = rest.astype(BF16)
    return high, middle, (rest - middle.astype(F32)).astype(BF16)


def one_hot(column, row):
    return jnp.where(column == row, 1.0, 0.0).astype(BF16)


def dot(a, b):
    return jnp.dot(a, b, preferred_element_type=F32)


def dot_nt(a, b):
    return lax.dot_general(a, b, (((1,), (1,)), ((), ())), preferred_element_type=F32)


def lane_ids():
    return lax.broadcasted_iota(jnp.int32, (TOKENS, TOKENS), 1)


def to_column(row):
    same = lax.broadcasted_iota(jnp.int32, (TOKENS, TOKENS), 0) == lane_ids()
    return jnp.sum(jnp.where(same, row.astype(F32), 0.0), axis=1, keepdims=True).astype(jnp.int32)


def pick_column(column, row_values):
    return jnp.sum(jnp.where(column == lane_ids(), row_values.astype(F32), 0.0), axis=1, keepdims=True).astype(jnp.int32)


def teacher_kernel(n, *refs):
    blocks, (tok_row, owner, w, out, wbuf, sem) = refs[:n], refs[n:]
    slots, chunk, _ = wbuf.shape
    count = w.shape[0] // chunk

    def copy(i):
        slot = i % slots
        return pltpu.make_async_copy(w.at[pl.ds(i * chunk, chunk), :], wbuf.at[slot], sem.at[slot])

    for i in range(slots):
        copy(i).start()
    for i in range(count):
        columns = slice(i * chunk, (i + 1) * chunk)
        rows = jnp.concatenate([block[:, columns] for block in blocks], axis=0)
        copy(i).wait()
        part = dot(rows, wbuf[i % slots])
        out[...] = part if i == 0 else out[...] + part
        if i + slots < count:
            copy(i + slots).start()
    owner_col = pick_column(to_column(tok_row[...]), owner[...])
    pick = one_hot(owner_col, tok_row[...])
    high, middle, low = split3(out[...])
    out[...] = (dot(pick, high) + dot(pick, middle)) + dot(pick, low)


def student_kernel(n, *refs):
    blocks, (at_ref, t_ref, tok_row, labels, w, s_out, g_out, stats_out, g, wbuf, table, label_at, sem) = refs[:n], refs[n:]
    chunk = 896
    count = w.shape[0] // chunk

    def copy(i):
        rows = pl.ds(pl.multiple_of(i * chunk, chunk), chunk)
        return pltpu.make_async_copy(w.at[rows, :], wbuf.at[rows, :], sem.at[i])

    for i in range(count):
        copy(i).start()
    at = 0
    for block in blocks:
        g[pl.ds(at, block.shape[0]), :] = block[...]
        at += block.shape[0]
    save = pltpu.make_async_copy(g, g_out, sem.at[count])
    save.start()
    s_out[...] = jnp.zeros_like(s_out)
    tok_col = to_column(tok_row[...])
    label_at[...] = pick_column(tok_col, labels[...]) - at_ref[0]

    @pl.loop(0, count)
    def _(i):
        rows = pl.ds(pl.multiple_of(i * chunk, chunk), chunk)
        copy(i).wait()
        s_out[...] += dot(g[:, rows], wbuf[rows, :])

    step = 32
    lane = lax.broadcasted_iota(jnp.int32, (step, 128), 1)

    @pl.loop(0, TOKENS // step)
    def _(i):
        rows = pl.ds(pl.multiple_of(i * step, step), step)
        t = t_ref[rows, :]
        s = s_out[rows, :]
        t_top = jnp.max(t, axis=1, keepdims=True)
        s_top = jnp.max(s, axis=1, keepdims=True)
        t_low, s_low, gap = t - t_top, s - s_top, t - s
        t_exp, s_exp = jnp.exp(t_low), jnp.exp(s_low)
        hits = lax.broadcasted_iota(jnp.int32, t.shape, 1) == label_at[rows, :]
        values = (
            t_top,
            jnp.sum(t_exp, axis=1, keepdims=True),
            jnp.sum(t_exp * t_low, axis=1, keepdims=True),
            jnp.sum(t_exp * gap, axis=1, keepdims=True),
            s_top,
            jnp.sum(s_exp, axis=1, keepdims=True),
            jnp.sum(-s_exp * gap, axis=1, keepdims=True),
            jnp.sum(jnp.where(hits, s, 0.0), axis=1, keepdims=True),
        )
        packed = jnp.zeros((step, 128), F32)
        for k, value in enumerate(values):
            packed = jnp.where(lane == k, value, packed)
        table[rows, :] = packed

    to_natural = one_hot(tok_col, lane_ids())
    high, middle, low = split3(table[...].T[:16])
    stats_out[...] = ((dot(high, to_natural) + dot(middle, to_natural)) + dot(low, to_natural))[:8]
    save.wait()


def weight_copies(w, wbuf, sem):
    chunk = 896
    slices = [slice(i * chunk, (i + 1) * chunk) for i in range(w.shape[0] // chunk)]
    copies = [(rows, pltpu.make_async_copy(w.at[rows, :], wbuf.at[rows, :], sem.at[i])) for i, rows in enumerate(slices)]
    for _, copy in copies:
        copy.start()
    return copies


def gradient_kernel(vocab, at_ref, t_ref, s_ref, stats, tok_row, labels, w, grads_out, send_out, loss_out, local, label_at, wbuf, sem):
    copies = weight_copies(w, wbuf, sem)
    t_top, t_sum, t_moment, t_gap, s_top, s_sum, s_gap, hit = (stats[k : k + 1, :] for k in range(8))
    t_log, s_log = jnp.log(t_sum), jnp.log(s_sum)
    t_lse, s_lse = t_top + t_log, s_top + s_log
    weight = (t_log - t_moment / t_sum) / math.log(vocab)
    forward = t_gap / t_sum - t_lse + s_lse
    reverse = s_gap / s_sum - s_lse + t_lse
    loss_out[...] = weight * forward + (1.0 - weight) * reverse + (s_lse - hit)
    rows8 = jnp.concatenate([t_lse, s_lse, weight, reverse] * 2, axis=0)
    tok_col = to_column(tok_row[...])
    from_natural = one_hot(tok_col, lane_ids())
    label_at[...] = pick_column(tok_col, labels[...]) - at_ref[0]
    high, middle, low = split3(rows8)
    local[...] = (dot_nt(from_natural, high) + dot_nt(from_natural, middle)) + dot_nt(from_natural, low)
    step = 32

    @pl.loop(0, TOKENS // step)
    def _(i):
        rows = pl.ds(pl.multiple_of(i * step, step), step)
        t_lse, s_lse, weight, reverse = (local[rows, k : k + 1] for k in range(4))
        t_log = t_ref[rows, :] - t_lse
        s_log = s_ref[rows, :] - s_lse
        t_prob, s_prob = jnp.exp(t_log), jnp.exp(s_log)
        mixed = weight * (s_prob - t_prob) + (1.0 - weight) * s_prob * (s_log - t_log - reverse)
        hits = lax.broadcasted_iota(jnp.int32, t_log.shape, 1) == label_at[rows, :]
        mixed = mixed + s_prob - jnp.where(hits, 1.0, 0.0)
        grads_out[rows, :] = (mixed / TOKENS).astype(BF16)

    for rows, copy in copies:
        copy.wait()
        send_out[:, rows] = dot_nt(grads_out[HALF:, :], wbuf[rows, :]).astype(BF16)


def keep_kernel(grads, w, out, wbuf, sem):
    for rows, copy in weight_copies(w, wbuf, sem):
        copy.wait()
        out[:, rows] = dot_nt(grads[:HALF, :], wbuf[rows, :])


def call(kernel, out, specs, args, scratch, vmem, flops, out_specs=None):
    return pl.pallas_call(
        kernel,
        out_shape=[jax.ShapeDtypeStruct(*o) for o in out],
        in_specs=specs,
        out_specs=out_specs or [VMEM] * len(out),
        scratch_shapes=scratch,
        compiler_params=pltpu.CompilerParams(vmem_limit_bytes=vmem << 20),
        cost_estimate=pl.CostEstimate(flops=flops, bytes_accessed=4 << 20, transcendentals=0),
    )(*args)


def merge(tables):
    t_top = functools.reduce(jnp.maximum, [v[0] for v in tables])
    s_top = functools.reduce(jnp.maximum, [v[4] for v in tables])
    total = 0.0
    for v in tables:
        t_low, s_low = v[0] - t_top, v[4] - s_top
        t_scale, s_scale = jnp.exp(t_low), jnp.exp(s_low)
        total += jnp.stack(
            [
                jnp.zeros_like(t_top), t_scale * v[1], t_scale * (v[2] + t_low * v[1]), t_scale * v[3],
                jnp.zeros_like(s_top), s_scale * v[5], s_scale * v[6], v[7],
            ]
        )
    row = lax.broadcasted_iota(jnp.int32, total.shape, 0)
    return jnp.where(row == 0, t_top, jnp.where(row == 4, s_top, total))


def ring_shift(value, dim):
    return lax.ppermute(value, AXES, [(d, moved(d, dim, -1 if coords(d)["c"] else 1)) for d in range(DEVICES)])


def across(value, dim):
    return lax.ppermute(value, AXES, [(d, moved(d, dim, 2)) for d in range(DEVICES)])


def shards(teacher_hidden, teacher_head, student_hidden, student_head, labels, owner_map):
    me = coords(lax.axis_index(AXES))
    vocab = teacher_head.shape[1]
    tk, sk = teacher_head.shape[0], student_head.shape[0]
    tok_row = token_order(me)
    at = (lax.axis_index(AXES) * vocab).astype(jnp.int32)[None]
    label_row, owner_row = labels[None, :], owner_map[None, :]

    block = jnp.concatenate([teacher_hidden, student_hidden], axis=1)
    block = jnp.concatenate([block] + [shift(block, 0, k) for k in (1, 2, 3)], axis=0)
    parts = [block] + [shift(block, 1, k) for k in (1, 2, 3)]
    t0 = jnp.concatenate([v[:, :tk] for v in parts], axis=0)
    s0 = jnp.concatenate([v[:, tk:] for v in parts], axis=0)
    t1, t3 = shift(t0, 2, 1), shift(t0, 2, -1)
    t1, t3, s0 = lax.optimization_barrier((t1, t3, s0))
    rows = t0.shape[0] // 2
    t2 = [shift(t1[:rows], 2, 1), shift(t3[rows:], 2, -1)]
    s_moved = [shift(s0, 2, k) for k in (1, 2, 3)]
    t2_other = [swap(v) for v in t2]
    t_blocks = [t0, t1, *t2, t3, swap(t0), swap(t1), *t2_other, swap(t3)]

    n = len(t_blocks)
    (t_logits,) = call(
        functools.partial(teacher_kernel, n),
        [((TOKENS, vocab), F32)],
        [VMEM] * (n + 2) + [HBM],
        [*t_blocks, tok_row, owner_row, teacher_head],
        [pltpu.VMEM((3, 1024, vocab), BF16), pltpu.SemaphoreType.DMA((3,))],
        48,
        2 * TOKENS * tk * vocab,
    )
    *s_moved, t_logits = lax.optimization_barrier((*s_moved, t_logits))
    s_own = [s0, *s_moved]
    s_blocks = s_own + [swap(v) for v in s_own]
    n = len(s_blocks)
    s_logits, hidden, stats = call(
        functools.partial(student_kernel, n),
        [((TOKENS, vocab), F32), ((TOKENS, sk), BF16), ((8, TOKENS), F32)],
        [VMEM] * n + [SMEM] + [VMEM] * 3 + [HBM],
        [*s_blocks, at, t_logits, tok_row, label_row, student_head],
        [
            pltpu.VMEM((TOKENS, sk), BF16),
            pltpu.VMEM((sk, vocab), BF16),
            pltpu.VMEM((TOKENS, 128), F32),
            pltpu.VMEM((TOKENS, 1), jnp.int32),
            pltpu.SemaphoreType.DMA((5,)),
        ],
        50,
        2 * TOKENS * sk * vocab,
        [VMEM, HBM, VMEM],
    )

    stats = merge([stats, swap(stats)])
    for dim in ("y", "x", "z"):
        near, far = ring_shift(stats, dim), across(stats, dim)
        stats = merge([stats, near, swap(near), far])

    wscratch = pltpu.VMEM((sk, vocab), BF16)
    grads, to_other, loss = call(
        functools.partial(gradient_kernel, vocab * DEVICES),
        [((TOKENS, vocab), BF16), ((HALF, sk), BF16), ((1, TOKENS), F32)],
        [SMEM] + [VMEM] * 5 + [HBM],
        [at, t_logits, s_logits, stats, tok_row, label_row, student_head],
        [pltpu.VMEM((TOKENS, 8), F32), pltpu.VMEM((TOKENS, 1), jnp.int32), wscratch, pltpu.SemaphoreType.DMA((4,))],
        56,
        TOKENS * sk * vocab,
    )
    (kept,) = call(keep_kernel, [((HALF, sk), F32)], [VMEM, HBM], [grads, student_head], [wscratch, pltpu.SemaphoreType.DMA((4,))], 56, TOKENS * sk * vocab)

    total = kept + swap(to_other).astype(F32)
    for stage in (2, 1, 0):
        size = total.shape[0] // 4
        parts = [shift(total[k * size : (k + 1) * size].astype(BF16), stage, -k) for k in (1, 2, 3)]
        if stage == 2:
            grad_head = lax.dot_general(hidden, grads, (((0,), (0,)), ((), ())), preferred_element_type=F32).astype(BF16)
            total, grad_head, *parts = lax.optimization_barrier((total, grad_head, *parts))
        total = total[:size] + sum(p.astype(F32) for p in parts)
    token_loss = lax.dynamic_slice_in_dim(loss[0], lax.axis_index(AXES) * ROWS, ROWS)
    return token_loss, grad_head, total.astype(BF16)


def solution(mesh):
    in_specs = (P(AXES, None), P(None, AXES), P(AXES, None), P(None, AXES), P(), P())
    out_specs = (P(AXES), P(None, AXES), P(AXES, None))
    return jax.shard_map(shards, mesh=mesh, in_specs=in_specs, out_specs=out_specs, check_vma=False)
```

time: 868 us -> 158 us (0.18)
  waiting for transfers between devices: 637 us -> 60.7 us
  blocking collectives: 105 us -> 0 us
  Pallas kernels: 0 us -> 37.3 us
  local copies, waits for them, and re-layouts: 37.1 us -> 4.77 us
  matrix products: 30.2 us -> 4.82 us
  starting transfers between devices: 25 us -> 43.3 us
  between operations: 14.1 us -> 1.15 us
  other arithmetic: 17.8 us -> 5.2 us
    all_gather x2 -> x0, waiting for transfers between devices: 600 us -> none  [the longest x1 305 us: shards(): lax.all_gather(student_hidden, ('grp', 'tp'), axis=0, tiled=True)]
    unnamed x1 -> x0, blocking collectives: 105 us -> none
    ppermute x0 -> x42, waiting for transfers between devices: none -> 60.7 us  [the longest x22 47.6 us: shift(): return lax.ppermute(value, AXES, pairs)]
    ppermute x0 -> x42, starting transfers between devices: none -> 43.3 us  [the longest x22 31.5 us: shift(): return lax.ppermute(value, AXES, pairs)]
    pallas_call x0 -> x4, Pallas kernels: none -> 37.3 us  [call(): pl.pallas_call(kernel, out_shape=[jax.ShapeDtypeStruct(*o) for o in out],...]
    all_to_all x3 -> x0, waiting for transfers between devices: 35.3 us -> none  [the longest x1 20.3 us: shards(): lax.all_to_all(teacher_logits, ('grp', 'tp'), split_axis=0, concat_axis=1...]
    unnamed x9 -> x15, local copies, waits for them, and re-layouts: 27.7 us -> 1.92 us
    dot_general x4 -> x1, matrix products: 30.2 us -> 4.82 us  [shards(): lax.dot_general(hidden, grads, (((0,), (0,)), ((), ())), preferred_elemen...]
  transfers between devices with their start and end apart: 5 -> 42, of which waited for: 4 -> 27; matrix products, arithmetic and copies ran while one was open for 5% -> 4% of each run, Pallas kernels for 0% -> 13%
where the time goes in v1:
time: 158 us; the launch traced here: 157 us
  waiting for transfers between devices  60.7 us (38%)
  starting transfers between devices  43.3 us (27%)
  Pallas kernels  37.3 us (24%)
  other arithmetic  5.2 us (3%)
  matrix products  4.82 us (3%)
  local copies, waits for them, and re-layouts  4.77 us (3%)
    ppermute x22, waiting for transfers between devices, shift(): return lax.ppermute(value, AXES, pairs)  47.6 us
    pallas_call x4, Pallas kernels, call(): pl.pallas_call(kernel, out_shape=[jax.ShapeDtypeStruct(*o) for o in out],...  37.3 us
    ppermute x22, starting transfers between devices, shift(): return lax.ppermute(value, AXES, pairs)  31.5 us
    ppermute x3, starting transfers between devices, across(): lax.ppermute(value, AXES, [(d, moved(d, dim, 2)) for d in range(DEVICES)])  6.77 us
    ppermute x3, waiting for transfers between devices, ring_shift(): lax.ppermute(value, AXES, [(d, moved(d, dim, -1 if coords(d)['c'] else 1)...  5.11 us
    dot_general x1, matrix products, shards(): lax.dot_general(hidden, grads, (((0,), (0,)), ((), ())), preferred_elemen...  4.82 us
    ppermute x14, waiting for transfers between devices, swap(): return lax.ppermute(value, AXES, [(d, d ^ 32) for d in range(DEVICES)])  4.19 us
    ppermute x3, waiting for transfers between devices, across(): lax.ppermute(value, AXES, [(d, moved(d, dim, 2)) for d in range(DEVICES)])  3.78 us
  transfers between devices with their start and end apart: 42, of which 27 were waited for; matrix products, arithmetic and copies ran while one was open for 4% of the time, Pallas kernels for 13%

profile of v1, /device:TPU:0, one launch (start us, length us, event | category | flops | bytes accessed | tf_op | source)
XLA Modules:
  0.0 157.2 jit_solution(8247648864011116587)
XLA Ops:
  0.6 0.9 constant_dynamic-update-slice_fusion.1
  1.5 0.8 constant_dynamic-update-slice_fusion
  2.3 3.2 %collective-permute-start.2 = (bf16[3,11776]{1,0:T(4,128)(2,1)S(1)}, bf16[3,11776]{1,0:T(4,128)(2,1)S(1)}, u32[]{:S(2)}, u32[]{:S(2)}) collective-permute-start(bf16[3,11776]{1,0:T(4,128)(2,1)S(1)} %constant_dynamic-update-slice_fusion), channel_id=1, source_target_pairs={{0,3},{1,0},{2,1},{3,2},{4,7},{5,4},{6,5},{7,6},{8,11},{9,8},{10,9... | collective-permute-start | bytes 211976 | tf_op jit(solution)/shard_map/ppermute | solution.py:45
  5.5 0.6 collective-permute-start.1
  6.1 1.0 collective-permute-start
  7.1 0.6 collective-permute-done.2
  7.6 4.0 %collective-permute-done.1 = bf16[3,11776]{1,0:T(4,128)(2,1)S(1)} collective-permute-done((bf16[3,11776]{1,0:T(4,128)(2,1)S(1)}, bf16[3,11776]{1,0:T(4,128)(2,1)S(1)}, u32[]{:S(2)}, u32[]{:S(2)}) %collective-permute-start.1) | collective-permute-done | bytes 70688 | tf_op jit(solution)/shard_map/ppermute | solution.py:45
  11.6 0.9 collective-permute-done
  12.5 0.3 pad_maximum_fusion.1
  12.8 2.8 %collective-permute-start.5 = (bf16[12,11776]{1,0:T(8,128)(2,1)S(1)}, bf16[12,11776]{1,0:T(8,128)(2,1)S(1)}, u32[]{:S(2)}, u32[]{:S(2)}) collective-permute-start(bf16[12,11776]{1,0:T(8,128)(2,1)S(1)} %pad_maximum_fusion.1), channel_id=1, source_target_pairs={{0,12},{1,13},{2,14},{3,15},{4,0},{5,1},{6,2},{7,3},{8,4},{9,5},{1... | collective-permute-start | bytes 847880 | tf_op jit(solution)/shard_map/ppermute | solution.py:45
  15.7 0.8 collective-permute-start.4
  16.5 0.9 collective-permute-start.3
  17.4 7.5 %collective-permute-done.5 = bf16[12,11776]{1,0:T(8,128)(2,1)S(1)} collective-permute-done((bf16[12,11776]{1,0:T(8,128)(2,1)S(1)}, bf16[12,11776]{1,0:T(8,128)(2,1)S(1)}, u32[]{:S(2)}, u32[]{:S(2)}) %collective-permute-start.5) | collective-permute-done | bytes 282656 | tf_op jit(solution)/shard_map/ppermute | solution.py:45
  24.9 3.9 %collective-permute-done.3 = bf16[12,11776]{1,0:T(8,128)(2,1)S(1)} collective-permute-done((bf16[12,11776]{1,0:T(8,128)(2,1)S(1)}, bf16[12,11776]{1,0:T(8,128)(2,1)S(1)}, u32[]{:S(2)}, u32[]{:S(2)}) %collective-permute-start.3) | collective-permute-done | bytes 282656 | tf_op jit(solution)/shard_map/ppermute | solution.py:45
  29.1 4.1 %collective-permute-start.7 = (bf16[48,8192]{1,0:T(8,128)(2,1)S(1)}, bf16[48,8192]{1,0:T(8,128)(2,1)S(1)}, u32[]{:S(2)}, u32[]{:S(2)}) collective-permute-start(bf16[48,8192]{1,0:T(8,128)(2,1)S(1)} %pad_maximum_fusion.refs_0_), channel_id=1, source_target_pairs={{0,80},{1,81},{2,82},{3,83},{4,84},{5,85},{6,86},{7,87},{8,88},{9,... | collective-permute-start | bytes 2359304 | tf_op jit(solution)/shard_map/ppermute | solution.py:45
  33.5 9.2 %collective-permute-done.7.refs_4_ = bf16[48,8192]{1,0:T(8,128)(2,1)S(1)} collective-permute-done((bf16[48,8192]{1,0:T(8,128)(2,1)S(1)}, bf16[48,8192]{1,0:T(8,128)(2,1)S(1)}, u32[]{:S(2)}, u32[]{:S(2)}) %collective-permute-start.7) | collective-permute-done | bytes 786464 | tf_op jit(solution)/shard_map/ppermute | solution.py:45
  42.7 3.7 %collective-permute-done.6.refs_1_ = bf16[48,8192]{1,0:T(8,128)(2,1)S(1)} collective-permute-done((bf16[48,8192]{1,0:T(8,128)(2,1)S(1)}, bf16[48,8192]{1,0:T(8,128)(2,1)S(1)}, u32[]{:S(2)}, u32[]{:S(2)}) %collective-permute-start.6) | collective-permute-done | bytes 786464 | tf_op jit(solution)/shard_map/ppermute | solution.py:45
  46.5 2.1 %collective-permute-start.11 = (bf16[24,8192]{1,0:T(8,128)(2,1)S(1)}, bf16[24,8192]{1,0:T(8,128)(2,1)}, u32[]{:S(2)}, u32[]{:S(2)}) collective-permute-start(bf16[24,8192]{1,0:T(8,128)(2,1)S(1)} %slice.461), channel_id=1, source_target_pairs={{0,64},{1,65},{2,66},{3,67},{4,68},{5,69},{6,70},{7,71},{8,72},{9,... | collective-permute-start | bytes 1179656 | tf_op jit(solution)/shard_map/ppermute | solution.py:45
  48.6 0.5 collective-permute-start.17
  49.1 5.2 %collective-permute-done.12.refs_3_ = bf16[24,8192]{1,0:T(8,128)(2,1)} collective-permute-done((bf16[24,8192]{1,0:T(8,128)(2,1)S(1)}, bf16[24,8192]{1,0:T(8,128)(2,1)}, u32[]{:S(2)}, u32[]{:S(2)}) %collective-permute-start.12) | collective-permute-done | bytes 393248 | tf_op jit(solution)/shard_map/ppermute | solution.py:45
  54.4 1.3 collective-permute-done.11.refs_2_
  55.9 0.6 collective-permute-start.18
  56.4 1.2 collective-permute-start.10
  57.8 1.5 collective-permute-start.9
  59.3 13.5 %shard_map.85.refs_9_.t_ref = f32[384,768]{1,0:T(8,128)} custom-call(bf16[48,8192]{1,0:T(8,128)(2,1)S(1)} %pad_maximum_fusion.refs_0_, bf16[48,8192]{1,0:T(8,128)(2,1)S(1)} %collective-permute-done.6.refs_1_, bf16[24,8192]{1,0:T(8,128)(2,1)} %collective-permute-done.11.refs_2_, bf16[24,8192]{1,0:T(8,128)(2,1)} %collective-permute-done.12.refs_3_, ...), custom_call_target="tpu_custom_call" | custom-call | flops 4831838208 | bytes 4194304 | tf_op jit(solution)/shard_map/pallas_call | solution.py:228
  73.0 0.5 collective-permute-start.20
  73.6 1.2 collective-permute-done.19.refs_5_
  74.8 0.5 collective-permute-done.20.refs_6_
  75.3 0.5 collective-permute-done.21.refs_7_
  75.8 10.0 %shard_map.86 = (f32[384,768]{1,0:T(8,128)S(1)}, bf16[384,3584]{1,0:T(8,128)(2,1)}, f32[8,384]{1,0:T(8,128)S(1)}) custom-call(bf16[48,3584]{1,0:T(8,128)(2,1)S(1)} %pad_maximum_fusion.2.refs_0_, bf16[48,3584]{1,0:T(8,128)(2,1)} %collective-permute-done.8.refs_1_, bf16[48,3584]{1,0:T(8,128)(2,1)} %collective-permute-done.9.refs_2_, ...), custom_call_target="tpu_custom_call" | custom-call | flops 2113929216 | bytes 4194304 | tf_op jit(solution)/shard_map/pallas_call | solution.py:228
  85.9 1.0 copy-done
  87.0 1.0 collective-permute-done.22
  88.3 2.0 %collective-permute-start.25 = (f32[8,384]{1,0:T(8,128)S(1)}, f32[8,384]{1,0:T(8,128)S(1)}, u32[]{:S(2)}, u32[]{:S(2)}) collective-permute-start(f32[8,384]{1,0:T(8,128)S(1)} %select_select_fusion.3), channel_id=1, source_target_pairs={{0,2},{1,3},{2,0},{3,1},{4,6},{5,7},{6,4},{7,5},{8,10},{9,11},{10,... | collective-permute-start | bytes 36872 | tf_op jit(solution)/shard_map/ppermute | solution.py:261
  90.3 2.9 %collective-permute-done.23 = f32[8,384]{1,0:T(8,128)S(1)} collective-permute-done((f32[8,384]{1,0:T(8,128)S(1)}, f32[8,384]{1,0:T(8,128)S(1)}, u32[]{:S(2)}, u32[]{:S(2)}) %collective-permute-start.23) | collective-permute-done | bytes 12320 | tf_op jit(solution)/shard_map/ppermute | solution.py:257
  93.2 0.4 collective-permute-done.25
  93.6 0.8 collective-permute-done.24
  94.8 1.3 collective-permute-start.26
  96.0 2.0 %collective-permute-start.28 = (f32[8,384]{1,0:T(8,128)S(1)}, f32[8,384]{1,0:T(8,128)S(1)}, u32[]{:S(2)}, u32[]{:S(2)}) collective-permute-start(f32[8,384]{1,0:T(8,128)S(1)} %select_select_fusion.2), channel_id=1, source_target_pairs={{0,8},{1,9},{2,10},{3,11},{4,12},{5,13},{6,14},{7,15},{8,0},{9,1},... | collective-permute-start | bytes 36872 | tf_op jit(solution)/shard_map/ppermute | solution.py:261
  98.0 1.6 %collective-permute-done.26 = f32[8,384]{1,0:T(8,128)S(1)} collective-permute-done((f32[8,384]{1,0:T(8,128)S(1)}, f32[8,384]{1,0:T(8,128)S(1)}, u32[]{:S(2)}, u32[]{:S(2)}) %collective-permute-start.26) | collective-permute-done | bytes 12320 | tf_op jit(solution)/shard_map/ppermute | solution.py:257
  99.7 1.5 collective-permute-done.28
  101.6 1.6 %collective-permute-start.29 = (f32[8,384]{1,0:T(8,128)S(1)}, f32[8,384]{1,0:T(8,128)S(1)}, u32[]{:S(2)}, u32[]{:S(2)}) collective-permute-start(f32[8,384]{1,0:T(8,128)S(1)} %select_select_fusion.1), channel_id=1, source_target_pairs={{0,64},{1,65},{2,66},{3,67},{4,68},{5,69},{6,70},{7,71},{8,72},{9,... | collective-permute-start | bytes 36872 | tf_op jit(solution)/shard_map/ppermute | solution.py:257
  103.2 2.8 %collective-permute-start.31 = (f32[8,384]{1,0:T(8,128)S(1)}, f32[8,384]{1,0:T(8,128)S(1)}, u32[]{:S(2)}, u32[]{:S(2)}) collective-permute-start(f32[8,384]{1,0:T(8,128)S(1)} %select_select_fusion.1), channel_id=1, source_target_pairs={{0,16},{1,17},{2,18},{3,19},{4,20},{5,21},{6,22},{7,23},{8,24},{9,... | collective-permute-start | bytes 36872 | tf_op jit(solution)/shard_map/ppermute | solution.py:261
  105.9 0.6 collective-permute-done.29
  106.5 1.9 %collective-permute-done.31 = f32[8,384]{1,0:T(8,128)S(1)} collective-permute-done((f32[8,384]{1,0:T(8,128)S(1)}, f32[8,384]{1,0:T(8,128)S(1)}, u32[]{:S(2)}, u32[]{:S(2)}) %collective-permute-start.31) | collective-permute-done | bytes 12320 | tf_op jit(solution)/shard_map/ppermute | solution.py:261
  108.6 0.7 select_select_fusion.stats
  109.3 7.4 %shard_map.87 = (bf16[384,768]{1,0:T(8,128)(2,1)}, bf16[192,3584]{1,0:T(8,128)(2,1)}, f32[1,384]{1,0:T(1,128)}) custom-call(s32[1]{0:T(128)} %bitcast.refs_8_.at_ref, f32[384,768]{1,0:T(8,128)} %shard_map.85.refs_9_.t_ref, f32[384,768]{1,0:T(8,128)} %copy-done, f32[8,384]{1,0:T(8,128)} %select_select_fusion.stats, s32[1,384]{1,0:T(1,128)} %copy-done.1, ...), custom_call_target="tpu_custom_call" | custom-call | flops 1056964608 | bytes 4194304 | tf_op jit(solution)/shard_map/pallas_call | solution.py:228
  116.9 6.4 %shard_map.88 = f32[192,3584]{1,0:T(8,128)} custom-call(bf16[384,768]{1,0:T(8,128)(2,1)} %get-tuple-element.31.grads, bf16[3584,768]{1,0:T(8,128)(2,1)} %w.3), custom_call_target="tpu_custom_call" | custom-call | flops 1056964608 | bytes 4194304 | tf_op jit(solution)/shard_map/pallas_call | solution.py:228
  123.3 2.3 %fusion.36 = (bf16[192,3584]{1,0:T(8,128)(2,1)S(1)}, f32[192,3584]{1,0:T(8,128)S(1)}) fusion(f32[192,3584]{1,0:T(8,128)} %shard_map.88, bf16[192,3584]{1,0:T(8,128)(2,1)S(1)} %collective-permute-done.32), kind=kLoop, calls=%fused_computation.199 | loop fusion | flops 2064384 | bytes 8257536 | tf_op jit(solution)/shard_map/convert.8
  125.8 1.4 collective-permute-start.35
  127.1 1.7 %collective-permute-start.34 = (bf16[48,3584]{1,0:T(8,128)(2,1)S(1)}, bf16[48,3584]{1,0:T(8,128)(2,1)S(1)}, u32[]{:S(2)}, u32[]{:S(2)}) collective-permute-start(bf16[48,3584]{1,0:T(8,128)(2,1)S(1)} %get-tuple-element.62), channel_id=1, source_target_pairs={{0,16},{1,17},{2,18},{3,19},{4,20},{5,21},{6,22},{7,23},{8,24},{9,... | collective-permute-start | bytes 1032200 | tf_op jit(solution)/shard_map/ppermute | solution.py:45
  128.9 2.3 %collective-permute-start.33 = (bf16[48,3584]{1,0:T(8,128)(2,1)S(1)}, bf16[48,3584]{1,0:T(8,128)(2,1)S(1)}, u32[]{:S(2)}, u32[]{:S(2)}) collective-permute-start(bf16[48,3584]{1,0:T(8,128)(2,1)S(1)} %get-tuple-element.63), channel_id=1, source_target_pairs={{0,80},{1,81},{2,82},{3,83},{4,84},{5,85},{6,86},{7,87},{8,88},{9,... | collective-permute-start | bytes 1032200 | tf_op jit(solution)/shard_map/ppermute | solution.py:45
  131.1 4.8 %convolution_convert_fusion = bf16[3584,768]{1,0:T(8,128)(2,1)} fusion(bf16[384,3584]{1,0:T(8,128)(2,1)S(1)} %copy-done.6, bf16[384,768]{1,0:T(8,128)(2,1)S(1)} %copy-done.3), kind=kOutput, calls=%fused_computation | convolution fusion | flops 2116681728 | bytes 8847360 | tf_op jit(solution)/shard_map/dot_general | solution.py:338
  135.9 2.0 %collective-permute-done.35 = bf16[48,3584]{1,0:T(8,128)(2,1)S(1)} collective-permute-done((bf16[48,3584]{1,0:T(8,128)(2,1)S(1)}, bf16[48,3584]{1,0:T(8,128)(2,1)S(1)}, u32[]{:S(2)}, u32[]{:S(2)}) %collective-permute-start.35) | collective-permute-done | bytes 344096 | tf_op jit(solution)/shard_map/ppermute | solution.py:45
  138.0 0.9 collective-permute-done.33
  139.1 2.3 %collective-permute-start.36 = (bf16[12,3584]{1,0:T(8,128)(2,1)S(1)}, bf16[12,3584]{1,0:T(8,128)(2,1)S(1)}, u32[]{:S(2)}, u32[]{:S(2)}) collective-permute-start(bf16[12,3584]{1,0:T(8,128)(2,1)S(1)} %get-tuple-element.64), channel_id=1, source_target_pairs={{0,12},{1,13},{2,14},{3,15},{4,0},{5,1},{6,2},{7,3},{8,4},{9,5},{1... | collective-permute-start | bytes 258056 | tf_op jit(solution)/shard_map/ppermute | solution.py:45
  141.4 1.5 collective-permute-start.37
  143.0 1.0 collective-permute-done.36
  144.0 4.7 %collective-permute-done.38 = bf16[12,3584]{1,0:T(8,128)(2,1)S(1)} collective-permute-done((bf16[12,3584]{1,0:T(8,128)(2,1)S(1)}, bf16[12,3584]{1,0:T(8,128)(2,1)S(1)}, u32[]{:S(2)}, u32[]{:S(2)}) %collective-permute-start.38) | collective-permute-done | bytes 86048 | tf_op jit(solution)/shard_map/ppermute | solution.py:45
  148.8 2.4 %collective-permute-start.39 = (bf16[3,3584]{1,0:T(4,128)(2,1)S(1)}, bf16[3,3584]{1,0:T(4,128)(2,1)S(1)}, u32[]{:S(2)}, u32[]{:S(2)}) collective-permute-start(bf16[3,3584]{1,0:T(4,128)(2,1)S(1)} %get-tuple-element.67), channel_id=1, source_target_pairs={{0,3},{1,0},{2,1},{3,2},{4,7},{5,4},{6,5},{7,6},{8,11},{9,8},{10,9... | collective-permute-start | bytes 64520 | tf_op jit(solution)/shard_map/ppermute | solution.py:45
  151.2 1.5 collective-permute-start.40
  152.7 1.3 dynamic-slice_bitcast_fusion
  154.0 2.3 %collective-permute-done.41 = bf16[3,3584]{1,0:T(4,128)(2,1)S(1)} collective-permute-done((bf16[3,3584]{1,0:T(4,128)(2,1)S(1)}, bf16[3,3584]{1,0:T(4,128)(2,1)S(1)}, u32[]{:S(2)}, u32[]{:S(2)}) %collective-permute-start.41) | collective-permute-done | bytes 21536 | tf_op jit(solution)/shard_map/ppermute | solution.py:45
  156.3 0.3 collective-permute-done.40
  156.6 0.6 fusion
  (103 shorter events, 3.0 us)
Async XLA Ops:
  2.3 5.4 %collective-permute-start.2 = (bf16[3,11776]{1,0:T(4,128)(2,1)S(1)}, bf16[3,11776]{1,0:T(4,128)(2,1)S(1)}, u32[]{:S(2)}, u32[]{:S(2)}) collective-permute-start(bf16[3,11776]{1,0:T(4,128)(2,1)S(1)} %constant_dynamic-update-slice_fusion), channel_id=1, source_target_pairs={{0,3},{1,0},{2,1},{3,2},{4,7},{5,4},{6,5},{7,6},{8,11},{9,8},{10,9... | collective-permute-start | bytes 211976 | tf_op jit(solution)/shard_map/ppermute | solution.py:45
  5.5 6.1 %collective-permute-start.1 = (bf16[3,11776]{1,0:T(4,128)(2,1)S(1)}, bf16[3,11776]{1,0:T(4,128)(2,1)S(1)}, u32[]{:S(2)}, u32[]{:S(2)}) collective-permute-start(bf16[3,11776]{1,0:T(4,128)(2,1)S(1)} %constant_dynamic-update-slice_fusion), channel_id=1, source_target_pairs={{0,2},{1,3},{2,0},{3,1},{4,6},{5,7},{6,4},{7,5},{8,10},{9,11},{10,... | collective-permute-start | bytes 211976 | tf_op jit(solution)/shard_map/ppermute | solution.py:45
  6.1 6.5 %collective-permute-start = (bf16[3,11776]{1,0:T(4,128)(2,1)S(1)}, bf16[3,11776]{1,0:T(4,128)(2,1)S(1)}, u32[]{:S(2)}, u32[]{:S(2)}) collective-permute-start(bf16[3,11776]{1,0:T(4,128)(2,1)S(1)} %constant_dynamic-update-slice_fusion), channel_id=1, source_target_pairs={{0,1},{1,2},{2,3},{3,0},{4,5},{5,6},{6,7},{7,4},{8,9},{9,10},{10,1... | collective-permute-start | bytes 211976 | tf_op jit(solution)/shard_map/ppermute | solution.py:45
  12.8 12.0 %collective-permute-start.5 = (bf16[12,11776]{1,0:T(8,128)(2,1)S(1)}, bf16[12,11776]{1,0:T(8,128)(2,1)S(1)}, u32[]{:S(2)}, u32[]{:S(2)}) collective-permute-start(bf16[12,11776]{1,0:T(8,128)(2,1)S(1)} %pad_maximum_fusion.1), channel_id=1, source_target_pairs={{0,12},{1,13},{2,14},{3,15},{4,0},{5,1},{6,2},{7,3},{8,4},{9,5},{1... | collective-permute-start | bytes 847880 | tf_op jit(solution)/shard_map/ppermute | solution.py:45
  15.7 9.2 %collective-permute-start.4 = (bf16[12,11776]{1,0:T(8,128)(2,1)S(1)}, bf16[12,11776]{1,0:T(8,128)(2,1)S(1)}, u32[]{:S(2)}, u32[]{:S(2)}) collective-permute-start(bf16[12,11776]{1,0:T(8,128)(2,1)S(1)} %pad_maximum_fusion.1), channel_id=1, source_target_pairs={{0,8},{1,9},{2,10},{3,11},{4,12},{5,13},{6,14},{7,15},{8,0},{9,1},... | collective-permute-start | bytes 847880 | tf_op jit(solution)/shard_map/ppermute | solution.py:45
  16.5 12.3 %collective-permute-start.3 = (bf16[12,11776]{1,0:T(8,128)(2,1)S(1)}, bf16[12,11776]{1,0:T(8,128)(2,1)S(1)}, u32[]{:S(2)}, u32[]{:S(2)}) collective-permute-start(bf16[12,11776]{1,0:T(8,128)(2,1)S(1)} %pad_maximum_fusion.1), channel_id=1, source_target_pairs={{0,4},{1,5},{2,6},{3,7},{4,8},{5,9},{6,10},{7,11},{8,12},{9,13},{1... | collective-permute-start | bytes 847880 | tf_op jit(solution)/shard_map/ppermute | solution.py:45
  28.8 26.9 %copy-start.4 = (s32[384]{0:T(512)S(1)}, s32[384]{0:T(512)}, u32[]{:S(2)}) copy-start(s32[384]{0:T(512)} %param.11) | copy-start | bytes 4612
  29.1 13.6 %collective-permute-start.7 = (bf16[48,8192]{1,0:T(8,128)(2,1)S(1)}, bf16[48,8192]{1,0:T(8,128)(2,1)S(1)}, u32[]{:S(2)}, u32[]{:S(2)}) collective-permute-start(bf16[48,8192]{1,0:T(8,128)(2,1)S(1)} %pad_maximum_fusion.refs_0_), channel_id=1, source_target_pairs={{0,80},{1,81},{2,82},{3,83},{4,84},{5,85},{6,86},{7,87},{8,88},{9,... | collective-permute-start | bytes 2359304 | tf_op jit(solution)/shard_map/ppermute | solution.py:45
  33.2 13.2 %collective-permute-start.6 = (bf16[48,8192]{1,0:T(8,128)(2,1)S(1)}, bf16[48,8192]{1,0:T(8,128)(2,1)S(1)}, u32[]{:S(2)}, u32[]{:S(2)}) collective-permute-start(bf16[48,8192]{1,0:T(8,128)(2,1)S(1)} %pad_maximum_fusion.refs_0_), channel_id=1, source_target_pairs={{0,64},{1,65},{2,66},{3,67},{4,68},{5,69},{6,70},{7,71},{8,72},{9,... | collective-permute-start | bytes 2359304 | tf_op jit(solution)/shard_map/ppermute | solution.py:45
  33.2 22.7 %collective-permute-start.13 = (bf16[48,8192]{1,0:T(8,128)(2,1)S(1)}, bf16[48,8192]{1,0:T(8,128)(2,1)S(1)}, u32[]{:S(2)}, u32[]{:S(2)}) collective-permute-start(bf16[48,8192]{1,0:T(8,128)(2,1)S(1)} %pad_maximum_fusion.refs_0_), channel_id=1, source_target_pairs={{0,32},{1,33},{2,34},{3,35},{4,36},{5,37},{6,38},{7,39},{8,40},{9,... | collective-permute-start | bytes 2359304 | tf_op jit(solution)/shard_map/ppermute | solution.py:40
  46.4 8.0 %collective-permute-start.12 = (bf16[24,8192]{1,0:T(8,128)(2,1)S(1)}, bf16[24,8192]{1,0:T(8,128)(2,1)}, u32[]{:S(2)}, u32[]{:S(2)}) collective-permute-start(bf16[24,8192]{1,0:T(8,128)(2,1)S(1)} %slice.462), channel_id=1, source_target_pairs={{0,80},{1,81},{2,82},{3,83},{4,84},{5,85},{6,86},{7,87},{8,88},{9,... | collective-permute-start | bytes 1179656 | tf_op jit(solution)/shard_map/ppermute | solution.py:45
  46.5 9.2 %collective-permute-start.11 = (bf16[24,8192]{1,0:T(8,128)(2,1)S(1)}, bf16[24,8192]{1,0:T(8,128)(2,1)}, u32[]{:S(2)}, u32[]{:S(2)}) collective-permute-start(bf16[24,8192]{1,0:T(8,128)(2,1)S(1)} %slice.461), channel_id=1, source_target_pairs={{0,64},{1,65},{2,66},{3,67},{4,68},{5,69},{6,70},{7,71},{8,72},{9,... | collective-permute-start | bytes 1179656 | tf_op jit(solution)/shard_map/ppermute | solution.py:45
  48.6 10.7 %collective-permute-start.14 = (bf16[48,8192]{1,0:T(8,128)(2,1)S(1)}, bf16[48,8192]{1,0:T(8,128)(2,1)}, u32[]{:S(2)}, u32[]{:S(2)}) collective-permute-start(bf16[48,8192]{1,0:T(8,128)(2,1)S(1)} %collective-permute-done.6.refs_1_), channel_id=1, source_target_pairs={{0,32},{1,33},{2,34},{3,35},{4,36},{5,37},{6,38},{7,39},{8,40},{9,... | collective-permute-start | bytes 2359304 | tf_op jit(solution)/shard_map/ppermute | solution.py:40
  48.6 10.7 %collective-permute-start.17 = (bf16[48,8192]{1,0:T(8,128)(2,1)S(1)}, bf16[48,8192]{1,0:T(8,128)(2,1)}, u32[]{:S(2)}, u32[]{:S(2)}) collective-permute-start(bf16[48,8192]{1,0:T(8,128)(2,1)S(1)} %collective-permute-done.7.refs_4_), channel_id=1, source_target_pairs={{0,32},{1,33},{2,34},{3,35},{4,36},{5,37},{6,38},{7,39},{8,40},{9,... | collective-permute-start | bytes 2359304 | tf_op jit(solution)/shard_map/ppermute | solution.py:40
  54.4 2.1 %collective-permute-start.16 = (bf16[24,8192]{1,0:T(8,128)(2,1)}, bf16[24,8192]{1,0:T(8,128)(2,1)}, u32[]{:S(2)}, u32[]{:S(2)}) collective-permute-start(bf16[24,8192]{1,0:T(8,128)(2,1)} %collective-permute-done.12.refs_3_), channel_id=1, source_target_pairs={{0,32},{1,33},{2,34},{3,35},{4,36},{5,37},{6,38},{7,39},{8,40},{9,... | collective-permute-start | bytes 1179656 | tf_op jit(solution)/shard_map/ppermute | solution.py:40
  55.7 2.1 %collective-permute-start.15 = (bf16[24,8192]{1,0:T(8,128)(2,1)}, bf16[24,8192]{1,0:T(8,128)(2,1)}, u32[]{:S(2)}, u32[]{:S(2)}) collective-permute-start(bf16[24,8192]{1,0:T(8,128)(2,1)} %collective-permute-done.11.refs_2_), channel_id=1, source_target_pairs={{0,32},{1,33},{2,34},{3,35},{4,36},{5,37},{6,38},{7,39},{8,40},{9,... | collective-permute-start | bytes 1179656 | tf_op jit(solution)/shard_map/ppermute | solution.py:40
  55.8 20.0 %copy-start.1 = (s32[1,384]{1,0:T(1,128)}, s32[1,384]{1,0:T(1,128)S(1)}, u32[]{:S(2)}) copy-start(s32[1,384]{1,0:T(1,128)S(1)} %compare_select_fusion.16.refs_10_.tok_row) | copy-start | bytes 4612
  55.9 17.7 %copy-start.5 = (s32[384]{0:T(512)S(1)}, s32[384]{0:T(512)}, u32[]{:S(2)}) copy-start(s32[384]{0:T(512)} %param.10) | copy-start | bytes 4612
  55.9 17.7 %collective-permute-start.18 = (bf16[48,3584]{1,0:T(8,128)(2,1)S(1)}, bf16[48,3584]{1,0:T(8,128)(2,1)}, u32[]{:S(2)}, u32[]{:S(2)}) collective-permute-start(bf16[48,3584]{1,0:T(8,128)(2,1)S(1)} %pad_maximum_fusion.2.refs_0_), channel_id=1, source_target_pairs={{0,32},{1,33},{2,34},{3,35},{4,36},{5,37},{6,38},{7,39},{8,40},{9,... | collective-permute-start | bytes 1032200 | tf_op jit(solution)/shard_map/ppermute | solution.py:40
  56.4 16.4 %collective-permute-start.10 = (bf16[48,3584]{1,0:T(8,128)(2,1)S(1)}, bf16[48,3584]{1,0:T(8,128)(2,1)}, u32[]{:S(2)}, u32[]{:S(2)}) collective-permute-start(bf16[48,3584]{1,0:T(8,128)(2,1)S(1)} %pad_maximum_fusion.2.refs_0_), channel_id=1, source_target_pairs={{0,80},{1,81},{2,82},{3,83},{4,84},{5,85},{6,86},{7,87},{8,88},{9,... | collective-permute-start | bytes 1032200 | tf_op jit(solution)/shard_map/ppermute | solution.py:45
  57.8 15.1 %collective-permute-start.9 = (bf16[48,3584]{1,0:T(8,128)(2,1)S(1)}, bf16[48,3584]{1,0:T(8,128)(2,1)}, u32[]{:S(2)}, u32[]{:S(2)}) collective-permute-start(bf16[48,3584]{1,0:T(8,128)(2,1)S(1)} %pad_maximum_fusion.2.refs_0_), channel_id=1, source_target_pairs={{0,16},{1,17},{2,18},{3,19},{4,20},{5,21},{6,22},{7,23},{8,24},{9,... | collective-permute-start | bytes 1032200 | tf_op jit(solution)/shard_map/ppermute | solution.py:45
  59.3 13.6 %collective-permute-start.8 = (bf16[48,3584]{1,0:T(8,128)(2,1)S(1)}, bf16[48,3584]{1,0:T(8,128)(2,1)}, u32[]{:S(2)}, u32[]{:S(2)}) collective-permute-start(bf16[48,3584]{1,0:T(8,128)(2,1)S(1)} %pad_maximum_fusion.2.refs_0_), channel_id=1, source_target_pairs={{0,64},{1,65},{2,66},{3,67},{4,68},{5,69},{6,70},{7,71},{8,72},{9,... | collective-permute-start | bytes 1032200 | tf_op jit(solution)/shard_map/ppermute | solution.py:45
  72.9 1.9 %collective-permute-start.19 = (bf16[48,3584]{1,0:T(8,128)(2,1)}, bf16[48,3584]{1,0:T(8,128)(2,1)S(1)}, u32[]{:S(2)}, u32[]{:S(2)}) collective-permute-start(bf16[48,3584]{1,0:T(8,128)(2,1)} %collective-permute-done.8.refs_1_), channel_id=1, source_target_pairs={{0,32},{1,33},{2,34},{3,35},{4,36},{5,37},{6,38},{7,39},{8,40},{9,... | collective-permute-start | bytes 1032200 | tf_op jit(solution)/shard_map/ppermute | solution.py:40
  73.0 2.3 %collective-permute-start.20 = (bf16[48,3584]{1,0:T(8,128)(2,1)}, bf16[48,3584]{1,0:T(8,128)(2,1)S(1)}, u32[]{:S(2)}, u32[]{:S(2)}) collective-permute-start(bf16[48,3584]{1,0:T(8,128)(2,1)} %collective-permute-done.9.refs_2_), channel_id=1, source_target_pairs={{0,32},{1,33},{2,34},{3,35},{4,36},{5,37},{6,38},{7,39},{8,40},{9,... | collective-permute-start | bytes 1032200 | tf_op jit(solution)/shard_map/ppermute | solution.py:40
  73.5 2.3 %collective-permute-start.21 = (bf16[48,3584]{1,0:T(8,128)(2,1)}, bf16[48,3584]{1,0:T(8,128)(2,1)S(1)}, u32[]{:S(2)}, u32[]{:S(2)}) collective-permute-start(bf16[48,3584]{1,0:T(8,128)(2,1)} %collective-permute-done.10.refs_3_), channel_id=1, source_target_pairs={{0,32},{1,33},{2,34},{3,35},{4,36},{5,37},{6,38},{7,39},{8,40},{9,... | collective-permute-start | bytes 1032200 | tf_op jit(solution)/shard_map/ppermute | solution.py:40
  73.6 12.3 %copy-start.2 = (s32[1,384]{1,0:T(1,128)}, s32[1,384]{1,0:T(1,128)S(1)}, u32[]{:S(2)}) copy-start(s32[1,384]{1,0:T(1,128)S(1)} %broadcast_in_dim.37.refs_11_.labels) | copy-start | bytes 4612
  85.9 1.0 copy-start
  86.9 1.2 collective-permute-start.22
  88.3 4.9 %collective-permute-start.23 = (f32[8,384]{1,0:T(8,128)S(1)}, f32[8,384]{1,0:T(8,128)S(1)}, u32[]{:S(2)}, u32[]{:S(2)}) collective-permute-start(f32[8,384]{1,0:T(8,128)S(1)} %select_select_fusion.3), channel_id=1, source_target_pairs={{0,1},{1,2},{2,3},{3,0},{4,5},{5,6},{6,7},{7,4},{8,9},{9,10},{10,1... | collective-permute-start | bytes 36872 | tf_op jit(solution)/shard_map/ppermute | solution.py:257
  88.3 5.3 %collective-permute-start.25 = (f32[8,384]{1,0:T(8,128)S(1)}, f32[8,384]{1,0:T(8,128)S(1)}, u32[]{:S(2)}, u32[]{:S(2)}) collective-permute-start(f32[8,384]{1,0:T(8,128)S(1)} %select_select_fusion.3), channel_id=1, source_target_pairs={{0,2},{1,3},{2,0},{3,1},{4,6},{5,7},{6,4},{7,5},{8,10},{9,11},{10,... | collective-permute-start | bytes 36872 | tf_op jit(solution)/shard_map/ppermute | solution.py:261
  93.2 1.2 collective-permute-start.24
  94.8 4.9 %collective-permute-start.26 = (f32[8,384]{1,0:T(8,128)S(1)}, f32[8,384]{1,0:T(8,128)S(1)}, u32[]{:S(2)}, u32[]{:S(2)}) collective-permute-start(f32[8,384]{1,0:T(8,128)S(1)} %select_select_fusion.2), channel_id=1, source_target_pairs={{0,4},{1,5},{2,6},{3,7},{4,8},{5,9},{6,10},{7,11},{8,12},{9,13},{1... | collective-permute-start | bytes 36872 | tf_op jit(solution)/shard_map/ppermute | solution.py:257
  96.0 5.2 %collective-permute-start.28 = (f32[8,384]{1,0:T(8,128)S(1)}, f32[8,384]{1,0:T(8,128)S(1)}, u32[]{:S(2)}, u32[]{:S(2)}) collective-permute-start(f32[8,384]{1,0:T(8,128)S(1)} %select_select_fusion.2), channel_id=1, source_target_pairs={{0,8},{1,9},{2,10},{3,11},{4,12},{5,13},{6,14},{7,15},{8,0},{9,1},... | collective-permute-start | bytes 36872 | tf_op jit(solution)/shard_map/ppermute | solution.py:261
  99.7 1.5 collective-permute-start.27
  101.6 4.9 %collective-permute-start.29 = (f32[8,384]{1,0:T(8,128)S(1)}, f32[8,384]{1,0:T(8,128)S(1)}, u32[]{:S(2)}, u32[]{:S(2)}) collective-permute-start(f32[8,384]{1,0:T(8,128)S(1)} %select_select_fusion.1), channel_id=1, source_target_pairs={{0,64},{1,65},{2,66},{3,67},{4,68},{5,69},{6,70},{7,71},{8,72},{9,... | collective-permute-start | bytes 36872 | tf_op jit(solution)/shard_map/ppermute | solution.py:257
  103.2 5.2 %collective-permute-start.31 = (f32[8,384]{1,0:T(8,128)S(1)}, f32[8,384]{1,0:T(8,128)S(1)}, u32[]{:S(2)}, u32[]{:S(2)}) collective-permute-start(f32[8,384]{1,0:T(8,128)S(1)} %select_select_fusion.1), channel_id=1, source_target_pairs={{0,16},{1,17},{2,18},{3,19},{4,20},{5,21},{6,22},{7,23},{8,24},{9,... | collective-permute-start | bytes 36872 | tf_op jit(solution)/shard_map/ppermute | solution.py:261
  106.5 1.9 %collective-permute-start.30 = (f32[8,384]{1,0:T(8,128)S(1)}, f32[8,384]{1,0:T(8,128)S(1)}, u32[]{:S(2)}, u32[]{:S(2)}) collective-permute-start(f32[8,384]{1,0:T(8,128)S(1)} %collective-permute-done.29), channel_id=1, source_target_pairs={{0,32},{1,33},{2,34},{3,35},{4,36},{5,37},{6,38},{7,39},{8,40},{9,... | collective-permute-start | bytes 36872 | tf_op jit(solution)/shard_map/ppermute | solution.py:40
  116.7 6.7 %collective-permute-start.32 = (bf16[192,3584]{1,0:T(8,128)(2,1)}, bf16[192,3584]{1,0:T(8,128)(2,1)S(1)}, u32[]{:S(2)}, u32[]{:S(2)}) collective-permute-start(bf16[192,3584]{1,0:T(8,128)(2,1)} %get-tuple-element.32), channel_id=1, source_target_pairs={{0,32},{1,33},{2,34},{3,35},{4,36},{5,37},{6,38},{7,39},{8,40},{9,... | collective-permute-start | bytes 4128776 | tf_op jit(solution)/shard_map/ppermute | solution.py:40
  123.3 7.8 %copy-start.3 = (bf16[384,768]{1,0:T(8,128)(2,1)S(1)}, bf16[384,768]{1,0:T(8,128)(2,1)}, u32[]{:S(2)}) copy-start(bf16[384,768]{1,0:T(8,128)(2,1)} %get-tuple-element.31.grads) | copy-start | bytes 1769476
  123.3 7.8 %copy-start.6 = (bf16[384,3584]{1,0:T(8,128)(2,1)S(1)}, bf16[384,3584]{1,0:T(8,128)(2,1)}, u32[]{:S(2)}) copy-start(bf16[384,3584]{1,0:T(8,128)(2,1)} %get-tuple-element.33) | copy-start | bytes 8257540
  125.8 12.2 %collective-permute-start.35 = (bf16[48,3584]{1,0:T(8,128)(2,1)S(1)}, bf16[48,3584]{1,0:T(8,128)(2,1)S(1)}, u32[]{:S(2)}, u32[]{:S(2)}) collective-permute-start(bf16[48,3584]{1,0:T(8,128)(2,1)S(1)} %get-tuple-element.61), channel_id=1, source_target_pairs={{0,64},{1,65},{2,66},{3,67},{4,68},{5,69},{6,70},{7,71},{8,72},{9,... | collective-permute-start | bytes 1032200 | tf_op jit(solution)/shard_map/ppermute | solution.py:45
  127.1 10.9 %collective-permute-start.34 = (bf16[48,3584]{1,0:T(8,128)(2,1)S(1)}, bf16[48,3584]{1,0:T(8,128)(2,1)S(1)}, u32[]{:S(2)}, u32[]{:S(2)}) collective-permute-start(bf16[48,3584]{1,0:T(8,128)(2,1)S(1)} %get-tuple-element.62), channel_id=1, source_target_pairs={{0,16},{1,17},{2,18},{3,19},{4,20},{5,21},{6,22},{7,23},{8,24},{9,... | collective-permute-start | bytes 1032200 | tf_op jit(solution)/shard_map/ppermute | solution.py:45
  128.9 10.0 %collective-permute-start.33 = (bf16[48,3584]{1,0:T(8,128)(2,1)S(1)}, bf16[48,3584]{1,0:T(8,128)(2,1)S(1)}, u32[]{:S(2)}, u32[]{:S(2)}) collective-permute-start(bf16[48,3584]{1,0:T(8,128)(2,1)S(1)} %get-tuple-element.63), channel_id=1, source_target_pairs={{0,80},{1,81},{2,82},{3,83},{4,84},{5,85},{6,86},{7,87},{8,88},{9,... | collective-permute-start | bytes 1032200 | tf_op jit(solution)/shard_map/ppermute | solution.py:45
  139.1 4.9 %collective-permute-start.36 = (bf16[12,3584]{1,0:T(8,128)(2,1)S(1)}, bf16[12,3584]{1,0:T(8,128)(2,1)S(1)}, u32[]{:S(2)}, u32[]{:S(2)}) collective-permute-start(bf16[12,3584]{1,0:T(8,128)(2,1)S(1)} %get-tuple-element.64), channel_id=1, source_target_pairs={{0,12},{1,13},{2,14},{3,15},{4,0},{5,1},{6,2},{7,3},{8,4},{9,5},{1... | collective-permute-start | bytes 258056 | tf_op jit(solution)/shard_map/ppermute | solution.py:45
  141.4 7.2 %collective-permute-start.38 = (bf16[12,3584]{1,0:T(8,128)(2,1)S(1)}, bf16[12,3584]{1,0:T(8,128)(2,1)S(1)}, u32[]{:S(2)}, u32[]{:S(2)}) collective-permute-start(bf16[12,3584]{1,0:T(8,128)(2,1)S(1)} %get-tuple-element.65), channel_id=1, source_target_pairs={{0,4},{1,5},{2,6},{3,7},{4,8},{5,9},{6,10},{7,11},{8,12},{9,13},{1... | collective-permute-start | bytes 258056 | tf_op jit(solution)/shard_map/ppermute | solution.py:45
  141.4 7.2 %collective-permute-start.37 = (bf16[12,3584]{1,0:T(8,128)(2,1)S(1)}, bf16[12,3584]{1,0:T(8,128)(2,1)S(1)}, u32[]{:S(2)}, u32[]{:S(2)}) collective-permute-start(bf16[12,3584]{1,0:T(8,128)(2,1)S(1)} %get-tuple-element.66), channel_id=1, source_target_pairs={{0,8},{1,9},{2,10},{3,11},{4,12},{5,13},{6,14},{7,15},{8,0},{9,1},... | collective-permute-start | bytes 258056 | tf_op jit(solution)/shard_map/ppermute | solution.py:45
  148.8 5.2 %collective-permute-start.39 = (bf16[3,3584]{1,0:T(4,128)(2,1)S(1)}, bf16[3,3584]{1,0:T(4,128)(2,1)S(1)}, u32[]{:S(2)}, u32[]{:S(2)}) collective-permute-start(bf16[3,3584]{1,0:T(4,128)(2,1)S(1)} %get-tuple-element.67), channel_id=1, source_target_pairs={{0,3},{1,0},{2,1},{3,2},{4,7},{5,4},{6,5},{7,6},{8,11},{9,8},{10,9... | collective-permute-start | bytes 64520 | tf_op jit(solution)/shard_map/ppermute | solution.py:45
  151.2 5.1 %collective-permute-start.41 = (bf16[3,3584]{1,0:T(4,128)(2,1)S(1)}, bf16[3,3584]{1,0:T(4,128)(2,1)S(1)}, u32[]{:S(2)}, u32[]{:S(2)}) collective-permute-start(bf16[3,3584]{1,0:T(4,128)(2,1)S(1)} %get-tuple-element.68), channel_id=1, source_target_pairs={{0,1},{1,2},{2,3},{3,0},{4,5},{5,6},{6,7},{7,4},{8,9},{9,10},{10,1... | collective-permute-start | bytes 64520 | tf_op jit(solution)/shard_map/ppermute | solution.py:45
  151.2 5.4 %collective-permute-start.40 = (bf16[3,3584]{1,0:T(4,128)(2,1)S(1)}, bf16[3,3584]{1,0:T(4,128)(2,1)S(1)}, u32[]{:S(2)}, u32[]{:S(2)}) collective-permute-start(bf16[3,3584]{1,0:T(4,128)(2,1)S(1)} %get-tuple-element.69), channel_id=1, source_target_pairs={{0,2},{1,3},{2,0},{3,1},{4,6},{5,7},{6,4},{7,5},{8,10},{9,11},{10,... | collective-permute-start | bytes 64520 | tf_op jit(solution)/shard_map/ppermute | solution.py:45

commit v2 on v1

--- a/solution.py
+++ b/solution.py
@@ -89,8 +89,12 @@
     return jnp.sum(jnp.where(column == lane_ids(), row_values.astype(F32), 0.0), axis=1, keepdims=True).astype(jnp.int32)
 
 
-def teacher_kernel(n, *refs):
-    blocks, (tok_row, owner, w, out, wbuf, sem) = refs[:n], refs[n:]
+def teacher_kernel(n, last, *refs):
+    blocks, refs = refs[:n], refs[n:]
+    if last:
+        (before, source, tok_row, owner, w, out, wbuf, part, sem) = refs
+    else:
+        (w, part, wbuf, sem) = refs
     slots, chunk, _ = wbuf.shape
     count = w.shape[0] // chunk
 
@@ -104,18 +108,20 @@
         columns = slice(i * chunk, (i + 1) * chunk)
         rows = jnp.concatenate([block[:, columns] for block in blocks], axis=0)
         copy(i).wait()
-        part = dot(rows, wbuf[i % slots])
-        out[...] = part if i == 0 else out[...] + part
+        value = dot(rows, wbuf[i % slots])
+        part[...] = value if i == 0 else part[...] + value
         if i + slots < count:
             copy(i + slots).start()
+    if not last:
+        return
     owner_col = pick_column(to_column(tok_row[...]), owner[...])
-    pick = one_hot(owner_col, tok_row[...])
-    high, middle, low = split3(out[...])
+    pick = one_hot(owner_col, source[...])
+    high, middle, low = split3(jnp.concatenate([before[...], part[...]], axis=0))
     out[...] = (dot(pick, high) + dot(pick, middle)) + dot(pick, low)
 
 
 def student_kernel(n, *refs):
-    blocks, (at_ref, t_ref, tok_row, labels, w, s_out, g_out, stats_out, g, wbuf, table, label_at, sem) = refs[:n], refs[n:]
+    blocks, (at_ref, t_ref, tok_row, labels, w, s_out, stats_out, g, wbuf, table, label_at, sem) = refs[:n], refs[n:]
     chunk = 896
     count = w.shape[0] // chunk
 
@@ -129,8 +135,6 @@
     for block in blocks:
         g[pl.ds(at, block.shape[0]), :] = block[...]
         at += block.shape[0]
-    save = pltpu.make_async_copy(g, g_out, sem.at[count])
-    save.start()
     s_out[...] = jnp.zeros_like(s_out)
     tok_col = to_column(tok_row[...])
     label_at[...] = pick_column(tok_col, labels[...]) - at_ref[0]
@@ -141,12 +145,10 @@
         copy(i).wait()
         s_out[...] += dot(g[:, rows], wbuf[rows, :])
 
-    step = 32
+    step = 64
     lane = lax.broadcasted_iota(jnp.int32, (step, 128), 1)
-
-    @pl.loop(0, TOKENS // step)
-    def _(i):
-        rows = pl.ds(pl.multiple_of(i * step, step), step)
+    for i in range(TOKENS // step):
+        rows = slice(i * step, (i + 1) * step)
         t = t_ref[rows, :]
         s = s_out[rows, :]
         t_top = jnp.max(t, axis=1, keepdims=True)
@@ -172,7 +174,6 @@
     to_natural = one_hot(tok_col, lane_ids())
     high, middle, low = split3(table[...].T[:16])
     stats_out[...] = ((dot(high, to_natural) + dot(middle, to_natural)) + dot(low, to_natural))[:8]
-    save.wait()
 
 
 def weight_copies(w, wbuf, sem):
@@ -184,7 +185,7 @@
     return copies
 
 
-def gradient_kernel(vocab, at_ref, t_ref, s_ref, stats, tok_row, labels, w, grads_out, send_out, loss_out, local, label_at, wbuf, sem):
+def gradient_kernel(vocab, at_ref, t_ref, s_ref, stats, tok_row, labels, w, grads_out, send_out, loss_out, wbuf, local, label_at, sem):
     copies = weight_copies(w, wbuf, sem)
     t_top, t_sum, t_moment, t_gap, s_top, s_sum, s_gap, hit = (stats[k : k + 1, :] for k in range(8))
     t_log, s_log = jnp.log(t_sum), jnp.log(s_sum)
@@ -199,11 +200,9 @@
     label_at[...] = pick_column(tok_col, labels[...]) - at_ref[0]
     high, middle, low = split3(rows8)
     local[...] = (dot_nt(from_natural, high) + dot_nt(from_natural, middle)) + dot_nt(from_natural, low)
-    step = 32
-
-    @pl.loop(0, TOKENS // step)
-    def _(i):
-        rows = pl.ds(pl.multiple_of(i * step, step), step)
+    step = 64
+    for i in range(TOKENS // step):
+        rows = slice(i * step, (i + 1) * step)
         t_lse, s_lse, weight, reverse = (local[rows, k : k + 1] for k in range(4))
         t_log = t_ref[rows, :] - t_lse
         s_log = s_ref[rows, :] - s_lse
@@ -218,10 +217,11 @@
         send_out[:, rows] = dot_nt(grads_out[HALF:, :], wbuf[rows, :]).astype(BF16)
 
 
-def keep_kernel(grads, w, out, wbuf, sem):
-    for rows, copy in weight_copies(w, wbuf, sem):
-        copy.wait()
-        out[:, rows] = dot_nt(grads[:HALF, :], wbuf[rows, :])
+def keep_kernel(grads, w, out):
+    chunk = 896
+    for i in range(w.shape[0] // chunk):
+        rows = slice(i * chunk, (i + 1) * chunk)
+        out[:, rows] = dot_nt(grads[:HALF, :], w[rows, :])
 
 
 def call(kernel, out, specs, args, scratch, vmem, flops, out_specs=None):
@@ -269,36 +269,49 @@
     at = (lax.axis_index(AXES) * vocab).astype(jnp.int32)[None]
     label_row, owner_row = labels[None, :], owner_map[None, :]
 
-    block = jnp.concatenate([teacher_hidden, student_hidden], axis=1)
-    block = jnp.concatenate([block] + [shift(block, 0, k) for k in (1, 2, 3)], axis=0)
-    parts = [block] + [shift(block, 1, k) for k in (1, 2, 3)]
-    t0 = jnp.concatenate([v[:, :tk] for v in parts], axis=0)
-    s0 = jnp.concatenate([v[:, tk:] for v in parts], axis=0)
-    t1, t3 = shift(t0, 2, 1), shift(t0, 2, -1)
-    t1, t3, s0 = lax.optimization_barrier((t1, t3, s0))
-    rows = t0.shape[0] // 2
-    t2 = [shift(t1[:rows], 2, 1), shift(t3[rows:], 2, -1)]
-    s_moved = [shift(s0, 2, k) for k in (1, 2, 3)]
-    t2_other = [swap(v) for v in t2]
-    t_blocks = [t0, t1, *t2, t3, swap(t0), swap(t1), *t2_other, swap(t3)]
-
-    n = len(t_blocks)
-    (t_logits,) = call(
-        functools.partial(teacher_kernel, n),
-        [((TOKENS, vocab), F32)],
-        [VMEM] * (n + 2) + [HBM],
-        [*t_blocks, tok_row, owner_row, teacher_head],
-        [pltpu.VMEM((3, 1024, vocab), BF16), pltpu.SemaphoreType.DMA((3,))],
-        48,
-        2 * TOKENS * tk * vocab,
-    )
+    parts = [teacher_hidden] + [shift(teacher_hidden, 0, k) for k in (1, 2, 3)]
+    t = jnp.concatenate(parts, axis=0)
+    t = jnp.concatenate([t] + [shift(t, 1, k) for k in (1, 2, 3)], axis=0)
+    parts = [student_hidden] + [shift(student_hidden, 0, k) for k in (1, 2, 3)]
+    s = jnp.concatenate(parts, axis=0)
+    s = lax.optimization_barrier(jnp.concatenate([s] + [shift(s, 1, k) for k in (1, 2, 3)], axis=0))
+    size = t.shape[0] // 2
+    a, b = t[:size], t[size:]
+    before_a, after_b = shift(a, 2, 1), shift(b, 2, -1)
+    before_b, after_a = shift(b, 2, 1), shift(a, 2, -1)
+    far = [shift(before_a, 2, 1), shift(after_b, 2, -1)]
+    s_moved = [shift(s, 2, k) for k in (1, 2, 3)]
+    near = [before_a, before_b, after_a, after_b]
+    near_other = [swap(v) for v in near]
+    near = [a, b, *near, swap(a), swap(b), *near_other]
+    far = far + [swap(v) for v in far]
+    s0 = s
+
+    def teacher(last, blocks, more, specs, scratch):
+        rows = sum(v.shape[0] for v in blocks)
+        return call(
+            functools.partial(teacher_kernel, len(blocks), last),
+            [((TOKENS if last else rows, vocab), F32)],
+            [VMEM] * len(blocks) + specs + [HBM],
+            [*blocks, *more, teacher_head],
+            [pltpu.VMEM((3, 1024, vocab), BF16), *scratch, pltpu.SemaphoreType.DMA((3,))],
+            44,
+            2 * rows * tk * vocab,
+        )[0]
+
+    t_first = teacher(False, near, [], [], [])
+    q = HALF // 4
+    pieces = [tok_row[:, at * q : (at + 1) * q] for at in (0, 1, 3, 4, 5, 7, 2, 6)]
+    source = jnp.concatenate(pieces, axis=1)
+    last_rows = pltpu.VMEM((sum(v.shape[0] for v in far), vocab), F32)
+    t_logits = teacher(True, far, [t_first, source, tok_row, owner_row], [VMEM] * 4, [last_rows])
     *s_moved, t_logits = lax.optimization_barrier((*s_moved, t_logits))
     s_own = [s0, *s_moved]
     s_blocks = s_own + [swap(v) for v in s_own]
     n = len(s_blocks)
-    s_logits, hidden, stats = call(
+    s_logits, stats = call(
         functools.partial(student_kernel, n),
-        [((TOKENS, vocab), F32), ((TOKENS, sk), BF16), ((8, TOKENS), F32)],
+        [((TOKENS, vocab), F32), ((8, TOKENS), F32)],
         [VMEM] * n + [SMEM] + [VMEM] * 3 + [HBM],
         [*s_blocks, at, t_logits, tok_row, label_row, student_head],
         [
@@ -306,11 +319,10 @@
             pltpu.VMEM((sk, vocab), BF16),
             pltpu.VMEM((TOKENS, 128), F32),
             pltpu.VMEM((TOKENS, 1), jnp.int32),
-            pltpu.SemaphoreType.DMA((5,)),
+            pltpu.SemaphoreType.DMA((4,)),
         ],
-        50,
+        44,
         2 * TOKENS * sk * vocab,
-        [VMEM, HBM, VMEM],
     )
 
     stats = merge([stats, swap(stats)])
@@ -318,23 +330,23 @@
         near, far = ring_shift(stats, dim), across(stats, dim)
         stats = merge([stats, near, swap(near), far])
 
-    wscratch = pltpu.VMEM((sk, vocab), BF16)
-    grads, to_other, loss = call(
+    grads, to_other, loss, weights = call(
         functools.partial(gradient_kernel, vocab * DEVICES),
-        [((TOKENS, vocab), BF16), ((HALF, sk), BF16), ((1, TOKENS), F32)],
+        [((TOKENS, vocab), BF16), ((HALF, sk), BF16), ((1, TOKENS), F32), ((sk, vocab), BF16)],
         [SMEM] + [VMEM] * 5 + [HBM],
         [at, t_logits, s_logits, stats, tok_row, label_row, student_head],
-        [pltpu.VMEM((TOKENS, 8), F32), pltpu.VMEM((TOKENS, 1), jnp.int32), wscratch, pltpu.SemaphoreType.DMA((4,))],
-        56,
+        [pltpu.VMEM((TOKENS, 8), F32), pltpu.VMEM((TOKENS, 1), jnp.int32), pltpu.SemaphoreType.DMA((4,))],
+        52,
         TOKENS * sk * vocab,
     )
-    (kept,) = call(keep_kernel, [((HALF, sk), F32)], [VMEM, HBM], [grads, student_head], [wscratch, pltpu.SemaphoreType.DMA((4,))], 56, TOKENS * sk * vocab)
+    (kept,) = call(keep_kernel, [((HALF, sk), F32)], [VMEM] * 2, [grads, weights], [], 52, TOKENS * sk * vocab)
 
     total = kept + swap(to_other).astype(F32)
     for stage in (2, 1, 0):
         size = total.shape[0] // 4
         parts = [shift(total[k * size : (k + 1) * size].astype(BF16), stage, -k) for k in (1, 2, 3)]
         if stage == 2:
+            hidden = jnp.concatenate(s_blocks, axis=0)
             grad_head = lax.dot_general(hidden, grads, (((0,), (0,)), ((), ())), preferred_element_type=F32).astype(BF16)
             total, grad_head, *parts = lax.optimization_barrier((total, grad_head, *parts))
         total = total[:size] + sum(p.astype(F32) for p in parts)

time: 158 us -> 173 us (1.095)
  waiting for transfers between devices: 60.7 us -> 44.3 us
  starting transfers between devices: 43.3 us -> 58.8 us
  local copies, waits for them, and re-layouts: 4.77 us -> 17.6 us
  Pallas kernels: 37.3 us -> 39.2 us
    ppermute x22 -> x30, starting transfers between devices: 31.5 us -> 44.9 us  [shift(): return lax.ppermute(value, AXES, pairs)]
    ppermute x22 -> x30, waiting for transfers between devices: 47.6 us -> 37.1 us  [shift(): return lax.ppermute(value, AXES, pairs)]
    unnamed x15 -> x31, local copies, waits for them, and re-layouts: 1.92 us -> 11.1 us
    concatenate x1 -> x4, local copies, waits for them, and re-layouts: 0.77 us -> 5.18 us  [the longest x1 2.33 us: shards(): jnp.concatenate([s] + [shift(s, 1, k) for k in (1, 2, 3)], axis=0)]
    ppermute x3, waiting for transfers between devices: 5.11 us -> 2.02 us  [ring_shift(): lax.ppermute(value, AXES, [(d, moved(d, dim, -1 if coords(d)['c'] else 1)...]
    pallas_call x4 -> x5, Pallas kernels: 37.3 us -> 39.2 us  [call(): pl.pallas_call(kernel, out_shape=[jax.ShapeDtypeStruct(*o) for o in out],...]
    ppermute x14 -> x17, waiting for transfers between devices: 4.19 us -> 3.01 us  [swap(): return lax.ppermute(value, AXES, [(d, d ^ 32) for d in range(DEVICES)])]
  transfers between devices with their start and end apart: 42 -> 53, of which waited for: 27 -> 23; matrix products, arithmetic and copies ran while one was open for 4% -> 12% of each run, Pallas kernels for 13% -> 14%
where the time goes in v2:
time: 173 us; the launch traced here: 172 us
  starting transfers between devices  58.8 us (34%)
  waiting for transfers between devices  44.3 us (26%)
  Pallas kernels  39.2 us (23%)
  local copies, waits for them, and re-layouts  17.6 us (10%)
  other arithmetic  6 us (3%)
  matrix products  4.82 us (3%)
    ppermute x30, starting transfers between devices, shift(): return lax.ppermute(value, AXES, pairs)  44.9 us
    pallas_call x5, Pallas kernels, call(): pl.pallas_call(kernel, out_shape=[jax.ShapeDtypeStruct(*o) for o in out],...  39.2 us
    ppermute x30, waiting for transfers between devices, shift(): return lax.ppermute(value, AXES, pairs)  37.1 us
    unnamed x31, local copies, waits for them, and re-layouts  11.1 us
    ppermute x3, starting transfers between devices, across(): lax.ppermute(value, AXES, [(d, moved(d, dim, 2)) for d in range(DEVICES)])  8.3 us
    dot_general x1, matrix products, shards(): lax.dot_general(hidden, grads, (((0,), (0,)), ((), ())), preferred_elemen...  4.82 us
  transfers between devices with their start and end apart: 53, of which 23 were waited for; matrix products, arithmetic and copies ran while one was open for 12% of the time, Pallas kernels for 14%

profile of v2, /device:TPU:0, one launch (start us, length us, event | category | flops | bytes accessed | tf_op | source)
XLA Modules:
  0.0 171.8 jit_solution(7726522681999496575)
XLA Ops:
  0.7 3.2 %collective-permute-start.11 = (bf16[3,8192]{1,0:T(4,128)(2,1)}, bf16[3,8192]{1,0:T(4,128)(2,1)S(1)}, u32[]{:S(2)}, u32[]{:S(2)}) collective-permute-start(bf16[3,8192]{1,0:T(4,128)(2,1)} %param.6), channel_id=1, source_target_pairs={{0,3},{1,0},{2,1},{3,2},{4,7},{5,4},{6,5},{7,6},{8,11},{9,8},{10,9... | collective-permute-start | bytes 147464 | tf_op jit(solution)/shard_map/ppermute | solution.py:45
  4.5 1.0 collective-permute-start.9
  5.4 2.3 %collective-permute-start.2 = (bf16[3,3584]{1,0:T(4,128)(2,1)}, bf16[3,3584]{1,0:T(4,128)(2,1)S(1)}, u32[]{:S(2)}, u32[]{:S(2)}) collective-permute-start(bf16[3,3584]{1,0:T(4,128)(2,1)} %param.8), channel_id=1, source_target_pairs={{0,3},{1,0},{2,1},{3,2},{4,7},{5,4},{6,5},{7,6},{8,11},{9,8},{10,9... | collective-permute-start | bytes 64520 | tf_op jit(solution)/shard_map/ppermute | solution.py:45
  7.7 1.7 collective-permute-start.1
  9.9 0.7 collective-permute-done.9
  10.5 1.0 pad_maximum_fusion.1
  11.6 2.8 %collective-permute-start.16 = (bf16[12,8192]{1,0:T(8,128)(2,1)S(1)}, bf16[12,8192]{1,0:T(8,128)(2,1)S(1)}, u32[]{:S(2)}, u32[]{:S(2)}) collective-permute-start(bf16[12,8192]{1,0:T(8,128)(2,1)S(1)} %pad_maximum_fusion.1), channel_id=1, source_target_pairs={{0,12},{1,13},{2,14},{3,15},{4,0},{5,1},{6,2},{7,3},{8,4},{9,5},{1... | collective-permute-start | bytes 589832 | tf_op jit(solution)/shard_map/ppermute | solution.py:45
  14.4 0.8 collective-permute-start.15
  15.2 0.9 collective-permute-start.12
  16.1 0.8 pad_maximum_fusion.2
  17.0 2.4 %collective-permute-start.5 = (bf16[12,3584]{1,0:T(8,128)(2,1)S(1)}, bf16[12,3584]{1,0:T(8,128)(2,1)S(1)}, u32[]{:S(2)}, u32[]{:S(2)}) collective-permute-start(bf16[12,3584]{1,0:T(8,128)(2,1)S(1)} %pad_maximum_fusion.2), channel_id=1, source_target_pairs={{0,12},{1,13},{2,14},{3,15},{4,0},{5,1},{6,2},{7,3},{8,4},{9,5},{1... | collective-permute-start | bytes 258056 | tf_op jit(solution)/shard_map/ppermute | solution.py:45
  19.4 5.7 %collective-permute-done.12 = bf16[12,8192]{1,0:T(8,128)(2,1)S(1)} collective-permute-done((bf16[12,8192]{1,0:T(8,128)(2,1)S(1)}, bf16[12,8192]{1,0:T(8,128)(2,1)S(1)}, u32[]{:S(2)}, u32[]{:S(2)}) %collective-permute-start.12) | collective-permute-done | bytes 196640 | tf_op jit(solution)/shard_map/ppermute | solution.py:45
  25.1 2.0 %concatenate.27.refs_0_ = bf16[24,8192]{1,0:T(8,128)(2,1)S(1)} concatenate(bf16[3,8192]{1,0:T(4,128)(2,1)} %param.6, bf16[3,8192]{1,0:T(4,128)(2,1)S(1)} %collective-permute-done.9, bf16[3,8192]{1,0:T(4,128)(2,1)S(1)} %collective-permute-done.10, bf16[3,8192]{1,0:T(4,128)(2,1)S(1)} %collective-permute-done.11, bf16[12,8192]{1,0:T(8,128)(2,1)S(1)} %collective-permute-done.12), dimensions={0} | concatenate | bytes 786432 | tf_op jit(solution)/shard_map/concatenate | solution.py:274
  27.2 4.1 %collective-permute-start.22 = (bf16[24,8192]{1,0:T(8,128)(2,1)S(1)}, bf16[24,8192]{1,0:T(8,128)(2,1)S(1)}, u32[]{:S(2)}, u32[]{:S(2)}) collective-permute-start(bf16[24,8192]{1,0:T(8,128)(2,1)S(1)} %concatenate.27.refs_0_), channel_id=1, source_target_pairs={{0,80},{1,81},{2,82},{3,83},{4,84},{5,85},{6,86},{7,87},{8,88},{9,... | collective-permute-start | bytes 1179656 | tf_op jit(solution)/shard_map/ppermute | solution.py:45
  31.4 3.3 %collective-permute-start.17 = (bf16[24,8192]{1,0:T(8,128)(2,1)S(1)}, bf16[24,8192]{1,0:T(8,128)(2,1)S(1)}, u32[]{:S(2)}, u32[]{:S(2)}) collective-permute-start(bf16[24,8192]{1,0:T(8,128)(2,1)S(1)} %pad_maximum_fusion.refs_1_), channel_id=1, source_target_pairs={{0,80},{1,81},{2,82},{3,83},{4,84},{5,85},{6,86},{7,87},{8,88},{9,... | collective-permute-start | bytes 1179656 | tf_op jit(solution)/shard_map/ppermute | solution.py:45
  34.7 0.8 collective-permute-start.4
  35.5 5.5 %collective-permute-done.4 = bf16[12,3584]{1,0:T(8,128)(2,1)S(1)} collective-permute-done((bf16[12,3584]{1,0:T(8,128)(2,1)S(1)}, bf16[12,3584]{1,0:T(8,128)(2,1)S(1)}, u32[]{:S(2)}, u32[]{:S(2)}) %collective-permute-start.4) | collective-permute-done | bytes 86048 | tf_op jit(solution)/shard_map/ppermute | solution.py:45
  41.0 6.2 %collective-permute-done.3 = bf16[12,3584]{1,0:T(8,128)(2,1)S(1)} collective-permute-done((bf16[12,3584]{1,0:T(8,128)(2,1)}, bf16[12,3584]{1,0:T(8,128)(2,1)S(1)}, u32[]{:S(2)}, u32[]{:S(2)}) %collective-permute-start.3) | collective-permute-done | bytes 86048 | tf_op jit(solution)/shard_map/ppermute | solution.py:45
  47.8 3.2 %collective-permute-start.18 = (bf16[24,8192]{1,0:T(8,128)(2,1)S(1)}, bf16[24,8192]{1,0:T(8,128)(2,1)}, u32[]{:S(2)}, u32[]{:S(2)}) collective-permute-start(bf16[24,8192]{1,0:T(8,128)(2,1)S(1)} %collective-permute-done.17.refs_5_), channel_id=1, source_target_pairs={{0,80},{1,81},{2,82},{3,83},{4,84},{5,85},{6,86},{7,87},{8,88},{9,... | collective-permute-start | bytes 1179656 | tf_op jit(solution)/shard_map/ppermute | solution.py:45
  51.1 5.2 %collective-permute-done.21.refs_3_ = bf16[24,8192]{1,0:T(8,128)(2,1)} collective-permute-done((bf16[24,8192]{1,0:T(8,128)(2,1)S(1)}, bf16[24,8192]{1,0:T(8,128)(2,1)}, u32[]{:S(2)}, u32[]{:S(2)}) %collective-permute-start.21) | collective-permute-done | bytes 393248 | tf_op jit(solution)/shard_map/ppermute | solution.py:45
  56.3 0.7 copy-done.3
  57.7 2.8 %collective-permute-done.14.refs_0_ = bf16[24,8192]{1,0:T(8,128)(2,1)} collective-permute-done((bf16[24,8192]{1,0:T(8,128)(2,1)S(1)}, bf16[24,8192]{1,0:T(8,128)(2,1)}, u32[]{:S(2)}, u32[]{:S(2)}) %collective-permute-start.14) | collective-permute-done | bytes 393248 | tf_op jit(solution)/shard_map/ppermute | solution.py:45
  61.3 2.3 %concatenate.25.refs_0_ = bf16[48,3584]{1,0:T(8,128)(2,1)S(1)} concatenate(bf16[3,3584]{1,0:T(4,128)(2,1)S(1)} %copy-done.6, bf16[3,3584]{1,0:T(4,128)(2,1)} %copy-done.8, bf16[3,3584]{1,0:T(4,128)(2,1)} %copy-done.7, bf16[3,3584]{1,0:T(4,128)(2,1)S(1)} %collective-permute-done.2, bf16[12,3584]{1,0:T(8,128)(2,1)S(1)} %collective-permute-done.3, ...), dimensions={0} | concatenate | bytes 688128 | tf_op jit(solution)/shard_map/concatenate | solution.py:277
  63.8 0.8 collective-permute-start.7
  64.6 1.4 collective-permute-start.6
  66.0 1.0 copy-done.2
  67.0 1.0 copy-done.4
  68.0 9.2 %shard_map.85.refs_4_ = f32[288,768]{1,0:T(8,128)S(1)} custom-call(bf16[24,8192]{1,0:T(8,128)(2,1)S(1)} %concatenate.27.refs_0_, bf16[24,8192]{1,0:T(8,128)(2,1)S(1)} %pad_maximum_fusion.refs_1_, bf16[24,8192]{1,0:T(8,128)(2,1)S(1)} %collective-permute-done.13.refs_2_, bf16[24,8192]{1,0:T(8,128)(2,1)} %collective-permute-done.21.refs_3_, ...), custom_call_target="tpu_custom_call" | custom-call | flops 3623878656 | bytes 4194304 | tf_op jit(solution)/shard_map/pallas_call | solution.py:228
  77.3 8.8 %shard_map.86.refs_9_.t_ref = f32[384,768]{1,0:T(8,128)S(1)} custom-call(bf16[24,8192]{1,0:T(8,128)(2,1)} %collective-permute-done.14.refs_0_, bf16[24,8192]{1,0:T(8,128)(2,1)} %collective-permute-done.18.refs_1_, bf16[24,8192]{1,0:T(8,128)(2,1)} %collective-permute-done.19.refs_2_, bf16[24,8192]{1,0:T(8,128)(2,1)} %collective-permute-done.20.refs_3_, ...), custom_call_target="tpu_custom_call" | custom-call | flops 1207959552 | bytes 4194304 | tf_op jit(solution)/shard_map/pallas_call | solution.py:228
  87.3 1.0 collective-permute-done.30.refs_5_
  89.2 7.4 %shard_map.87 = (f32[384,768]{1,0:T(8,128)S(1)}, f32[8,384]{1,0:T(8,128)S(1)}) custom-call(bf16[48,3584]{1,0:T(8,128)(2,1)S(1)} %concatenate.25.refs_0_, bf16[48,3584]{1,0:T(8,128)(2,1)} %collective-permute-done.6.refs_1_, bf16[48,3584]{1,0:T(8,128)(2,1)} %collective-permute-done.7.refs_2_, bf16[48,3584]{1,0:T(8,128)(2,1)S(1)} %collective-permute-done.8.refs_3_, ...), custom_call_target="tpu_custom_call" | custom-call | flops 2113929216 | bytes 4194304 | tf_op jit(solution)/shard_map/pallas_call | solution.py:228
  96.7 1.0 copy-done
  98.1 0.8 collective-permute-done.33
  99.1 0.7 collective-permute-start.34
  99.8 2.9 %collective-permute-start.36 = (f32[8,384]{1,0:T(8,128)S(1)}, f32[8,384]{1,0:T(8,128)S(1)}, u32[]{:S(2)}, u32[]{:S(2)}) collective-permute-start(f32[8,384]{1,0:T(8,128)S(1)} %select_select_fusion.3), channel_id=1, source_target_pairs={{0,2},{1,3},{2,0},{3,1},{4,6},{5,7},{6,4},{7,5},{8,10},{9,11},{10,... | collective-permute-start | bytes 36872 | tf_op jit(solution)/shard_map/ppermute | solution.py:261
  102.7 1.3 collective-permute-done.34
  104.1 0.8 constant_dynamic-update-slice_fusion.7
  105.6 0.8 collective-permute-start.37
  106.4 1.7 %constant_dynamic-update-slice_fusion.6 = bf16[384,3584]{1,0:T(8,128)(2,1)} fusion(bf16[384,3584]{1,0:T(8,128)(2,1)} %constant_dynamic-update-slice_fusion.7, bf16[48,3584]{1,0:T(8,128)(2,1)} %collective-permute-done.6.refs_1_), kind=kLoop, calls=%fused_computation.15 | loop fusion | bytes 688128
  108.2 2.6 %collective-permute-start.39 = (f32[8,384]{1,0:T(8,128)S(1)}, f32[8,384]{1,0:T(8,128)S(1)}, u32[]{:S(2)}, u32[]{:S(2)}) collective-permute-start(f32[8,384]{1,0:T(8,128)S(1)} %select_select_fusion.2), channel_id=1, source_target_pairs={{0,8},{1,9},{2,10},{3,11},{4,12},{5,13},{6,14},{7,15},{8,0},{9,1},... | collective-permute-start | bytes 36872 | tf_op jit(solution)/shard_map/ppermute | solution.py:261
  110.7 1.7 %constant_dynamic-update-slice_fusion.5 = bf16[384,3584]{1,0:T(8,128)(2,1)} fusion(bf16[384,3584]{1,0:T(8,128)(2,1)} %constant_dynamic-update-slice_fusion.6, bf16[48,3584]{1,0:T(8,128)(2,1)} %collective-permute-done.7.refs_2_), kind=kLoop, calls=%fused_computation.14 | loop fusion | bytes 688128
  112.5 1.0 collective-permute-done.39
  114.5 0.7 constant_dynamic-update-slice_fusion.4
  115.2 2.8 %collective-permute-start.42 = (f32[8,384]{1,0:T(8,128)S(1)}, f32[8,384]{1,0:T(8,128)S(1)}, u32[]{:S(2)}, u32[]{:S(2)}) collective-permute-start(f32[8,384]{1,0:T(8,128)S(1)} %select_select_fusion.1), channel_id=1, source_target_pairs={{0,16},{1,17},{2,18},{3,19},{4,20},{5,21},{6,22},{7,23},{8,24},{9,... | collective-permute-start | bytes 36872 | tf_op jit(solution)/shard_map/ppermute | solution.py:261
  118.0 0.7 collective-permute-done.40
  118.7 0.8 constant_dynamic-update-slice_fusion.3
  119.5 1.0 collective-permute-done.42
  120.8 7.9 %shard_map.88 = (bf16[384,768]{1,0:T(8,128)(2,1)S(1)}, bf16[192,3584]{1,0:T(8,128)(2,1)}, f32[1,384]{1,0:T(1,128)S(1)}, bf16[3584,768]{1,0:T(8,128)(2,1)}) custom-call(s32[1]{0:T(128)} %bitcast.refs_8_.at_ref, f32[384,768]{1,0:T(8,128)S(1)} %shard_map.86.refs_9_.t_ref, f32[384,768]{1,0:T(8,128)} %copy-done, f32[8,384]{1,0:T(8,128)S(1)} %select_select_fusion.stats, ...), custom_call_target="tpu_custom_call" | custom-call | flops 1056964608 | bytes 4194304 | tf_op jit(solution)/shard_map/pallas_call | solution.py:228
  128.9 0.8 constant_dynamic-update-slice_fusion.2
  129.7 0.8 constant_dynamic-update-slice_fusion.1
  130.4 0.8 constant_dynamic-update-slice_fusion
  131.2 5.9 %shard_map.89 = f32[192,3584]{1,0:T(8,128)} custom-call(bf16[384,768]{1,0:T(8,128)(2,1)S(1)} %get-tuple-element.25.grads, bf16[3584,768]{1,0:T(8,128)(2,1)} %get-tuple-element.26.w), custom_call_target="tpu_custom_call" | custom-call | flops 1056964608 | bytes 4194304 | tf_op jit(solution)/shard_map/pallas_call | solution.py:228
  137.1 2.3 %fusion.36 = (bf16[192,3584]{1,0:T(8,128)(2,1)S(1)}, f32[192,3584]{1,0:T(8,128)S(1)}) fusion(f32[192,3584]{1,0:T(8,128)} %shard_map.89, bf16[192,3584]{1,0:T(8,128)(2,1)S(1)} %collective-permute-done.43), kind=kLoop, calls=%fused_computation.205 | loop fusion | flops 2064384 | bytes 8257536 | tf_op jit(solution)/shard_map/convert.8
  139.6 2.4 %collective-permute-start.46 = (bf16[48,3584]{1,0:T(8,128)(2,1)S(1)}, bf16[48,3584]{1,0:T(8,128)(2,1)S(1)}, u32[]{:S(2)}, u32[]{:S(2)}) collective-permute-start(bf16[48,3584]{1,0:T(8,128)(2,1)S(1)} %get-tuple-element.55), channel_id=1, source_target_pairs={{0,64},{1,65},{2,66},{3,67},{4,68},{5,69},{6,70},{7,71},{8,72},{9,... | collective-permute-start | bytes 1032200 | tf_op jit(solution)/shard_map/ppermute | solution.py:45
  142.0 1.5 collective-permute-start.45
  143.5 1.4 collective-permute-start.44
  144.9 4.8 %convolution_convert_fusion = bf16[3584,768]{1,0:T(8,128)(2,1)} fusion(bf16[384,3584]{1,0:T(8,128)(2,1)S(1)} %copy-done.9, bf16[384,768]{1,0:T(8,128)(2,1)S(1)} %get-tuple-element.25.grads), kind=kOutput, calls=%fused_computation | convolution fusion | flops 2116681728 | bytes 8847360 | tf_op jit(solution)/shard_map/dot_general | solution.py:350
  149.8 2.7 %collective-permute-done.45 = bf16[48,3584]{1,0:T(8,128)(2,1)S(1)} collective-permute-done((bf16[48,3584]{1,0:T(8,128)(2,1)S(1)}, bf16[48,3584]{1,0:T(8,128)(2,1)S(1)}, u32[]{:S(2)}, u32[]{:S(2)}) %collective-permute-start.45) | collective-permute-done | bytes 344096 | tf_op jit(solution)/shard_map/ppermute | solution.py:45
  152.9 3.1 %collective-permute-start.47 = (bf16[12,3584]{1,0:T(8,128)(2,1)S(1)}, bf16[12,3584]{1,0:T(8,128)(2,1)S(1)}, u32[]{:S(2)}, u32[]{:S(2)}) collective-permute-start(bf16[12,3584]{1,0:T(8,128)(2,1)S(1)} %get-tuple-element.58), channel_id=1, source_target_pairs={{0,12},{1,13},{2,14},{3,15},{4,0},{5,1},{6,2},{7,3},{8,4},{9,5},{1... | collective-permute-start | bytes 258056 | tf_op jit(solution)/shard_map/ppermute | solution.py:45
  156.1 2.1 %collective-permute-start.48 = (bf16[12,3584]{1,0:T(8,128)(2,1)S(1)}, bf16[12,3584]{1,0:T(8,128)(2,1)S(1)}, u32[]{:S(2)}, u32[]{:S(2)}) collective-permute-start(bf16[12,3584]{1,0:T(8,128)(2,1)S(1)} %get-tuple-element.60), channel_id=1, source_target_pairs={{0,8},{1,9},{2,10},{3,11},{4,12},{5,13},{6,14},{7,15},{8,0},{9,1},... | collective-permute-start | bytes 258056 | tf_op jit(solution)/shard_map/ppermute | solution.py:45
  158.4 4.9 %collective-permute-done.49 = bf16[12,3584]{1,0:T(8,128)(2,1)S(1)} collective-permute-done((bf16[12,3584]{1,0:T(8,128)(2,1)S(1)}, bf16[12,3584]{1,0:T(8,128)(2,1)S(1)}, u32[]{:S(2)}, u32[]{:S(2)}) %collective-permute-start.49) | collective-permute-done | bytes 86048 | tf_op jit(solution)/shard_map/ppermute | solution.py:45
  163.4 2.4 %collective-permute-start.50 = (bf16[3,3584]{1,0:T(4,128)(2,1)S(1)}, bf16[3,3584]{1,0:T(4,128)(2,1)S(1)}, u32[]{:S(2)}, u32[]{:S(2)}) collective-permute-start(bf16[3,3584]{1,0:T(4,128)(2,1)S(1)} %get-tuple-element.61), channel_id=1, source_target_pairs={{0,3},{1,0},{2,1},{3,2},{4,7},{5,4},{6,5},{7,6},{8,11},{9,8},{10,9... | collective-permute-start | bytes 64520 | tf_op jit(solution)/shard_map/ppermute | solution.py:45
  165.8 2.4 %collective-permute-start.51 = (bf16[3,3584]{1,0:T(4,128)(2,1)S(1)}, bf16[3,3584]{1,0:T(4,128)(2,1)S(1)}, u32[]{:S(2)}, u32[]{:S(2)}) collective-permute-start(bf16[3,3584]{1,0:T(4,128)(2,1)S(1)} %get-tuple-element.63), channel_id=1, source_target_pairs={{0,2},{1,3},{2,0},{3,1},{4,6},{5,7},{6,4},{7,5},{8,10},{9,11},{10,... | collective-permute-start | bytes 64520 | tf_op jit(solution)/shard_map/ppermute | solution.py:45
  168.8 2.1 %collective-permute-done.52 = bf16[3,3584]{1,0:T(4,128)(2,1)S(1)} collective-permute-done((bf16[3,3584]{1,0:T(4,128)(2,1)S(1)}, bf16[3,3584]{1,0:T(4,128)(2,1)S(1)}, u32[]{:S(2)}, u32[]{:S(2)}) %collective-permute-start.52) | collective-permute-done | bytes 21536 | tf_op jit(solution)/shard_map/ppermute | solution.py:45
  (138 shorter events, 10.7 us)
Async XLA Ops:
  0.6 60.7 %copy-start.6 = (bf16[3,3584]{1,0:T(4,128)(2,1)S(1)}, bf16[3,3584]{1,0:T(4,128)(2,1)}, u32[]{:S(2)}) copy-start(bf16[3,3584]{1,0:T(4,128)(2,1)} %param.8) | copy-start | bytes 64516
  0.6 60.6 %copy-start.10 = (s32[384]{0:T(512)S(1)}, s32[384]{0:T(512)}, u32[]{:S(2)}) copy-start(s32[384]{0:T(512)} %param.11) | copy-start | bytes 4612
  0.7 8.8 %collective-permute-start.11 = (bf16[3,8192]{1,0:T(4,128)(2,1)}, bf16[3,8192]{1,0:T(4,128)(2,1)S(1)}, u32[]{:S(2)}, u32[]{:S(2)}) collective-permute-start(bf16[3,8192]{1,0:T(4,128)(2,1)} %param.6), channel_id=1, source_target_pairs={{0,3},{1,0},{2,1},{3,2},{4,7},{5,4},{6,5},{7,6},{8,11},{9,8},{10,9... | collective-permute-start | bytes 147464 | tf_op jit(solution)/shard_map/ppermute | solution.py:45
  3.8 6.0 %collective-permute-start.10 = (bf16[3,8192]{1,0:T(4,128)(2,1)}, bf16[3,8192]{1,0:T(4,128)(2,1)S(1)}, u32[]{:S(2)}, u32[]{:S(2)}) collective-permute-start(bf16[3,8192]{1,0:T(4,128)(2,1)} %param.6), channel_id=1, source_target_pairs={{0,2},{1,3},{2,0},{3,1},{4,6},{5,7},{6,4},{7,5},{8,10},{9,11},{10,... | collective-permute-start | bytes 147464 | tf_op jit(solution)/shard_map/ppermute | solution.py:45
  4.5 6.1 %collective-permute-start.9 = (bf16[3,8192]{1,0:T(4,128)(2,1)}, bf16[3,8192]{1,0:T(4,128)(2,1)S(1)}, u32[]{:S(2)}, u32[]{:S(2)}) collective-permute-start(bf16[3,8192]{1,0:T(4,128)(2,1)} %param.6), channel_id=1, source_target_pairs={{0,1},{1,2},{2,3},{3,0},{4,5},{5,6},{6,7},{7,4},{8,9},{9,10},{10,1... | collective-permute-start | bytes 147464 | tf_op jit(solution)/shard_map/ppermute | solution.py:45
  5.4 9.8 %collective-permute-start.2 = (bf16[3,3584]{1,0:T(4,128)(2,1)}, bf16[3,3584]{1,0:T(4,128)(2,1)S(1)}, u32[]{:S(2)}, u32[]{:S(2)}) collective-permute-start(bf16[3,3584]{1,0:T(4,128)(2,1)} %param.8), channel_id=1, source_target_pairs={{0,3},{1,0},{2,1},{3,2},{4,7},{5,4},{6,5},{7,6},{8,11},{9,8},{10,9... | collective-permute-start | bytes 64520 | tf_op jit(solution)/shard_map/ppermute | solution.py:45
  7.7 8.4 %collective-permute-start.1 = (bf16[3,3584]{1,0:T(4,128)(2,1)}, bf16[3,3584]{1,0:T(4,128)(2,1)S(1)}, u32[]{:S(2)}, u32[]{:S(2)}) collective-permute-start(bf16[3,3584]{1,0:T(4,128)(2,1)} %param.8), channel_id=1, source_target_pairs={{0,2},{1,3},{2,0},{3,1},{4,6},{5,7},{6,4},{7,5},{8,10},{9,11},{10,... | collective-permute-start | bytes 64520 | tf_op jit(solution)/shard_map/ppermute | solution.py:45
  9.4 6.7 %collective-permute-start = (bf16[3,3584]{1,0:T(4,128)(2,1)}, bf16[3,3584]{1,0:T(4,128)(2,1)S(1)}, u32[]{:S(2)}, u32[]{:S(2)}) collective-permute-start(bf16[3,3584]{1,0:T(4,128)(2,1)} %param.8), channel_id=1, source_target_pairs={{0,1},{1,2},{2,3},{3,0},{4,5},{5,6},{6,7},{7,4},{8,9},{9,10},{10,1... | collective-permute-start | bytes 64520 | tf_op jit(solution)/shard_map/ppermute | solution.py:45
  11.6 19.7 %collective-permute-start.16 = (bf16[12,8192]{1,0:T(8,128)(2,1)S(1)}, bf16[12,8192]{1,0:T(8,128)(2,1)S(1)}, u32[]{:S(2)}, u32[]{:S(2)}) collective-permute-start(bf16[12,8192]{1,0:T(8,128)(2,1)S(1)} %pad_maximum_fusion.1), channel_id=1, source_target_pairs={{0,12},{1,13},{2,14},{3,15},{4,0},{5,1},{6,2},{7,3},{8,4},{9,5},{1... | collective-permute-start | bytes 589832 | tf_op jit(solution)/shard_map/ppermute | solution.py:45
  14.4 16.9 %collective-permute-start.15 = (bf16[12,8192]{1,0:T(8,128)(2,1)S(1)}, bf16[12,8192]{1,0:T(8,128)(2,1)S(1)}, u32[]{:S(2)}, u32[]{:S(2)}) collective-permute-start(bf16[12,8192]{1,0:T(8,128)(2,1)S(1)} %pad_maximum_fusion.1), channel_id=1, source_target_pairs={{0,8},{1,9},{2,10},{3,11},{4,12},{5,13},{6,14},{7,15},{8,0},{9,1},... | collective-permute-start | bytes 589832 | tf_op jit(solution)/shard_map/ppermute | solution.py:45
  15.2 9.9 %collective-permute-start.12 = (bf16[12,8192]{1,0:T(8,128)(2,1)S(1)}, bf16[12,8192]{1,0:T(8,128)(2,1)S(1)}, u32[]{:S(2)}, u32[]{:S(2)}) collective-permute-start(bf16[12,8192]{1,0:T(8,128)(2,1)S(1)} %pad_maximum_fusion.1), channel_id=1, source_target_pairs={{0,4},{1,5},{2,6},{3,7},{4,8},{5,9},{6,10},{7,11},{8,12},{9,13},{1... | collective-permute-start | bytes 589832 | tf_op jit(solution)/shard_map/ppermute | solution.py:45
  16.1 9.0 %copy-start.7 = (bf16[3,3584]{1,0:T(4,128)(2,1)}, bf16[3,3584]{1,0:T(4,128)(2,1)S(1)}, u32[]{:S(2)}) copy-start(bf16[3,3584]{1,0:T(4,128)(2,1)S(1)} %collective-permute-done.1) | copy-start | bytes 64516
  16.1 9.0 %copy-start.8 = (bf16[3,3584]{1,0:T(4,128)(2,1)}, bf16[3,3584]{1,0:T(4,128)(2,1)S(1)}, u32[]{:S(2)}) copy-start(bf16[3,3584]{1,0:T(4,128)(2,1)S(1)} %collective-permute-done) | copy-start | bytes 64516
  17.0 18.6 %copy-start.5 = (bf16[12,3584]{1,0:T(8,128)(2,1)}, bf16[12,3584]{1,0:T(8,128)(2,1)S(1)}, u32[]{:S(2)}) copy-start(bf16[12,3584]{1,0:T(8,128)(2,1)S(1)} %pad_maximum_fusion.2) | copy-start | bytes 258052
  17.0 17.7 %collective-permute-start.5 = (bf16[12,3584]{1,0:T(8,128)(2,1)S(1)}, bf16[12,3584]{1,0:T(8,128)(2,1)S(1)}, u32[]{:S(2)}, u32[]{:S(2)}) collective-permute-start(bf16[12,3584]{1,0:T(8,128)(2,1)S(1)} %pad_maximum_fusion.2), channel_id=1, source_target_pairs={{0,12},{1,13},{2,14},{3,15},{4,0},{5,1},{6,2},{7,3},{8,4},{9,5},{1... | collective-permute-start | bytes 258056 | tf_op jit(solution)/shard_map/ppermute | solution.py:45
  27.1 20.1 %collective-permute-start.23 = (bf16[24,8192]{1,0:T(8,128)(2,1)S(1)}, bf16[24,8192]{1,0:T(8,128)(2,1)S(1)}, u32[]{:S(2)}, u32[]{:S(2)}) collective-permute-start(bf16[24,8192]{1,0:T(8,128)(2,1)S(1)} %concatenate.27.refs_0_), channel_id=1, source_target_pairs={{0,32},{1,33},{2,34},{3,35},{4,36},{5,37},{6,38},{7,39},{8,40},{9,... | collective-permute-start | bytes 1179656 | tf_op jit(solution)/shard_map/ppermute | solution.py:40
  27.2 20.1 %collective-permute-start.22 = (bf16[24,8192]{1,0:T(8,128)(2,1)S(1)}, bf16[24,8192]{1,0:T(8,128)(2,1)S(1)}, u32[]{:S(2)}, u32[]{:S(2)}) collective-permute-start(bf16[24,8192]{1,0:T(8,128)(2,1)S(1)} %concatenate.27.refs_0_), channel_id=1, source_target_pairs={{0,80},{1,81},{2,82},{3,83},{4,84},{5,85},{6,86},{7,87},{8,88},{9,... | collective-permute-start | bytes 1179656 | tf_op jit(solution)/shard_map/ppermute | solution.py:45
  31.3 16.5 %collective-permute-start.13 = (bf16[24,8192]{1,0:T(8,128)(2,1)S(1)}, bf16[24,8192]{1,0:T(8,128)(2,1)S(1)}, u32[]{:S(2)}, u32[]{:S(2)}) collective-permute-start(bf16[24,8192]{1,0:T(8,128)(2,1)S(1)} %concatenate.27.refs_0_), channel_id=1, source_target_pairs={{0,64},{1,65},{2,66},{3,67},{4,68},{5,69},{6,70},{7,71},{8,72},{9,... | collective-permute-start | bytes 1179656 | tf_op jit(solution)/shard_map/ppermute | solution.py:45
  31.4 16.4 %collective-permute-start.17 = (bf16[24,8192]{1,0:T(8,128)(2,1)S(1)}, bf16[24,8192]{1,0:T(8,128)(2,1)S(1)}, u32[]{:S(2)}, u32[]{:S(2)}) collective-permute-start(bf16[24,8192]{1,0:T(8,128)(2,1)S(1)} %pad_maximum_fusion.refs_1_), channel_id=1, source_target_pairs={{0,80},{1,81},{2,82},{3,83},{4,84},{5,85},{6,86},{7,87},{8,88},{9,... | collective-permute-start | bytes 1179656 | tf_op jit(solution)/shard_map/ppermute | solution.py:45
  34.7 6.3 %collective-permute-start.4 = (bf16[12,3584]{1,0:T(8,128)(2,1)S(1)}, bf16[12,3584]{1,0:T(8,128)(2,1)S(1)}, u32[]{:S(2)}, u32[]{:S(2)}) collective-permute-start(bf16[12,3584]{1,0:T(8,128)(2,1)S(1)} %pad_maximum_fusion.2), channel_id=1, source_target_pairs={{0,8},{1,9},{2,10},{3,11},{4,12},{5,13},{6,14},{7,15},{8,0},{9,1},... | collective-permute-start | bytes 258056 | tf_op jit(solution)/shard_map/ppermute | solution.py:45
  41.0 6.2 %collective-permute-start.3 = (bf16[12,3584]{1,0:T(8,128)(2,1)}, bf16[12,3584]{1,0:T(8,128)(2,1)S(1)}, u32[]{:S(2)}, u32[]{:S(2)}) collective-permute-start(bf16[12,3584]{1,0:T(8,128)(2,1)} %copy-done.5), channel_id=1, source_target_pairs={{0,4},{1,5},{2,6},{3,7},{4,8},{5,9},{6,10},{7,11},{8,12},{9,13},{1... | collective-permute-start | bytes 258056 | tf_op jit(solution)/shard_map/ppermute | solution.py:45
  47.2 3.9 %collective-permute-start.24 = (bf16[24,8192]{1,0:T(8,128)(2,1)S(1)}, bf16[24,8192]{1,0:T(8,128)(2,1)S(1)}, u32[]{:S(2)}, u32[]{:S(2)}) collective-permute-start(bf16[24,8192]{1,0:T(8,128)(2,1)S(1)} %pad_maximum_fusion.refs_1_), channel_id=1, source_target_pairs={{0,32},{1,33},{2,34},{3,35},{4,36},{5,37},{6,38},{7,39},{8,40},{9,... | collective-permute-start | bytes 1179656 | tf_op jit(solution)/shard_map/ppermute | solution.py:40
  47.2 9.1 %collective-permute-start.21 = (bf16[24,8192]{1,0:T(8,128)(2,1)S(1)}, bf16[24,8192]{1,0:T(8,128)(2,1)}, u32[]{:S(2)}, u32[]{:S(2)}) collective-permute-start(bf16[24,8192]{1,0:T(8,128)(2,1)S(1)} %pad_maximum_fusion.refs_1_), channel_id=1, source_target_pairs={{0,64},{1,65},{2,66},{3,67},{4,68},{5,69},{6,70},{7,71},{8,72},{9,... | collective-permute-start | bytes 1179656 | tf_op jit(solution)/shard_map/ppermute | solution.py:45
  47.3 9.1 %collective-permute-start.27 = (bf16[24,8192]{1,0:T(8,128)(2,1)S(1)}, bf16[24,8192]{1,0:T(8,128)(2,1)S(1)}, u32[]{:S(2)}, u32[]{:S(2)}) collective-permute-start(bf16[24,8192]{1,0:T(8,128)(2,1)S(1)} %collective-permute-done.22.refs_4_), channel_id=1, source_target_pairs={{0,32},{1,33},{2,34},{3,35},{4,36},{5,37},{6,38},{7,39},{8,40},{9,... | collective-permute-start | bytes 1179656 | tf_op jit(solution)/shard_map/ppermute | solution.py:40
  47.8 12.7 %collective-permute-start.14 = (bf16[24,8192]{1,0:T(8,128)(2,1)S(1)}, bf16[24,8192]{1,0:T(8,128)(2,1)}, u32[]{:S(2)}, u32[]{:S(2)}) collective-permute-start(bf16[24,8192]{1,0:T(8,128)(2,1)S(1)} %collective-permute-done.13.refs_2_), channel_id=1, source_target_pairs={{0,64},{1,65},{2,66},{3,67},{4,68},{5,69},{6,70},{7,71},{8,72},{9,... | collective-permute-start | bytes 1179656 | tf_op jit(solution)/shard_map/ppermute | solution.py:45
  47.8 12.7 %collective-permute-start.18 = (bf16[24,8192]{1,0:T(8,128)(2,1)S(1)}, bf16[24,8192]{1,0:T(8,128)(2,1)}, u32[]{:S(2)}, u32[]{:S(2)}) collective-permute-start(bf16[24,8192]{1,0:T(8,128)(2,1)S(1)} %collective-permute-done.17.refs_5_), channel_id=1, source_target_pairs={{0,80},{1,81},{2,82},{3,83},{4,84},{5,85},{6,86},{7,87},{8,88},{9,... | collective-permute-start | bytes 1179656 | tf_op jit(solution)/shard_map/ppermute | solution.py:45
  51.1 12.6 %copy-start.1 = (bf16[24,8192]{1,0:T(8,128)(2,1)}, bf16[24,8192]{1,0:T(8,128)(2,1)S(1)}, u32[]{:S(2)}) copy-start(bf16[24,8192]{1,0:T(8,128)(2,1)S(1)} %collective-permute-done.24.refs_7_) | copy-start | bytes 1179652
  51.1 12.6 %collective-permute-start.25 = (bf16[24,8192]{1,0:T(8,128)(2,1)S(1)}, bf16[24,8192]{1,0:T(8,128)(2,1)}, u32[]{:S(2)}, u32[]{:S(2)}) collective-permute-start(bf16[24,8192]{1,0:T(8,128)(2,1)S(1)} %collective-permute-done.13.refs_2_), channel_id=1, source_target_pairs={{0,32},{1,33},{2,34},{3,35},{4,36},{5,37},{6,38},{7,39},{8,40},{9,... | collective-permute-start | bytes 1179656 | tf_op jit(solution)/shard_map/ppermute | solution.py:40
  56.3 7.4 %collective-permute-start.26 = (bf16[24,8192]{1,0:T(8,128)(2,1)}, bf16[24,8192]{1,0:T(8,128)(2,1)}, u32[]{:S(2)}, u32[]{:S(2)}) collective-permute-start(bf16[24,8192]{1,0:T(8,128)(2,1)} %collective-permute-done.21.refs_3_), channel_id=1, source_target_pairs={{0,32},{1,33},{2,34},{3,35},{4,36},{5,37},{6,38},{7,39},{8,40},{9,... | collective-permute-start | bytes 1179656 | tf_op jit(solution)/shard_map/ppermute | solution.py:40
  57.1 7.5 %collective-permute-start.28 = (bf16[24,8192]{1,0:T(8,128)(2,1)S(1)}, bf16[24,8192]{1,0:T(8,128)(2,1)}, u32[]{:S(2)}, u32[]{:S(2)}) collective-permute-start(bf16[24,8192]{1,0:T(8,128)(2,1)S(1)} %collective-permute-done.17.refs_5_), channel_id=1, source_target_pairs={{0,32},{1,33},{2,34},{3,35},{4,36},{5,37},{6,38},{7,39},{8,40},{9,... | collective-permute-start | bytes 1179656 | tf_op jit(solution)/shard_map/ppermute | solution.py:40
  60.5 16.7 %collective-permute-start.19 = (bf16[24,8192]{1,0:T(8,128)(2,1)}, bf16[24,8192]{1,0:T(8,128)(2,1)}, u32[]{:S(2)}, u32[]{:S(2)}) collective-permute-start(bf16[24,8192]{1,0:T(8,128)(2,1)} %collective-permute-done.14.refs_0_), channel_id=1, source_target_pairs={{0,32},{1,33},{2,34},{3,35},{4,36},{5,37},{6,38},{7,39},{8,40},{9,... | collective-permute-start | bytes 1179656 | tf_op jit(solution)/shard_map/ppermute | solution.py:40
  60.5 16.8 %collective-permute-start.20 = (bf16[24,8192]{1,0:T(8,128)(2,1)}, bf16[24,8192]{1,0:T(8,128)(2,1)}, u32[]{:S(2)}, u32[]{:S(2)}) collective-permute-start(bf16[24,8192]{1,0:T(8,128)(2,1)} %collective-permute-done.18.refs_1_), channel_id=1, source_target_pairs={{0,32},{1,33},{2,34},{3,35},{4,36},{5,37},{6,38},{7,39},{8,40},{9,... | collective-permute-start | bytes 1179656 | tf_op jit(solution)/shard_map/ppermute | solution.py:40
  63.7 22.5 %collective-permute-start.8 = (bf16[48,3584]{1,0:T(8,128)(2,1)S(1)}, bf16[48,3584]{1,0:T(8,128)(2,1)S(1)}, u32[]{:S(2)}, u32[]{:S(2)}) collective-permute-start(bf16[48,3584]{1,0:T(8,128)(2,1)S(1)} %concatenate.25.refs_0_), channel_id=1, source_target_pairs={{0,80},{1,81},{2,82},{3,83},{4,84},{5,85},{6,86},{7,87},{8,88},{9,... | collective-permute-start | bytes 1032200 | tf_op jit(solution)/shard_map/ppermute | solution.py:45
  63.8 22.4 %collective-permute-start.7 = (bf16[48,3584]{1,0:T(8,128)(2,1)S(1)}, bf16[48,3584]{1,0:T(8,128)(2,1)}, u32[]{:S(2)}, u32[]{:S(2)}) collective-permute-start(bf16[48,3584]{1,0:T(8,128)(2,1)S(1)} %concatenate.25.refs_0_), channel_id=1, source_target_pairs={{0,16},{1,17},{2,18},{3,19},{4,20},{5,21},{6,22},{7,23},{8,24},{9,... | collective-permute-start | bytes 1032200 | tf_op jit(solution)/shard_map/ppermute | solution.py:45
  64.6 21.6 %collective-permute-start.6 = (bf16[48,3584]{1,0:T(8,128)(2,1)S(1)}, bf16[48,3584]{1,0:T(8,128)(2,1)}, u32[]{:S(2)}, u32[]{:S(2)}) collective-permute-start(bf16[48,3584]{1,0:T(8,128)(2,1)S(1)} %concatenate.25.refs_0_), channel_id=1, source_target_pairs={{0,64},{1,65},{2,66},{3,67},{4,68},{5,69},{6,70},{7,71},{8,72},{9,... | collective-permute-start | bytes 1032200 | tf_op jit(solution)/shard_map/ppermute | solution.py:45
  66.0 1.0 copy-start.2
  67.0 1.0 copy-start.4
  77.2 10.1 %copy-start.11 = (s32[384]{0:T(512)S(1)}, s32[384]{0:T(512)}, u32[]{:S(2)}) copy-start(s32[384]{0:T(512)} %param.10) | copy-start | bytes 4612
  77.2 10.1 %collective-permute-start.29 = (bf16[48,3584]{1,0:T(8,128)(2,1)S(1)}, bf16[48,3584]{1,0:T(8,128)(2,1)S(1)}, u32[]{:S(2)}, u32[]{:S(2)}) collective-permute-start(bf16[48,3584]{1,0:T(8,128)(2,1)S(1)} %concatenate.25.refs_0_), channel_id=1, source_target_pairs={{0,32},{1,33},{2,34},{3,35},{4,36},{5,37},{6,38},{7,39},{8,40},{9,... | collective-permute-start | bytes 1032200 | tf_op jit(solution)/shard_map/ppermute | solution.py:40
  86.2 2.1 %collective-permute-start.30 = (bf16[48,3584]{1,0:T(8,128)(2,1)}, bf16[48,3584]{1,0:T(8,128)(2,1)S(1)}, u32[]{:S(2)}, u32[]{:S(2)}) collective-permute-start(bf16[48,3584]{1,0:T(8,128)(2,1)} %collective-permute-done.6.refs_1_), channel_id=1, source_target_pairs={{0,32},{1,33},{2,34},{3,35},{4,36},{5,37},{6,38},{7,39},{8,40},{9,... | collective-permute-start | bytes 1032200 | tf_op jit(solution)/shard_map/ppermute | solution.py:40
  86.8 2.0 %collective-permute-start.31 = (bf16[48,3584]{1,0:T(8,128)(2,1)}, bf16[48,3584]{1,0:T(8,128)(2,1)S(1)}, u32[]{:S(2)}, u32[]{:S(2)}) collective-permute-start(bf16[48,3584]{1,0:T(8,128)(2,1)} %collective-permute-done.7.refs_2_), channel_id=1, source_target_pairs={{0,32},{1,33},{2,34},{3,35},{4,36},{5,37},{6,38},{7,39},{8,40},{9,... | collective-permute-start | bytes 1032200 | tf_op jit(solution)/shard_map/ppermute | solution.py:40
  86.9 2.4 %collective-permute-start.32 = (bf16[48,3584]{1,0:T(8,128)(2,1)S(1)}, bf16[48,3584]{1,0:T(8,128)(2,1)S(1)}, u32[]{:S(2)}, u32[]{:S(2)}) collective-permute-start(bf16[48,3584]{1,0:T(8,128)(2,1)S(1)} %collective-permute-done.8.refs_3_), channel_id=1, source_target_pairs={{0,32},{1,33},{2,34},{3,35},{4,36},{5,37},{6,38},{7,39},{8,40},{9,... | collective-permute-start | bytes 1032200 | tf_op jit(solution)/shard_map/ppermute | solution.py:40
  96.7 1.0 copy-start
  97.7 1.2 collective-permute-start.33
  99.1 4.9 %collective-permute-start.34 = (f32[8,384]{1,0:T(8,128)S(1)}, f32[8,384]{1,0:T(8,128)S(1)}, u32[]{:S(2)}, u32[]{:S(2)}) collective-permute-start(f32[8,384]{1,0:T(8,128)S(1)} %select_select_fusion.3), channel_id=1, source_target_pairs={{0,1},{1,2},{2,3},{3,0},{4,5},{5,6},{6,7},{7,4},{8,9},{9,10},{10,1... | collective-permute-start | bytes 36872 | tf_op jit(solution)/shard_map/ppermute | solution.py:257
  99.8 5.2 %collective-permute-start.36 = (f32[8,384]{1,0:T(8,128)S(1)}, f32[8,384]{1,0:T(8,128)S(1)}, u32[]{:S(2)}, u32[]{:S(2)}) collective-permute-start(f32[8,384]{1,0:T(8,128)S(1)} %select_select_fusion.3), channel_id=1, source_target_pairs={{0,2},{1,3},{2,0},{3,1},{4,6},{5,7},{6,4},{7,5},{8,10},{9,11},{10,... | collective-permute-start | bytes 36872 | tf_op jit(solution)/shard_map/ppermute | solution.py:261
  104.1 1.2 collective-permute-start.35
  105.6 5.1 %collective-permute-start.37 = (f32[8,384]{1,0:T(8,128)S(1)}, f32[8,384]{1,0:T(8,128)S(1)}, u32[]{:S(2)}, u32[]{:S(2)}) collective-permute-start(f32[8,384]{1,0:T(8,128)S(1)} %select_select_fusion.2), channel_id=1, source_target_pairs={{0,4},{1,5},{2,6},{3,7},{4,8},{5,9},{6,10},{7,11},{8,12},{9,13},{1... | collective-permute-start | bytes 36872 | tf_op jit(solution)/shard_map/ppermute | solution.py:257
  108.2 5.3 %collective-permute-start.39 = (f32[8,384]{1,0:T(8,128)S(1)}, f32[8,384]{1,0:T(8,128)S(1)}, u32[]{:S(2)}, u32[]{:S(2)}) collective-permute-start(f32[8,384]{1,0:T(8,128)S(1)} %select_select_fusion.2), channel_id=1, source_target_pairs={{0,8},{1,9},{2,10},{3,11},{4,12},{5,13},{6,14},{7,15},{8,0},{9,1},... | collective-permute-start | bytes 36872 | tf_op jit(solution)/shard_map/ppermute | solution.py:261
  110.7 2.7 %collective-permute-start.38 = (f32[8,384]{1,0:T(8,128)S(1)}, f32[8,384]{1,0:T(8,128)S(1)}, u32[]{:S(2)}, u32[]{:S(2)}) collective-permute-start(f32[8,384]{1,0:T(8,128)S(1)} %collective-permute-done.37), channel_id=1, source_target_pairs={{0,32},{1,33},{2,34},{3,35},{4,36},{5,37},{6,38},{7,39},{8,40},{9,... | collective-permute-start | bytes 36872 | tf_op jit(solution)/shard_map/ppermute | solution.py:40
  113.8 4.9 %collective-permute-start.40 = (f32[8,384]{1,0:T(8,128)S(1)}, f32[8,384]{1,0:T(8,128)S(1)}, u32[]{:S(2)}, u32[]{:S(2)}) collective-permute-start(f32[8,384]{1,0:T(8,128)S(1)} %select_select_fusion.1), channel_id=1, source_target_pairs={{0,64},{1,65},{2,66},{3,67},{4,68},{5,69},{6,70},{7,71},{8,72},{9,... | collective-permute-start | bytes 36872 | tf_op jit(solution)/shard_map/ppermute | solution.py:257
  115.2 5.3 %collective-permute-start.42 = (f32[8,384]{1,0:T(8,128)S(1)}, f32[8,384]{1,0:T(8,128)S(1)}, u32[]{:S(2)}, u32[]{:S(2)}) collective-permute-start(f32[8,384]{1,0:T(8,128)S(1)} %select_select_fusion.1), channel_id=1, source_target_pairs={{0,16},{1,17},{2,18},{3,19},{4,20},{5,21},{6,22},{7,23},{8,24},{9,... | collective-permute-start | bytes 36872 | tf_op jit(solution)/shard_map/ppermute | solution.py:261
  118.7 1.7 %collective-permute-start.41 = (f32[8,384]{1,0:T(8,128)S(1)}, f32[8,384]{1,0:T(8,128)S(1)}, u32[]{:S(2)}, u32[]{:S(2)}) collective-permute-start(f32[8,384]{1,0:T(8,128)S(1)} %collective-permute-done.40), channel_id=1, source_target_pairs={{0,32},{1,33},{2,34},{3,35},{4,36},{5,37},{6,38},{7,39},{8,40},{9,... | collective-permute-start | bytes 36872 | tf_op jit(solution)/shard_map/ppermute | solution.py:40
  128.7 8.4 %collective-permute-start.43 = (bf16[192,3584]{1,0:T(8,128)(2,1)}, bf16[192,3584]{1,0:T(8,128)(2,1)S(1)}, u32[]{:S(2)}, u32[]{:S(2)}) collective-permute-start(bf16[192,3584]{1,0:T(8,128)(2,1)} %get-tuple-element.27), channel_id=1, source_target_pairs={{0,32},{1,33},{2,34},{3,35},{4,36},{5,37},{6,38},{7,39},{8,40},{9,... | collective-permute-start | bytes 4128776 | tf_op jit(solution)/shard_map/ppermute | solution.py:40
  137.1 7.8 %copy-start.9 = (bf16[384,3584]{1,0:T(8,128)(2,1)S(1)}, bf16[384,3584]{1,0:T(8,128)(2,1)}, u32[]{:S(2)}) copy-start(bf16[384,3584]{1,0:T(8,128)(2,1)} %constant_dynamic-update-slice_fusion) | copy-start | bytes 8257540
  139.6 10.2 %collective-permute-start.46 = (bf16[48,3584]{1,0:T(8,128)(2,1)S(1)}, bf16[48,3584]{1,0:T(8,128)(2,1)S(1)}, u32[]{:S(2)}, u32[]{:S(2)}) collective-permute-start(bf16[48,3584]{1,0:T(8,128)(2,1)S(1)} %get-tuple-element.55), channel_id=1, source_target_pairs={{0,64},{1,65},{2,66},{3,67},{4,68},{5,69},{6,70},{7,71},{8,72},{9,... | collective-permute-start | bytes 1032200 | tf_op jit(solution)/shard_map/ppermute | solution.py:45
  142.0 10.5 %collective-permute-start.45 = (bf16[48,3584]{1,0:T(8,128)(2,1)S(1)}, bf16[48,3584]{1,0:T(8,128)(2,1)S(1)}, u32[]{:S(2)}, u32[]{:S(2)}) collective-permute-start(bf16[48,3584]{1,0:T(8,128)(2,1)S(1)} %get-tuple-element.56), channel_id=1, source_target_pairs={{0,16},{1,17},{2,18},{3,19},{4,20},{5,21},{6,22},{7,23},{8,24},{9,... | collective-permute-start | bytes 1032200 | tf_op jit(solution)/shard_map/ppermute | solution.py:45
  143.5 9.1 %collective-permute-start.44 = (bf16[48,3584]{1,0:T(8,128)(2,1)S(1)}, bf16[48,3584]{1,0:T(8,128)(2,1)S(1)}, u32[]{:S(2)}, u32[]{:S(2)}) collective-permute-start(bf16[48,3584]{1,0:T(8,128)(2,1)S(1)} %get-tuple-element.57), channel_id=1, source_target_pairs={{0,80},{1,81},{2,82},{3,83},{4,84},{5,85},{6,86},{7,87},{8,88},{9,... | collective-permute-start | bytes 1032200 | tf_op jit(solution)/shard_map/ppermute | solution.py:45
  152.9 5.5 %collective-permute-start.47 = (bf16[12,3584]{1,0:T(8,128)(2,1)S(1)}, bf16[12,3584]{1,0:T(8,128)(2,1)S(1)}, u32[]{:S(2)}, u32[]{:S(2)}) collective-permute-start(bf16[12,3584]{1,0:T(8,128)(2,1)S(1)} %get-tuple-element.58), channel_id=1, source_target_pairs={{0,12},{1,13},{2,14},{3,15},{4,0},{5,1},{6,2},{7,3},{8,4},{9,5},{1... | collective-permute-start | bytes 258056 | tf_op jit(solution)/shard_map/ppermute | solution.py:45
  156.0 7.2 %collective-permute-start.49 = (bf16[12,3584]{1,0:T(8,128)(2,1)S(1)}, bf16[12,3584]{1,0:T(8,128)(2,1)S(1)}, u32[]{:S(2)}, u32[]{:S(2)}) collective-permute-start(bf16[12,3584]{1,0:T(8,128)(2,1)S(1)} %get-tuple-element.59), channel_id=1, source_target_pairs={{0,4},{1,5},{2,6},{3,7},{4,8},{5,9},{6,10},{7,11},{8,12},{9,13},{1... | collective-permute-start | bytes 258056 | tf_op jit(solution)/shard_map/ppermute | solution.py:45
  156.1 7.2 %collective-permute-start.48 = (bf16[12,3584]{1,0:T(8,128)(2,1)S(1)}, bf16[12,3584]{1,0:T(8,128)(2,1)S(1)}, u32[]{:S(2)}, u32[]{:S(2)}) collective-permute-start(bf16[12,3584]{1,0:T(8,128)(2,1)S(1)} %get-tuple-element.60), channel_id=1, source_target_pairs={{0,8},{1,9},{2,10},{3,11},{4,12},{5,13},{6,14},{7,15},{8,0},{9,1},... | collective-permute-start | bytes 258056 | tf_op jit(solution)/shard_map/ppermute | solution.py:45
  163.4 5.4 %collective-permute-start.50 = (bf16[3,3584]{1,0:T(4,128)(2,1)S(1)}, bf16[3,3584]{1,0:T(4,128)(2,1)S(1)}, u32[]{:S(2)}, u32[]{:S(2)}) collective-permute-start(bf16[3,3584]{1,0:T(4,128)(2,1)S(1)} %get-tuple-element.61), channel_id=1, source_target_pairs={{0,3},{1,0},{2,1},{3,2},{4,7},{5,4},{6,5},{7,6},{8,11},{9,8},{10,9... | collective-permute-start | bytes 64520 | tf_op jit(solution)/shard_map/ppermute | solution.py:45
  165.8 5.1 %collective-permute-start.52 = (bf16[3,3584]{1,0:T(4,128)(2,1)S(1)}, bf16[3,3584]{1,0:T(4,128)(2,1)S(1)}, u32[]{:S(2)}, u32[]{:S(2)}) collective-permute-start(bf16[3,3584]{1,0:T(4,128)(2,1)S(1)} %get-tuple-element.62), channel_id=1, source_target_pairs={{0,1},{1,2},{2,3},{3,0},{4,5},{5,6},{6,7},{7,4},{8,9},{9,10},{10,1... | collective-permute-start | bytes 64520 | tf_op jit(solution)/shard_map/ppermute | solution.py:45
  165.8 5.4 %collective-permute-start.51 = (bf16[3,3584]{1,0:T(4,128)(2,1)S(1)}, bf16[3,3584]{1,0:T(4,128)(2,1)S(1)}, u32[]{:S(2)}, u32[]{:S(2)}) collective-permute-start(bf16[3,3584]{1,0:T(4,128)(2,1)S(1)} %get-tuple-element.63), channel_id=1, source_target_pairs={{0,2},{1,3},{2,0},{3,1},{4,6},{5,7},{6,4},{7,5},{8,10},{9,11},{10,... | collective-permute-start | bytes 64520 | tf_op jit(solution)/shard_map/ppermute | solution.py:45
  (1 other events, 0.7 us)

commit v3 on v2

--- a/solution.py
+++ b/solution.py
@@ -89,12 +89,8 @@
     return jnp.sum(jnp.where(column == lane_ids(), row_values.astype(F32), 0.0), axis=1, keepdims=True).astype(jnp.int32)
 
 
-def teacher_kernel(n, last, *refs):
-    blocks, refs = refs[:n], refs[n:]
-    if last:
-        (before, source, tok_row, owner, w, out, wbuf, part, sem) = refs
-    else:
-        (w, part, wbuf, sem) = refs
+def teacher_kernel(n, *refs):
+    blocks, (source, tok_row, owner, w, out, wbuf, sem) = refs[:n], refs[n:]
     slots, chunk, _ = wbuf.shape
     count = w.shape[0] // chunk
 
@@ -108,20 +104,19 @@
         columns = slice(i * chunk, (i + 1) * chunk)
         rows = jnp.concatenate([block[:, columns] for block in blocks], axis=0)
         copy(i).wait()
-        value = dot(rows, wbuf[i % slots])
-        part[...] = value if i == 0 else part[...] + value
+        part = dot(rows, wbuf[i % slots])
+        out[...] = part if i == 0 else out[...] + part
         if i + slots < count:
             copy(i + slots).start()
-    if not last:
-        return
     owner_col = pick_column(to_column(tok_row[...]), owner[...])
     pick = one_hot(owner_col, source[...])
-    high, middle, low = split3(jnp.concatenate([before[...], part[...]], axis=0))
+    high, middle, low = split3(out[...])
     out[...] = (dot(pick, high) + dot(pick, middle)) + dot(pick, low)
 
 
 def student_kernel(n, *refs):
-    blocks, (at_ref, t_ref, tok_row, labels, w, s_out, stats_out, g, wbuf, table, label_at, sem) = refs[:n], refs[n:]
+    blocks, refs = refs[:n], refs[n:]
+    at_ref, t_ref, tok_row, labels, w, s_save, t_save, g_save, stats_out, s_out, g, wbuf, table, label_at, sem = refs
     chunk = 896
     count = w.shape[0] // chunk
 
@@ -135,6 +130,9 @@
     for block in blocks:
         g[pl.ds(at, block.shape[0]), :] = block[...]
         at += block.shape[0]
+    saves = [pltpu.make_async_copy(*pair, sem.at[count + i]) for i, pair in enumerate([(t_ref, t_save), (g, g_save), (s_out, s_save)])]
+    saves[0].start()
+    saves[1].start()
     s_out[...] = jnp.zeros_like(s_out)
     tok_col = to_column(tok_row[...])
     label_at[...] = pick_column(tok_col, labels[...]) - at_ref[0]
@@ -145,6 +143,7 @@
         copy(i).wait()
         s_out[...] += dot(g[:, rows], wbuf[rows, :])
 
+    saves[2].start()
     step = 64
     lane = lax.broadcasted_iota(jnp.int32, (step, 128), 1)
     for i in range(TOKENS // step):
@@ -174,6 +173,8 @@
     to_natural = one_hot(tok_col, lane_ids())
     high, middle, low = split3(table[...].T[:16])
     stats_out[...] = ((dot(high, to_natural) + dot(middle, to_natural)) + dot(low, to_natural))[:8]
+    for save in saves:
+        save.wait()
 
 
 def weight_copies(w, wbuf, sem):
@@ -185,7 +186,10 @@
     return copies
 
 
-def gradient_kernel(vocab, at_ref, t_ref, s_ref, stats, tok_row, labels, w, grads_out, send_out, loss_out, wbuf, local, label_at, sem):
+def gradient_kernel(vocab, at_ref, t_in, s_in, stats, tok_row, labels, w, grads_out, send_out, keep_out, loss_out, t_ref, s_ref, wbuf, local, label_at, sem):
+    loads = [pltpu.make_async_copy(*pair, sem.at[4 + i]) for i, pair in enumerate([(t_in, t_ref), (s_in, s_ref)])]
+    for load in loads:
+        load.start()
     copies = weight_copies(w, wbuf, sem)
     t_top, t_sum, t_moment, t_gap, s_top, s_sum, s_gap, hit = (stats[k : k + 1, :] for k in range(8))
     t_log, s_log = jnp.log(t_sum), jnp.log(s_sum)
@@ -200,6 +204,8 @@
     label_at[...] = pick_column(tok_col, labels[...]) - at_ref[0]
     high, middle, low = split3(rows8)
     local[...] = (dot_nt(from_natural, high) + dot_nt(from_natural, middle)) + dot_nt(from_natural, low)
+    for load in loads:
+        load.wait()
     step = 64
     for i in range(TOKENS // step):
         rows = slice(i * step, (i + 1) * step)
@@ -214,14 +220,9 @@
 
     for rows, copy in copies:
         copy.wait()
-        send_out[:, rows] = dot_nt(grads_out[HALF:, :], wbuf[rows, :]).astype(BF16)
-
-
-def keep_kernel(grads, w, out):
-    chunk = 896
-    for i in range(w.shape[0] // chunk):
-        rows = slice(i * chunk, (i + 1) * chunk)
-        out[:, rows] = dot_nt(grads[:HALF, :], w[rows, :])
+        part = dot_nt(grads_out[...], wbuf[rows, :])
+        send_out[:, rows] = part[HALF:].astype(BF16)
+        keep_out[:, rows] = part[:HALF]
 
 
 def call(kernel, out, specs, args, scratch, vmem, flops, out_specs=None):
@@ -282,73 +283,74 @@
     far = [shift(before_a, 2, 1), shift(after_b, 2, -1)]
     s_moved = [shift(s, 2, k) for k in (1, 2, 3)]
     near = [before_a, before_b, after_a, after_b]
-    near_other = [swap(v) for v in near]
-    near = [a, b, *near, swap(a), swap(b), *near_other]
+    near = [a, b, *near, swap(a), swap(b), *[swap(v) for v in near]]
     far = far + [swap(v) for v in far]
     s0 = s
 
-    def teacher(last, blocks, more, specs, scratch):
-        rows = sum(v.shape[0] for v in blocks)
-        return call(
-            functools.partial(teacher_kernel, len(blocks), last),
-            [((TOKENS if last else rows, vocab), F32)],
-            [VMEM] * len(blocks) + specs + [HBM],
-            [*blocks, *more, teacher_head],
-            [pltpu.VMEM((3, 1024, vocab), BF16), *scratch, pltpu.SemaphoreType.DMA((3,))],
-            44,
-            2 * rows * tk * vocab,
-        )[0]
-
-    t_first = teacher(False, near, [], [], [])
+    blocks = near + far
     q = HALF // 4
     pieces = [tok_row[:, at * q : (at + 1) * q] for at in (0, 1, 3, 4, 5, 7, 2, 6)]
     source = jnp.concatenate(pieces, axis=1)
-    last_rows = pltpu.VMEM((sum(v.shape[0] for v in far), vocab), F32)
-    t_logits = teacher(True, far, [t_first, source, tok_row, owner_row], [VMEM] * 4, [last_rows])
+    (t_logits,) = call(
+        functools.partial(teacher_kernel, len(blocks)),
+        [((TOKENS, vocab), F32)],
+        [VMEM] * (len(blocks) + 3) + [HBM],
+        [*blocks, source, tok_row, owner_row, teacher_head],
+        [pltpu.VMEM((3, 1024, vocab), BF16), pltpu.SemaphoreType.DMA((3,))],
+        44,
+        2 * TOKENS * tk * vocab,
+    )
     *s_moved, t_logits = lax.optimization_barrier((*s_moved, t_logits))
     s_own = [s0, *s_moved]
     s_blocks = s_own + [swap(v) for v in s_own]
     n = len(s_blocks)
-    s_logits, stats = call(
+    s_logits, t_logits, hidden, stats = call(
         functools.partial(student_kernel, n),
-        [((TOKENS, vocab), F32), ((8, TOKENS), F32)],
+        [((TOKENS, vocab), F32), ((TOKENS, vocab), F32), ((TOKENS, sk), BF16), ((8, TOKENS), F32)],
         [VMEM] * n + [SMEM] + [VMEM] * 3 + [HBM],
         [*s_blocks, at, t_logits, tok_row, label_row, student_head],
         [
+            pltpu.VMEM((TOKENS, vocab), F32),
             pltpu.VMEM((TOKENS, sk), BF16),
             pltpu.VMEM((sk, vocab), BF16),
             pltpu.VMEM((TOKENS, 128), F32),
             pltpu.VMEM((TOKENS, 1), jnp.int32),
-            pltpu.SemaphoreType.DMA((4,)),
+            pltpu.SemaphoreType.DMA((7,)),
+        ],
+        50,
+        2 * TOKENS * sk * vocab,
+        [HBM, HBM, HBM, VMEM],
+    )
+
+    stats = merge([stats, swap(stats)])
+    for dim in ("y", "x", "z"):
+        near, far = ring_shift(stats, dim), across(stats, dim)
+        stats = merge([stats, near, swap(near), far])
+
+    grads, to_other, kept, loss = call(
+        functools.partial(gradient_kernel, vocab * DEVICES),
+        [((TOKENS, vocab), BF16), ((HALF, sk), BF16), ((HALF, sk), F32), ((1, TOKENS), F32)],
+        [SMEM] + [HBM] * 2 + [VMEM] * 3 + [HBM],
+        [at, t_logits, s_logits, stats, tok_row, label_row, student_head],
+        [
+            pltpu.VMEM((TOKENS, vocab), F32),
+            pltpu.VMEM((TOKENS, vocab), F32),
+            pltpu.VMEM((sk, vocab), BF16),
+            pltpu.VMEM((TOKENS, 8), F32),
+            pltpu.VMEM((TOKENS, 1), jnp.int32),
+            pltpu.SemaphoreType.DMA((6,)),
         ],
         44,
         2 * TOKENS * sk * vocab,
     )
 
-    stats = merge([stats, swap(stats)])
-    for dim in ("y", "x", "z"):
-        near, far = ring_shift(stats, dim), across(stats, dim)
-        stats = merge([stats, near, swap(near), far])
-
-    grads, to_other, loss, weights = call(
-        functools.partial(gradient_kernel, vocab * DEVICES),
-        [((TOKENS, vocab), BF16), ((HALF, sk), BF16), ((1, TOKENS), F32), ((sk, vocab), BF16)],
-        [SMEM] + [VMEM] * 5 + [HBM],
-        [at, t_logits, s_logits, stats, tok_row, label_row, student_head],
-        [pltpu.VMEM((TOKENS, 8), F32), pltpu.VMEM((TOKENS, 1), jnp.int32), pltpu.SemaphoreType.DMA((4,))],
-        52,
-        TOKENS * sk * vocab,
-    )
-    (kept,) = call(keep_kernel, [((HALF, sk), F32)], [VMEM] * 2, [grads, weights], [], 52, TOKENS * sk * vocab)
-
-    total = kept + swap(to_other).astype(F32)
+    received = swap(to_other)
+    grad_head = lax.dot_general(hidden, grads, (((0,), (0,)), ((), ())), preferred_element_type=F32).astype(BF16)
+    kept, received, grad_head = lax.optimization_barrier((kept, received, grad_head))
+    total = kept + received.astype(F32)
     for stage in (2, 1, 0):
         size = total.shape[0] // 4
         parts = [shift(total[k * size : (k + 1) * size].astype(BF16), stage, -k) for k in (1, 2, 3)]
-        if stage == 2:
-            hidden = jnp.concatenate(s_blocks, axis=0)
-            grad_head = lax.dot_general(hidden, grads, (((0,), (0,)), ((), ())), preferred_element_type=F32).astype(BF16)
-            total, grad_head, *parts = lax.optimization_barrier((total, grad_head, *parts))
         total = total[:size] + sum(p.astype(F32) for p in parts)
     token_loss = lax.dynamic_slice_in_dim(loss[0], lax.axis_index(AXES) * ROWS, ROWS)
     return token_loss, grad_head, total.astype(BF16)

time: 173 us -> 166 us (0.960)
  waiting for transfers between devices: 44.3 us -> 59.4 us
  Pallas kernels: 39.2 us -> 26.8 us
  starting transfers between devices: 58.8 us -> 54.1 us
  local copies, waits for them, and re-layouts: 17.6 us -> 15 us
  other arithmetic: 6 us -> 4.08 us
    pallas_call x5 -> x3, Pallas kernels: 39.2 us -> 26.8 us  [call(): pl.pallas_call(kernel, out_shape=[jax.ShapeDtypeStruct(*o) for o in out],...]
    ppermute x30, waiting for transfers between devices: 37.1 us -> 46.3 us  [shift(): return lax.ppermute(value, AXES, pairs)]
    unnamed x31 -> x28, local copies, waits for them, and re-layouts: 11.1 us -> 4.53 us
    concatenate x1, local copies, waits for them, and re-layouts: 2.33 us -> 6.98 us  [shards(): jnp.concatenate([s] + [shift(s, 1, k) for k in (1, 2, 3)], axis=0)]
    ppermute x3, waiting for transfers between devices: 2.02 us -> 5.46 us  [ring_shift(): lax.ppermute(value, AXES, [(d, moved(d, dim, -1 if coords(d)['c'] else 1)...]
    ppermute x30, starting transfers between devices: 44.9 us -> 41.8 us  [shift(): return lax.ppermute(value, AXES, pairs)]
    another operation x3, other arithmetic: 2.56 us -> 0.64 us
  transfers between devices with their start and end apart: 53 -> 53, of which waited for: 23 -> 30; matrix products, arithmetic and copies ran while one was open for 12% -> 9% of each run, Pallas kernels for 14% -> 8%
where the time goes in v3:
time: 166 us; the launch traced here: 165 us
  waiting for transfers between devices  59.4 us (36%)
  starting transfers between devices  54.1 us (33%)
  Pallas kernels  26.8 us (16%)
  local copies, waits for them, and re-layouts  15 us (9%)
  matrix products  4.82 us (3%)
  other arithmetic  4.08 us (2%)
    ppermute x30, waiting for transfers between devices, shift(): return lax.ppermute(value, AXES, pairs)  46.3 us
    ppermute x30, starting transfers between devices, shift(): return lax.ppermute(value, AXES, pairs)  41.8 us
    pallas_call x3, Pallas kernels, call(): pl.pallas_call(kernel, out_shape=[jax.ShapeDtypeStruct(*o) for o in out],...  26.8 us
    concatenate x1, local copies, waits for them, and re-layouts, shards(): jnp.concatenate([s] + [shift(s, 1, k) for k in (1, 2, 3)], axis=0)  6.98 us
    ppermute x3, starting transfers between devices, across(): lax.ppermute(value, AXES, [(d, moved(d, dim, 2)) for d in range(DEVICES)])  6.92 us
    ppermute x3, waiting for transfers between devices, ring_shift(): lax.ppermute(value, AXES, [(d, moved(d, dim, -1 if coords(d)['c'] else 1)...  5.46 us
    dot_general x1, matrix products, shards(): lax.dot_general(hidden, grads, (((0,), (0,)), ((), ())), preferred_elemen...  4.82 us
    unnamed x28, local copies, waits for them, and re-layouts  4.53 us
  transfers between devices with their start and end apart: 53, of which 30 were waited for; matrix products, arithmetic and copies ran while one was open for 9% of the time, Pallas kernels for 8%

profile of v3, /device:TPU:0, one launch (start us, length us, event | category | flops | bytes accessed | tf_op | source)
XLA Modules:
  0.0 165.2 jit_solution(7440514268479540903)
XLA Ops:
  0.7 3.2 %collective-permute-start.11 = (bf16[3,8192]{1,0:T(4,128)(2,1)}, bf16[3,8192]{1,0:T(4,128)(2,1)S(1)}, u32[]{:S(2)}, u32[]{:S(2)}) collective-permute-start(bf16[3,8192]{1,0:T(4,128)(2,1)} %param.6), channel_id=1, source_target_pairs={{0,3},{1,0},{2,1},{3,2},{4,7},{5,4},{6,5},{7,6},{8,11},{9,8},{10,9... | collective-permute-start | bytes 147464 | tf_op jit(solution)/shard_map/ppermute | solution.py:45
  3.8 0.6 collective-permute-start.10
  4.5 1.0 collective-permute-start.9
  5.4 0.6 collective-permute-done.11
  6.1 3.8 %collective-permute-done.10 = bf16[3,8192]{1,0:T(4,128)(2,1)S(1)} collective-permute-done((bf16[3,8192]{1,0:T(4,128)(2,1)}, bf16[3,8192]{1,0:T(4,128)(2,1)S(1)}, u32[]{:S(2)}, u32[]{:S(2)}) %collective-permute-start.10) | collective-permute-done | bytes 49184 | tf_op jit(solution)/shard_map/ppermute | solution.py:45
  9.9 0.7 collective-permute-done.9
  10.5 1.0 pad_maximum_fusion.1
  11.6 1.6 collective-permute-start.12
  13.1 1.7 %collective-permute-start.14 = (bf16[12,8192]{1,0:T(8,128)(2,1)S(1)}, bf16[12,8192]{1,0:T(8,128)(2,1)S(1)}, u32[]{:S(2)}, u32[]{:S(2)}) collective-permute-start(bf16[12,8192]{1,0:T(8,128)(2,1)S(1)} %pad_maximum_fusion.1), channel_id=1, source_target_pairs={{0,12},{1,13},{2,14},{3,15},{4,0},{5,1},{6,2},{7,3},{8,4},{9,5},{1... | collective-permute-start | bytes 589832 | tf_op jit(solution)/shard_map/ppermute | solution.py:45
  14.9 1.8 %collective-permute-start.13 = (bf16[12,8192]{1,0:T(8,128)(2,1)S(1)}, bf16[12,8192]{1,0:T(8,128)(2,1)S(1)}, u32[]{:S(2)}, u32[]{:S(2)}) collective-permute-start(bf16[12,8192]{1,0:T(8,128)(2,1)S(1)} %pad_maximum_fusion.1), channel_id=1, source_target_pairs={{0,8},{1,9},{2,10},{3,11},{4,12},{5,13},{6,14},{7,15},{8,0},{9,1},... | collective-permute-start | bytes 589832 | tf_op jit(solution)/shard_map/ppermute | solution.py:45
  17.3 0.9 collective-permute-start.1
  18.2 1.1 collective-permute-done.12
  19.4 2.0 %concatenate.24.refs_0_ = bf16[24,8192]{1,0:T(8,128)(2,1)S(1)} concatenate(bf16[3,8192]{1,0:T(4,128)(2,1)} %param.6, bf16[3,8192]{1,0:T(4,128)(2,1)S(1)} %collective-permute-done.9, bf16[3,8192]{1,0:T(4,128)(2,1)S(1)} %collective-permute-done.10, bf16[3,8192]{1,0:T(4,128)(2,1)S(1)} %collective-permute-done.11, bf16[12,8192]{1,0:T(8,128)(2,1)S(1)} %collective-permute-done.12), dimensions={0} | concatenate | bytes 786432 | tf_op jit(solution)/shard_map/concatenate | solution.py:275
  21.6 1.4 collective-permute-done.13
  23.0 4.0 %collective-permute-start.17 = (bf16[24,8192]{1,0:T(8,128)(2,1)S(1)}, bf16[24,8192]{1,0:T(8,128)(2,1)S(1)}, u32[]{:S(2)}, u32[]{:S(2)}) collective-permute-start(bf16[24,8192]{1,0:T(8,128)(2,1)S(1)} %concatenate.24.refs_0_), channel_id=1, source_target_pairs={{0,80},{1,81},{2,82},{3,83},{4,84},{5,85},{6,86},{7,87},{8,88},{9,... | collective-permute-start | bytes 1179656 | tf_op jit(solution)/shard_map/ppermute | solution.py:45
  27.3 3.2 %collective-permute-start.18 = (bf16[24,8192]{1,0:T(8,128)(2,1)S(1)}, bf16[24,8192]{1,0:T(8,128)(2,1)S(1)}, u32[]{:S(2)}, u32[]{:S(2)}) collective-permute-start(bf16[24,8192]{1,0:T(8,128)(2,1)S(1)} %pad_maximum_fusion.refs_1_), channel_id=1, source_target_pairs={{0,80},{1,81},{2,82},{3,83},{4,84},{5,85},{6,86},{7,87},{8,88},{9,... | collective-permute-start | bytes 1179656 | tf_op jit(solution)/shard_map/ppermute | solution.py:45
  30.5 0.8 pad_maximum_fusion.2
  31.3 2.3 %collective-permute-start.5 = (bf16[12,3584]{1,0:T(8,128)(2,1)S(1)}, bf16[12,3584]{1,0:T(8,128)(2,1)S(1)}, u32[]{:S(2)}, u32[]{:S(2)}) collective-permute-start(bf16[12,3584]{1,0:T(8,128)(2,1)S(1)} %pad_maximum_fusion.2), channel_id=1, source_target_pairs={{0,12},{1,13},{2,14},{3,15},{4,0},{5,1},{6,2},{7,3},{8,4},{9,5},{1... | collective-permute-start | bytes 258056 | tf_op jit(solution)/shard_map/ppermute | solution.py:45
  33.7 2.5 %collective-permute-done.5 = bf16[12,3584]{1,0:T(8,128)(2,1)S(1)} collective-permute-done((bf16[12,3584]{1,0:T(8,128)(2,1)S(1)}, bf16[12,3584]{1,0:T(8,128)(2,1)S(1)}, u32[]{:S(2)}, u32[]{:S(2)}) %collective-permute-start.5) | collective-permute-done | bytes 86048 | tf_op jit(solution)/shard_map/ppermute | solution.py:45
  36.2 1.7 %collective-permute-start.4 = (bf16[12,3584]{1,0:T(8,128)(2,1)S(1)}, bf16[12,3584]{1,0:T(8,128)(2,1)S(1)}, u32[]{:S(2)}, u32[]{:S(2)}) collective-permute-start(bf16[12,3584]{1,0:T(8,128)(2,1)S(1)} %pad_maximum_fusion.2), channel_id=1, source_target_pairs={{0,8},{1,9},{2,10},{3,11},{4,12},{5,13},{6,14},{7,15},{8,0},{9,1},... | collective-permute-start | bytes 258056 | tf_op jit(solution)/shard_map/ppermute | solution.py:45
  37.9 4.6 %collective-permute-done.4 = bf16[12,3584]{1,0:T(8,128)(2,1)S(1)} collective-permute-done((bf16[12,3584]{1,0:T(8,128)(2,1)S(1)}, bf16[12,3584]{1,0:T(8,128)(2,1)S(1)}, u32[]{:S(2)}, u32[]{:S(2)}) %collective-permute-start.4) | collective-permute-done | bytes 86048 | tf_op jit(solution)/shard_map/ppermute | solution.py:45
  42.5 1.4 collective-permute-start.3
  43.9 4.8 %collective-permute-done.3 = bf16[12,3584]{1,0:T(8,128)(2,1)S(1)} collective-permute-done((bf16[12,3584]{1,0:T(8,128)(2,1)S(1)}, bf16[12,3584]{1,0:T(8,128)(2,1)S(1)}, u32[]{:S(2)}, u32[]{:S(2)}) %collective-permute-start.3) | collective-permute-done | bytes 86048 | tf_op jit(solution)/shard_map/ppermute | solution.py:45
  49.6 3.1 %collective-permute-start.26 = (bf16[24,8192]{1,0:T(8,128)(2,1)S(1)}, bf16[24,8192]{1,0:T(8,128)(2,1)}, u32[]{:S(2)}, u32[]{:S(2)}) collective-permute-start(bf16[24,8192]{1,0:T(8,128)(2,1)S(1)} %collective-permute-done.18.refs_5_), channel_id=1, source_target_pairs={{0,80},{1,81},{2,82},{3,83},{4,84},{5,85},{6,86},{7,87},{8,88},{9,... | collective-permute-start | bytes 1179656 | tf_op jit(solution)/shard_map/ppermute | solution.py:45
  52.7 5.1 %collective-permute-done.16.refs_3_ = bf16[24,8192]{1,0:T(8,128)(2,1)S(1)} collective-permute-done((bf16[24,8192]{1,0:T(8,128)(2,1)S(1)}, bf16[24,8192]{1,0:T(8,128)(2,1)S(1)}, u32[]{:S(2)}, u32[]{:S(2)}) %collective-permute-start.16) | collective-permute-done | bytes 393248 | tf_op jit(solution)/shard_map/ppermute | solution.py:45
  57.8 0.7 copy-done.2
  59.1 3.1 %collective-permute-done.25.refs_12_ = bf16[24,8192]{1,0:T(8,128)(2,1)} collective-permute-done((bf16[24,8192]{1,0:T(8,128)(2,1)S(1)}, bf16[24,8192]{1,0:T(8,128)(2,1)}, u32[]{:S(2)}, u32[]{:S(2)}) %collective-permute-start.25) | collective-permute-done | bytes 393248 | tf_op jit(solution)/shard_map/ppermute | solution.py:45
  63.0 7.0 %concatenate.22.refs_0_ = bf16[48,3584]{1,0:T(8,128)(2,1)S(1)} concatenate(bf16[3,3584]{1,0:T(4,128)(2,1)S(1)} %copy-done.7, bf16[3,3584]{1,0:T(4,128)(2,1)} %copy-done.10, bf16[3,3584]{1,0:T(4,128)(2,1)} %copy-done.9, bf16[3,3584]{1,0:T(4,128)(2,1)} %copy-done.8, bf16[12,3584]{1,0:T(8,128)(2,1)} %copy-done.6, bf16[12,3584]{1,0:T(8,128)(2,1)} %copy-done.5, bf16[12,3584]{1,0:T(8,128)(2,1)} %copy-done.4), dimensions={0} | concatenate | bytes 688128 | tf_op jit(solution)/shard_map/concatenate | solution.py:278
  70.7 0.9 collective-permute-start.7
  71.6 0.9 collective-permute-start.6
  72.5 1.0 copy-done.3
  73.5 12.4 %shard_map.85.refs_9_ = f32[384,768]{1,0:T(8,128)S(1)} custom-call(bf16[24,8192]{1,0:T(8,128)(2,1)S(1)} %concatenate.24.refs_0_, bf16[24,8192]{1,0:T(8,128)(2,1)S(1)} %pad_maximum_fusion.refs_1_, bf16[24,8192]{1,0:T(8,128)(2,1)S(1)} %collective-permute-done.15.refs_2_, bf16[24,8192]{1,0:T(8,128)(2,1)S(1)} %collective-permute-done.16.refs_3_, ...), custom_call_target="tpu_custom_call" | custom-call | flops 4831838208 | bytes 4194304 | tf_op jit(solution)/shard_map/pallas_call | solution.py:229
  85.9 1.0 copy-done
  87.0 0.6 collective-permute-start.30
  88.1 1.0 collective-permute-done.30.refs_5_
  90.1 9.0 %shard_map.86 = (f32[384,768]{1,0:T(8,128)S(1)}, f32[384,768]{1,0:T(8,128)}, bf16[384,3584]{1,0:T(8,128)(2,1)}, f32[8,384]{1,0:T(8,128)S(1)}) custom-call(bf16[48,3584]{1,0:T(8,128)(2,1)S(1)} %concatenate.22.refs_0_, bf16[48,3584]{1,0:T(8,128)(2,1)} %collective-permute-done.6.refs_1_, bf16[48,3584]{1,0:T(8,128)(2,1)} %collective-permute-done.7.refs_2_, ...), custom_call_target="tpu_custom_call" | custom-call | flops 2113929216 | bytes 4194304 | tf_op jit(solution)/shard_map/pallas_call | solution.py:229
  99.6 0.8 collective-permute-done.33
  100.7 2.6 %collective-permute-start.36 = (f32[8,384]{1,0:T(8,128)S(1)}, f32[8,384]{1,0:T(8,128)S(1)}, u32[]{:S(2)}, u32[]{:S(2)}) collective-permute-start(f32[8,384]{1,0:T(8,128)S(1)} %select_select_fusion.3), channel_id=1, source_target_pairs={{0,2},{1,3},{2,0},{3,1},{4,6},{5,7},{6,4},{7,5},{8,10},{9,11},{10,... | collective-permute-start | bytes 36872 | tf_op jit(solution)/shard_map/ppermute | solution.py:262
  103.3 2.2 %collective-permute-done.34 = f32[8,384]{1,0:T(8,128)S(1)} collective-permute-done((f32[8,384]{1,0:T(8,128)S(1)}, f32[8,384]{1,0:T(8,128)S(1)}, u32[]{:S(2)}, u32[]{:S(2)}) %collective-permute-start.34) | collective-permute-done | bytes 12320 | tf_op jit(solution)/shard_map/ppermute | solution.py:258
  106.1 0.7 collective-permute-done.35
  107.1 2.3 %collective-permute-start.37 = (f32[8,384]{1,0:T(8,128)S(1)}, f32[8,384]{1,0:T(8,128)S(1)}, u32[]{:S(2)}, u32[]{:S(2)}) collective-permute-start(f32[8,384]{1,0:T(8,128)S(1)} %select_select_fusion.2), channel_id=1, source_target_pairs={{0,4},{1,5},{2,6},{3,7},{4,8},{5,9},{6,10},{7,11},{8,12},{9,13},{1... | collective-permute-start | bytes 36872 | tf_op jit(solution)/shard_map/ppermute | solution.py:258
  109.4 1.7 %collective-permute-start.39 = (f32[8,384]{1,0:T(8,128)S(1)}, f32[8,384]{1,0:T(8,128)S(1)}, u32[]{:S(2)}, u32[]{:S(2)}) collective-permute-start(f32[8,384]{1,0:T(8,128)S(1)} %select_select_fusion.2), channel_id=1, source_target_pairs={{0,8},{1,9},{2,10},{3,11},{4,12},{5,13},{6,14},{7,15},{8,0},{9,1},... | collective-permute-start | bytes 36872 | tf_op jit(solution)/shard_map/ppermute | solution.py:262
  111.1 0.9 collective-permute-done.37
  112.0 2.6 %collective-permute-done.39 = f32[8,384]{1,0:T(8,128)S(1)} collective-permute-done((f32[8,384]{1,0:T(8,128)S(1)}, f32[8,384]{1,0:T(8,128)S(1)}, u32[]{:S(2)}, u32[]{:S(2)}) %collective-permute-start.39) | collective-permute-done | bytes 12320 | tf_op jit(solution)/shard_map/ppermute | solution.py:262
  115.0 2.5 %collective-permute-start.42 = (f32[8,384]{1,0:T(8,128)S(1)}, f32[8,384]{1,0:T(8,128)S(1)}, u32[]{:S(2)}, u32[]{:S(2)}) collective-permute-start(f32[8,384]{1,0:T(8,128)S(1)} %select_select_fusion.1), channel_id=1, source_target_pairs={{0,16},{1,17},{2,18},{3,19},{4,20},{5,21},{6,22},{7,23},{8,24},{9,... | collective-permute-start | bytes 36872 | tf_op jit(solution)/shard_map/ppermute | solution.py:262
  117.6 2.3 %collective-permute-done.40 = f32[8,384]{1,0:T(8,128)S(1)} collective-permute-done((f32[8,384]{1,0:T(8,128)S(1)}, f32[8,384]{1,0:T(8,128)S(1)}, u32[]{:S(2)}, u32[]{:S(2)}) %collective-permute-start.40) | collective-permute-done | bytes 12320 | tf_op jit(solution)/shard_map/ppermute | solution.py:258
  119.9 0.6 collective-permute-done.42
  121.4 1.3 copy-done.1
  122.7 5.3 %shard_map.87 = (bf16[384,768]{1,0:T(8,128)(2,1)S(1)}, bf16[192,3584]{1,0:T(8,128)(2,1)S(1)}, f32[192,3584]{1,0:T(8,128)S(1)}, f32[1,384]{1,0:T(1,128)S(1)}) custom-call(s32[1]{0:T(128)} %bitcast.refs_8_.at_ref, f32[384,768]{1,0:T(8,128)S(1)} %copy-done.1, f32[384,768]{1,0:T(8,128)S(1)} %get-tuple-element.23.s_in, f32[8,384]{1,0:T(8,128)S(1)} %select_select_fusion.stats, ...), custom_call_target="tpu_custom_call" | custom-call | flops 2113929216 | bytes 4194304 | tf_op jit(solution)/shard_map/pallas_call | solution.py:229
  128.3 4.8 %convolution_convert_fusion = bf16[3584,768]{1,0:T(8,128)(2,1)} fusion(bf16[384,3584]{1,0:T(8,128)(2,1)S(1)} %copy-done.13, bf16[384,768]{1,0:T(8,128)(2,1)S(1)} %get-tuple-element.29), kind=kOutput, calls=%fused_computation | convolution fusion | flops 2116681728 | bytes 8847360 | tf_op jit(solution)/shard_map/dot_general | solution.py:348
  133.6 2.3 %collective-permute-start.44 = (bf16[48,3584]{1,0:T(8,128)(2,1)S(1)}, bf16[48,3584]{1,0:T(8,128)(2,1)S(1)}, u32[]{:S(2)}, u32[]{:S(2)}) collective-permute-start(bf16[48,3584]{1,0:T(8,128)(2,1)S(1)} %get-tuple-element.55), channel_id=1, source_target_pairs={{0,80},{1,81},{2,82},{3,83},{4,84},{5,85},{6,86},{7,87},{8,88},{9,... | collective-permute-start | bytes 1032200 | tf_op jit(solution)/shard_map/ppermute | solution.py:45
  135.9 1.5 collective-permute-start.45
  137.5 3.5 %collective-permute-done.44 = bf16[48,3584]{1,0:T(8,128)(2,1)S(1)} collective-permute-done((bf16[48,3584]{1,0:T(8,128)(2,1)S(1)}, bf16[48,3584]{1,0:T(8,128)(2,1)S(1)}, u32[]{:S(2)}, u32[]{:S(2)}) %collective-permute-start.44) | collective-permute-done | bytes 344096 | tf_op jit(solution)/shard_map/ppermute | solution.py:45
  140.9 7.1 %collective-permute-done.46 = bf16[48,3584]{1,0:T(8,128)(2,1)S(1)} collective-permute-done((bf16[48,3584]{1,0:T(8,128)(2,1)S(1)}, bf16[48,3584]{1,0:T(8,128)(2,1)S(1)}, u32[]{:S(2)}, u32[]{:S(2)}) %collective-permute-start.46) | collective-permute-done | bytes 344096 | tf_op jit(solution)/shard_map/ppermute | solution.py:45
  148.3 1.0 collective-permute-start.47
  149.3 1.1 collective-permute-start.49
  150.4 1.7 %collective-permute-start.48 = (bf16[12,3584]{1,0:T(8,128)(2,1)S(1)}, bf16[12,3584]{1,0:T(8,128)(2,1)S(1)}, u32[]{:S(2)}, u32[]{:S(2)}) collective-permute-start(bf16[12,3584]{1,0:T(8,128)(2,1)S(1)} %get-tuple-element.60), channel_id=1, source_target_pairs={{0,8},{1,9},{2,10},{3,11},{4,12},{5,13},{6,14},{7,15},{8,0},{9,1},... | collective-permute-start | bytes 258056 | tf_op jit(solution)/shard_map/ppermute | solution.py:45
  152.1 1.0 collective-permute-done.47
  153.1 2.2 %collective-permute-done.49 = bf16[12,3584]{1,0:T(8,128)(2,1)S(1)} collective-permute-done((bf16[12,3584]{1,0:T(8,128)(2,1)S(1)}, bf16[12,3584]{1,0:T(8,128)(2,1)S(1)}, u32[]{:S(2)}, u32[]{:S(2)}) %collective-permute-start.49) | collective-permute-done | bytes 86048 | tf_op jit(solution)/shard_map/ppermute | solution.py:45
  155.3 1.4 collective-permute-done.48
  156.8 2.4 %collective-permute-start.50 = (bf16[3,3584]{1,0:T(4,128)(2,1)S(1)}, bf16[3,3584]{1,0:T(4,128)(2,1)S(1)}, u32[]{:S(2)}, u32[]{:S(2)}) collective-permute-start(bf16[3,3584]{1,0:T(4,128)(2,1)S(1)} %get-tuple-element.61), channel_id=1, source_target_pairs={{0,3},{1,0},{2,1},{3,2},{4,7},{5,4},{6,5},{7,6},{8,11},{9,8},{10,9... | collective-permute-start | bytes 64520 | tf_op jit(solution)/shard_map/ppermute | solution.py:45
  159.2 1.5 collective-permute-start.51
  161.3 3.0 %collective-permute-done.52 = bf16[3,3584]{1,0:T(4,128)(2,1)S(1)} collective-permute-done((bf16[3,3584]{1,0:T(4,128)(2,1)S(1)}, bf16[3,3584]{1,0:T(4,128)(2,1)S(1)}, u32[]{:S(2)}, u32[]{:S(2)}) %collective-permute-start.52) | collective-permute-done | bytes 21536 | tf_op jit(solution)/shard_map/ppermute | solution.py:45
  164.6 0.6 fusion
  (132 shorter events, 10.2 us)
Async XLA Ops:
  0.6 62.4 %copy-start.7 = (bf16[3,3584]{1,0:T(4,128)(2,1)S(1)}, bf16[3,3584]{1,0:T(4,128)(2,1)}, u32[]{:S(2)}) copy-start(bf16[3,3584]{1,0:T(4,128)(2,1)} %param.8) | copy-start | bytes 64516
  0.6 62.2 %copy-start.11 = (s32[384]{0:T(512)S(1)}, s32[384]{0:T(512)}, u32[]{:S(2)}) copy-start(s32[384]{0:T(512)} %param.11) | copy-start | bytes 4612
  0.7 5.4 %collective-permute-start.11 = (bf16[3,8192]{1,0:T(4,128)(2,1)}, bf16[3,8192]{1,0:T(4,128)(2,1)S(1)}, u32[]{:S(2)}, u32[]{:S(2)}) collective-permute-start(bf16[3,8192]{1,0:T(4,128)(2,1)} %param.6), channel_id=1, source_target_pairs={{0,3},{1,0},{2,1},{3,2},{4,7},{5,4},{6,5},{7,6},{8,11},{9,8},{10,9... | collective-permute-start | bytes 147464 | tf_op jit(solution)/shard_map/ppermute | solution.py:45
  3.8 6.0 %collective-permute-start.10 = (bf16[3,8192]{1,0:T(4,128)(2,1)}, bf16[3,8192]{1,0:T(4,128)(2,1)S(1)}, u32[]{:S(2)}, u32[]{:S(2)}) collective-permute-start(bf16[3,8192]{1,0:T(4,128)(2,1)} %param.6), channel_id=1, source_target_pairs={{0,2},{1,3},{2,0},{3,1},{4,6},{5,7},{6,4},{7,5},{8,10},{9,11},{10,... | collective-permute-start | bytes 147464 | tf_op jit(solution)/shard_map/ppermute | solution.py:45
  4.5 6.1 %collective-permute-start.9 = (bf16[3,8192]{1,0:T(4,128)(2,1)}, bf16[3,8192]{1,0:T(4,128)(2,1)S(1)}, u32[]{:S(2)}, u32[]{:S(2)}) collective-permute-start(bf16[3,8192]{1,0:T(4,128)(2,1)} %param.6), channel_id=1, source_target_pairs={{0,1},{1,2},{2,3},{3,0},{4,5},{5,6},{6,7},{7,4},{8,9},{9,10},{10,1... | collective-permute-start | bytes 147464 | tf_op jit(solution)/shard_map/ppermute | solution.py:45
  11.6 7.7 %collective-permute-start.12 = (bf16[12,8192]{1,0:T(8,128)(2,1)S(1)}, bf16[12,8192]{1,0:T(8,128)(2,1)S(1)}, u32[]{:S(2)}, u32[]{:S(2)}) collective-permute-start(bf16[12,8192]{1,0:T(8,128)(2,1)S(1)} %pad_maximum_fusion.1), channel_id=1, source_target_pairs={{0,4},{1,5},{2,6},{3,7},{4,8},{5,9},{6,10},{7,11},{8,12},{9,13},{1... | collective-permute-start | bytes 589832 | tf_op jit(solution)/shard_map/ppermute | solution.py:45
  13.1 8.5 %collective-permute-start.14 = (bf16[12,8192]{1,0:T(8,128)(2,1)S(1)}, bf16[12,8192]{1,0:T(8,128)(2,1)S(1)}, u32[]{:S(2)}, u32[]{:S(2)}) collective-permute-start(bf16[12,8192]{1,0:T(8,128)(2,1)S(1)} %pad_maximum_fusion.1), channel_id=1, source_target_pairs={{0,12},{1,13},{2,14},{3,15},{4,0},{5,1},{6,2},{7,3},{8,4},{9,5},{1... | collective-permute-start | bytes 589832 | tf_op jit(solution)/shard_map/ppermute | solution.py:45
  14.9 8.1 %collective-permute-start.13 = (bf16[12,8192]{1,0:T(8,128)(2,1)S(1)}, bf16[12,8192]{1,0:T(8,128)(2,1)S(1)}, u32[]{:S(2)}, u32[]{:S(2)}) collective-permute-start(bf16[12,8192]{1,0:T(8,128)(2,1)S(1)} %pad_maximum_fusion.1), channel_id=1, source_target_pairs={{0,8},{1,9},{2,10},{3,11},{4,12},{5,13},{6,14},{7,15},{8,0},{9,1},... | collective-permute-start | bytes 589832 | tf_op jit(solution)/shard_map/ppermute | solution.py:45
  16.7 10.5 %collective-permute-start.2 = (bf16[3,3584]{1,0:T(4,128)(2,1)}, bf16[3,3584]{1,0:T(4,128)(2,1)S(1)}, u32[]{:S(2)}, u32[]{:S(2)}) collective-permute-start(bf16[3,3584]{1,0:T(4,128)(2,1)} %param.8), channel_id=1, source_target_pairs={{0,3},{1,0},{2,1},{3,2},{4,7},{5,4},{6,5},{7,6},{8,11},{9,8},{10,9... | collective-permute-start | bytes 64520 | tf_op jit(solution)/shard_map/ppermute | solution.py:45
  17.3 10.0 %collective-permute-start.1 = (bf16[3,3584]{1,0:T(4,128)(2,1)}, bf16[3,3584]{1,0:T(4,128)(2,1)S(1)}, u32[]{:S(2)}, u32[]{:S(2)}) collective-permute-start(bf16[3,3584]{1,0:T(4,128)(2,1)} %param.8), channel_id=1, source_target_pairs={{0,2},{1,3},{2,0},{3,1},{4,6},{5,7},{6,4},{7,5},{8,10},{9,11},{10,... | collective-permute-start | bytes 64520 | tf_op jit(solution)/shard_map/ppermute | solution.py:45
  19.2 11.3 %collective-permute-start = (bf16[3,3584]{1,0:T(4,128)(2,1)}, bf16[3,3584]{1,0:T(4,128)(2,1)S(1)}, u32[]{:S(2)}, u32[]{:S(2)}) collective-permute-start(bf16[3,3584]{1,0:T(4,128)(2,1)} %param.8), channel_id=1, source_target_pairs={{0,1},{1,2},{2,3},{3,0},{4,5},{5,6},{6,7},{7,4},{8,9},{9,10},{10,1... | collective-permute-start | bytes 64520 | tf_op jit(solution)/shard_map/ppermute | solution.py:45
  21.6 27.1 %collective-permute-start.19 = (bf16[24,8192]{1,0:T(8,128)(2,1)S(1)}, bf16[24,8192]{1,0:T(8,128)(2,1)S(1)}, u32[]{:S(2)}, u32[]{:S(2)}) collective-permute-start(bf16[24,8192]{1,0:T(8,128)(2,1)S(1)} %concatenate.24.refs_0_), channel_id=1, source_target_pairs={{0,32},{1,33},{2,34},{3,35},{4,36},{5,37},{6,38},{7,39},{8,40},{9,... | collective-permute-start | bytes 1179656 | tf_op jit(solution)/shard_map/ppermute | solution.py:40
  23.0 26.4 %collective-permute-start.17 = (bf16[24,8192]{1,0:T(8,128)(2,1)S(1)}, bf16[24,8192]{1,0:T(8,128)(2,1)S(1)}, u32[]{:S(2)}, u32[]{:S(2)}) collective-permute-start(bf16[24,8192]{1,0:T(8,128)(2,1)S(1)} %concatenate.24.refs_0_), channel_id=1, source_target_pairs={{0,80},{1,81},{2,82},{3,83},{4,84},{5,85},{6,86},{7,87},{8,88},{9,... | collective-permute-start | bytes 1179656 | tf_op jit(solution)/shard_map/ppermute | solution.py:45
  27.2 16.8 %copy-start.8 = (bf16[3,3584]{1,0:T(4,128)(2,1)}, bf16[3,3584]{1,0:T(4,128)(2,1)S(1)}, u32[]{:S(2)}) copy-start(bf16[3,3584]{1,0:T(4,128)(2,1)S(1)} %collective-permute-done.2) | copy-start | bytes 64516
  27.2 22.2 %collective-permute-start.15 = (bf16[24,8192]{1,0:T(8,128)(2,1)S(1)}, bf16[24,8192]{1,0:T(8,128)(2,1)S(1)}, u32[]{:S(2)}, u32[]{:S(2)}) collective-permute-start(bf16[24,8192]{1,0:T(8,128)(2,1)S(1)} %concatenate.24.refs_0_), channel_id=1, source_target_pairs={{0,64},{1,65},{2,66},{3,67},{4,68},{5,69},{6,70},{7,71},{8,72},{9,... | collective-permute-start | bytes 1179656 | tf_op jit(solution)/shard_map/ppermute | solution.py:45
  27.3 16.7 %copy-start.9 = (bf16[3,3584]{1,0:T(4,128)(2,1)}, bf16[3,3584]{1,0:T(4,128)(2,1)S(1)}, u32[]{:S(2)}) copy-start(bf16[3,3584]{1,0:T(4,128)(2,1)S(1)} %collective-permute-done.1) | copy-start | bytes 64516
  27.3 22.3 %collective-permute-start.18 = (bf16[24,8192]{1,0:T(8,128)(2,1)S(1)}, bf16[24,8192]{1,0:T(8,128)(2,1)S(1)}, u32[]{:S(2)}, u32[]{:S(2)}) collective-permute-start(bf16[24,8192]{1,0:T(8,128)(2,1)S(1)} %pad_maximum_fusion.refs_1_), channel_id=1, source_target_pairs={{0,80},{1,81},{2,82},{3,83},{4,84},{5,85},{6,86},{7,87},{8,88},{9,... | collective-permute-start | bytes 1179656 | tf_op jit(solution)/shard_map/ppermute | solution.py:45
  30.5 13.4 %copy-start.10 = (bf16[3,3584]{1,0:T(4,128)(2,1)}, bf16[3,3584]{1,0:T(4,128)(2,1)S(1)}, u32[]{:S(2)}) copy-start(bf16[3,3584]{1,0:T(4,128)(2,1)S(1)} %collective-permute-done) | copy-start | bytes 64516
  31.3 4.9 %collective-permute-start.5 = (bf16[12,3584]{1,0:T(8,128)(2,1)S(1)}, bf16[12,3584]{1,0:T(8,128)(2,1)S(1)}, u32[]{:S(2)}, u32[]{:S(2)}) collective-permute-start(bf16[12,3584]{1,0:T(8,128)(2,1)S(1)} %pad_maximum_fusion.2), channel_id=1, source_target_pairs={{0,12},{1,13},{2,14},{3,15},{4,0},{5,1},{6,2},{7,3},{8,4},{9,5},{1... | collective-permute-start | bytes 258056 | tf_op jit(solution)/shard_map/ppermute | solution.py:45
  36.2 12.7 %copy-start.4 = (bf16[12,3584]{1,0:T(8,128)(2,1)}, bf16[12,3584]{1,0:T(8,128)(2,1)S(1)}, u32[]{:S(2)}) copy-start(bf16[12,3584]{1,0:T(8,128)(2,1)S(1)} %collective-permute-done.5) | copy-start | bytes 258052
  36.2 6.3 %collective-permute-start.4 = (bf16[12,3584]{1,0:T(8,128)(2,1)S(1)}, bf16[12,3584]{1,0:T(8,128)(2,1)S(1)}, u32[]{:S(2)}, u32[]{:S(2)}) collective-permute-start(bf16[12,3584]{1,0:T(8,128)(2,1)S(1)} %pad_maximum_fusion.2), channel_id=1, source_target_pairs={{0,8},{1,9},{2,10},{3,11},{4,12},{5,13},{6,14},{7,15},{8,0},{9,1},... | collective-permute-start | bytes 258056 | tf_op jit(solution)/shard_map/ppermute | solution.py:45
  42.5 6.4 %copy-start.5 = (bf16[12,3584]{1,0:T(8,128)(2,1)}, bf16[12,3584]{1,0:T(8,128)(2,1)S(1)}, u32[]{:S(2)}) copy-start(bf16[12,3584]{1,0:T(8,128)(2,1)S(1)} %collective-permute-done.4) | copy-start | bytes 258052
  42.5 6.2 %collective-permute-start.3 = (bf16[12,3584]{1,0:T(8,128)(2,1)S(1)}, bf16[12,3584]{1,0:T(8,128)(2,1)S(1)}, u32[]{:S(2)}, u32[]{:S(2)}) collective-permute-start(bf16[12,3584]{1,0:T(8,128)(2,1)S(1)} %pad_maximum_fusion.2), channel_id=1, source_target_pairs={{0,4},{1,5},{2,6},{3,7},{4,8},{5,9},{6,10},{7,11},{8,12},{9,13},{1... | collective-permute-start | bytes 258056 | tf_op jit(solution)/shard_map/ppermute | solution.py:45
  48.8 4.0 %collective-permute-start.20 = (bf16[24,8192]{1,0:T(8,128)(2,1)S(1)}, bf16[24,8192]{1,0:T(8,128)(2,1)S(1)}, u32[]{:S(2)}, u32[]{:S(2)}) collective-permute-start(bf16[24,8192]{1,0:T(8,128)(2,1)S(1)} %pad_maximum_fusion.refs_1_), channel_id=1, source_target_pairs={{0,32},{1,33},{2,34},{3,35},{4,36},{5,37},{6,38},{7,39},{8,40},{9,... | collective-permute-start | bytes 1179656 | tf_op jit(solution)/shard_map/ppermute | solution.py:40
  48.8 9.1 %collective-permute-start.16 = (bf16[24,8192]{1,0:T(8,128)(2,1)S(1)}, bf16[24,8192]{1,0:T(8,128)(2,1)S(1)}, u32[]{:S(2)}, u32[]{:S(2)}) collective-permute-start(bf16[24,8192]{1,0:T(8,128)(2,1)S(1)} %pad_maximum_fusion.refs_1_), channel_id=1, source_target_pairs={{0,64},{1,65},{2,66},{3,67},{4,68},{5,69},{6,70},{7,71},{8,72},{9,... | collective-permute-start | bytes 1179656 | tf_op jit(solution)/shard_map/ppermute | solution.py:45
  49.4 8.4 %collective-permute-start.23 = (bf16[24,8192]{1,0:T(8,128)(2,1)S(1)}, bf16[24,8192]{1,0:T(8,128)(2,1)S(1)}, u32[]{:S(2)}, u32[]{:S(2)}) collective-permute-start(bf16[24,8192]{1,0:T(8,128)(2,1)S(1)} %collective-permute-done.17.refs_4_), channel_id=1, source_target_pairs={{0,32},{1,33},{2,34},{3,35},{4,36},{5,37},{6,38},{7,39},{8,40},{9,... | collective-permute-start | bytes 1179656 | tf_op jit(solution)/shard_map/ppermute | solution.py:40
  49.4 12.7 %collective-permute-start.25 = (bf16[24,8192]{1,0:T(8,128)(2,1)S(1)}, bf16[24,8192]{1,0:T(8,128)(2,1)}, u32[]{:S(2)}, u32[]{:S(2)}) collective-permute-start(bf16[24,8192]{1,0:T(8,128)(2,1)S(1)} %collective-permute-done.15.refs_2_), channel_id=1, source_target_pairs={{0,64},{1,65},{2,66},{3,67},{4,68},{5,69},{6,70},{7,71},{8,72},{9,... | collective-permute-start | bytes 1179656 | tf_op jit(solution)/shard_map/ppermute | solution.py:45
  49.6 12.6 %collective-permute-start.26 = (bf16[24,8192]{1,0:T(8,128)(2,1)S(1)}, bf16[24,8192]{1,0:T(8,128)(2,1)}, u32[]{:S(2)}, u32[]{:S(2)}) collective-permute-start(bf16[24,8192]{1,0:T(8,128)(2,1)S(1)} %collective-permute-done.18.refs_5_), channel_id=1, source_target_pairs={{0,80},{1,81},{2,82},{3,83},{4,84},{5,85},{6,86},{7,87},{8,88},{9,... | collective-permute-start | bytes 1179656 | tf_op jit(solution)/shard_map/ppermute | solution.py:45
  52.7 17.3 %collective-permute-start.21 = (bf16[24,8192]{1,0:T(8,128)(2,1)S(1)}, bf16[24,8192]{1,0:T(8,128)(2,1)}, u32[]{:S(2)}, u32[]{:S(2)}) collective-permute-start(bf16[24,8192]{1,0:T(8,128)(2,1)S(1)} %collective-permute-done.15.refs_2_), channel_id=1, source_target_pairs={{0,32},{1,33},{2,34},{3,35},{4,36},{5,37},{6,38},{7,39},{8,40},{9,... | collective-permute-start | bytes 1179656 | tf_op jit(solution)/shard_map/ppermute | solution.py:40
  57.8 12.3 %collective-permute-start.24 = (bf16[24,8192]{1,0:T(8,128)(2,1)S(1)}, bf16[24,8192]{1,0:T(8,128)(2,1)}, u32[]{:S(2)}, u32[]{:S(2)}) collective-permute-start(bf16[24,8192]{1,0:T(8,128)(2,1)S(1)} %collective-permute-done.18.refs_5_), channel_id=1, source_target_pairs={{0,32},{1,33},{2,34},{3,35},{4,36},{5,37},{6,38},{7,39},{8,40},{9,... | collective-permute-start | bytes 1179656 | tf_op jit(solution)/shard_map/ppermute | solution.py:40
  58.6 12.1 %collective-permute-start.22 = (bf16[24,8192]{1,0:T(8,128)(2,1)S(1)}, bf16[24,8192]{1,0:T(8,128)(2,1)}, u32[]{:S(2)}, u32[]{:S(2)}) collective-permute-start(bf16[24,8192]{1,0:T(8,128)(2,1)S(1)} %collective-permute-done.16.refs_3_), channel_id=1, source_target_pairs={{0,32},{1,33},{2,34},{3,35},{4,36},{5,37},{6,38},{7,39},{8,40},{9,... | collective-permute-start | bytes 1179656 | tf_op jit(solution)/shard_map/ppermute | solution.py:40
  62.1 9.5 %collective-permute-start.27 = (bf16[24,8192]{1,0:T(8,128)(2,1)}, bf16[24,8192]{1,0:T(8,128)(2,1)}, u32[]{:S(2)}, u32[]{:S(2)}) collective-permute-start(bf16[24,8192]{1,0:T(8,128)(2,1)} %collective-permute-done.25.refs_12_), channel_id=1, source_target_pairs={{0,32},{1,33},{2,34},{3,35},{4,36},{5,37},{6,38},{7,39},{8,40},{9,... | collective-permute-start | bytes 1179656 | tf_op jit(solution)/shard_map/ppermute | solution.py:40
  62.1 10.4 %collective-permute-start.28 = (bf16[24,8192]{1,0:T(8,128)(2,1)}, bf16[24,8192]{1,0:T(8,128)(2,1)}, u32[]{:S(2)}, u32[]{:S(2)}) collective-permute-start(bf16[24,8192]{1,0:T(8,128)(2,1)} %collective-permute-done.26.refs_13_), channel_id=1, source_target_pairs={{0,32},{1,33},{2,34},{3,35},{4,36},{5,37},{6,38},{7,39},{8,40},{9,... | collective-permute-start | bytes 1179656 | tf_op jit(solution)/shard_map/ppermute | solution.py:40
  63.0 25.1 %copy-start.12 = (s32[384]{0:T(512)S(1)}, s32[384]{0:T(512)}, u32[]{:S(2)}) copy-start(s32[384]{0:T(512)} %param.10) | copy-start | bytes 4612
  70.0 18.1 %collective-permute-start.29 = (bf16[48,3584]{1,0:T(8,128)(2,1)S(1)}, bf16[48,3584]{1,0:T(8,128)(2,1)}, u32[]{:S(2)}, u32[]{:S(2)}) collective-permute-start(bf16[48,3584]{1,0:T(8,128)(2,1)S(1)} %concatenate.22.refs_0_), channel_id=1, source_target_pairs={{0,32},{1,33},{2,34},{3,35},{4,36},{5,37},{6,38},{7,39},{8,40},{9,... | collective-permute-start | bytes 1032200 | tf_op jit(solution)/shard_map/ppermute | solution.py:40
  70.1 16.8 %collective-permute-start.8 = (bf16[48,3584]{1,0:T(8,128)(2,1)S(1)}, bf16[48,3584]{1,0:T(8,128)(2,1)}, u32[]{:S(2)}, u32[]{:S(2)}) collective-permute-start(bf16[48,3584]{1,0:T(8,128)(2,1)S(1)} %concatenate.22.refs_0_), channel_id=1, source_target_pairs={{0,80},{1,81},{2,82},{3,83},{4,84},{5,85},{6,86},{7,87},{8,88},{9,... | collective-permute-start | bytes 1032200 | tf_op jit(solution)/shard_map/ppermute | solution.py:45
  70.7 16.3 %collective-permute-start.7 = (bf16[48,3584]{1,0:T(8,128)(2,1)S(1)}, bf16[48,3584]{1,0:T(8,128)(2,1)}, u32[]{:S(2)}, u32[]{:S(2)}) collective-permute-start(bf16[48,3584]{1,0:T(8,128)(2,1)S(1)} %concatenate.22.refs_0_), channel_id=1, source_target_pairs={{0,16},{1,17},{2,18},{3,19},{4,20},{5,21},{6,22},{7,23},{8,24},{9,... | collective-permute-start | bytes 1032200 | tf_op jit(solution)/shard_map/ppermute | solution.py:45
  71.6 15.4 %collective-permute-start.6 = (bf16[48,3584]{1,0:T(8,128)(2,1)S(1)}, bf16[48,3584]{1,0:T(8,128)(2,1)}, u32[]{:S(2)}, u32[]{:S(2)}) collective-permute-start(bf16[48,3584]{1,0:T(8,128)(2,1)S(1)} %concatenate.22.refs_0_), channel_id=1, source_target_pairs={{0,64},{1,65},{2,66},{3,67},{4,68},{5,69},{6,70},{7,71},{8,72},{9,... | collective-permute-start | bytes 1032200 | tf_op jit(solution)/shard_map/ppermute | solution.py:45
  85.9 1.1 copy-start
  87.0 2.1 %collective-permute-start.30 = (bf16[48,3584]{1,0:T(8,128)(2,1)}, bf16[48,3584]{1,0:T(8,128)(2,1)S(1)}, u32[]{:S(2)}, u32[]{:S(2)}) collective-permute-start(bf16[48,3584]{1,0:T(8,128)(2,1)} %collective-permute-done.6.refs_1_), channel_id=1, source_target_pairs={{0,32},{1,33},{2,34},{3,35},{4,36},{5,37},{6,38},{7,39},{8,40},{9,... | collective-permute-start | bytes 1032200 | tf_op jit(solution)/shard_map/ppermute | solution.py:40
  87.6 2.0 %collective-permute-start.31 = (bf16[48,3584]{1,0:T(8,128)(2,1)}, bf16[48,3584]{1,0:T(8,128)(2,1)S(1)}, u32[]{:S(2)}, u32[]{:S(2)}) collective-permute-start(bf16[48,3584]{1,0:T(8,128)(2,1)} %collective-permute-done.7.refs_2_), channel_id=1, source_target_pairs={{0,32},{1,33},{2,34},{3,35},{4,36},{5,37},{6,38},{7,39},{8,40},{9,... | collective-permute-start | bytes 1032200 | tf_op jit(solution)/shard_map/ppermute | solution.py:40
  87.7 2.4 %collective-permute-start.32 = (bf16[48,3584]{1,0:T(8,128)(2,1)}, bf16[48,3584]{1,0:T(8,128)(2,1)S(1)}, u32[]{:S(2)}, u32[]{:S(2)}) collective-permute-start(bf16[48,3584]{1,0:T(8,128)(2,1)} %collective-permute-done.8.refs_3_), channel_id=1, source_target_pairs={{0,32},{1,33},{2,34},{3,35},{4,36},{5,37},{6,38},{7,39},{8,40},{9,... | collective-permute-start | bytes 1032200 | tf_op jit(solution)/shard_map/ppermute | solution.py:40
  99.1 1.3 collective-permute-start.33
  100.6 4.9 %collective-permute-start.34 = (f32[8,384]{1,0:T(8,128)S(1)}, f32[8,384]{1,0:T(8,128)S(1)}, u32[]{:S(2)}, u32[]{:S(2)}) collective-permute-start(f32[8,384]{1,0:T(8,128)S(1)} %select_select_fusion.3), channel_id=1, source_target_pairs={{0,1},{1,2},{2,3},{3,0},{4,5},{5,6},{6,7},{7,4},{8,9},{9,10},{10,1... | collective-permute-start | bytes 36872 | tf_op jit(solution)/shard_map/ppermute | solution.py:258
  100.7 5.4 %collective-permute-start.36 = (f32[8,384]{1,0:T(8,128)S(1)}, f32[8,384]{1,0:T(8,128)S(1)}, u32[]{:S(2)}, u32[]{:S(2)}) collective-permute-start(f32[8,384]{1,0:T(8,128)S(1)} %select_select_fusion.3), channel_id=1, source_target_pairs={{0,2},{1,3},{2,0},{3,1},{4,6},{5,7},{6,4},{7,5},{8,10},{9,11},{10,... | collective-permute-start | bytes 36872 | tf_op jit(solution)/shard_map/ppermute | solution.py:262
  105.6 1.2 collective-permute-start.35
  107.1 4.9 %collective-permute-start.37 = (f32[8,384]{1,0:T(8,128)S(1)}, f32[8,384]{1,0:T(8,128)S(1)}, u32[]{:S(2)}, u32[]{:S(2)}) collective-permute-start(f32[8,384]{1,0:T(8,128)S(1)} %select_select_fusion.2), channel_id=1, source_target_pairs={{0,4},{1,5},{2,6},{3,7},{4,8},{5,9},{6,10},{7,11},{8,12},{9,13},{1... | collective-permute-start | bytes 36872 | tf_op jit(solution)/shard_map/ppermute | solution.py:258
  109.4 5.2 %collective-permute-start.39 = (f32[8,384]{1,0:T(8,128)S(1)}, f32[8,384]{1,0:T(8,128)S(1)}, u32[]{:S(2)}, u32[]{:S(2)}) collective-permute-start(f32[8,384]{1,0:T(8,128)S(1)} %select_select_fusion.2), channel_id=1, source_target_pairs={{0,8},{1,9},{2,10},{3,11},{4,12},{5,13},{6,14},{7,15},{8,0},{9,1},... | collective-permute-start | bytes 36872 | tf_op jit(solution)/shard_map/ppermute | solution.py:262
  112.0 2.6 %collective-permute-start.38 = (f32[8,384]{1,0:T(8,128)S(1)}, f32[8,384]{1,0:T(8,128)S(1)}, u32[]{:S(2)}, u32[]{:S(2)}) collective-permute-start(f32[8,384]{1,0:T(8,128)S(1)} %collective-permute-done.37), channel_id=1, source_target_pairs={{0,32},{1,33},{2,34},{3,35},{4,36},{5,37},{6,38},{7,39},{8,40},{9,... | collective-permute-start | bytes 36872 | tf_op jit(solution)/shard_map/ppermute | solution.py:40
  114.9 4.9 %collective-permute-start.40 = (f32[8,384]{1,0:T(8,128)S(1)}, f32[8,384]{1,0:T(8,128)S(1)}, u32[]{:S(2)}, u32[]{:S(2)}) collective-permute-start(f32[8,384]{1,0:T(8,128)S(1)} %select_select_fusion.1), channel_id=1, source_target_pairs={{0,64},{1,65},{2,66},{3,67},{4,68},{5,69},{6,70},{7,71},{8,72},{9,... | collective-permute-start | bytes 36872 | tf_op jit(solution)/shard_map/ppermute | solution.py:258
  115.0 5.5 %collective-permute-start.42 = (f32[8,384]{1,0:T(8,128)S(1)}, f32[8,384]{1,0:T(8,128)S(1)}, u32[]{:S(2)}, u32[]{:S(2)}) collective-permute-start(f32[8,384]{1,0:T(8,128)S(1)} %select_select_fusion.1), channel_id=1, source_target_pairs={{0,16},{1,17},{2,18},{3,19},{4,20},{5,21},{6,22},{7,23},{8,24},{9,... | collective-permute-start | bytes 36872 | tf_op jit(solution)/shard_map/ppermute | solution.py:262
  119.9 1.2 collective-permute-start.41
  121.4 1.3 copy-start.1
  122.7 5.6 %copy-start.13 = (bf16[384,3584]{1,0:T(8,128)(2,1)S(1)}, bf16[384,3584]{1,0:T(8,128)(2,1)}, u32[]{:S(2)}) copy-start(bf16[384,3584]{1,0:T(8,128)(2,1)} %get-tuple-element.28) | copy-start | bytes 8257540
  128.0 5.1 %collective-permute-start.43 = (bf16[192,3584]{1,0:T(8,128)(2,1)S(1)}, bf16[192,3584]{1,0:T(8,128)(2,1)S(1)}, u32[]{:S(2)}, u32[]{:S(2)}) collective-permute-start(bf16[192,3584]{1,0:T(8,128)(2,1)S(1)} %get-tuple-element.27), channel_id=1, source_target_pairs={{0,32},{1,33},{2,34},{3,35},{4,36},{5,37},{6,38},{7,39},{8,40},{9,... | collective-permute-start | bytes 4128776 | tf_op jit(solution)/shard_map/ppermute | solution.py:40
  133.6 7.3 %collective-permute-start.44 = (bf16[48,3584]{1,0:T(8,128)(2,1)S(1)}, bf16[48,3584]{1,0:T(8,128)(2,1)S(1)}, u32[]{:S(2)}, u32[]{:S(2)}) collective-permute-start(bf16[48,3584]{1,0:T(8,128)(2,1)S(1)} %get-tuple-element.55), channel_id=1, source_target_pairs={{0,80},{1,81},{2,82},{3,83},{4,84},{5,85},{6,86},{7,87},{8,88},{9,... | collective-permute-start | bytes 1032200 | tf_op jit(solution)/shard_map/ppermute | solution.py:45
  135.9 12.1 %collective-permute-start.46 = (bf16[48,3584]{1,0:T(8,128)(2,1)S(1)}, bf16[48,3584]{1,0:T(8,128)(2,1)S(1)}, u32[]{:S(2)}, u32[]{:S(2)}) collective-permute-start(bf16[48,3584]{1,0:T(8,128)(2,1)S(1)} %get-tuple-element.56), channel_id=1, source_target_pairs={{0,64},{1,65},{2,66},{3,67},{4,68},{5,69},{6,70},{7,71},{8,72},{9,... | collective-permute-start | bytes 1032200 | tf_op jit(solution)/shard_map/ppermute | solution.py:45
  135.9 12.1 %collective-permute-start.45 = (bf16[48,3584]{1,0:T(8,128)(2,1)S(1)}, bf16[48,3584]{1,0:T(8,128)(2,1)S(1)}, u32[]{:S(2)}, u32[]{:S(2)}) collective-permute-start(bf16[48,3584]{1,0:T(8,128)(2,1)S(1)} %get-tuple-element.57), channel_id=1, source_target_pairs={{0,16},{1,17},{2,18},{3,19},{4,20},{5,21},{6,22},{7,23},{8,24},{9,... | collective-permute-start | bytes 1032200 | tf_op jit(solution)/shard_map/ppermute | solution.py:45
  148.3 4.9 %collective-permute-start.47 = (bf16[12,3584]{1,0:T(8,128)(2,1)S(1)}, bf16[12,3584]{1,0:T(8,128)(2,1)S(1)}, u32[]{:S(2)}, u32[]{:S(2)}) collective-permute-start(bf16[12,3584]{1,0:T(8,128)(2,1)S(1)} %get-tuple-element.58), channel_id=1, source_target_pairs={{0,12},{1,13},{2,14},{3,15},{4,0},{5,1},{6,2},{7,3},{8,4},{9,5},{1... | collective-permute-start | bytes 258056 | tf_op jit(solution)/shard_map/ppermute | solution.py:45
  149.3 6.0 %collective-permute-start.49 = (bf16[12,3584]{1,0:T(8,128)(2,1)S(1)}, bf16[12,3584]{1,0:T(8,128)(2,1)S(1)}, u32[]{:S(2)}, u32[]{:S(2)}) collective-permute-start(bf16[12,3584]{1,0:T(8,128)(2,1)S(1)} %get-tuple-element.59), channel_id=1, source_target_pairs={{0,4},{1,5},{2,6},{3,7},{4,8},{5,9},{6,10},{7,11},{8,12},{9,13},{1... | collective-permute-start | bytes 258056 | tf_op jit(solution)/shard_map/ppermute | solution.py:45
  150.4 6.3 %collective-permute-start.48 = (bf16[12,3584]{1,0:T(8,128)(2,1)S(1)}, bf16[12,3584]{1,0:T(8,128)(2,1)S(1)}, u32[]{:S(2)}, u32[]{:S(2)}) collective-permute-start(bf16[12,3584]{1,0:T(8,128)(2,1)S(1)} %get-tuple-element.60), channel_id=1, source_target_pairs={{0,8},{1,9},{2,10},{3,11},{4,12},{5,13},{6,14},{7,15},{8,0},{9,1},... | collective-permute-start | bytes 258056 | tf_op jit(solution)/shard_map/ppermute | solution.py:45
  156.8 4.6 %collective-permute-start.50 = (bf16[3,3584]{1,0:T(4,128)(2,1)S(1)}, bf16[3,3584]{1,0:T(4,128)(2,1)S(1)}, u32[]{:S(2)}, u32[]{:S(2)}) collective-permute-start(bf16[3,3584]{1,0:T(4,128)(2,1)S(1)} %get-tuple-element.61), channel_id=1, source_target_pairs={{0,3},{1,0},{2,1},{3,2},{4,7},{5,4},{6,5},{7,6},{8,11},{9,8},{10,9... | collective-permute-start | bytes 64520 | tf_op jit(solution)/shard_map/ppermute | solution.py:45
  159.2 5.1 %collective-permute-start.52 = (bf16[3,3584]{1,0:T(4,128)(2,1)S(1)}, bf16[3,3584]{1,0:T(4,128)(2,1)S(1)}, u32[]{:S(2)}, u32[]{:S(2)}) collective-permute-start(bf16[3,3584]{1,0:T(4,128)(2,1)S(1)} %get-tuple-element.62), channel_id=1, source_target_pairs={{0,1},{1,2},{2,3},{3,0},{4,5},{5,6},{6,7},{7,4},{8,9},{9,10},{10,1... | collective-permute-start | bytes 64520 | tf_op jit(solution)/shard_map/ppermute | solution.py:45
  159.2 5.4 %collective-permute-start.51 = (bf16[3,3584]{1,0:T(4,128)(2,1)S(1)}, bf16[3,3584]{1,0:T(4,128)(2,1)S(1)}, u32[]{:S(2)}, u32[]{:S(2)}) collective-permute-start(bf16[3,3584]{1,0:T(4,128)(2,1)S(1)} %get-tuple-element.63), channel_id=1, source_target_pairs={{0,2},{1,3},{2,0},{3,1},{4,6},{5,7},{6,4},{7,5},{8,10},{9,11},{10,... | collective-permute-start | bytes 64520 | tf_op jit(solution)/shard_map/ppermute | solution.py:45
  (3 other events, 2.4 us)

commit v4 on v3

--- a/solution.py
+++ b/solution.py
@@ -57,6 +57,16 @@
     return jnp.where(first, tokens[0], tokens[1])[None, :]
 
 
+def stack(pieces):
+    total, at = sum(p.shape[0] for p in pieces), 0
+    padded = []
+    for p in pieces:
+        low = jnp.array(-jnp.inf, p.dtype)
+        padded.append(lax.pad(p, low, ((at, total - at - p.shape[0], 0), (0, 0, 0))))
+        at += p.shape[0]
+    return functools.reduce(jnp.maximum, padded)
+
+
 def split3(v):
     high = v.astype(BF16)
     rest = v - high.astype(F32)
@@ -90,7 +100,7 @@
 
 
 def teacher_kernel(n, *refs):
-    blocks, (source, tok_row, owner, w, out, wbuf, sem) = refs[:n], refs[n:]
+    blocks, (source, tok_row, owner, w, saved, out, wbuf, sem) = refs[:n], refs[n:]
     slots, chunk, _ = wbuf.shape
     count = w.shape[0] // chunk
 
@@ -111,12 +121,19 @@
     owner_col = pick_column(to_column(tok_row[...]), owner[...])
     pick = one_hot(owner_col, source[...])
     high, middle, low = split3(out[...])
-    out[...] = (dot(pick, high) + dot(pick, middle)) + dot(pick, low)
+    saves = []
+    for i in range(3):
+        rows = slice(i * 128, (i + 1) * 128)
+        out[rows, :] = (dot(pick[rows], high) + dot(pick[rows], middle)) + dot(pick[rows], low)
+        saves.append(pltpu.make_async_copy(out.at[rows, :], saved.at[rows, :], sem.at[slots + i]))
+        saves[-1].start()
+    for save in saves:
+        save.wait()
 
 
 def student_kernel(n, *refs):
     blocks, refs = refs[:n], refs[n:]
-    at_ref, t_ref, tok_row, labels, w, s_save, t_save, g_save, stats_out, s_out, g, wbuf, table, label_at, sem = refs
+    at_ref, t_in, tok_row, labels, w, s_save, g_save, stats_out, t_ref, s_out, g, wbuf, table, label_at, sem = refs
     chunk = 896
     count = w.shape[0] // chunk
 
@@ -130,9 +147,10 @@
     for block in blocks:
         g[pl.ds(at, block.shape[0]), :] = block[...]
         at += block.shape[0]
-    saves = [pltpu.make_async_copy(*pair, sem.at[count + i]) for i, pair in enumerate([(t_ref, t_save), (g, g_save), (s_out, s_save)])]
+    load = pltpu.make_async_copy(t_in, t_ref, sem.at[count + 2])
+    load.start()
+    saves = [pltpu.make_async_copy(*pair, sem.at[count + i]) for i, pair in enumerate([(g, g_save), (s_out, s_save)])]
     saves[0].start()
-    saves[1].start()
     s_out[...] = jnp.zeros_like(s_out)
     tok_col = to_column(tok_row[...])
     label_at[...] = pick_column(tok_col, labels[...]) - at_ref[0]
@@ -143,7 +161,8 @@
         copy(i).wait()
         s_out[...] += dot(g[:, rows], wbuf[rows, :])
 
-    saves[2].start()
+    saves[1].start()
+    load.wait()
     step = 64
     lane = lax.broadcasted_iota(jnp.int32, (step, 128), 1)
     for i in range(TOKENS // step):
@@ -271,13 +290,12 @@
     label_row, owner_row = labels[None, :], owner_map[None, :]
 
     parts = [teacher_hidden] + [shift(teacher_hidden, 0, k) for k in (1, 2, 3)]
-    t = jnp.concatenate(parts, axis=0)
-    t = jnp.concatenate([t] + [shift(t, 1, k) for k in (1, 2, 3)], axis=0)
+    t = stack(parts)
+    t = [t] + [shift(t, 1, k) for k in (1, 2, 3)]
     parts = [student_hidden] + [shift(student_hidden, 0, k) for k in (1, 2, 3)]
-    s = jnp.concatenate(parts, axis=0)
-    s = lax.optimization_barrier(jnp.concatenate([s] + [shift(s, 1, k) for k in (1, 2, 3)], axis=0))
-    size = t.shape[0] // 2
-    a, b = t[:size], t[size:]
+    s = stack(parts)
+    s = stack([s] + [shift(s, 1, k) for k in (1, 2, 3)])
+    a, b = stack(t[:2]), stack(t[2:])
     before_a, after_b = shift(a, 2, 1), shift(b, 2, -1)
     before_b, after_a = shift(b, 2, 1), shift(a, 2, -1)
     far = [shift(before_a, 2, 1), shift(after_b, 2, -1)]
@@ -296,20 +314,22 @@
         [((TOKENS, vocab), F32)],
         [VMEM] * (len(blocks) + 3) + [HBM],
         [*blocks, source, tok_row, owner_row, teacher_head],
-        [pltpu.VMEM((3, 1024, vocab), BF16), pltpu.SemaphoreType.DMA((3,))],
-        44,
+        [pltpu.VMEM((TOKENS, vocab), F32), pltpu.VMEM((3, 1024, vocab), BF16), pltpu.SemaphoreType.DMA((6,))],
+        50,
         2 * TOKENS * tk * vocab,
+        [HBM],
     )
     *s_moved, t_logits = lax.optimization_barrier((*s_moved, t_logits))
     s_own = [s0, *s_moved]
     s_blocks = s_own + [swap(v) for v in s_own]
     n = len(s_blocks)
-    s_logits, t_logits, hidden, stats = call(
+    s_logits, hidden, stats = call(
         functools.partial(student_kernel, n),
-        [((TOKENS, vocab), F32), ((TOKENS, vocab), F32), ((TOKENS, sk), BF16), ((8, TOKENS), F32)],
-        [VMEM] * n + [SMEM] + [VMEM] * 3 + [HBM],
+        [((TOKENS, vocab), F32), ((TOKENS, sk), BF16), ((8, TOKENS), F32)],
+        [VMEM] * n + [SMEM, HBM] + [VMEM] * 2 + [HBM],
         [*s_blocks, at, t_logits, tok_row, label_row, student_head],
         [
+            pltpu.VMEM((TOKENS, vocab), F32),
             pltpu.VMEM((TOKENS, vocab), F32),
             pltpu.VMEM((TOKENS, sk), BF16),
             pltpu.VMEM((sk, vocab), BF16),
@@ -319,7 +339,7 @@
         ],
         50,
         2 * TOKENS * sk * vocab,
-        [HBM, HBM, HBM, VMEM],
+        [HBM, HBM, VMEM],
     )
 
     stats = merge([stats, swap(stats)])
@@ -340,7 +360,7 @@
             pltpu.VMEM((TOKENS, 1), jnp.int32),
             pltpu.SemaphoreType.DMA((6,)),
         ],
-        44,
+        46,
         2 * TOKENS * sk * vocab,
     )
 

time: 166 us -> 163 us (0.982)
  local copies, waits for them, and re-layouts: 15 us -> 3.97 us
  starting transfers between devices: 54.1 us -> 59.1 us
    concatenate x2 -> x0, local copies, waits for them, and re-layouts: 8.98 us -> none  [the longest x1 6.98 us: shards(): jnp.concatenate([s] + [shift(s, 1, k) for k in (1, 2, 3)], axis=0)]
    ppermute x30, starting transfers between devices: 41.8 us -> 45.5 us  [shift(): return lax.ppermute(value, AXES, pairs)]
    max x0 -> x5, other arithmetic: none -> 3.24 us  [stack(): return functools.reduce(jnp.maximum, padded)]
    ppermute x30, waiting for transfers between devices: 46.3 us -> 48.3 us  [shift(): return lax.ppermute(value, AXES, pairs)]
    unnamed x28 -> x26, local copies, waits for them, and re-layouts: 4.53 us -> 2.49 us
    concatenate x3 -> x0, other arithmetic: 1.99 us -> none  [the longest x1 1.04 us: shards(): t = jnp.concatenate(parts, axis=0)]
  transfers between devices with their start and end apart: 53 -> 53, of which waited for: 30 -> 30; matrix products, arithmetic and copies ran while one was open for 9% -> 5% of each run, Pallas kernels for 8% -> 8%
where the time goes in v4:
time: 163 us; the launch traced here: 162 us
  waiting for transfers between devices  60.8 us (37%)
  starting transfers between devices  59.1 us (36%)
  Pallas kernels  27 us (17%)
  other arithmetic  5.32 us (3%)
  matrix products  4.82 us (3%)
  local copies, waits for them, and re-layouts  3.97 us (2%)
    ppermute x30, waiting for transfers between devices, shift(): return lax.ppermute(value, AXES, pairs)  48.3 us
    ppermute x30, starting transfers between devices, shift(): return lax.ppermute(value, AXES, pairs)  45.5 us
    pallas_call x3, Pallas kernels, call(): pl.pallas_call(kernel, out_shape=[jax.ShapeDtypeStruct(*o) for o in out],...  27 us
    ppermute x3, starting transfers between devices, across(): lax.ppermute(value, AXES, [(d, moved(d, dim, 2)) for d in range(DEVICES)])  6.91 us
    ppermute x3, waiting for transfers between devices, ring_shift(): lax.ppermute(value, AXES, [(d, moved(d, dim, -1 if coords(d)['c'] else 1)...  4.89 us
    dot_general x1, matrix products, shards(): lax.dot_general(hidden, grads, (((0,), (0,)), ((), ())), preferred_elemen...  4.82 us
    ppermute x3, waiting for transfers between devices, across(): lax.ppermute(value, AXES, [(d, moved(d, dim, 2)) for d in range(DEVICES)])  3.83 us
    ppermute x17, waiting for transfers between devices, swap(): return lax.ppermute(value, AXES, [(d, d ^ 32) for d in range(DEVICES)])  3.81 us
  transfers between devices with their start and end apart: 53, of which 30 were waited for; matrix products, arithmetic and copies ran while one was open for 5% of the time, Pallas kernels for 8%

profile of v4, /device:TPU:0, one launch (start us, length us, event | category | flops | bytes accessed | tf_op | source)
XLA Modules:
  0.0 162.2 jit_solution(8216057850232732865)
XLA Ops:
  0.6 1.8 %collective-permute-start.9 = (bf16[3,8192]{1,0:T(4,128)(2,1)}, bf16[3,8192]{1,0:T(4,128)(2,1)S(1)}, u32[]{:S(2)}, u32[]{:S(2)}) collective-permute-start(bf16[3,8192]{1,0:T(4,128)(2,1)} %param.6), channel_id=1, source_target_pairs={{0,1},{1,2},{2,3},{3,0},{4,5},{5,6},{6,7},{7,4},{8,9},{9,10},{10,1... | collective-permute-start | bytes 147464 | tf_op jit(solution)/shard_map/ppermute | solution.py:45
  2.4 1.5 collective-permute-start.11
  3.9 2.1 %collective-permute-start.10 = (bf16[3,8192]{1,0:T(4,128)(2,1)}, bf16[3,8192]{1,0:T(4,128)(2,1)S(1)}, u32[]{:S(2)}, u32[]{:S(2)}) collective-permute-start(bf16[3,8192]{1,0:T(4,128)(2,1)} %param.6), channel_id=1, source_target_pairs={{0,2},{1,3},{2,0},{3,1},{4,6},{5,7},{6,4},{7,5},{8,10},{9,11},{10,... | collective-permute-start | bytes 147464 | tf_op jit(solution)/shard_map/ppermute | solution.py:45
  6.9 3.1 %collective-permute-done.10 = bf16[3,8192]{1,0:T(4,128)(2,1)S(1)} collective-permute-done((bf16[3,8192]{1,0:T(4,128)(2,1)}, bf16[3,8192]{1,0:T(4,128)(2,1)S(1)}, u32[]{:S(2)}, u32[]{:S(2)}) %collective-permute-start.10) | collective-permute-done | bytes 49184 | tf_op jit(solution)/shard_map/ppermute | solution.py:45
  9.9 1.0 pad_maximum_fusion.3
  11.0 1.7 %collective-permute-start.12 = (bf16[12,8192]{1,0:T(8,128)(2,1)S(1)}, bf16[12,8192]{1,0:T(8,128)(2,1)S(1)}, u32[]{:S(2)}, u32[]{:S(2)}) collective-permute-start(bf16[12,8192]{1,0:T(8,128)(2,1)S(1)} %pad_maximum_fusion.3), channel_id=1, source_target_pairs={{0,4},{1,5},{2,6},{3,7},{4,8},{5,9},{6,10},{7,11},{8,12},{9,13},{1... | collective-permute-start | bytes 589832 | tf_op jit(solution)/shard_map/ppermute | solution.py:45
  13.0 2.9 %collective-permute-start.2 = (bf16[3,3584]{1,0:T(4,128)(2,1)}, bf16[3,3584]{1,0:T(4,128)(2,1)S(1)}, u32[]{:S(2)}, u32[]{:S(2)}) collective-permute-start(bf16[3,3584]{1,0:T(4,128)(2,1)} %param.8), channel_id=1, source_target_pairs={{0,3},{1,0},{2,1},{3,2},{4,7},{5,4},{6,5},{7,6},{8,11},{9,8},{10,9... | collective-permute-start | bytes 64520 | tf_op jit(solution)/shard_map/ppermute | solution.py:45
  15.9 0.8 collective-permute-start.1
  16.7 1.7 %collective-permute-start.14 = (bf16[12,8192]{1,0:T(8,128)(2,1)S(1)}, bf16[12,8192]{1,0:T(8,128)(2,1)S(1)}, u32[]{:S(2)}, u32[]{:S(2)}) collective-permute-start(bf16[12,8192]{1,0:T(8,128)(2,1)S(1)} %pad_maximum_fusion.3), channel_id=1, source_target_pairs={{0,12},{1,13},{2,14},{3,15},{4,0},{5,1},{6,2},{7,3},{8,4},{9,5},{1... | collective-permute-start | bytes 589832 | tf_op jit(solution)/shard_map/ppermute | solution.py:45
  18.6 1.9 %collective-permute-start.13 = (bf16[12,8192]{1,0:T(8,128)(2,1)S(1)}, bf16[12,8192]{1,0:T(8,128)(2,1)S(1)}, u32[]{:S(2)}, u32[]{:S(2)}) collective-permute-start(bf16[12,8192]{1,0:T(8,128)(2,1)S(1)} %pad_maximum_fusion.3), channel_id=1, source_target_pairs={{0,8},{1,9},{2,10},{3,11},{4,12},{5,13},{6,14},{7,15},{8,0},{9,1},... | collective-permute-start | bytes 589832 | tf_op jit(solution)/shard_map/ppermute | solution.py:45
  20.6 4.5 %collective-permute-done.14 = bf16[12,8192]{1,0:T(8,128)(2,1)S(1)} collective-permute-done((bf16[12,8192]{1,0:T(8,128)(2,1)S(1)}, bf16[12,8192]{1,0:T(8,128)(2,1)S(1)}, u32[]{:S(2)}, u32[]{:S(2)}) %collective-permute-start.14) | collective-permute-done | bytes 196640 | tf_op jit(solution)/shard_map/ppermute | solution.py:45
  25.1 1.4 collective-permute-done.13
  26.5 4.1 %collective-permute-start.17 = (bf16[24,8192]{1,0:T(8,128)(2,1)S(1)}, bf16[24,8192]{1,0:T(8,128)(2,1)S(1)}, u32[]{:S(2)}, u32[]{:S(2)}) collective-permute-start(bf16[24,8192]{1,0:T(8,128)(2,1)S(1)} %pad_maximum_fusion.1.refs_0_), channel_id=1, source_target_pairs={{0,80},{1,81},{2,82},{3,83},{4,84},{5,85},{6,86},{7,87},{8,88},{9,... | collective-permute-start | bytes 1179656 | tf_op jit(solution)/shard_map/ppermute | solution.py:45
  30.9 3.2 %collective-permute-start.18 = (bf16[24,8192]{1,0:T(8,128)(2,1)S(1)}, bf16[24,8192]{1,0:T(8,128)(2,1)S(1)}, u32[]{:S(2)}, u32[]{:S(2)}) collective-permute-start(bf16[24,8192]{1,0:T(8,128)(2,1)S(1)} %pad_maximum_fusion.refs_1_), channel_id=1, source_target_pairs={{0,80},{1,81},{2,82},{3,83},{4,84},{5,85},{6,86},{7,87},{8,88},{9,... | collective-permute-start | bytes 1179656 | tf_op jit(solution)/shard_map/ppermute | solution.py:45
  34.1 0.8 pad_maximum_fusion.4
  34.9 2.3 %collective-permute-start.5 = (bf16[12,3584]{1,0:T(8,128)(2,1)S(1)}, bf16[12,3584]{1,0:T(8,128)(2,1)S(1)}, u32[]{:S(2)}, u32[]{:S(2)}) collective-permute-start(bf16[12,3584]{1,0:T(8,128)(2,1)S(1)} %pad_maximum_fusion.4), channel_id=1, source_target_pairs={{0,12},{1,13},{2,14},{3,15},{4,0},{5,1},{6,2},{7,3},{8,4},{9,5},{1... | collective-permute-start | bytes 258056 | tf_op jit(solution)/shard_map/ppermute | solution.py:45
  37.2 2.6 %collective-permute-done.5 = bf16[12,3584]{1,0:T(8,128)(2,1)S(1)} collective-permute-done((bf16[12,3584]{1,0:T(8,128)(2,1)S(1)}, bf16[12,3584]{1,0:T(8,128)(2,1)S(1)}, u32[]{:S(2)}, u32[]{:S(2)}) %collective-permute-start.5) | collective-permute-done | bytes 86048 | tf_op jit(solution)/shard_map/ppermute | solution.py:45
  39.8 1.8 %collective-permute-start.4 = (bf16[12,3584]{1,0:T(8,128)(2,1)S(1)}, bf16[12,3584]{1,0:T(8,128)(2,1)S(1)}, u32[]{:S(2)}, u32[]{:S(2)}) collective-permute-start(bf16[12,3584]{1,0:T(8,128)(2,1)S(1)} %pad_maximum_fusion.4), channel_id=1, source_target_pairs={{0,8},{1,9},{2,10},{3,11},{4,12},{5,13},{6,14},{7,15},{8,0},{9,1},... | collective-permute-start | bytes 258056 | tf_op jit(solution)/shard_map/ppermute | solution.py:45
  41.6 4.5 %collective-permute-done.4 = bf16[12,3584]{1,0:T(8,128)(2,1)S(1)} collective-permute-done((bf16[12,3584]{1,0:T(8,128)(2,1)S(1)}, bf16[12,3584]{1,0:T(8,128)(2,1)S(1)}, u32[]{:S(2)}, u32[]{:S(2)}) %collective-permute-start.4) | collective-permute-done | bytes 86048 | tf_op jit(solution)/shard_map/ppermute | solution.py:45
  46.1 1.4 collective-permute-start.3
  47.5 4.8 %collective-permute-done.3 = bf16[12,3584]{1,0:T(8,128)(2,1)S(1)} collective-permute-done((bf16[12,3584]{1,0:T(8,128)(2,1)S(1)}, bf16[12,3584]{1,0:T(8,128)(2,1)S(1)}, u32[]{:S(2)}, u32[]{:S(2)}) %collective-permute-start.3) | collective-permute-done | bytes 86048 | tf_op jit(solution)/shard_map/ppermute | solution.py:45
  53.0 3.1 %collective-permute-start.26 = (bf16[24,8192]{1,0:T(8,128)(2,1)S(1)}, bf16[24,8192]{1,0:T(8,128)(2,1)}, u32[]{:S(2)}, u32[]{:S(2)}) collective-permute-start(bf16[24,8192]{1,0:T(8,128)(2,1)S(1)} %collective-permute-done.18.refs_5_), channel_id=1, source_target_pairs={{0,80},{1,81},{2,82},{3,83},{4,84},{5,85},{6,86},{7,87},{8,88},{9,... | collective-permute-start | bytes 1179656 | tf_op jit(solution)/shard_map/ppermute | solution.py:45
  56.6 4.7 %collective-permute-done.16.refs_3_ = bf16[24,8192]{1,0:T(8,128)(2,1)S(1)} collective-permute-done((bf16[24,8192]{1,0:T(8,128)(2,1)S(1)}, bf16[24,8192]{1,0:T(8,128)(2,1)S(1)}, u32[]{:S(2)}, u32[]{:S(2)}) %collective-permute-start.16) | collective-permute-done | bytes 393248 | tf_op jit(solution)/shard_map/ppermute | solution.py:45
  61.3 0.5 collective-permute-start.22
  61.8 3.8 %collective-permute-done.25.refs_12_ = bf16[24,8192]{1,0:T(8,128)(2,1)} collective-permute-done((bf16[24,8192]{1,0:T(8,128)(2,1)S(1)}, bf16[24,8192]{1,0:T(8,128)(2,1)}, u32[]{:S(2)}, u32[]{:S(2)}) %collective-permute-start.25) | collective-permute-done | bytes 393248 | tf_op jit(solution)/shard_map/ppermute | solution.py:45
  66.2 1.2 pad_maximum_fusion.2.refs_0_
  68.0 0.9 collective-permute-start.7
  68.9 0.9 collective-permute-start.6
  69.9 0.7 copy-done.6
  70.6 13.4 %shard_map.85.refs_9_.t_in = f32[384,768]{1,0:T(8,128)} custom-call(bf16[24,8192]{1,0:T(8,128)(2,1)S(1)} %pad_maximum_fusion.1.refs_0_, bf16[24,8192]{1,0:T(8,128)(2,1)S(1)} %pad_maximum_fusion.refs_1_, bf16[24,8192]{1,0:T(8,128)(2,1)S(1)} %collective-permute-done.15.refs_2_, bf16[24,8192]{1,0:T(8,128)(2,1)S(1)} %collective-permute-done.16.refs_3_, ...), custom_call_target="tpu_custom_call" | custom-call | flops 4831838208 | bytes 4194304 | tf_op jit(solution)/shard_map/pallas_call | solution.py:248
  84.0 0.7 collective-permute-start.30
  85.2 1.0 collective-permute-done.30.refs_5_
  87.2 0.7 copy-done.1
  87.9 1.0 copy-done.2
  88.9 8.3 %shard_map.86 = (f32[384,768]{1,0:T(8,128)S(1)}, bf16[384,3584]{1,0:T(8,128)(2,1)}, f32[8,384]{1,0:T(8,128)S(1)}) custom-call(bf16[48,3584]{1,0:T(8,128)(2,1)S(1)} %pad_maximum_fusion.2.refs_0_, bf16[48,3584]{1,0:T(8,128)(2,1)} %collective-permute-done.6.refs_1_, bf16[48,3584]{1,0:T(8,128)(2,1)} %collective-permute-done.7.refs_2_, ...), custom_call_target="tpu_custom_call" | custom-call | flops 2113929216 | bytes 4194304 | tf_op jit(solution)/shard_map/pallas_call | solution.py:248
  97.6 0.8 collective-permute-done.33
  98.7 0.7 collective-permute-start.34
  99.4 2.2 %collective-permute-start.36 = (f32[8,384]{1,0:T(8,128)S(1)}, f32[8,384]{1,0:T(8,128)S(1)}, u32[]{:S(2)}, u32[]{:S(2)}) collective-permute-start(f32[8,384]{1,0:T(8,128)S(1)} %select_select_fusion.3), channel_id=1, source_target_pairs={{0,2},{1,3},{2,0},{3,1},{4,6},{5,7},{6,4},{7,5},{8,10},{9,11},{10,... | collective-permute-start | bytes 36872 | tf_op jit(solution)/shard_map/ppermute | solution.py:281
  101.6 2.1 %collective-permute-done.34 = f32[8,384]{1,0:T(8,128)S(1)} collective-permute-done((f32[8,384]{1,0:T(8,128)S(1)}, f32[8,384]{1,0:T(8,128)S(1)}, u32[]{:S(2)}, u32[]{:S(2)}) %collective-permute-start.34) | collective-permute-done | bytes 12320 | tf_op jit(solution)/shard_map/ppermute | solution.py:277
  103.6 1.0 collective-permute-done.36
  105.2 2.2 %collective-permute-start.37 = (f32[8,384]{1,0:T(8,128)S(1)}, f32[8,384]{1,0:T(8,128)S(1)}, u32[]{:S(2)}, u32[]{:S(2)}) collective-permute-start(f32[8,384]{1,0:T(8,128)S(1)} %select_select_fusion.2), channel_id=1, source_target_pairs={{0,4},{1,5},{2,6},{3,7},{4,8},{5,9},{6,10},{7,11},{8,12},{9,13},{1... | collective-permute-start | bytes 36872 | tf_op jit(solution)/shard_map/ppermute | solution.py:277
  107.4 1.7 %collective-permute-start.39 = (f32[8,384]{1,0:T(8,128)S(1)}, f32[8,384]{1,0:T(8,128)S(1)}, u32[]{:S(2)}, u32[]{:S(2)}) collective-permute-start(f32[8,384]{1,0:T(8,128)S(1)} %select_select_fusion.2), channel_id=1, source_target_pairs={{0,8},{1,9},{2,10},{3,11},{4,12},{5,13},{6,14},{7,15},{8,0},{9,1},... | collective-permute-start | bytes 36872 | tf_op jit(solution)/shard_map/ppermute | solution.py:281
  109.1 1.0 collective-permute-done.37
  110.1 2.5 %collective-permute-done.39 = f32[8,384]{1,0:T(8,128)S(1)} collective-permute-done((f32[8,384]{1,0:T(8,128)S(1)}, f32[8,384]{1,0:T(8,128)S(1)}, u32[]{:S(2)}, u32[]{:S(2)}) %collective-permute-start.39) | collective-permute-done | bytes 12320 | tf_op jit(solution)/shard_map/ppermute | solution.py:281
  113.2 3.0 %collective-permute-start.42 = (f32[8,384]{1,0:T(8,128)S(1)}, f32[8,384]{1,0:T(8,128)S(1)}, u32[]{:S(2)}, u32[]{:S(2)}) collective-permute-start(f32[8,384]{1,0:T(8,128)S(1)} %select_select_fusion.1), channel_id=1, source_target_pairs={{0,16},{1,17},{2,18},{3,19},{4,20},{5,21},{6,22},{7,23},{8,24},{9,... | collective-permute-start | bytes 36872 | tf_op jit(solution)/shard_map/ppermute | solution.py:281
  116.2 1.9 %collective-permute-done.40 = f32[8,384]{1,0:T(8,128)S(1)} collective-permute-done((f32[8,384]{1,0:T(8,128)S(1)}, f32[8,384]{1,0:T(8,128)S(1)}, u32[]{:S(2)}, u32[]{:S(2)}) %collective-permute-start.40) | collective-permute-done | bytes 12320 | tf_op jit(solution)/shard_map/ppermute | solution.py:277
  118.4 0.8 collective-permute-done.41
  119.6 5.3 %shard_map.87 = (bf16[384,768]{1,0:T(8,128)(2,1)S(1)}, bf16[192,3584]{1,0:T(8,128)(2,1)S(1)}, f32[192,3584]{1,0:T(8,128)S(1)}, f32[1,384]{1,0:T(1,128)S(1)}) custom-call(s32[1]{0:T(128)} %bitcast.refs_8_.at_ref, f32[384,768]{1,0:T(8,128)S(1)} %copy-done, f32[384,768]{1,0:T(8,128)S(1)} %get-tuple-element.21.s_in, f32[8,384]{1,0:T(8,128)S(1)} %select_select_fusion.stats, ...), custom_call_target="tpu_custom_call" | custom-call | flops 2113929216 | bytes 4194304 | tf_op jit(solution)/shard_map/pallas_call | solution.py:248
  125.2 4.8 %convolution_convert_fusion = bf16[3584,768]{1,0:T(8,128)(2,1)} fusion(bf16[384,3584]{1,0:T(8,128)(2,1)S(1)} %copy-done.12, bf16[384,768]{1,0:T(8,128)(2,1)S(1)} %get-tuple-element.27), kind=kOutput, calls=%fused_computation | convolution fusion | flops 2116681728 | bytes 8847360 | tf_op jit(solution)/shard_map/dot_general | solution.py:368
  130.5 2.3 %collective-permute-start.44 = (bf16[48,3584]{1,0:T(8,128)(2,1)S(1)}, bf16[48,3584]{1,0:T(8,128)(2,1)S(1)}, u32[]{:S(2)}, u32[]{:S(2)}) collective-permute-start(bf16[48,3584]{1,0:T(8,128)(2,1)S(1)} %get-tuple-element.53), channel_id=1, source_target_pairs={{0,80},{1,81},{2,82},{3,83},{4,84},{5,85},{6,86},{7,87},{8,88},{9,... | collective-permute-start | bytes 1032200 | tf_op jit(solution)/shard_map/ppermute | solution.py:45
  132.8 1.8 %collective-permute-start.45 = (bf16[48,3584]{1,0:T(8,128)(2,1)S(1)}, bf16[48,3584]{1,0:T(8,128)(2,1)S(1)}, u32[]{:S(2)}, u32[]{:S(2)}) collective-permute-start(bf16[48,3584]{1,0:T(8,128)(2,1)S(1)} %get-tuple-element.55), channel_id=1, source_target_pairs={{0,16},{1,17},{2,18},{3,19},{4,20},{5,21},{6,22},{7,23},{8,24},{9,... | collective-permute-start | bytes 1032200 | tf_op jit(solution)/shard_map/ppermute | solution.py:45
  134.7 3.2 %collective-permute-done.44 = bf16[48,3584]{1,0:T(8,128)(2,1)S(1)} collective-permute-done((bf16[48,3584]{1,0:T(8,128)(2,1)S(1)}, bf16[48,3584]{1,0:T(8,128)(2,1)S(1)}, u32[]{:S(2)}, u32[]{:S(2)}) %collective-permute-start.44) | collective-permute-done | bytes 344096 | tf_op jit(solution)/shard_map/ppermute | solution.py:45
  137.9 7.1 %collective-permute-done.46 = bf16[48,3584]{1,0:T(8,128)(2,1)S(1)} collective-permute-done((bf16[48,3584]{1,0:T(8,128)(2,1)S(1)}, bf16[48,3584]{1,0:T(8,128)(2,1)S(1)}, u32[]{:S(2)}, u32[]{:S(2)}) %collective-permute-start.46) | collective-permute-done | bytes 344096 | tf_op jit(solution)/shard_map/ppermute | solution.py:45
  145.2 1.1 collective-permute-start.47
  146.3 1.0 collective-permute-start.49
  147.3 1.7 %collective-permute-start.48 = (bf16[12,3584]{1,0:T(8,128)(2,1)S(1)}, bf16[12,3584]{1,0:T(8,128)(2,1)S(1)}, u32[]{:S(2)}, u32[]{:S(2)}) collective-permute-start(bf16[12,3584]{1,0:T(8,128)(2,1)S(1)} %get-tuple-element.58), channel_id=1, source_target_pairs={{0,8},{1,9},{2,10},{3,11},{4,12},{5,13},{6,14},{7,15},{8,0},{9,1},... | collective-permute-start | bytes 258056 | tf_op jit(solution)/shard_map/ppermute | solution.py:45
  149.0 1.0 collective-permute-done.47
  150.1 2.3 %collective-permute-done.49 = bf16[12,3584]{1,0:T(8,128)(2,1)S(1)} collective-permute-done((bf16[12,3584]{1,0:T(8,128)(2,1)S(1)}, bf16[12,3584]{1,0:T(8,128)(2,1)S(1)}, u32[]{:S(2)}, u32[]{:S(2)}) %collective-permute-start.49) | collective-permute-done | bytes 86048 | tf_op jit(solution)/shard_map/ppermute | solution.py:45
  152.3 1.3 collective-permute-done.48
  153.7 2.4 %collective-permute-start.50 = (bf16[3,3584]{1,0:T(4,128)(2,1)S(1)}, bf16[3,3584]{1,0:T(4,128)(2,1)S(1)}, u32[]{:S(2)}, u32[]{:S(2)}) collective-permute-start(bf16[3,3584]{1,0:T(4,128)(2,1)S(1)} %get-tuple-element.59), channel_id=1, source_target_pairs={{0,3},{1,0},{2,1},{3,2},{4,7},{5,4},{6,5},{7,6},{8,11},{9,8},{10,9... | collective-permute-start | bytes 64520 | tf_op jit(solution)/shard_map/ppermute | solution.py:45
  156.1 1.7 %collective-permute-start.51 = (bf16[3,3584]{1,0:T(4,128)(2,1)S(1)}, bf16[3,3584]{1,0:T(4,128)(2,1)S(1)}, u32[]{:S(2)}, u32[]{:S(2)}) collective-permute-start(bf16[3,3584]{1,0:T(4,128)(2,1)S(1)} %get-tuple-element.61), channel_id=1, source_target_pairs={{0,2},{1,3},{2,0},{3,1},{4,6},{5,7},{6,4},{7,5},{8,10},{9,11},{10,... | collective-permute-start | bytes 64520 | tf_op jit(solution)/shard_map/ppermute | solution.py:45
  157.9 0.6 dynamic-slice_bitcast_fusion
  158.5 2.8 %collective-permute-done.52 = bf16[3,3584]{1,0:T(4,128)(2,1)S(1)} collective-permute-done((bf16[3,3584]{1,0:T(4,128)(2,1)S(1)}, bf16[3,3584]{1,0:T(4,128)(2,1)S(1)}, u32[]{:S(2)}, u32[]{:S(2)}) %collective-permute-start.52) | collective-permute-done | bytes 21536 | tf_op jit(solution)/shard_map/ppermute | solution.py:45
  161.5 0.6 fusion
  (130 shorter events, 9.4 us)
Async XLA Ops:
  0.6 55.7 %copy-start.10 = (s32[384]{0:T(512)S(1)}, s32[384]{0:T(512)}, u32[]{:S(2)}) copy-start(s32[384]{0:T(512)} %param.11) | copy-start | bytes 4612
  0.6 5.8 %collective-permute-start.9 = (bf16[3,8192]{1,0:T(4,128)(2,1)}, bf16[3,8192]{1,0:T(4,128)(2,1)S(1)}, u32[]{:S(2)}, u32[]{:S(2)}) collective-permute-start(bf16[3,8192]{1,0:T(4,128)(2,1)} %param.6), channel_id=1, source_target_pairs={{0,1},{1,2},{2,3},{3,0},{4,5},{5,6},{6,7},{7,4},{8,9},{9,10},{10,1... | collective-permute-start | bytes 147464 | tf_op jit(solution)/shard_map/ppermute | solution.py:45
  2.4 4.5 %collective-permute-start.11 = (bf16[3,8192]{1,0:T(4,128)(2,1)}, bf16[3,8192]{1,0:T(4,128)(2,1)S(1)}, u32[]{:S(2)}, u32[]{:S(2)}) collective-permute-start(bf16[3,8192]{1,0:T(4,128)(2,1)} %param.6), channel_id=1, source_target_pairs={{0,3},{1,0},{2,1},{3,2},{4,7},{5,4},{6,5},{7,6},{8,11},{9,8},{10,9... | collective-permute-start | bytes 147464 | tf_op jit(solution)/shard_map/ppermute | solution.py:45
  3.9 6.0 %collective-permute-start.10 = (bf16[3,8192]{1,0:T(4,128)(2,1)}, bf16[3,8192]{1,0:T(4,128)(2,1)S(1)}, u32[]{:S(2)}, u32[]{:S(2)}) collective-permute-start(bf16[3,8192]{1,0:T(4,128)(2,1)} %param.6), channel_id=1, source_target_pairs={{0,2},{1,3},{2,0},{3,1},{4,6},{5,7},{6,4},{7,5},{8,10},{9,11},{10,... | collective-permute-start | bytes 147464 | tf_op jit(solution)/shard_map/ppermute | solution.py:45
  11.0 7.7 %collective-permute-start.12 = (bf16[12,8192]{1,0:T(8,128)(2,1)S(1)}, bf16[12,8192]{1,0:T(8,128)(2,1)S(1)}, u32[]{:S(2)}, u32[]{:S(2)}) collective-permute-start(bf16[12,8192]{1,0:T(8,128)(2,1)S(1)} %pad_maximum_fusion.3), channel_id=1, source_target_pairs={{0,4},{1,5},{2,6},{3,7},{4,8},{5,9},{6,10},{7,11},{8,12},{9,13},{1... | collective-permute-start | bytes 589832 | tf_op jit(solution)/shard_map/ppermute | solution.py:45
  12.6 18.1 %collective-permute-start = (bf16[3,3584]{1,0:T(4,128)(2,1)}, bf16[3,3584]{1,0:T(4,128)(2,1)S(1)}, u32[]{:S(2)}, u32[]{:S(2)}) collective-permute-start(bf16[3,3584]{1,0:T(4,128)(2,1)} %param.8), channel_id=1, source_target_pairs={{0,1},{1,2},{2,3},{3,0},{4,5},{5,6},{6,7},{7,4},{8,9},{9,10},{10,1... | collective-permute-start | bytes 64520 | tf_op jit(solution)/shard_map/ppermute | solution.py:45
  13.0 17.8 %collective-permute-start.2 = (bf16[3,3584]{1,0:T(4,128)(2,1)}, bf16[3,3584]{1,0:T(4,128)(2,1)S(1)}, u32[]{:S(2)}, u32[]{:S(2)}) collective-permute-start(bf16[3,3584]{1,0:T(4,128)(2,1)} %param.8), channel_id=1, source_target_pairs={{0,3},{1,0},{2,1},{3,2},{4,7},{5,4},{6,5},{7,6},{8,11},{9,8},{10,9... | collective-permute-start | bytes 64520 | tf_op jit(solution)/shard_map/ppermute | solution.py:45
  15.9 18.2 %collective-permute-start.1 = (bf16[3,3584]{1,0:T(4,128)(2,1)}, bf16[3,3584]{1,0:T(4,128)(2,1)S(1)}, u32[]{:S(2)}, u32[]{:S(2)}) collective-permute-start(bf16[3,3584]{1,0:T(4,128)(2,1)} %param.8), channel_id=1, source_target_pairs={{0,2},{1,3},{2,0},{3,1},{4,6},{5,7},{6,4},{7,5},{8,10},{9,11},{10,... | collective-permute-start | bytes 64520 | tf_op jit(solution)/shard_map/ppermute | solution.py:45
  16.7 8.5 %collective-permute-start.14 = (bf16[12,8192]{1,0:T(8,128)(2,1)S(1)}, bf16[12,8192]{1,0:T(8,128)(2,1)S(1)}, u32[]{:S(2)}, u32[]{:S(2)}) collective-permute-start(bf16[12,8192]{1,0:T(8,128)(2,1)S(1)} %pad_maximum_fusion.3), channel_id=1, source_target_pairs={{0,12},{1,13},{2,14},{3,15},{4,0},{5,1},{6,2},{7,3},{8,4},{9,5},{1... | collective-permute-start | bytes 589832 | tf_op jit(solution)/shard_map/ppermute | solution.py:45
  18.6 7.9 %collective-permute-start.13 = (bf16[12,8192]{1,0:T(8,128)(2,1)S(1)}, bf16[12,8192]{1,0:T(8,128)(2,1)S(1)}, u32[]{:S(2)}, u32[]{:S(2)}) collective-permute-start(bf16[12,8192]{1,0:T(8,128)(2,1)S(1)} %pad_maximum_fusion.3), channel_id=1, source_target_pairs={{0,8},{1,9},{2,10},{3,11},{4,12},{5,13},{6,14},{7,15},{8,0},{9,1},... | collective-permute-start | bytes 589832 | tf_op jit(solution)/shard_map/ppermute | solution.py:45
  25.1 27.1 %collective-permute-start.19 = (bf16[24,8192]{1,0:T(8,128)(2,1)S(1)}, bf16[24,8192]{1,0:T(8,128)(2,1)S(1)}, u32[]{:S(2)}, u32[]{:S(2)}) collective-permute-start(bf16[24,8192]{1,0:T(8,128)(2,1)S(1)} %pad_maximum_fusion.1.refs_0_), channel_id=1, source_target_pairs={{0,32},{1,33},{2,34},{3,35},{4,36},{5,37},{6,38},{7,39},{8,40},{9,... | collective-permute-start | bytes 1179656 | tf_op jit(solution)/shard_map/ppermute | solution.py:40
  26.5 25.9 %collective-permute-start.17 = (bf16[24,8192]{1,0:T(8,128)(2,1)S(1)}, bf16[24,8192]{1,0:T(8,128)(2,1)S(1)}, u32[]{:S(2)}, u32[]{:S(2)}) collective-permute-start(bf16[24,8192]{1,0:T(8,128)(2,1)S(1)} %pad_maximum_fusion.1.refs_0_), channel_id=1, source_target_pairs={{0,80},{1,81},{2,82},{3,83},{4,84},{5,85},{6,86},{7,87},{8,88},{9,... | collective-permute-start | bytes 1179656 | tf_op jit(solution)/shard_map/ppermute | solution.py:45
  30.8 22.1 %collective-permute-start.15 = (bf16[24,8192]{1,0:T(8,128)(2,1)S(1)}, bf16[24,8192]{1,0:T(8,128)(2,1)S(1)}, u32[]{:S(2)}, u32[]{:S(2)}) collective-permute-start(bf16[24,8192]{1,0:T(8,128)(2,1)S(1)} %pad_maximum_fusion.1.refs_0_), channel_id=1, source_target_pairs={{0,64},{1,65},{2,66},{3,67},{4,68},{5,69},{6,70},{7,71},{8,72},{9,... | collective-permute-start | bytes 1179656 | tf_op jit(solution)/shard_map/ppermute | solution.py:45
  30.9 22.1 %collective-permute-start.18 = (bf16[24,8192]{1,0:T(8,128)(2,1)S(1)}, bf16[24,8192]{1,0:T(8,128)(2,1)S(1)}, u32[]{:S(2)}, u32[]{:S(2)}) collective-permute-start(bf16[24,8192]{1,0:T(8,128)(2,1)S(1)} %pad_maximum_fusion.refs_1_), channel_id=1, source_target_pairs={{0,80},{1,81},{2,82},{3,83},{4,84},{5,85},{6,86},{7,87},{8,88},{9,... | collective-permute-start | bytes 1179656 | tf_op jit(solution)/shard_map/ppermute | solution.py:45
  34.9 18.1 %copy-start.3 = (bf16[12,3584]{1,0:T(8,128)(2,1)}, bf16[12,3584]{1,0:T(8,128)(2,1)S(1)}, u32[]{:S(2)}) copy-start(bf16[12,3584]{1,0:T(8,128)(2,1)S(1)} %pad_maximum_fusion.4) | copy-start | bytes 258052
  34.9 4.9 %collective-permute-start.5 = (bf16[12,3584]{1,0:T(8,128)(2,1)S(1)}, bf16[12,3584]{1,0:T(8,128)(2,1)S(1)}, u32[]{:S(2)}, u32[]{:S(2)}) collective-permute-start(bf16[12,3584]{1,0:T(8,128)(2,1)S(1)} %pad_maximum_fusion.4), channel_id=1, source_target_pairs={{0,12},{1,13},{2,14},{3,15},{4,0},{5,1},{6,2},{7,3},{8,4},{9,5},{1... | collective-permute-start | bytes 258056 | tf_op jit(solution)/shard_map/ppermute | solution.py:45
  39.8 16.3 %copy-start.7 = (bf16[12,3584]{1,0:T(8,128)(2,1)}, bf16[12,3584]{1,0:T(8,128)(2,1)S(1)}, u32[]{:S(2)}) copy-start(bf16[12,3584]{1,0:T(8,128)(2,1)S(1)} %collective-permute-done.5) | copy-start | bytes 258052
  39.8 6.3 %collective-permute-start.4 = (bf16[12,3584]{1,0:T(8,128)(2,1)S(1)}, bf16[12,3584]{1,0:T(8,128)(2,1)S(1)}, u32[]{:S(2)}, u32[]{:S(2)}) collective-permute-start(bf16[12,3584]{1,0:T(8,128)(2,1)S(1)} %pad_maximum_fusion.4), channel_id=1, source_target_pairs={{0,8},{1,9},{2,10},{3,11},{4,12},{5,13},{6,14},{7,15},{8,0},{9,1},... | collective-permute-start | bytes 258056 | tf_op jit(solution)/shard_map/ppermute | solution.py:45
  46.1 10.0 %copy-start.8 = (bf16[12,3584]{1,0:T(8,128)(2,1)}, bf16[12,3584]{1,0:T(8,128)(2,1)S(1)}, u32[]{:S(2)}) copy-start(bf16[12,3584]{1,0:T(8,128)(2,1)S(1)} %collective-permute-done.4) | copy-start | bytes 258052
  46.1 6.2 %collective-permute-start.3 = (bf16[12,3584]{1,0:T(8,128)(2,1)S(1)}, bf16[12,3584]{1,0:T(8,128)(2,1)S(1)}, u32[]{:S(2)}, u32[]{:S(2)}) collective-permute-start(bf16[12,3584]{1,0:T(8,128)(2,1)S(1)} %pad_maximum_fusion.4), channel_id=1, source_target_pairs={{0,4},{1,5},{2,6},{3,7},{4,8},{5,9},{6,10},{7,11},{8,12},{9,13},{1... | collective-permute-start | bytes 258056 | tf_op jit(solution)/shard_map/ppermute | solution.py:45
  52.3 3.9 %copy-start.9 = (bf16[12,3584]{1,0:T(8,128)(2,1)}, bf16[12,3584]{1,0:T(8,128)(2,1)S(1)}, u32[]{:S(2)}) copy-start(bf16[12,3584]{1,0:T(8,128)(2,1)S(1)} %collective-permute-done.3) | copy-start | bytes 258052
  52.3 4.2 %collective-permute-start.20 = (bf16[24,8192]{1,0:T(8,128)(2,1)S(1)}, bf16[24,8192]{1,0:T(8,128)(2,1)S(1)}, u32[]{:S(2)}, u32[]{:S(2)}) collective-permute-start(bf16[24,8192]{1,0:T(8,128)(2,1)S(1)} %pad_maximum_fusion.refs_1_), channel_id=1, source_target_pairs={{0,32},{1,33},{2,34},{3,35},{4,36},{5,37},{6,38},{7,39},{8,40},{9,... | collective-permute-start | bytes 1179656 | tf_op jit(solution)/shard_map/ppermute | solution.py:40
  52.3 9.1 %collective-permute-start.16 = (bf16[24,8192]{1,0:T(8,128)(2,1)S(1)}, bf16[24,8192]{1,0:T(8,128)(2,1)S(1)}, u32[]{:S(2)}, u32[]{:S(2)}) collective-permute-start(bf16[24,8192]{1,0:T(8,128)(2,1)S(1)} %pad_maximum_fusion.refs_1_), channel_id=1, source_target_pairs={{0,64},{1,65},{2,66},{3,67},{4,68},{5,69},{6,70},{7,71},{8,72},{9,... | collective-permute-start | bytes 1179656 | tf_op jit(solution)/shard_map/ppermute | solution.py:45
  52.4 8.9 %collective-permute-start.23 = (bf16[24,8192]{1,0:T(8,128)(2,1)S(1)}, bf16[24,8192]{1,0:T(8,128)(2,1)}, u32[]{:S(2)}, u32[]{:S(2)}) collective-permute-start(bf16[24,8192]{1,0:T(8,128)(2,1)S(1)} %collective-permute-done.17.refs_4_), channel_id=1, source_target_pairs={{0,32},{1,33},{2,34},{3,35},{4,36},{5,37},{6,38},{7,39},{8,40},{9,... | collective-permute-start | bytes 1179656 | tf_op jit(solution)/shard_map/ppermute | solution.py:40
  52.9 12.8 %collective-permute-start.25 = (bf16[24,8192]{1,0:T(8,128)(2,1)S(1)}, bf16[24,8192]{1,0:T(8,128)(2,1)}, u32[]{:S(2)}, u32[]{:S(2)}) collective-permute-start(bf16[24,8192]{1,0:T(8,128)(2,1)S(1)} %collective-permute-done.15.refs_2_), channel_id=1, source_target_pairs={{0,64},{1,65},{2,66},{3,67},{4,68},{5,69},{6,70},{7,71},{8,72},{9,... | collective-permute-start | bytes 1179656 | tf_op jit(solution)/shard_map/ppermute | solution.py:45
  53.0 12.7 %collective-permute-start.26 = (bf16[24,8192]{1,0:T(8,128)(2,1)S(1)}, bf16[24,8192]{1,0:T(8,128)(2,1)}, u32[]{:S(2)}, u32[]{:S(2)}) collective-permute-start(bf16[24,8192]{1,0:T(8,128)(2,1)S(1)} %collective-permute-done.18.refs_5_), channel_id=1, source_target_pairs={{0,80},{1,81},{2,82},{3,83},{4,84},{5,85},{6,86},{7,87},{8,88},{9,... | collective-permute-start | bytes 1179656 | tf_op jit(solution)/shard_map/ppermute | solution.py:45
  56.5 10.9 %collective-permute-start.21 = (bf16[24,8192]{1,0:T(8,128)(2,1)S(1)}, bf16[24,8192]{1,0:T(8,128)(2,1)S(1)}, u32[]{:S(2)}, u32[]{:S(2)}) collective-permute-start(bf16[24,8192]{1,0:T(8,128)(2,1)S(1)} %collective-permute-done.15.refs_2_), channel_id=1, source_target_pairs={{0,32},{1,33},{2,34},{3,35},{4,36},{5,37},{6,38},{7,39},{8,40},{9,... | collective-permute-start | bytes 1179656 | tf_op jit(solution)/shard_map/ppermute | solution.py:40
  61.3 6.1 %collective-permute-start.24 = (bf16[24,8192]{1,0:T(8,128)(2,1)S(1)}, bf16[24,8192]{1,0:T(8,128)(2,1)S(1)}, u32[]{:S(2)}, u32[]{:S(2)}) collective-permute-start(bf16[24,8192]{1,0:T(8,128)(2,1)S(1)} %collective-permute-done.18.refs_5_), channel_id=1, source_target_pairs={{0,32},{1,33},{2,34},{3,35},{4,36},{5,37},{6,38},{7,39},{8,40},{9,... | collective-permute-start | bytes 1179656 | tf_op jit(solution)/shard_map/ppermute | solution.py:40
  61.3 6.6 %collective-permute-start.22 = (bf16[24,8192]{1,0:T(8,128)(2,1)S(1)}, bf16[24,8192]{1,0:T(8,128)(2,1)S(1)}, u32[]{:S(2)}, u32[]{:S(2)}) collective-permute-start(bf16[24,8192]{1,0:T(8,128)(2,1)S(1)} %collective-permute-done.16.refs_3_), channel_id=1, source_target_pairs={{0,32},{1,33},{2,34},{3,35},{4,36},{5,37},{6,38},{7,39},{8,40},{9,... | collective-permute-start | bytes 1179656 | tf_op jit(solution)/shard_map/ppermute | solution.py:40
  65.6 3.3 %collective-permute-start.27 = (bf16[24,8192]{1,0:T(8,128)(2,1)}, bf16[24,8192]{1,0:T(8,128)(2,1)S(1)}, u32[]{:S(2)}, u32[]{:S(2)}) collective-permute-start(bf16[24,8192]{1,0:T(8,128)(2,1)} %collective-permute-done.25.refs_12_), channel_id=1, source_target_pairs={{0,32},{1,33},{2,34},{3,35},{4,36},{5,37},{6,38},{7,39},{8,40},{9,... | collective-permute-start | bytes 1179656 | tf_op jit(solution)/shard_map/ppermute | solution.py:40
  65.6 4.2 %collective-permute-start.28 = (bf16[24,8192]{1,0:T(8,128)(2,1)}, bf16[24,8192]{1,0:T(8,128)(2,1)S(1)}, u32[]{:S(2)}, u32[]{:S(2)}) collective-permute-start(bf16[24,8192]{1,0:T(8,128)(2,1)} %collective-permute-done.26.refs_13_), channel_id=1, source_target_pairs={{0,32},{1,33},{2,34},{3,35},{4,36},{5,37},{6,38},{7,39},{8,40},{9,... | collective-permute-start | bytes 1179656 | tf_op jit(solution)/shard_map/ppermute | solution.py:40
  67.3 17.9 %copy-start.11 = (s32[384]{0:T(512)S(1)}, s32[384]{0:T(512)}, u32[]{:S(2)}) copy-start(s32[384]{0:T(512)} %param.10) | copy-start | bytes 4612
  67.3 17.9 %collective-permute-start.29 = (bf16[48,3584]{1,0:T(8,128)(2,1)S(1)}, bf16[48,3584]{1,0:T(8,128)(2,1)}, u32[]{:S(2)}, u32[]{:S(2)}) collective-permute-start(bf16[48,3584]{1,0:T(8,128)(2,1)S(1)} %pad_maximum_fusion.2.refs_0_), channel_id=1, source_target_pairs={{0,32},{1,33},{2,34},{3,35},{4,36},{5,37},{6,38},{7,39},{8,40},{9,... | collective-permute-start | bytes 1032200 | tf_op jit(solution)/shard_map/ppermute | solution.py:40
  67.5 2.4 %copy-start.4 = (bf16[24,8192]{1,0:T(8,128)(2,1)}, bf16[24,8192]{1,0:T(8,128)(2,1)S(1)}, u32[]{:S(2)}) copy-start(bf16[24,8192]{1,0:T(8,128)(2,1)S(1)} %collective-permute-done.24.refs_11_) | copy-start | bytes 1179652
  67.5 16.5 %collective-permute-start.8 = (bf16[48,3584]{1,0:T(8,128)(2,1)S(1)}, bf16[48,3584]{1,0:T(8,128)(2,1)}, u32[]{:S(2)}, u32[]{:S(2)}) collective-permute-start(bf16[48,3584]{1,0:T(8,128)(2,1)S(1)} %pad_maximum_fusion.2.refs_0_), channel_id=1, source_target_pairs={{0,80},{1,81},{2,82},{3,83},{4,84},{5,85},{6,86},{7,87},{8,88},{9,... | collective-permute-start | bytes 1032200 | tf_op jit(solution)/shard_map/ppermute | solution.py:45
  68.0 16.0 %collective-permute-start.7 = (bf16[48,3584]{1,0:T(8,128)(2,1)S(1)}, bf16[48,3584]{1,0:T(8,128)(2,1)}, u32[]{:S(2)}, u32[]{:S(2)}) collective-permute-start(bf16[48,3584]{1,0:T(8,128)(2,1)S(1)} %pad_maximum_fusion.2.refs_0_), channel_id=1, source_target_pairs={{0,16},{1,17},{2,18},{3,19},{4,20},{5,21},{6,22},{7,23},{8,24},{9,... | collective-permute-start | bytes 1032200 | tf_op jit(solution)/shard_map/ppermute | solution.py:45
  68.9 0.9 copy-start.5
  68.9 15.1 %collective-permute-start.6 = (bf16[48,3584]{1,0:T(8,128)(2,1)S(1)}, bf16[48,3584]{1,0:T(8,128)(2,1)}, u32[]{:S(2)}, u32[]{:S(2)}) collective-permute-start(bf16[48,3584]{1,0:T(8,128)(2,1)S(1)} %pad_maximum_fusion.2.refs_0_), channel_id=1, source_target_pairs={{0,64},{1,65},{2,66},{3,67},{4,68},{5,69},{6,70},{7,71},{8,72},{9,... | collective-permute-start | bytes 1032200 | tf_op jit(solution)/shard_map/ppermute | solution.py:45
  84.0 2.2 %collective-permute-start.30 = (bf16[48,3584]{1,0:T(8,128)(2,1)}, bf16[48,3584]{1,0:T(8,128)(2,1)S(1)}, u32[]{:S(2)}, u32[]{:S(2)}) collective-permute-start(bf16[48,3584]{1,0:T(8,128)(2,1)} %collective-permute-done.6.refs_1_), channel_id=1, source_target_pairs={{0,32},{1,33},{2,34},{3,35},{4,36},{5,37},{6,38},{7,39},{8,40},{9,... | collective-permute-start | bytes 1032200 | tf_op jit(solution)/shard_map/ppermute | solution.py:40
  84.7 2.0 %collective-permute-start.31 = (bf16[48,3584]{1,0:T(8,128)(2,1)}, bf16[48,3584]{1,0:T(8,128)(2,1)S(1)}, u32[]{:S(2)}, u32[]{:S(2)}) collective-permute-start(bf16[48,3584]{1,0:T(8,128)(2,1)} %collective-permute-done.7.refs_2_), channel_id=1, source_target_pairs={{0,32},{1,33},{2,34},{3,35},{4,36},{5,37},{6,38},{7,39},{8,40},{9,... | collective-permute-start | bytes 1032200 | tf_op jit(solution)/shard_map/ppermute | solution.py:40
  84.8 2.4 %collective-permute-start.32 = (bf16[48,3584]{1,0:T(8,128)(2,1)}, bf16[48,3584]{1,0:T(8,128)(2,1)S(1)}, u32[]{:S(2)}, u32[]{:S(2)}) collective-permute-start(bf16[48,3584]{1,0:T(8,128)(2,1)} %collective-permute-done.8.refs_3_), channel_id=1, source_target_pairs={{0,32},{1,33},{2,34},{3,35},{4,36},{5,37},{6,38},{7,39},{8,40},{9,... | collective-permute-start | bytes 1032200 | tf_op jit(solution)/shard_map/ppermute | solution.py:40
  87.9 1.0 copy-start.2
  88.9 30.7 %copy-start = (f32[384,768]{1,0:T(8,128)S(1)}, f32[384,768]{1,0:T(8,128)}, u32[]{:S(2)}) copy-start(f32[384,768]{1,0:T(8,128)} %shard_map.85.refs_9_.t_in) | copy-start | bytes 3538948
  97.2 1.3 collective-permute-start.33
  98.7 4.9 %collective-permute-start.34 = (f32[8,384]{1,0:T(8,128)S(1)}, f32[8,384]{1,0:T(8,128)S(1)}, u32[]{:S(2)}, u32[]{:S(2)}) collective-permute-start(f32[8,384]{1,0:T(8,128)S(1)} %select_select_fusion.3), channel_id=1, source_target_pairs={{0,1},{1,2},{2,3},{3,0},{4,5},{5,6},{6,7},{7,4},{8,9},{9,10},{10,1... | collective-permute-start | bytes 36872 | tf_op jit(solution)/shard_map/ppermute | solution.py:277
  99.4 5.2 %collective-permute-start.36 = (f32[8,384]{1,0:T(8,128)S(1)}, f32[8,384]{1,0:T(8,128)S(1)}, u32[]{:S(2)}, u32[]{:S(2)}) collective-permute-start(f32[8,384]{1,0:T(8,128)S(1)} %select_select_fusion.3), channel_id=1, source_target_pairs={{0,2},{1,3},{2,0},{3,1},{4,6},{5,7},{6,4},{7,5},{8,10},{9,11},{10,... | collective-permute-start | bytes 36872 | tf_op jit(solution)/shard_map/ppermute | solution.py:281
  103.6 1.2 collective-permute-start.35
  105.2 4.9 %collective-permute-start.37 = (f32[8,384]{1,0:T(8,128)S(1)}, f32[8,384]{1,0:T(8,128)S(1)}, u32[]{:S(2)}, u32[]{:S(2)}) collective-permute-start(f32[8,384]{1,0:T(8,128)S(1)} %select_select_fusion.2), channel_id=1, source_target_pairs={{0,4},{1,5},{2,6},{3,7},{4,8},{5,9},{6,10},{7,11},{8,12},{9,13},{1... | collective-permute-start | bytes 36872 | tf_op jit(solution)/shard_map/ppermute | solution.py:277
  107.4 5.2 %collective-permute-start.39 = (f32[8,384]{1,0:T(8,128)S(1)}, f32[8,384]{1,0:T(8,128)S(1)}, u32[]{:S(2)}, u32[]{:S(2)}) collective-permute-start(f32[8,384]{1,0:T(8,128)S(1)} %select_select_fusion.2), channel_id=1, source_target_pairs={{0,8},{1,9},{2,10},{3,11},{4,12},{5,13},{6,14},{7,15},{8,0},{9,1},... | collective-permute-start | bytes 36872 | tf_op jit(solution)/shard_map/ppermute | solution.py:281
  110.1 2.5 %collective-permute-start.38 = (f32[8,384]{1,0:T(8,128)S(1)}, f32[8,384]{1,0:T(8,128)S(1)}, u32[]{:S(2)}, u32[]{:S(2)}) collective-permute-start(f32[8,384]{1,0:T(8,128)S(1)} %collective-permute-done.37), channel_id=1, source_target_pairs={{0,32},{1,33},{2,34},{3,35},{4,36},{5,37},{6,38},{7,39},{8,40},{9,... | collective-permute-start | bytes 36872 | tf_op jit(solution)/shard_map/ppermute | solution.py:40
  112.9 5.1 %collective-permute-start.40 = (f32[8,384]{1,0:T(8,128)S(1)}, f32[8,384]{1,0:T(8,128)S(1)}, u32[]{:S(2)}, u32[]{:S(2)}) collective-permute-start(f32[8,384]{1,0:T(8,128)S(1)} %select_select_fusion.1), channel_id=1, source_target_pairs={{0,64},{1,65},{2,66},{3,67},{4,68},{5,69},{6,70},{7,71},{8,72},{9,... | collective-permute-start | bytes 36872 | tf_op jit(solution)/shard_map/ppermute | solution.py:277
  113.2 5.2 %collective-permute-start.42 = (f32[8,384]{1,0:T(8,128)S(1)}, f32[8,384]{1,0:T(8,128)S(1)}, u32[]{:S(2)}, u32[]{:S(2)}) collective-permute-start(f32[8,384]{1,0:T(8,128)S(1)} %select_select_fusion.1), channel_id=1, source_target_pairs={{0,16},{1,17},{2,18},{3,19},{4,20},{5,21},{6,22},{7,23},{8,24},{9,... | collective-permute-start | bytes 36872 | tf_op jit(solution)/shard_map/ppermute | solution.py:281
  118.1 1.2 collective-permute-start.41
  119.6 5.6 %copy-start.12 = (bf16[384,3584]{1,0:T(8,128)(2,1)S(1)}, bf16[384,3584]{1,0:T(8,128)(2,1)}, u32[]{:S(2)}) copy-start(bf16[384,3584]{1,0:T(8,128)(2,1)} %get-tuple-element.26) | copy-start | bytes 8257540
  124.9 5.1 %collective-permute-start.43 = (bf16[192,3584]{1,0:T(8,128)(2,1)S(1)}, bf16[192,3584]{1,0:T(8,128)(2,1)S(1)}, u32[]{:S(2)}, u32[]{:S(2)}) collective-permute-start(bf16[192,3584]{1,0:T(8,128)(2,1)S(1)} %get-tuple-element.25), channel_id=1, source_target_pairs={{0,32},{1,33},{2,34},{3,35},{4,36},{5,37},{6,38},{7,39},{8,40},{9,... | collective-permute-start | bytes 4128776 | tf_op jit(solution)/shard_map/ppermute | solution.py:40
  130.5 7.3 %collective-permute-start.44 = (bf16[48,3584]{1,0:T(8,128)(2,1)S(1)}, bf16[48,3584]{1,0:T(8,128)(2,1)S(1)}, u32[]{:S(2)}, u32[]{:S(2)}) collective-permute-start(bf16[48,3584]{1,0:T(8,128)(2,1)S(1)} %get-tuple-element.53), channel_id=1, source_target_pairs={{0,80},{1,81},{2,82},{3,83},{4,84},{5,85},{6,86},{7,87},{8,88},{9,... | collective-permute-start | bytes 1032200 | tf_op jit(solution)/shard_map/ppermute | solution.py:45
  132.8 12.1 %collective-permute-start.46 = (bf16[48,3584]{1,0:T(8,128)(2,1)S(1)}, bf16[48,3584]{1,0:T(8,128)(2,1)S(1)}, u32[]{:S(2)}, u32[]{:S(2)}) collective-permute-start(bf16[48,3584]{1,0:T(8,128)(2,1)S(1)} %get-tuple-element.54), channel_id=1, source_target_pairs={{0,64},{1,65},{2,66},{3,67},{4,68},{5,69},{6,70},{7,71},{8,72},{9,... | collective-permute-start | bytes 1032200 | tf_op jit(solution)/shard_map/ppermute | solution.py:45
  132.8 12.1 %collective-permute-start.45 = (bf16[48,3584]{1,0:T(8,128)(2,1)S(1)}, bf16[48,3584]{1,0:T(8,128)(2,1)S(1)}, u32[]{:S(2)}, u32[]{:S(2)}) collective-permute-start(bf16[48,3584]{1,0:T(8,128)(2,1)S(1)} %get-tuple-element.55), channel_id=1, source_target_pairs={{0,16},{1,17},{2,18},{3,19},{4,20},{5,21},{6,22},{7,23},{8,24},{9,... | collective-permute-start | bytes 1032200 | tf_op jit(solution)/shard_map/ppermute | solution.py:45
  145.2 4.9 %collective-permute-start.47 = (bf16[12,3584]{1,0:T(8,128)(2,1)S(1)}, bf16[12,3584]{1,0:T(8,128)(2,1)S(1)}, u32[]{:S(2)}, u32[]{:S(2)}) collective-permute-start(bf16[12,3584]{1,0:T(8,128)(2,1)S(1)} %get-tuple-element.56), channel_id=1, source_target_pairs={{0,12},{1,13},{2,14},{3,15},{4,0},{5,1},{6,2},{7,3},{8,4},{9,5},{1... | collective-permute-start | bytes 258056 | tf_op jit(solution)/shard_map/ppermute | solution.py:45
  146.3 6.0 %collective-permute-start.49 = (bf16[12,3584]{1,0:T(8,128)(2,1)S(1)}, bf16[12,3584]{1,0:T(8,128)(2,1)S(1)}, u32[]{:S(2)}, u32[]{:S(2)}) collective-permute-start(bf16[12,3584]{1,0:T(8,128)(2,1)S(1)} %get-tuple-element.57), channel_id=1, source_target_pairs={{0,4},{1,5},{2,6},{3,7},{4,8},{5,9},{6,10},{7,11},{8,12},{9,13},{1... | collective-permute-start | bytes 258056 | tf_op jit(solution)/shard_map/ppermute | solution.py:45
  147.3 6.3 %collective-permute-start.48 = (bf16[12,3584]{1,0:T(8,128)(2,1)S(1)}, bf16[12,3584]{1,0:T(8,128)(2,1)S(1)}, u32[]{:S(2)}, u32[]{:S(2)}) collective-permute-start(bf16[12,3584]{1,0:T(8,128)(2,1)S(1)} %get-tuple-element.58), channel_id=1, source_target_pairs={{0,8},{1,9},{2,10},{3,11},{4,12},{5,13},{6,14},{7,15},{8,0},{9,1},... | collective-permute-start | bytes 258056 | tf_op jit(solution)/shard_map/ppermute | solution.py:45
  153.7 4.8 %collective-permute-start.50 = (bf16[3,3584]{1,0:T(4,128)(2,1)S(1)}, bf16[3,3584]{1,0:T(4,128)(2,1)S(1)}, u32[]{:S(2)}, u32[]{:S(2)}) collective-permute-start(bf16[3,3584]{1,0:T(4,128)(2,1)S(1)} %get-tuple-element.59), channel_id=1, source_target_pairs={{0,3},{1,0},{2,1},{3,2},{4,7},{5,4},{6,5},{7,6},{8,11},{9,8},{10,9... | collective-permute-start | bytes 64520 | tf_op jit(solution)/shard_map/ppermute | solution.py:45
  156.1 5.1 %collective-permute-start.52 = (bf16[3,3584]{1,0:T(4,128)(2,1)S(1)}, bf16[3,3584]{1,0:T(4,128)(2,1)S(1)}, u32[]{:S(2)}, u32[]{:S(2)}) collective-permute-start(bf16[3,3584]{1,0:T(4,128)(2,1)S(1)} %get-tuple-element.60), channel_id=1, source_target_pairs={{0,1},{1,2},{2,3},{3,0},{4,5},{5,6},{6,7},{7,4},{8,9},{9,10},{10,1... | collective-permute-start | bytes 64520 | tf_op jit(solution)/shard_map/ppermute | solution.py:45
  156.1 5.4 %collective-permute-start.51 = (bf16[3,3584]{1,0:T(4,128)(2,1)S(1)}, bf16[3,3584]{1,0:T(4,128)(2,1)S(1)}, u32[]{:S(2)}, u32[]{:S(2)}) collective-permute-start(bf16[3,3584]{1,0:T(4,128)(2,1)S(1)} %get-tuple-element.61), channel_id=1, source_target_pairs={{0,2},{1,3},{2,0},{3,1},{4,6},{5,7},{6,4},{7,5},{8,10},{9,11},{10,... | collective-permute-start | bytes 64520 | tf_op jit(solution)/shard_map/ppermute | solution.py:45
  (2 other events, 1.5 us)

commit v5 on v4

--- a/solution.py
+++ b/solution.py
@@ -99,8 +99,11 @@
     return jnp.sum(jnp.where(column == lane_ids(), row_values.astype(F32), 0.0), axis=1, keepdims=True).astype(jnp.int32)
 
 
-def teacher_kernel(n, *refs):
-    blocks, (source, tok_row, owner, w, saved, out, wbuf, sem) = refs[:n], refs[n:]
+def teacher_kernel(n, fetched, *refs):
+    blocks, (source, tok_row, owner, w, saved, out, wbuf, gbuf, sem, gsem) = list(refs[:n]), refs[n:]
+    fetches = [pltpu.make_async_copy(blocks[at], gbuf.at[i], gsem.at[i]) for i, at in enumerate(fetched)]
+    for fetch in fetches:
+        fetch.start()
     slots, chunk, _ = wbuf.shape
     count = w.shape[0] // chunk
 
@@ -110,6 +113,11 @@
 
     for i in range(slots):
         copy(i).start()
+    owner_col = pick_column(to_column(tok_row[...]), owner[...])
+    pick = one_hot(owner_col, source[...])
+    for i, at in enumerate(fetched):
+        fetches[i].wait()
+        blocks[at] = gbuf.at[i]
     for i in range(count):
         columns = slice(i * chunk, (i + 1) * chunk)
         rows = jnp.concatenate([block[:, columns] for block in blocks], axis=0)
@@ -118,8 +126,6 @@
         out[...] = part if i == 0 else out[...] + part
         if i + slots < count:
             copy(i + slots).start()
-    owner_col = pick_column(to_column(tok_row[...]), owner[...])
-    pick = one_hot(owner_col, source[...])
     high, middle, low = split3(out[...])
     saves = []
     for i in range(3):
@@ -154,6 +160,7 @@
     s_out[...] = jnp.zeros_like(s_out)
     tok_col = to_column(tok_row[...])
     label_at[...] = pick_column(tok_col, labels[...]) - at_ref[0]
+    to_natural = one_hot(tok_col, lane_ids())
 
     @pl.loop(0, count)
     def _(i):
@@ -189,7 +196,6 @@
             packed = jnp.where(lane == k, value, packed)
         table[rows, :] = packed
 
-    to_natural = one_hot(tok_col, lane_ids())
     high, middle, low = split3(table[...].T[:16])
     stats_out[...] = ((dot(high, to_natural) + dot(middle, to_natural)) + dot(low, to_natural))[:8]
     for save in saves:
@@ -306,16 +312,23 @@
     s0 = s
 
     blocks = near + far
+    fetched = (6, 7, 8, 9, 10, 11, 14, 15)
     q = HALF // 4
     pieces = [tok_row[:, at * q : (at + 1) * q] for at in (0, 1, 3, 4, 5, 7, 2, 6)]
     source = jnp.concatenate(pieces, axis=1)
     (t_logits,) = call(
-        functools.partial(teacher_kernel, len(blocks)),
+        functools.partial(teacher_kernel, len(blocks), fetched),
         [((TOKENS, vocab), F32)],
-        [VMEM] * (len(blocks) + 3) + [HBM],
+        [HBM if i in fetched else VMEM for i in range(len(blocks))] + [VMEM] * 3 + [HBM],
         [*blocks, source, tok_row, owner_row, teacher_head],
-        [pltpu.VMEM((TOKENS, vocab), F32), pltpu.VMEM((3, 1024, vocab), BF16), pltpu.SemaphoreType.DMA((6,))],
-        50,
+        [
+            pltpu.VMEM((TOKENS, vocab), F32),
+            pltpu.VMEM((3, 1024, vocab), BF16),
+            pltpu.VMEM((len(fetched), *blocks[0].shape), BF16),
+            pltpu.SemaphoreType.DMA((6,)),
+            pltpu.SemaphoreType.DMA((len(fetched),)),
+        ],
+        47,
         2 * TOKENS * tk * vocab,
         [HBM],
     )
@@ -337,7 +350,7 @@
             pltpu.VMEM((TOKENS, 1), jnp.int32),
             pltpu.SemaphoreType.DMA((7,)),
         ],
-        50,
+        51,
         2 * TOKENS * sk * vocab,
         [HBM, HBM, VMEM],
     )
@@ -360,17 +373,18 @@
             pltpu.VMEM((TOKENS, 1), jnp.int32),
             pltpu.SemaphoreType.DMA((6,)),
         ],
-        46,
+        44,
         2 * TOKENS * sk * vocab,
     )
 
     received = swap(to_other)
     grad_head = lax.dot_general(hidden, grads, (((0,), (0,)), ((), ())), preferred_element_type=F32).astype(BF16)
-    kept, received, grad_head = lax.optimization_barrier((kept, received, grad_head))
     total = kept + received.astype(F32)
     for stage in (2, 1, 0):
         size = total.shape[0] // 4
         parts = [shift(total[k * size : (k + 1) * size].astype(BF16), stage, -k) for k in (1, 2, 3)]
+        if stage == 2:
+            total, grad_head, *parts = lax.optimization_barrier((total, grad_head, *parts))
         total = total[:size] + sum(p.astype(F32) for p in parts)
     token_loss = lax.dynamic_slice_in_dim(loss[0], lax.axis_index(AXES) * ROWS, ROWS)
     return token_loss, grad_head, total.astype(BF16)

time: 163 us -> 159 us (0.975)
  waiting for transfers between devices: 60.8 us -> 58.7 us
    ppermute x30, waiting for transfers between devices: 48.3 us -> 42.6 us  [shift(): return lax.ppermute(value, AXES, pairs)]
    ppermute x17, waiting for transfers between devices: 3.81 us -> 6.79 us  [swap(): return lax.ppermute(value, AXES, [(d, d ^ 32) for d in range(DEVICES)])]
  transfers between devices with their start and end apart: 53 -> 53, of which waited for: 30 -> 30; matrix products, arithmetic and copies ran while one was open for 5% -> 5% of each run, Pallas kernels for 8% -> 9%
where the time goes in v5:
time: 159 us
  waiting for transfers between devices  58.7 us (37%)
  starting transfers between devices  58.5 us (37%)
  Pallas kernels  27.5 us (17%)
  other arithmetic  5.31 us (3%)
  matrix products  4.82 us (3%)
  local copies, waits for them, and re-layouts  2.78 us (2%)
    ppermute x30, starting transfers between devices, shift(): return lax.ppermute(value, AXES, pairs)  45.5 us
    ppermute x30, waiting for transfers between devices, shift(): return lax.ppermute(value, AXES, pairs)  42.6 us
    pallas_call x3, Pallas kernels, call(): pl.pallas_call(kernel, out_shape=[jax.ShapeDtypeStruct(*o) for o in out],...  27.5 us
    ppermute x17, waiting for transfers between devices, swap(): return lax.ppermute(value, AXES, [(d, d ^ 32) for d in range(DEVICES)])  6.79 us
    ppermute x3, starting transfers between devices, across(): lax.ppermute(value, AXES, [(d, moved(d, dim, 2)) for d in range(DEVICES)])  6.31 us
    ppermute x3, waiting for transfers between devices, ring_shift(): lax.ppermute(value, AXES, [(d, moved(d, dim, -1 if coords(d)['c'] else 1)...  5.43 us
    dot_general x1, matrix products, shards(): lax.dot_general(hidden, grads, (((0,), (0,)), ((), ())), preferred_elemen...  4.82 us
    ppermute x3, waiting for transfers between devices, across(): lax.ppermute(value, AXES, [(d, moved(d, dim, 2)) for d in range(DEVICES)])  3.89 us
  transfers between devices with their start and end apart: 53, of which 30 were waited for; matrix products, arithmetic and copies ran while one was open for 5% of the time, Pallas kernels for 9%

profile of v5, /device:TPU:0, one launch (start us, length us, event | category | flops | bytes accessed | tf_op | source)
XLA Modules:
  0.0 158.7 jit_solution(8419557988544159596)
XLA Ops:
  0.6 1.8 %collective-permute-start.9 = (bf16[3,8192]{1,0:T(4,128)(2,1)}, bf16[3,8192]{1,0:T(4,128)(2,1)S(1)}, u32[]{:S(2)}, u32[]{:S(2)}) collective-permute-start(bf16[3,8192]{1,0:T(4,128)(2,1)} %param.6), channel_id=1, source_target_pairs={{0,1},{1,2},{2,3},{3,0},{4,5},{5,6},{6,7},{7,4},{8,9},{9,10},{10,1... | collective-permute-start | bytes 147464 | tf_op jit(solution)/shard_map/ppermute | solution.py:45
  2.4 1.5 collective-permute-start.11
  3.9 2.1 %collective-permute-start.10 = (bf16[3,8192]{1,0:T(4,128)(2,1)}, bf16[3,8192]{1,0:T(4,128)(2,1)S(1)}, u32[]{:S(2)}, u32[]{:S(2)}) collective-permute-start(bf16[3,8192]{1,0:T(4,128)(2,1)} %param.6), channel_id=1, source_target_pairs={{0,2},{1,3},{2,0},{3,1},{4,6},{5,7},{6,4},{7,5},{8,10},{9,11},{10,... | collective-permute-start | bytes 147464 | tf_op jit(solution)/shard_map/ppermute | solution.py:45
  6.9 3.1 %collective-permute-done.10 = bf16[3,8192]{1,0:T(4,128)(2,1)S(1)} collective-permute-done((bf16[3,8192]{1,0:T(4,128)(2,1)}, bf16[3,8192]{1,0:T(4,128)(2,1)S(1)}, u32[]{:S(2)}, u32[]{:S(2)}) %collective-permute-start.10) | collective-permute-done | bytes 49184 | tf_op jit(solution)/shard_map/ppermute | solution.py:45
  9.9 1.0 pad_maximum_fusion.3
  11.0 1.7 %collective-permute-start.12 = (bf16[12,8192]{1,0:T(8,128)(2,1)S(1)}, bf16[12,8192]{1,0:T(8,128)(2,1)S(1)}, u32[]{:S(2)}, u32[]{:S(2)}) collective-permute-start(bf16[12,8192]{1,0:T(8,128)(2,1)S(1)} %pad_maximum_fusion.3), channel_id=1, source_target_pairs={{0,4},{1,5},{2,6},{3,7},{4,8},{5,9},{6,10},{7,11},{8,12},{9,13},{1... | collective-permute-start | bytes 589832 | tf_op jit(solution)/shard_map/ppermute | solution.py:45
  13.0 2.9 %collective-permute-start.2 = (bf16[3,3584]{1,0:T(4,128)(2,1)}, bf16[3,3584]{1,0:T(4,128)(2,1)S(1)}, u32[]{:S(2)}, u32[]{:S(2)}) collective-permute-start(bf16[3,3584]{1,0:T(4,128)(2,1)} %param.8), channel_id=1, source_target_pairs={{0,3},{1,0},{2,1},{3,2},{4,7},{5,4},{6,5},{7,6},{8,11},{9,8},{10,9... | collective-permute-start | bytes 64520 | tf_op jit(solution)/shard_map/ppermute | solution.py:45
  15.9 0.8 collective-permute-start.1
  16.7 1.7 %collective-permute-start.14 = (bf16[12,8192]{1,0:T(8,128)(2,1)S(1)}, bf16[12,8192]{1,0:T(8,128)(2,1)S(1)}, u32[]{:S(2)}, u32[]{:S(2)}) collective-permute-start(bf16[12,8192]{1,0:T(8,128)(2,1)S(1)} %pad_maximum_fusion.3), channel_id=1, source_target_pairs={{0,12},{1,13},{2,14},{3,15},{4,0},{5,1},{6,2},{7,3},{8,4},{9,5},{1... | collective-permute-start | bytes 589832 | tf_op jit(solution)/shard_map/ppermute | solution.py:45
  18.6 1.9 %collective-permute-start.13 = (bf16[12,8192]{1,0:T(8,128)(2,1)S(1)}, bf16[12,8192]{1,0:T(8,128)(2,1)S(1)}, u32[]{:S(2)}, u32[]{:S(2)}) collective-permute-start(bf16[12,8192]{1,0:T(8,128)(2,1)S(1)} %pad_maximum_fusion.3), channel_id=1, source_target_pairs={{0,8},{1,9},{2,10},{3,11},{4,12},{5,13},{6,14},{7,15},{8,0},{9,1},... | collective-permute-start | bytes 589832 | tf_op jit(solution)/shard_map/ppermute | solution.py:45
  20.6 4.5 %collective-permute-done.14 = bf16[12,8192]{1,0:T(8,128)(2,1)S(1)} collective-permute-done((bf16[12,8192]{1,0:T(8,128)(2,1)S(1)}, bf16[12,8192]{1,0:T(8,128)(2,1)S(1)}, u32[]{:S(2)}, u32[]{:S(2)}) %collective-permute-start.14) | collective-permute-done | bytes 196640 | tf_op jit(solution)/shard_map/ppermute | solution.py:45
  25.1 1.4 collective-permute-done.13
  26.5 4.1 %collective-permute-start.17 = (bf16[24,8192]{1,0:T(8,128)(2,1)S(1)}, bf16[24,8192]{1,0:T(8,128)(2,1)S(1)}, u32[]{:S(2)}, u32[]{:S(2)}) collective-permute-start(bf16[24,8192]{1,0:T(8,128)(2,1)S(1)} %pad_maximum_fusion.1.refs_0_), channel_id=1, source_target_pairs={{0,80},{1,81},{2,82},{3,83},{4,84},{5,85},{6,86},{7,87},{8,88},{9,... | collective-permute-start | bytes 1179656 | tf_op jit(solution)/shard_map/ppermute | solution.py:45
  30.9 3.2 %collective-permute-start.18 = (bf16[24,8192]{1,0:T(8,128)(2,1)S(1)}, bf16[24,8192]{1,0:T(8,128)(2,1)S(1)}, u32[]{:S(2)}, u32[]{:S(2)}) collective-permute-start(bf16[24,8192]{1,0:T(8,128)(2,1)S(1)} %pad_maximum_fusion.refs_1_), channel_id=1, source_target_pairs={{0,80},{1,81},{2,82},{3,83},{4,84},{5,85},{6,86},{7,87},{8,88},{9,... | collective-permute-start | bytes 1179656 | tf_op jit(solution)/shard_map/ppermute | solution.py:45
  34.1 0.8 pad_maximum_fusion.4
  34.9 2.3 %collective-permute-start.5 = (bf16[12,3584]{1,0:T(8,128)(2,1)S(1)}, bf16[12,3584]{1,0:T(8,128)(2,1)S(1)}, u32[]{:S(2)}, u32[]{:S(2)}) collective-permute-start(bf16[12,3584]{1,0:T(8,128)(2,1)S(1)} %pad_maximum_fusion.4), channel_id=1, source_target_pairs={{0,12},{1,13},{2,14},{3,15},{4,0},{5,1},{6,2},{7,3},{8,4},{9,5},{1... | collective-permute-start | bytes 258056 | tf_op jit(solution)/shard_map/ppermute | solution.py:45
  37.2 2.6 %collective-permute-done.5 = bf16[12,3584]{1,0:T(8,128)(2,1)S(1)} collective-permute-done((bf16[12,3584]{1,0:T(8,128)(2,1)S(1)}, bf16[12,3584]{1,0:T(8,128)(2,1)S(1)}, u32[]{:S(2)}, u32[]{:S(2)}) %collective-permute-start.5) | collective-permute-done | bytes 86048 | tf_op jit(solution)/shard_map/ppermute | solution.py:45
  39.8 1.8 %collective-permute-start.4 = (bf16[12,3584]{1,0:T(8,128)(2,1)S(1)}, bf16[12,3584]{1,0:T(8,128)(2,1)S(1)}, u32[]{:S(2)}, u32[]{:S(2)}) collective-permute-start(bf16[12,3584]{1,0:T(8,128)(2,1)S(1)} %pad_maximum_fusion.4), channel_id=1, source_target_pairs={{0,8},{1,9},{2,10},{3,11},{4,12},{5,13},{6,14},{7,15},{8,0},{9,1},... | collective-permute-start | bytes 258056 | tf_op jit(solution)/shard_map/ppermute | solution.py:45
  41.6 4.5 %collective-permute-done.4 = bf16[12,3584]{1,0:T(8,128)(2,1)S(1)} collective-permute-done((bf16[12,3584]{1,0:T(8,128)(2,1)S(1)}, bf16[12,3584]{1,0:T(8,128)(2,1)S(1)}, u32[]{:S(2)}, u32[]{:S(2)}) %collective-permute-start.4) | collective-permute-done | bytes 86048 | tf_op jit(solution)/shard_map/ppermute | solution.py:45
  46.1 1.4 collective-permute-start.3
  47.5 4.8 %collective-permute-done.3 = bf16[12,3584]{1,0:T(8,128)(2,1)S(1)} collective-permute-done((bf16[12,3584]{1,0:T(8,128)(2,1)S(1)}, bf16[12,3584]{1,0:T(8,128)(2,1)S(1)}, u32[]{:S(2)}, u32[]{:S(2)}) %collective-permute-start.3) | collective-permute-done | bytes 86048 | tf_op jit(solution)/shard_map/ppermute | solution.py:45
  53.0 3.1 %collective-permute-start.26 = (bf16[24,8192]{1,0:T(8,128)(2,1)S(1)}, bf16[24,8192]{1,0:T(8,128)(2,1)}, u32[]{:S(2)}, u32[]{:S(2)}) collective-permute-start(bf16[24,8192]{1,0:T(8,128)(2,1)S(1)} %collective-permute-done.18.refs_5_), channel_id=1, source_target_pairs={{0,80},{1,81},{2,82},{3,83},{4,84},{5,85},{6,86},{7,87},{8,88},{9,... | collective-permute-start | bytes 1179656 | tf_op jit(solution)/shard_map/ppermute | solution.py:45
  56.6 4.7 %collective-permute-done.16.refs_3_ = bf16[24,8192]{1,0:T(8,128)(2,1)S(1)} collective-permute-done((bf16[24,8192]{1,0:T(8,128)(2,1)S(1)}, bf16[24,8192]{1,0:T(8,128)(2,1)S(1)}, u32[]{:S(2)}, u32[]{:S(2)}) %collective-permute-start.16) | collective-permute-done | bytes 393248 | tf_op jit(solution)/shard_map/ppermute | solution.py:45
  61.3 0.5 collective-permute-start.22
  61.8 3.8 %collective-permute-done.25.refs_12_ = bf16[24,8192]{1,0:T(8,128)(2,1)} collective-permute-done((bf16[24,8192]{1,0:T(8,128)(2,1)S(1)}, bf16[24,8192]{1,0:T(8,128)(2,1)}, u32[]{:S(2)}, u32[]{:S(2)}) %collective-permute-start.25) | collective-permute-done | bytes 393248 | tf_op jit(solution)/shard_map/ppermute | solution.py:45
  65.6 0.5 collective-permute-start.28
  66.2 1.2 pad_maximum_fusion.2.refs_0_
  67.5 0.5 collective-permute-start.8
  68.0 0.9 collective-permute-start.7
  68.9 0.9 collective-permute-start.6
  69.8 14.4 %shard_map.85.refs_9_.t_in = f32[384,768]{1,0:T(8,128)} custom-call(bf16[24,8192]{1,0:T(8,128)(2,1)S(1)} %pad_maximum_fusion.1.refs_0_, bf16[24,8192]{1,0:T(8,128)(2,1)S(1)} %pad_maximum_fusion.refs_1_, bf16[24,8192]{1,0:T(8,128)(2,1)S(1)} %collective-permute-done.15.refs_2_, bf16[24,8192]{1,0:T(8,128)(2,1)S(1)} %collective-permute-done.16.refs_3_, ...), custom_call_target="tpu_custom_call" | custom-call | flops 4831838208 | bytes 4194304 | tf_op jit(solution)/shard_map/pallas_call | solution.py:254
  84.2 0.6 collective-permute-start.30
  85.4 1.0 collective-permute-done.30.refs_5_
  86.3 0.5 collective-permute-done.31.refs_6_
  87.3 8.0 %shard_map.86 = (f32[384,768]{1,0:T(8,128)}, bf16[384,3584]{1,0:T(8,128)(2,1)}, f32[8,384]{1,0:T(8,128)S(1)}) custom-call(bf16[48,3584]{1,0:T(8,128)(2,1)S(1)} %pad_maximum_fusion.2.refs_0_, bf16[48,3584]{1,0:T(8,128)(2,1)} %collective-permute-done.6.refs_1_, bf16[48,3584]{1,0:T(8,128)(2,1)} %collective-permute-done.7.refs_2_, ...), custom_call_target="tpu_custom_call" | custom-call | flops 2113929216 | bytes 4194304 | tf_op jit(solution)/shard_map/pallas_call | solution.py:254
  95.8 0.8 collective-permute-done.33
  96.9 0.7 collective-permute-start.34
  97.6 2.2 %collective-permute-start.36 = (f32[8,384]{1,0:T(8,128)S(1)}, f32[8,384]{1,0:T(8,128)S(1)}, u32[]{:S(2)}, u32[]{:S(2)}) collective-permute-start(f32[8,384]{1,0:T(8,128)S(1)} %select_select_fusion.3), channel_id=1, source_target_pairs={{0,2},{1,3},{2,0},{3,1},{4,6},{5,7},{6,4},{7,5},{8,10},{9,11},{10,... | collective-permute-start | bytes 36872 | tf_op jit(solution)/shard_map/ppermute | solution.py:287
  99.8 2.0 %collective-permute-done.34 = f32[8,384]{1,0:T(8,128)S(1)} collective-permute-done((f32[8,384]{1,0:T(8,128)S(1)}, f32[8,384]{1,0:T(8,128)S(1)}, u32[]{:S(2)}, u32[]{:S(2)}) %collective-permute-start.34) | collective-permute-done | bytes 12320 | tf_op jit(solution)/shard_map/ppermute | solution.py:283
  101.8 1.0 collective-permute-done.36
  103.3 2.3 %collective-permute-start.37 = (f32[8,384]{1,0:T(8,128)S(1)}, f32[8,384]{1,0:T(8,128)S(1)}, u32[]{:S(2)}, u32[]{:S(2)}) collective-permute-start(f32[8,384]{1,0:T(8,128)S(1)} %select_select_fusion.2), channel_id=1, source_target_pairs={{0,4},{1,5},{2,6},{3,7},{4,8},{5,9},{6,10},{7,11},{8,12},{9,13},{1... | collective-permute-start | bytes 36872 | tf_op jit(solution)/shard_map/ppermute | solution.py:283
  105.6 1.7 %collective-permute-start.39 = (f32[8,384]{1,0:T(8,128)S(1)}, f32[8,384]{1,0:T(8,128)S(1)}, u32[]{:S(2)}, u32[]{:S(2)}) collective-permute-start(f32[8,384]{1,0:T(8,128)S(1)} %select_select_fusion.2), channel_id=1, source_target_pairs={{0,8},{1,9},{2,10},{3,11},{4,12},{5,13},{6,14},{7,15},{8,0},{9,1},... | collective-permute-start | bytes 36872 | tf_op jit(solution)/shard_map/ppermute | solution.py:287
  107.4 0.9 collective-permute-done.37
  108.3 2.6 %collective-permute-done.39 = f32[8,384]{1,0:T(8,128)S(1)} collective-permute-done((f32[8,384]{1,0:T(8,128)S(1)}, f32[8,384]{1,0:T(8,128)S(1)}, u32[]{:S(2)}, u32[]{:S(2)}) %collective-permute-start.39) | collective-permute-done | bytes 12320 | tf_op jit(solution)/shard_map/ppermute | solution.py:287
  111.5 2.3 %collective-permute-start.42 = (f32[8,384]{1,0:T(8,128)S(1)}, f32[8,384]{1,0:T(8,128)S(1)}, u32[]{:S(2)}, u32[]{:S(2)}) collective-permute-start(f32[8,384]{1,0:T(8,128)S(1)} %select_select_fusion.1), channel_id=1, source_target_pairs={{0,16},{1,17},{2,18},{3,19},{4,20},{5,21},{6,22},{7,23},{8,24},{9,... | collective-permute-start | bytes 36872 | tf_op jit(solution)/shard_map/ppermute | solution.py:287
  113.8 2.5 %collective-permute-done.40 = f32[8,384]{1,0:T(8,128)S(1)} collective-permute-done((f32[8,384]{1,0:T(8,128)S(1)}, f32[8,384]{1,0:T(8,128)S(1)}, u32[]{:S(2)}, u32[]{:S(2)}) %collective-permute-start.40) | collective-permute-done | bytes 12320 | tf_op jit(solution)/shard_map/ppermute | solution.py:283
  116.7 0.8 collective-permute-done.41
  117.9 1.3 copy-done.1
  119.1 5.1 %shard_map.87 = (bf16[384,768]{1,0:T(8,128)(2,1)S(1)}, bf16[192,3584]{1,0:T(8,128)(2,1)S(1)}, f32[192,3584]{1,0:T(8,128)S(1)}, f32[1,384]{1,0:T(1,128)S(1)}) custom-call(s32[1]{0:T(128)} %bitcast.refs_8_.at_ref, f32[384,768]{1,0:T(8,128)S(1)} %copy-done, f32[384,768]{1,0:T(8,128)S(1)} %copy-done.1, f32[8,384]{1,0:T(8,128)S(1)} %select_select_fusion.stats, ...), custom_call_target="tpu_custom_call" | custom-call | flops 2113929216 | bytes 4194304 | tf_op jit(solution)/shard_map/pallas_call | solution.py:254
  124.5 3.0 %collective-permute-done.43 = bf16[192,3584]{1,0:T(8,128)(2,1)S(1)} collective-permute-done((bf16[192,3584]{1,0:T(8,128)(2,1)S(1)}, bf16[192,3584]{1,0:T(8,128)(2,1)S(1)}, u32[]{:S(2)}, u32[]{:S(2)}) %collective-permute-start.43) | collective-permute-done | bytes 1376288 | tf_op jit(solution)/shard_map/ppermute | solution.py:40
  128.0 1.4 collective-permute-start.46
  129.4 2.4 %collective-permute-start.45 = (bf16[48,3584]{1,0:T(8,128)(2,1)S(1)}, bf16[48,3584]{1,0:T(8,128)(2,1)S(1)}, u32[]{:S(2)}, u32[]{:S(2)}) collective-permute-start(bf16[48,3584]{1,0:T(8,128)(2,1)S(1)} %get-tuple-element.58), channel_id=1, source_target_pairs={{0,16},{1,17},{2,18},{3,19},{4,20},{5,21},{6,22},{7,23},{8,24},{9,... | collective-permute-start | bytes 1032200 | tf_op jit(solution)/shard_map/ppermute | solution.py:45
  132.2 4.8 %convolution_convert_fusion = bf16[3584,768]{1,0:T(8,128)(2,1)} fusion(bf16[384,3584]{1,0:T(8,128)(2,1)S(1)} %copy-done.8, bf16[384,768]{1,0:T(8,128)(2,1)S(1)} %get-tuple-element.29), kind=kOutput, calls=%fused_computation | convolution fusion | flops 2116681728 | bytes 8847360 | tf_op jit(solution)/shard_map/dot_general | solution.py:381
  137.0 3.8 %collective-permute-done.45 = bf16[48,3584]{1,0:T(8,128)(2,1)S(1)} collective-permute-done((bf16[48,3584]{1,0:T(8,128)(2,1)S(1)}, bf16[48,3584]{1,0:T(8,128)(2,1)S(1)}, u32[]{:S(2)}, u32[]{:S(2)}) %collective-permute-start.45) | collective-permute-done | bytes 344096 | tf_op jit(solution)/shard_map/ppermute | solution.py:45
  141.3 1.6 collective-permute-start.47
  142.9 0.5 collective-permute-start.49
  143.4 1.7 %collective-permute-start.48 = (bf16[12,3584]{1,0:T(8,128)(2,1)S(1)}, bf16[12,3584]{1,0:T(8,128)(2,1)S(1)}, u32[]{:S(2)}, u32[]{:S(2)}) collective-permute-start(bf16[12,3584]{1,0:T(8,128)(2,1)S(1)} %get-tuple-element.62), channel_id=1, source_target_pairs={{0,8},{1,9},{2,10},{3,11},{4,12},{5,13},{6,14},{7,15},{8,0},{9,1},... | collective-permute-start | bytes 258056 | tf_op jit(solution)/shard_map/ppermute | solution.py:45
  145.2 1.0 collective-permute-done.47
  146.2 4.0 %collective-permute-done.49 = bf16[12,3584]{1,0:T(8,128)(2,1)S(1)} collective-permute-done((bf16[12,3584]{1,0:T(8,128)(2,1)S(1)}, bf16[12,3584]{1,0:T(8,128)(2,1)S(1)}, u32[]{:S(2)}, u32[]{:S(2)}) %collective-permute-start.49) | collective-permute-done | bytes 86048 | tf_op jit(solution)/shard_map/ppermute | solution.py:45
  150.3 2.4 %collective-permute-start.50 = (bf16[3,3584]{1,0:T(4,128)(2,1)S(1)}, bf16[3,3584]{1,0:T(4,128)(2,1)S(1)}, u32[]{:S(2)}, u32[]{:S(2)}) collective-permute-start(bf16[3,3584]{1,0:T(4,128)(2,1)S(1)} %get-tuple-element.63), channel_id=1, source_target_pairs={{0,3},{1,0},{2,1},{3,2},{4,7},{5,4},{6,5},{7,6},{8,11},{9,8},{10,9... | collective-permute-start | bytes 64520 | tf_op jit(solution)/shard_map/ppermute | solution.py:45
  152.7 1.6 %collective-permute-start.51 = (bf16[3,3584]{1,0:T(4,128)(2,1)S(1)}, bf16[3,3584]{1,0:T(4,128)(2,1)S(1)}, u32[]{:S(2)}, u32[]{:S(2)}) collective-permute-start(bf16[3,3584]{1,0:T(4,128)(2,1)S(1)} %get-tuple-element.65), channel_id=1, source_target_pairs={{0,2},{1,3},{2,0},{3,1},{4,6},{5,7},{6,4},{7,5},{8,10},{9,11},{10,... | collective-permute-start | bytes 64520 | tf_op jit(solution)/shard_map/ppermute | solution.py:45
  154.3 0.6 dynamic-slice_bitcast_fusion
  154.9 2.9 %collective-permute-done.52 = bf16[3,3584]{1,0:T(4,128)(2,1)S(1)} collective-permute-done((bf16[3,3584]{1,0:T(4,128)(2,1)S(1)}, bf16[3,3584]{1,0:T(4,128)(2,1)S(1)}, u32[]{:S(2)}, u32[]{:S(2)}) %collective-permute-start.52) | collective-permute-done | bytes 21536 | tf_op jit(solution)/shard_map/ppermute | solution.py:45
  158.1 0.6 fusion
  (122 shorter events, 8.5 us)
Async XLA Ops:
  0.6 55.7 %copy-start.6 = (s32[384]{0:T(512)S(1)}, s32[384]{0:T(512)}, u32[]{:S(2)}) copy-start(s32[384]{0:T(512)} %param.11) | copy-start | bytes 4612
  0.6 5.8 %collective-permute-start.9 = (bf16[3,8192]{1,0:T(4,128)(2,1)}, bf16[3,8192]{1,0:T(4,128)(2,1)S(1)}, u32[]{:S(2)}, u32[]{:S(2)}) collective-permute-start(bf16[3,8192]{1,0:T(4,128)(2,1)} %param.6), channel_id=1, source_target_pairs={{0,1},{1,2},{2,3},{3,0},{4,5},{5,6},{6,7},{7,4},{8,9},{9,10},{10,1... | collective-permute-start | bytes 147464 | tf_op jit(solution)/shard_map/ppermute | solution.py:45
  2.4 4.5 %collective-permute-start.11 = (bf16[3,8192]{1,0:T(4,128)(2,1)}, bf16[3,8192]{1,0:T(4,128)(2,1)S(1)}, u32[]{:S(2)}, u32[]{:S(2)}) collective-permute-start(bf16[3,8192]{1,0:T(4,128)(2,1)} %param.6), channel_id=1, source_target_pairs={{0,3},{1,0},{2,1},{3,2},{4,7},{5,4},{6,5},{7,6},{8,11},{9,8},{10,9... | collective-permute-start | bytes 147464 | tf_op jit(solution)/shard_map/ppermute | solution.py:45
  3.9 6.0 %collective-permute-start.10 = (bf16[3,8192]{1,0:T(4,128)(2,1)}, bf16[3,8192]{1,0:T(4,128)(2,1)S(1)}, u32[]{:S(2)}, u32[]{:S(2)}) collective-permute-start(bf16[3,8192]{1,0:T(4,128)(2,1)} %param.6), channel_id=1, source_target_pairs={{0,2},{1,3},{2,0},{3,1},{4,6},{5,7},{6,4},{7,5},{8,10},{9,11},{10,... | collective-permute-start | bytes 147464 | tf_op jit(solution)/shard_map/ppermute | solution.py:45
  11.0 7.7 %collective-permute-start.12 = (bf16[12,8192]{1,0:T(8,128)(2,1)S(1)}, bf16[12,8192]{1,0:T(8,128)(2,1)S(1)}, u32[]{:S(2)}, u32[]{:S(2)}) collective-permute-start(bf16[12,8192]{1,0:T(8,128)(2,1)S(1)} %pad_maximum_fusion.3), channel_id=1, source_target_pairs={{0,4},{1,5},{2,6},{3,7},{4,8},{5,9},{6,10},{7,11},{8,12},{9,13},{1... | collective-permute-start | bytes 589832 | tf_op jit(solution)/shard_map/ppermute | solution.py:45
  12.6 18.1 %collective-permute-start = (bf16[3,3584]{1,0:T(4,128)(2,1)}, bf16[3,3584]{1,0:T(4,128)(2,1)S(1)}, u32[]{:S(2)}, u32[]{:S(2)}) collective-permute-start(bf16[3,3584]{1,0:T(4,128)(2,1)} %param.8), channel_id=1, source_target_pairs={{0,1},{1,2},{2,3},{3,0},{4,5},{5,6},{6,7},{7,4},{8,9},{9,10},{10,1... | collective-permute-start | bytes 64520 | tf_op jit(solution)/shard_map/ppermute | solution.py:45
  13.0 17.8 %collective-permute-start.2 = (bf16[3,3584]{1,0:T(4,128)(2,1)}, bf16[3,3584]{1,0:T(4,128)(2,1)S(1)}, u32[]{:S(2)}, u32[]{:S(2)}) collective-permute-start(bf16[3,3584]{1,0:T(4,128)(2,1)} %param.8), channel_id=1, source_target_pairs={{0,3},{1,0},{2,1},{3,2},{4,7},{5,4},{6,5},{7,6},{8,11},{9,8},{10,9... | collective-permute-start | bytes 64520 | tf_op jit(solution)/shard_map/ppermute | solution.py:45
  15.9 18.2 %collective-permute-start.1 = (bf16[3,3584]{1,0:T(4,128)(2,1)}, bf16[3,3584]{1,0:T(4,128)(2,1)S(1)}, u32[]{:S(2)}, u32[]{:S(2)}) collective-permute-start(bf16[3,3584]{1,0:T(4,128)(2,1)} %param.8), channel_id=1, source_target_pairs={{0,2},{1,3},{2,0},{3,1},{4,6},{5,7},{6,4},{7,5},{8,10},{9,11},{10,... | collective-permute-start | bytes 64520 | tf_op jit(solution)/shard_map/ppermute | solution.py:45
  16.7 8.5 %collective-permute-start.14 = (bf16[12,8192]{1,0:T(8,128)(2,1)S(1)}, bf16[12,8192]{1,0:T(8,128)(2,1)S(1)}, u32[]{:S(2)}, u32[]{:S(2)}) collective-permute-start(bf16[12,8192]{1,0:T(8,128)(2,1)S(1)} %pad_maximum_fusion.3), channel_id=1, source_target_pairs={{0,12},{1,13},{2,14},{3,15},{4,0},{5,1},{6,2},{7,3},{8,4},{9,5},{1... | collective-permute-start | bytes 589832 | tf_op jit(solution)/shard_map/ppermute | solution.py:45
  18.6 7.9 %collective-permute-start.13 = (bf16[12,8192]{1,0:T(8,128)(2,1)S(1)}, bf16[12,8192]{1,0:T(8,128)(2,1)S(1)}, u32[]{:S(2)}, u32[]{:S(2)}) collective-permute-start(bf16[12,8192]{1,0:T(8,128)(2,1)S(1)} %pad_maximum_fusion.3), channel_id=1, source_target_pairs={{0,8},{1,9},{2,10},{3,11},{4,12},{5,13},{6,14},{7,15},{8,0},{9,1},... | collective-permute-start | bytes 589832 | tf_op jit(solution)/shard_map/ppermute | solution.py:45
  25.1 27.1 %collective-permute-start.19 = (bf16[24,8192]{1,0:T(8,128)(2,1)S(1)}, bf16[24,8192]{1,0:T(8,128)(2,1)S(1)}, u32[]{:S(2)}, u32[]{:S(2)}) collective-permute-start(bf16[24,8192]{1,0:T(8,128)(2,1)S(1)} %pad_maximum_fusion.1.refs_0_), channel_id=1, source_target_pairs={{0,32},{1,33},{2,34},{3,35},{4,36},{5,37},{6,38},{7,39},{8,40},{9,... | collective-permute-start | bytes 1179656 | tf_op jit(solution)/shard_map/ppermute | solution.py:40
  26.5 25.9 %collective-permute-start.17 = (bf16[24,8192]{1,0:T(8,128)(2,1)S(1)}, bf16[24,8192]{1,0:T(8,128)(2,1)S(1)}, u32[]{:S(2)}, u32[]{:S(2)}) collective-permute-start(bf16[24,8192]{1,0:T(8,128)(2,1)S(1)} %pad_maximum_fusion.1.refs_0_), channel_id=1, source_target_pairs={{0,80},{1,81},{2,82},{3,83},{4,84},{5,85},{6,86},{7,87},{8,88},{9,... | collective-permute-start | bytes 1179656 | tf_op jit(solution)/shard_map/ppermute | solution.py:45
  30.8 22.1 %collective-permute-start.15 = (bf16[24,8192]{1,0:T(8,128)(2,1)S(1)}, bf16[24,8192]{1,0:T(8,128)(2,1)S(1)}, u32[]{:S(2)}, u32[]{:S(2)}) collective-permute-start(bf16[24,8192]{1,0:T(8,128)(2,1)S(1)} %pad_maximum_fusion.1.refs_0_), channel_id=1, source_target_pairs={{0,64},{1,65},{2,66},{3,67},{4,68},{5,69},{6,70},{7,71},{8,72},{9,... | collective-permute-start | bytes 1179656 | tf_op jit(solution)/shard_map/ppermute | solution.py:45
  30.9 22.1 %collective-permute-start.18 = (bf16[24,8192]{1,0:T(8,128)(2,1)S(1)}, bf16[24,8192]{1,0:T(8,128)(2,1)S(1)}, u32[]{:S(2)}, u32[]{:S(2)}) collective-permute-start(bf16[24,8192]{1,0:T(8,128)(2,1)S(1)} %pad_maximum_fusion.refs_1_), channel_id=1, source_target_pairs={{0,80},{1,81},{2,82},{3,83},{4,84},{5,85},{6,86},{7,87},{8,88},{9,... | collective-permute-start | bytes 1179656 | tf_op jit(solution)/shard_map/ppermute | solution.py:45
  34.9 18.1 %copy-start.2 = (bf16[12,3584]{1,0:T(8,128)(2,1)}, bf16[12,3584]{1,0:T(8,128)(2,1)S(1)}, u32[]{:S(2)}) copy-start(bf16[12,3584]{1,0:T(8,128)(2,1)S(1)} %pad_maximum_fusion.4) | copy-start | bytes 258052
  34.9 4.9 %collective-permute-start.5 = (bf16[12,3584]{1,0:T(8,128)(2,1)S(1)}, bf16[12,3584]{1,0:T(8,128)(2,1)S(1)}, u32[]{:S(2)}, u32[]{:S(2)}) collective-permute-start(bf16[12,3584]{1,0:T(8,128)(2,1)S(1)} %pad_maximum_fusion.4), channel_id=1, source_target_pairs={{0,12},{1,13},{2,14},{3,15},{4,0},{5,1},{6,2},{7,3},{8,4},{9,5},{1... | collective-permute-start | bytes 258056 | tf_op jit(solution)/shard_map/ppermute | solution.py:45
  39.8 16.3 %copy-start.3 = (bf16[12,3584]{1,0:T(8,128)(2,1)}, bf16[12,3584]{1,0:T(8,128)(2,1)S(1)}, u32[]{:S(2)}) copy-start(bf16[12,3584]{1,0:T(8,128)(2,1)S(1)} %collective-permute-done.5) | copy-start | bytes 258052
  39.8 6.3 %collective-permute-start.4 = (bf16[12,3584]{1,0:T(8,128)(2,1)S(1)}, bf16[12,3584]{1,0:T(8,128)(2,1)S(1)}, u32[]{:S(2)}, u32[]{:S(2)}) collective-permute-start(bf16[12,3584]{1,0:T(8,128)(2,1)S(1)} %pad_maximum_fusion.4), channel_id=1, source_target_pairs={{0,8},{1,9},{2,10},{3,11},{4,12},{5,13},{6,14},{7,15},{8,0},{9,1},... | collective-permute-start | bytes 258056 | tf_op jit(solution)/shard_map/ppermute | solution.py:45
  46.1 10.0 %copy-start.4 = (bf16[12,3584]{1,0:T(8,128)(2,1)}, bf16[12,3584]{1,0:T(8,128)(2,1)S(1)}, u32[]{:S(2)}) copy-start(bf16[12,3584]{1,0:T(8,128)(2,1)S(1)} %collective-permute-done.4) | copy-start | bytes 258052
  46.1 6.2 %collective-permute-start.3 = (bf16[12,3584]{1,0:T(8,128)(2,1)S(1)}, bf16[12,3584]{1,0:T(8,128)(2,1)S(1)}, u32[]{:S(2)}, u32[]{:S(2)}) collective-permute-start(bf16[12,3584]{1,0:T(8,128)(2,1)S(1)} %pad_maximum_fusion.4), channel_id=1, source_target_pairs={{0,4},{1,5},{2,6},{3,7},{4,8},{5,9},{6,10},{7,11},{8,12},{9,13},{1... | collective-permute-start | bytes 258056 | tf_op jit(solution)/shard_map/ppermute | solution.py:45
  52.3 3.9 %copy-start.5 = (bf16[12,3584]{1,0:T(8,128)(2,1)}, bf16[12,3584]{1,0:T(8,128)(2,1)S(1)}, u32[]{:S(2)}) copy-start(bf16[12,3584]{1,0:T(8,128)(2,1)S(1)} %collective-permute-done.3) | copy-start | bytes 258052
  52.3 4.2 %collective-permute-start.20 = (bf16[24,8192]{1,0:T(8,128)(2,1)S(1)}, bf16[24,8192]{1,0:T(8,128)(2,1)S(1)}, u32[]{:S(2)}, u32[]{:S(2)}) collective-permute-start(bf16[24,8192]{1,0:T(8,128)(2,1)S(1)} %pad_maximum_fusion.refs_1_), channel_id=1, source_target_pairs={{0,32},{1,33},{2,34},{3,35},{4,36},{5,37},{6,38},{7,39},{8,40},{9,... | collective-permute-start | bytes 1179656 | tf_op jit(solution)/shard_map/ppermute | solution.py:40
  52.3 9.1 %collective-permute-start.16 = (bf16[24,8192]{1,0:T(8,128)(2,1)S(1)}, bf16[24,8192]{1,0:T(8,128)(2,1)S(1)}, u32[]{:S(2)}, u32[]{:S(2)}) collective-permute-start(bf16[24,8192]{1,0:T(8,128)(2,1)S(1)} %pad_maximum_fusion.refs_1_), channel_id=1, source_target_pairs={{0,64},{1,65},{2,66},{3,67},{4,68},{5,69},{6,70},{7,71},{8,72},{9,... | collective-permute-start | bytes 1179656 | tf_op jit(solution)/shard_map/ppermute | solution.py:45
  52.4 8.9 %collective-permute-start.23 = (bf16[24,8192]{1,0:T(8,128)(2,1)S(1)}, bf16[24,8192]{1,0:T(8,128)(2,1)}, u32[]{:S(2)}, u32[]{:S(2)}) collective-permute-start(bf16[24,8192]{1,0:T(8,128)(2,1)S(1)} %collective-permute-done.17.refs_4_), channel_id=1, source_target_pairs={{0,32},{1,33},{2,34},{3,35},{4,36},{5,37},{6,38},{7,39},{8,40},{9,... | collective-permute-start | bytes 1179656 | tf_op jit(solution)/shard_map/ppermute | solution.py:40
  52.9 12.8 %collective-permute-start.25 = (bf16[24,8192]{1,0:T(8,128)(2,1)S(1)}, bf16[24,8192]{1,0:T(8,128)(2,1)}, u32[]{:S(2)}, u32[]{:S(2)}) collective-permute-start(bf16[24,8192]{1,0:T(8,128)(2,1)S(1)} %collective-permute-done.15.refs_2_), channel_id=1, source_target_pairs={{0,64},{1,65},{2,66},{3,67},{4,68},{5,69},{6,70},{7,71},{8,72},{9,... | collective-permute-start | bytes 1179656 | tf_op jit(solution)/shard_map/ppermute | solution.py:45
  53.0 12.7 %collective-permute-start.26 = (bf16[24,8192]{1,0:T(8,128)(2,1)S(1)}, bf16[24,8192]{1,0:T(8,128)(2,1)}, u32[]{:S(2)}, u32[]{:S(2)}) collective-permute-start(bf16[24,8192]{1,0:T(8,128)(2,1)S(1)} %collective-permute-done.18.refs_5_), channel_id=1, source_target_pairs={{0,80},{1,81},{2,82},{3,83},{4,84},{5,85},{6,86},{7,87},{8,88},{9,... | collective-permute-start | bytes 1179656 | tf_op jit(solution)/shard_map/ppermute | solution.py:45
  56.5 10.9 %collective-permute-start.21 = (bf16[24,8192]{1,0:T(8,128)(2,1)S(1)}, bf16[24,8192]{1,0:T(8,128)(2,1)S(1)}, u32[]{:S(2)}, u32[]{:S(2)}) collective-permute-start(bf16[24,8192]{1,0:T(8,128)(2,1)S(1)} %collective-permute-done.15.refs_2_), channel_id=1, source_target_pairs={{0,32},{1,33},{2,34},{3,35},{4,36},{5,37},{6,38},{7,39},{8,40},{9,... | collective-permute-start | bytes 1179656 | tf_op jit(solution)/shard_map/ppermute | solution.py:40
  61.3 6.1 %collective-permute-start.24 = (bf16[24,8192]{1,0:T(8,128)(2,1)S(1)}, bf16[24,8192]{1,0:T(8,128)(2,1)S(1)}, u32[]{:S(2)}, u32[]{:S(2)}) collective-permute-start(bf16[24,8192]{1,0:T(8,128)(2,1)S(1)} %collective-permute-done.18.refs_5_), channel_id=1, source_target_pairs={{0,32},{1,33},{2,34},{3,35},{4,36},{5,37},{6,38},{7,39},{8,40},{9,... | collective-permute-start | bytes 1179656 | tf_op jit(solution)/shard_map/ppermute | solution.py:40
  61.3 6.6 %collective-permute-start.22 = (bf16[24,8192]{1,0:T(8,128)(2,1)S(1)}, bf16[24,8192]{1,0:T(8,128)(2,1)S(1)}, u32[]{:S(2)}, u32[]{:S(2)}) collective-permute-start(bf16[24,8192]{1,0:T(8,128)(2,1)S(1)} %collective-permute-done.16.refs_3_), channel_id=1, source_target_pairs={{0,32},{1,33},{2,34},{3,35},{4,36},{5,37},{6,38},{7,39},{8,40},{9,... | collective-permute-start | bytes 1179656 | tf_op jit(solution)/shard_map/ppermute | solution.py:40
  65.6 3.3 %collective-permute-start.27 = (bf16[24,8192]{1,0:T(8,128)(2,1)}, bf16[24,8192]{1,0:T(8,128)(2,1)S(1)}, u32[]{:S(2)}, u32[]{:S(2)}) collective-permute-start(bf16[24,8192]{1,0:T(8,128)(2,1)} %collective-permute-done.25.refs_12_), channel_id=1, source_target_pairs={{0,32},{1,33},{2,34},{3,35},{4,36},{5,37},{6,38},{7,39},{8,40},{9,... | collective-permute-start | bytes 1179656 | tf_op jit(solution)/shard_map/ppermute | solution.py:40
  65.6 4.2 %collective-permute-start.28 = (bf16[24,8192]{1,0:T(8,128)(2,1)}, bf16[24,8192]{1,0:T(8,128)(2,1)S(1)}, u32[]{:S(2)}, u32[]{:S(2)}) collective-permute-start(bf16[24,8192]{1,0:T(8,128)(2,1)} %collective-permute-done.26.refs_13_), channel_id=1, source_target_pairs={{0,32},{1,33},{2,34},{3,35},{4,36},{5,37},{6,38},{7,39},{8,40},{9,... | collective-permute-start | bytes 1179656 | tf_op jit(solution)/shard_map/ppermute | solution.py:40
  67.3 18.0 %copy-start.7 = (s32[384]{0:T(512)S(1)}, s32[384]{0:T(512)}, u32[]{:S(2)}) copy-start(s32[384]{0:T(512)} %param.10) | copy-start | bytes 4612
  67.3 18.0 %collective-permute-start.29 = (bf16[48,3584]{1,0:T(8,128)(2,1)S(1)}, bf16[48,3584]{1,0:T(8,128)(2,1)}, u32[]{:S(2)}, u32[]{:S(2)}) collective-permute-start(bf16[48,3584]{1,0:T(8,128)(2,1)S(1)} %pad_maximum_fusion.2.refs_0_), channel_id=1, source_target_pairs={{0,32},{1,33},{2,34},{3,35},{4,36},{5,37},{6,38},{7,39},{8,40},{9,... | collective-permute-start | bytes 1032200 | tf_op jit(solution)/shard_map/ppermute | solution.py:40
  67.5 16.7 %collective-permute-start.8 = (bf16[48,3584]{1,0:T(8,128)(2,1)S(1)}, bf16[48,3584]{1,0:T(8,128)(2,1)}, u32[]{:S(2)}, u32[]{:S(2)}) collective-permute-start(bf16[48,3584]{1,0:T(8,128)(2,1)S(1)} %pad_maximum_fusion.2.refs_0_), channel_id=1, source_target_pairs={{0,80},{1,81},{2,82},{3,83},{4,84},{5,85},{6,86},{7,87},{8,88},{9,... | collective-permute-start | bytes 1032200 | tf_op jit(solution)/shard_map/ppermute | solution.py:45
  68.0 16.2 %collective-permute-start.7 = (bf16[48,3584]{1,0:T(8,128)(2,1)S(1)}, bf16[48,3584]{1,0:T(8,128)(2,1)}, u32[]{:S(2)}, u32[]{:S(2)}) collective-permute-start(bf16[48,3584]{1,0:T(8,128)(2,1)S(1)} %pad_maximum_fusion.2.refs_0_), channel_id=1, source_target_pairs={{0,16},{1,17},{2,18},{3,19},{4,20},{5,21},{6,22},{7,23},{8,24},{9,... | collective-permute-start | bytes 1032200 | tf_op jit(solution)/shard_map/ppermute | solution.py:45
  68.9 15.3 %collective-permute-start.6 = (bf16[48,3584]{1,0:T(8,128)(2,1)S(1)}, bf16[48,3584]{1,0:T(8,128)(2,1)}, u32[]{:S(2)}, u32[]{:S(2)}) collective-permute-start(bf16[48,3584]{1,0:T(8,128)(2,1)S(1)} %pad_maximum_fusion.2.refs_0_), channel_id=1, source_target_pairs={{0,64},{1,65},{2,66},{3,67},{4,68},{5,69},{6,70},{7,71},{8,72},{9,... | collective-permute-start | bytes 1032200 | tf_op jit(solution)/shard_map/ppermute | solution.py:45
  84.2 2.1 %collective-permute-start.30 = (bf16[48,3584]{1,0:T(8,128)(2,1)}, bf16[48,3584]{1,0:T(8,128)(2,1)S(1)}, u32[]{:S(2)}, u32[]{:S(2)}) collective-permute-start(bf16[48,3584]{1,0:T(8,128)(2,1)} %collective-permute-done.6.refs_1_), channel_id=1, source_target_pairs={{0,32},{1,33},{2,34},{3,35},{4,36},{5,37},{6,38},{7,39},{8,40},{9,... | collective-permute-start | bytes 1032200 | tf_op jit(solution)/shard_map/ppermute | solution.py:40
  84.8 2.0 %collective-permute-start.31 = (bf16[48,3584]{1,0:T(8,128)(2,1)}, bf16[48,3584]{1,0:T(8,128)(2,1)S(1)}, u32[]{:S(2)}, u32[]{:S(2)}) collective-permute-start(bf16[48,3584]{1,0:T(8,128)(2,1)} %collective-permute-done.7.refs_2_), channel_id=1, source_target_pairs={{0,32},{1,33},{2,34},{3,35},{4,36},{5,37},{6,38},{7,39},{8,40},{9,... | collective-permute-start | bytes 1032200 | tf_op jit(solution)/shard_map/ppermute | solution.py:40
  84.9 2.4 %collective-permute-start.32 = (bf16[48,3584]{1,0:T(8,128)(2,1)}, bf16[48,3584]{1,0:T(8,128)(2,1)S(1)}, u32[]{:S(2)}, u32[]{:S(2)}) collective-permute-start(bf16[48,3584]{1,0:T(8,128)(2,1)} %collective-permute-done.8.refs_3_), channel_id=1, source_target_pairs={{0,32},{1,33},{2,34},{3,35},{4,36},{5,37},{6,38},{7,39},{8,40},{9,... | collective-permute-start | bytes 1032200 | tf_op jit(solution)/shard_map/ppermute | solution.py:40
  87.3 30.5 %copy-start = (f32[384,768]{1,0:T(8,128)S(1)}, f32[384,768]{1,0:T(8,128)}, u32[]{:S(2)}) copy-start(f32[384,768]{1,0:T(8,128)} %shard_map.85.refs_9_.t_in) | copy-start | bytes 3538948
  95.4 1.3 collective-permute-start.33
  96.9 4.9 %collective-permute-start.34 = (f32[8,384]{1,0:T(8,128)S(1)}, f32[8,384]{1,0:T(8,128)S(1)}, u32[]{:S(2)}, u32[]{:S(2)}) collective-permute-start(f32[8,384]{1,0:T(8,128)S(1)} %select_select_fusion.3), channel_id=1, source_target_pairs={{0,1},{1,2},{2,3},{3,0},{4,5},{5,6},{6,7},{7,4},{8,9},{9,10},{10,1... | collective-permute-start | bytes 36872 | tf_op jit(solution)/shard_map/ppermute | solution.py:283
  97.6 5.2 %collective-permute-start.36 = (f32[8,384]{1,0:T(8,128)S(1)}, f32[8,384]{1,0:T(8,128)S(1)}, u32[]{:S(2)}, u32[]{:S(2)}) collective-permute-start(f32[8,384]{1,0:T(8,128)S(1)} %select_select_fusion.3), channel_id=1, source_target_pairs={{0,2},{1,3},{2,0},{3,1},{4,6},{5,7},{6,4},{7,5},{8,10},{9,11},{10,... | collective-permute-start | bytes 36872 | tf_op jit(solution)/shard_map/ppermute | solution.py:287
  101.8 1.2 collective-permute-start.35
  103.3 4.9 %collective-permute-start.37 = (f32[8,384]{1,0:T(8,128)S(1)}, f32[8,384]{1,0:T(8,128)S(1)}, u32[]{:S(2)}, u32[]{:S(2)}) collective-permute-start(f32[8,384]{1,0:T(8,128)S(1)} %select_select_fusion.2), channel_id=1, source_target_pairs={{0,4},{1,5},{2,6},{3,7},{4,8},{5,9},{6,10},{7,11},{8,12},{9,13},{1... | collective-permute-start | bytes 36872 | tf_op jit(solution)/shard_map/ppermute | solution.py:283
  105.6 5.2 %collective-permute-start.39 = (f32[8,384]{1,0:T(8,128)S(1)}, f32[8,384]{1,0:T(8,128)S(1)}, u32[]{:S(2)}, u32[]{:S(2)}) collective-permute-start(f32[8,384]{1,0:T(8,128)S(1)} %select_select_fusion.2), channel_id=1, source_target_pairs={{0,8},{1,9},{2,10},{3,11},{4,12},{5,13},{6,14},{7,15},{8,0},{9,1},... | collective-permute-start | bytes 36872 | tf_op jit(solution)/shard_map/ppermute | solution.py:287
  108.3 2.6 %collective-permute-start.38 = (f32[8,384]{1,0:T(8,128)S(1)}, f32[8,384]{1,0:T(8,128)S(1)}, u32[]{:S(2)}, u32[]{:S(2)}) collective-permute-start(f32[8,384]{1,0:T(8,128)S(1)} %collective-permute-done.37), channel_id=1, source_target_pairs={{0,32},{1,33},{2,34},{3,35},{4,36},{5,37},{6,38},{7,39},{8,40},{9,... | collective-permute-start | bytes 36872 | tf_op jit(solution)/shard_map/ppermute | solution.py:40
  111.2 5.1 %collective-permute-start.40 = (f32[8,384]{1,0:T(8,128)S(1)}, f32[8,384]{1,0:T(8,128)S(1)}, u32[]{:S(2)}, u32[]{:S(2)}) collective-permute-start(f32[8,384]{1,0:T(8,128)S(1)} %select_select_fusion.1), channel_id=1, source_target_pairs={{0,64},{1,65},{2,66},{3,67},{4,68},{5,69},{6,70},{7,71},{8,72},{9,... | collective-permute-start | bytes 36872 | tf_op jit(solution)/shard_map/ppermute | solution.py:283
  111.5 5.2 %collective-permute-start.42 = (f32[8,384]{1,0:T(8,128)S(1)}, f32[8,384]{1,0:T(8,128)S(1)}, u32[]{:S(2)}, u32[]{:S(2)}) collective-permute-start(f32[8,384]{1,0:T(8,128)S(1)} %select_select_fusion.1), channel_id=1, source_target_pairs={{0,16},{1,17},{2,18},{3,19},{4,20},{5,21},{6,22},{7,23},{8,24},{9,... | collective-permute-start | bytes 36872 | tf_op jit(solution)/shard_map/ppermute | solution.py:287
  116.3 1.2 collective-permute-start.41
  117.9 1.3 copy-start.1
  124.3 3.2 %collective-permute-start.43 = (bf16[192,3584]{1,0:T(8,128)(2,1)S(1)}, bf16[192,3584]{1,0:T(8,128)(2,1)S(1)}, u32[]{:S(2)}, u32[]{:S(2)}) collective-permute-start(bf16[192,3584]{1,0:T(8,128)(2,1)S(1)} %get-tuple-element.27), channel_id=1, source_target_pairs={{0,32},{1,33},{2,34},{3,35},{4,36},{5,37},{6,38},{7,39},{8,40},{9,... | collective-permute-start | bytes 4128776 | tf_op jit(solution)/shard_map/ppermute | solution.py:40
  127.5 4.7 %copy-start.8 = (bf16[384,3584]{1,0:T(8,128)(2,1)S(1)}, bf16[384,3584]{1,0:T(8,128)(2,1)}, u32[]{:S(2)}) copy-start(bf16[384,3584]{1,0:T(8,128)(2,1)} %get-tuple-element.28) | copy-start | bytes 8257540
  128.0 9.0 %collective-permute-start.46 = (bf16[48,3584]{1,0:T(8,128)(2,1)S(1)}, bf16[48,3584]{1,0:T(8,128)(2,1)S(1)}, u32[]{:S(2)}, u32[]{:S(2)}) collective-permute-start(bf16[48,3584]{1,0:T(8,128)(2,1)S(1)} %get-tuple-element.57), channel_id=1, source_target_pairs={{0,64},{1,65},{2,66},{3,67},{4,68},{5,69},{6,70},{7,71},{8,72},{9,... | collective-permute-start | bytes 1032200 | tf_op jit(solution)/shard_map/ppermute | solution.py:45
  129.4 11.3 %collective-permute-start.45 = (bf16[48,3584]{1,0:T(8,128)(2,1)S(1)}, bf16[48,3584]{1,0:T(8,128)(2,1)S(1)}, u32[]{:S(2)}, u32[]{:S(2)}) collective-permute-start(bf16[48,3584]{1,0:T(8,128)(2,1)S(1)} %get-tuple-element.58), channel_id=1, source_target_pairs={{0,16},{1,17},{2,18},{3,19},{4,20},{5,21},{6,22},{7,23},{8,24},{9,... | collective-permute-start | bytes 1032200 | tf_op jit(solution)/shard_map/ppermute | solution.py:45
  131.9 9.2 %collective-permute-start.44 = (bf16[48,3584]{1,0:T(8,128)(2,1)S(1)}, bf16[48,3584]{1,0:T(8,128)(2,1)S(1)}, u32[]{:S(2)}, u32[]{:S(2)}) collective-permute-start(bf16[48,3584]{1,0:T(8,128)(2,1)S(1)} %get-tuple-element.59), channel_id=1, source_target_pairs={{0,80},{1,81},{2,82},{3,83},{4,84},{5,85},{6,86},{7,87},{8,88},{9,... | collective-permute-start | bytes 1032200 | tf_op jit(solution)/shard_map/ppermute | solution.py:45
  141.3 4.9 %collective-permute-start.47 = (bf16[12,3584]{1,0:T(8,128)(2,1)S(1)}, bf16[12,3584]{1,0:T(8,128)(2,1)S(1)}, u32[]{:S(2)}, u32[]{:S(2)}) collective-permute-start(bf16[12,3584]{1,0:T(8,128)(2,1)S(1)} %get-tuple-element.60), channel_id=1, source_target_pairs={{0,12},{1,13},{2,14},{3,15},{4,0},{5,1},{6,2},{7,3},{8,4},{9,5},{1... | collective-permute-start | bytes 258056 | tf_op jit(solution)/shard_map/ppermute | solution.py:45
  142.9 7.2 %collective-permute-start.49 = (bf16[12,3584]{1,0:T(8,128)(2,1)S(1)}, bf16[12,3584]{1,0:T(8,128)(2,1)S(1)}, u32[]{:S(2)}, u32[]{:S(2)}) collective-permute-start(bf16[12,3584]{1,0:T(8,128)(2,1)S(1)} %get-tuple-element.61), channel_id=1, source_target_pairs={{0,4},{1,5},{2,6},{3,7},{4,8},{5,9},{6,10},{7,11},{8,12},{9,13},{1... | collective-permute-start | bytes 258056 | tf_op jit(solution)/shard_map/ppermute | solution.py:45
  143.4 6.7 %collective-permute-start.48 = (bf16[12,3584]{1,0:T(8,128)(2,1)S(1)}, bf16[12,3584]{1,0:T(8,128)(2,1)S(1)}, u32[]{:S(2)}, u32[]{:S(2)}) collective-permute-start(bf16[12,3584]{1,0:T(8,128)(2,1)S(1)} %get-tuple-element.62), channel_id=1, source_target_pairs={{0,8},{1,9},{2,10},{3,11},{4,12},{5,13},{6,14},{7,15},{8,0},{9,1},... | collective-permute-start | bytes 258056 | tf_op jit(solution)/shard_map/ppermute | solution.py:45
  150.3 4.7 %collective-permute-start.50 = (bf16[3,3584]{1,0:T(4,128)(2,1)S(1)}, bf16[3,3584]{1,0:T(4,128)(2,1)S(1)}, u32[]{:S(2)}, u32[]{:S(2)}) collective-permute-start(bf16[3,3584]{1,0:T(4,128)(2,1)S(1)} %get-tuple-element.63), channel_id=1, source_target_pairs={{0,3},{1,0},{2,1},{3,2},{4,7},{5,4},{6,5},{7,6},{8,11},{9,8},{10,9... | collective-permute-start | bytes 64520 | tf_op jit(solution)/shard_map/ppermute | solution.py:45
  152.7 5.1 %collective-permute-start.52 = (bf16[3,3584]{1,0:T(4,128)(2,1)S(1)}, bf16[3,3584]{1,0:T(4,128)(2,1)S(1)}, u32[]{:S(2)}, u32[]{:S(2)}) collective-permute-start(bf16[3,3584]{1,0:T(4,128)(2,1)S(1)} %get-tuple-element.64), channel_id=1, source_target_pairs={{0,1},{1,2},{2,3},{3,0},{4,5},{5,6},{6,7},{7,4},{8,9},{9,10},{10,1... | collective-permute-start | bytes 64520 | tf_op jit(solution)/shard_map/ppermute | solution.py:45
  152.7 5.4 %collective-permute-start.51 = (bf16[3,3584]{1,0:T(4,128)(2,1)S(1)}, bf16[3,3584]{1,0:T(4,128)(2,1)S(1)}, u32[]{:S(2)}, u32[]{:S(2)}) collective-permute-start(bf16[3,3584]{1,0:T(4,128)(2,1)S(1)} %get-tuple-element.65), channel_id=1, source_target_pairs={{0,2},{1,3},{2,0},{3,1},{4,6},{5,7},{6,4},{7,5},{8,10},{9,11},{10,... | collective-permute-start | bytes 64520 | tf_op jit(solution)/shard_map/ppermute | solution.py:45

commit v6 on v4

--- a/solution.py
+++ b/solution.py
@@ -315,7 +315,7 @@
         [VMEM] * (len(blocks) + 3) + [HBM],
         [*blocks, source, tok_row, owner_row, teacher_head],
         [pltpu.VMEM((TOKENS, vocab), F32), pltpu.VMEM((3, 1024, vocab), BF16), pltpu.SemaphoreType.DMA((6,))],
-        50,
+        47,
         2 * TOKENS * tk * vocab,
         [HBM],
     )
@@ -337,7 +337,7 @@
             pltpu.VMEM((TOKENS, 1), jnp.int32),
             pltpu.SemaphoreType.DMA((7,)),
         ],
-        50,
+        51,
         2 * TOKENS * sk * vocab,
         [HBM, HBM, VMEM],
     )
@@ -360,17 +360,20 @@
             pltpu.VMEM((TOKENS, 1), jnp.int32),
             pltpu.SemaphoreType.DMA((6,)),
         ],
-        46,
+        44,
         2 * TOKENS * sk * vocab,
     )
 
     received = swap(to_other)
     grad_head = lax.dot_general(hidden, grads, (((0,), (0,)), ((), ())), preferred_element_type=F32).astype(BF16)
-    kept, received, grad_head = lax.optimization_barrier((kept, received, grad_head))
     total = kept + received.astype(F32)
     for stage in (2, 1, 0):
         size = total.shape[0] // 4
-        parts = [shift(total[k * size : (k + 1) * size].astype(BF16), stage, -k) for k in (1, 2, 3)]
+        pieces = [total[k * size : (k + 1) * size].astype(BF16) for k in range(4)]
+        parts = [shift(pieces[k], stage, -k) for k in (1, 3)]
+        parts.insert(1, shift(pieces[2], stage, -2))
+        if stage == 2:
+            total, grad_head, *parts = lax.optimization_barrier((total, grad_head, *parts))
         total = total[:size] + sum(p.astype(F32) for p in parts)
     token_loss = lax.dynamic_slice_in_dim(loss[0], lax.axis_index(AXES) * ROWS, ROWS)
     return token_loss, grad_head, total.astype(BF16)

time: 163 us -> 158 us (0.969)
  waiting for transfers between devices: 60.8 us -> 58.8 us
    ppermute x30, waiting for transfers between devices: 48.3 us -> 42.7 us  [shift(): return lax.ppermute(value, AXES, pairs)]
    ppermute x17, waiting for transfers between devices: 3.81 us -> 6.78 us  [swap(): return lax.ppermute(value, AXES, [(d, d ^ 32) for d in range(DEVICES)])]
where the time goes in v6:
time: 158 us; the launch traced here: 157 us
  waiting for transfers between devices  58.8 us (37%)
  starting transfers between devices  58.5 us (37%)
  Pallas kernels  26.2 us (17%)
  other arithmetic  5.31 us (3%)
  matrix products  4.82 us (3%)
  local copies, waits for them, and re-layouts  2.78 us (2%)
    ppermute x30, starting transfers between devices, shift(): return lax.ppermute(value, AXES, pairs)  45.5 us
    ppermute x30, waiting for transfers between devices, shift(): return lax.ppermute(value, AXES, pairs)  42.7 us
    pallas_call x3, Pallas kernels, call(): pl.pallas_call(kernel, out_shape=[jax.ShapeDtypeStruct(*o) for o in out],...  26.2 us
    ppermute x17, waiting for transfers between devices, swap(): return lax.ppermute(value, AXES, [(d, d ^ 32) for d in range(DEVICES)])  6.78 us
    ppermute x3, starting transfers between devices, across(): lax.ppermute(value, AXES, [(d, moved(d, dim, 2)) for d in range(DEVICES)])  6.3 us
    ppermute x3, waiting for transfers between devices, ring_shift(): lax.ppermute(value, AXES, [(d, moved(d, dim, -1 if coords(d)['c'] else 1)...  5.43 us
    dot_general x1, matrix products, shards(): lax.dot_general(hidden, grads, (((0,), (0,)), ((), ())), preferred_elemen...  4.82 us
    ppermute x3, waiting for transfers between devices, across(): lax.ppermute(value, AXES, [(d, moved(d, dim, 2)) for d in range(DEVICES)])  3.9 us
  transfers between devices with their start and end apart: 53, of which 30 were waited for; matrix products, arithmetic and copies ran while one was open for 5% of the time, Pallas kernels for 8%

profile of v6, /device:TPU:0, one launch (start us, length us, event | category | flops | bytes accessed | tf_op | source)
XLA Modules:
  0.0 157.4 jit_solution(13064943205086898861)
XLA Ops:
  0.6 1.8 %collective-permute-start.9 = (bf16[3,8192]{1,0:T(4,128)(2,1)}, bf16[3,8192]{1,0:T(4,128)(2,1)S(1)}, u32[]{:S(2)}, u32[]{:S(2)}) collective-permute-start(bf16[3,8192]{1,0:T(4,128)(2,1)} %param.6), channel_id=1, source_target_pairs={{0,1},{1,2},{2,3},{3,0},{4,5},{5,6},{6,7},{7,4},{8,9},{9,10},{10,1... | collective-permute-start | bytes 147464 | tf_op jit(solution)/shard_map/ppermute | solution.py:45
  2.4 1.5 collective-permute-start.11
  3.9 2.1 %collective-permute-start.10 = (bf16[3,8192]{1,0:T(4,128)(2,1)}, bf16[3,8192]{1,0:T(4,128)(2,1)S(1)}, u32[]{:S(2)}, u32[]{:S(2)}) collective-permute-start(bf16[3,8192]{1,0:T(4,128)(2,1)} %param.6), channel_id=1, source_target_pairs={{0,2},{1,3},{2,0},{3,1},{4,6},{5,7},{6,4},{7,5},{8,10},{9,11},{10,... | collective-permute-start | bytes 147464 | tf_op jit(solution)/shard_map/ppermute | solution.py:45
  6.9 3.1 %collective-permute-done.10 = bf16[3,8192]{1,0:T(4,128)(2,1)S(1)} collective-permute-done((bf16[3,8192]{1,0:T(4,128)(2,1)}, bf16[3,8192]{1,0:T(4,128)(2,1)S(1)}, u32[]{:S(2)}, u32[]{:S(2)}) %collective-permute-start.10) | collective-permute-done | bytes 49184 | tf_op jit(solution)/shard_map/ppermute | solution.py:45
  9.9 1.0 pad_maximum_fusion.3
  11.0 1.7 %collective-permute-start.12 = (bf16[12,8192]{1,0:T(8,128)(2,1)S(1)}, bf16[12,8192]{1,0:T(8,128)(2,1)S(1)}, u32[]{:S(2)}, u32[]{:S(2)}) collective-permute-start(bf16[12,8192]{1,0:T(8,128)(2,1)S(1)} %pad_maximum_fusion.3), channel_id=1, source_target_pairs={{0,4},{1,5},{2,6},{3,7},{4,8},{5,9},{6,10},{7,11},{8,12},{9,13},{1... | collective-permute-start | bytes 589832 | tf_op jit(solution)/shard_map/ppermute | solution.py:45
  13.0 2.9 %collective-permute-start.2 = (bf16[3,3584]{1,0:T(4,128)(2,1)}, bf16[3,3584]{1,0:T(4,128)(2,1)S(1)}, u32[]{:S(2)}, u32[]{:S(2)}) collective-permute-start(bf16[3,3584]{1,0:T(4,128)(2,1)} %param.8), channel_id=1, source_target_pairs={{0,3},{1,0},{2,1},{3,2},{4,7},{5,4},{6,5},{7,6},{8,11},{9,8},{10,9... | collective-permute-start | bytes 64520 | tf_op jit(solution)/shard_map/ppermute | solution.py:45
  15.9 0.8 collective-permute-start.1
  16.7 1.7 %collective-permute-start.14 = (bf16[12,8192]{1,0:T(8,128)(2,1)S(1)}, bf16[12,8192]{1,0:T(8,128)(2,1)S(1)}, u32[]{:S(2)}, u32[]{:S(2)}) collective-permute-start(bf16[12,8192]{1,0:T(8,128)(2,1)S(1)} %pad_maximum_fusion.3), channel_id=1, source_target_pairs={{0,12},{1,13},{2,14},{3,15},{4,0},{5,1},{6,2},{7,3},{8,4},{9,5},{1... | collective-permute-start | bytes 589832 | tf_op jit(solution)/shard_map/ppermute | solution.py:45
  18.6 1.9 %collective-permute-start.13 = (bf16[12,8192]{1,0:T(8,128)(2,1)S(1)}, bf16[12,8192]{1,0:T(8,128)(2,1)S(1)}, u32[]{:S(2)}, u32[]{:S(2)}) collective-permute-start(bf16[12,8192]{1,0:T(8,128)(2,1)S(1)} %pad_maximum_fusion.3), channel_id=1, source_target_pairs={{0,8},{1,9},{2,10},{3,11},{4,12},{5,13},{6,14},{7,15},{8,0},{9,1},... | collective-permute-start | bytes 589832 | tf_op jit(solution)/shard_map/ppermute | solution.py:45
  20.6 4.5 %collective-permute-done.14 = bf16[12,8192]{1,0:T(8,128)(2,1)S(1)} collective-permute-done((bf16[12,8192]{1,0:T(8,128)(2,1)S(1)}, bf16[12,8192]{1,0:T(8,128)(2,1)S(1)}, u32[]{:S(2)}, u32[]{:S(2)}) %collective-permute-start.14) | collective-permute-done | bytes 196640 | tf_op jit(solution)/shard_map/ppermute | solution.py:45
  25.1 1.4 collective-permute-done.13
  26.5 4.1 %collective-permute-start.17 = (bf16[24,8192]{1,0:T(8,128)(2,1)S(1)}, bf16[24,8192]{1,0:T(8,128)(2,1)S(1)}, u32[]{:S(2)}, u32[]{:S(2)}) collective-permute-start(bf16[24,8192]{1,0:T(8,128)(2,1)S(1)} %pad_maximum_fusion.1.refs_0_), channel_id=1, source_target_pairs={{0,80},{1,81},{2,82},{3,83},{4,84},{5,85},{6,86},{7,87},{8,88},{9,... | collective-permute-start | bytes 1179656 | tf_op jit(solution)/shard_map/ppermute | solution.py:45
  30.9 3.2 %collective-permute-start.18 = (bf16[24,8192]{1,0:T(8,128)(2,1)S(1)}, bf16[24,8192]{1,0:T(8,128)(2,1)S(1)}, u32[]{:S(2)}, u32[]{:S(2)}) collective-permute-start(bf16[24,8192]{1,0:T(8,128)(2,1)S(1)} %pad_maximum_fusion.refs_1_), channel_id=1, source_target_pairs={{0,80},{1,81},{2,82},{3,83},{4,84},{5,85},{6,86},{7,87},{8,88},{9,... | collective-permute-start | bytes 1179656 | tf_op jit(solution)/shard_map/ppermute | solution.py:45
  34.1 0.8 pad_maximum_fusion.4
  34.9 2.3 %collective-permute-start.5 = (bf16[12,3584]{1,0:T(8,128)(2,1)S(1)}, bf16[12,3584]{1,0:T(8,128)(2,1)S(1)}, u32[]{:S(2)}, u32[]{:S(2)}) collective-permute-start(bf16[12,3584]{1,0:T(8,128)(2,1)S(1)} %pad_maximum_fusion.4), channel_id=1, source_target_pairs={{0,12},{1,13},{2,14},{3,15},{4,0},{5,1},{6,2},{7,3},{8,4},{9,5},{1... | collective-permute-start | bytes 258056 | tf_op jit(solution)/shard_map/ppermute | solution.py:45
  37.2 2.6 %collective-permute-done.5 = bf16[12,3584]{1,0:T(8,128)(2,1)S(1)} collective-permute-done((bf16[12,3584]{1,0:T(8,128)(2,1)S(1)}, bf16[12,3584]{1,0:T(8,128)(2,1)S(1)}, u32[]{:S(2)}, u32[]{:S(2)}) %collective-permute-start.5) | collective-permute-done | bytes 86048 | tf_op jit(solution)/shard_map/ppermute | solution.py:45
  39.8 1.8 %collective-permute-start.4 = (bf16[12,3584]{1,0:T(8,128)(2,1)S(1)}, bf16[12,3584]{1,0:T(8,128)(2,1)S(1)}, u32[]{:S(2)}, u32[]{:S(2)}) collective-permute-start(bf16[12,3584]{1,0:T(8,128)(2,1)S(1)} %pad_maximum_fusion.4), channel_id=1, source_target_pairs={{0,8},{1,9},{2,10},{3,11},{4,12},{5,13},{6,14},{7,15},{8,0},{9,1},... | collective-permute-start | bytes 258056 | tf_op jit(solution)/shard_map/ppermute | solution.py:45
  41.6 4.5 %collective-permute-done.4 = bf16[12,3584]{1,0:T(8,128)(2,1)S(1)} collective-permute-done((bf16[12,3584]{1,0:T(8,128)(2,1)S(1)}, bf16[12,3584]{1,0:T(8,128)(2,1)S(1)}, u32[]{:S(2)}, u32[]{:S(2)}) %collective-permute-start.4) | collective-permute-done | bytes 86048 | tf_op jit(solution)/shard_map/ppermute | solution.py:45
  46.1 1.4 collective-permute-start.3
  47.5 4.8 %collective-permute-done.3 = bf16[12,3584]{1,0:T(8,128)(2,1)S(1)} collective-permute-done((bf16[12,3584]{1,0:T(8,128)(2,1)S(1)}, bf16[12,3584]{1,0:T(8,128)(2,1)S(1)}, u32[]{:S(2)}, u32[]{:S(2)}) %collective-permute-start.3) | collective-permute-done | bytes 86048 | tf_op jit(solution)/shard_map/ppermute | solution.py:45
  53.0 3.1 %collective-permute-start.26 = (bf16[24,8192]{1,0:T(8,128)(2,1)S(1)}, bf16[24,8192]{1,0:T(8,128)(2,1)}, u32[]{:S(2)}, u32[]{:S(2)}) collective-permute-start(bf16[24,8192]{1,0:T(8,128)(2,1)S(1)} %collective-permute-done.18.refs_5_), channel_id=1, source_target_pairs={{0,80},{1,81},{2,82},{3,83},{4,84},{5,85},{6,86},{7,87},{8,88},{9,... | collective-permute-start | bytes 1179656 | tf_op jit(solution)/shard_map/ppermute | solution.py:45
  56.6 4.7 %collective-permute-done.16.refs_3_ = bf16[24,8192]{1,0:T(8,128)(2,1)S(1)} collective-permute-done((bf16[24,8192]{1,0:T(8,128)(2,1)S(1)}, bf16[24,8192]{1,0:T(8,128)(2,1)S(1)}, u32[]{:S(2)}, u32[]{:S(2)}) %collective-permute-start.16) | collective-permute-done | bytes 393248 | tf_op jit(solution)/shard_map/ppermute | solution.py:45
  61.3 0.5 collective-permute-start.22
  61.8 3.8 %collective-permute-done.25.refs_12_ = bf16[24,8192]{1,0:T(8,128)(2,1)} collective-permute-done((bf16[24,8192]{1,0:T(8,128)(2,1)S(1)}, bf16[24,8192]{1,0:T(8,128)(2,1)}, u32[]{:S(2)}, u32[]{:S(2)}) %collective-permute-start.25) | collective-permute-done | bytes 393248 | tf_op jit(solution)/shard_map/ppermute | solution.py:45
  65.6 0.5 collective-permute-start.28
  66.2 1.2 pad_maximum_fusion.2.refs_0_
  67.5 0.5 collective-permute-start.8
  68.0 0.9 collective-permute-start.7
  68.9 0.9 collective-permute-start.6
  69.8 13.0 %shard_map.85.refs_9_.t_in = f32[384,768]{1,0:T(8,128)} custom-call(bf16[24,8192]{1,0:T(8,128)(2,1)S(1)} %pad_maximum_fusion.1.refs_0_, bf16[24,8192]{1,0:T(8,128)(2,1)S(1)} %pad_maximum_fusion.refs_1_, bf16[24,8192]{1,0:T(8,128)(2,1)S(1)} %collective-permute-done.15.refs_2_, bf16[24,8192]{1,0:T(8,128)(2,1)S(1)} %collective-permute-done.16.refs_3_, ...), custom_call_target="tpu_custom_call" | custom-call | flops 4831838208 | bytes 4194304 | tf_op jit(solution)/shard_map/pallas_call | solution.py:248
  82.9 0.6 collective-permute-start.30
  84.0 1.0 collective-permute-done.30.refs_5_
  85.0 0.5 collective-permute-done.31.refs_6_
  86.0 8.0 %shard_map.86 = (f32[384,768]{1,0:T(8,128)}, bf16[384,3584]{1,0:T(8,128)(2,1)}, f32[8,384]{1,0:T(8,128)S(1)}) custom-call(bf16[48,3584]{1,0:T(8,128)(2,1)S(1)} %pad_maximum_fusion.2.refs_0_, bf16[48,3584]{1,0:T(8,128)(2,1)} %collective-permute-done.6.refs_1_, bf16[48,3584]{1,0:T(8,128)(2,1)} %collective-permute-done.7.refs_2_, ...), custom_call_target="tpu_custom_call" | custom-call | flops 2113929216 | bytes 4194304 | tf_op jit(solution)/shard_map/pallas_call | solution.py:248
  94.5 0.8 collective-permute-done.33
  95.6 0.7 collective-permute-start.34
  96.2 2.2 %collective-permute-start.36 = (f32[8,384]{1,0:T(8,128)S(1)}, f32[8,384]{1,0:T(8,128)S(1)}, u32[]{:S(2)}, u32[]{:S(2)}) collective-permute-start(f32[8,384]{1,0:T(8,128)S(1)} %select_select_fusion.3), channel_id=1, source_target_pairs={{0,2},{1,3},{2,0},{3,1},{4,6},{5,7},{6,4},{7,5},{8,10},{9,11},{10,... | collective-permute-start | bytes 36872 | tf_op jit(solution)/shard_map/ppermute | solution.py:281
  98.5 2.0 %collective-permute-done.34 = f32[8,384]{1,0:T(8,128)S(1)} collective-permute-done((f32[8,384]{1,0:T(8,128)S(1)}, f32[8,384]{1,0:T(8,128)S(1)}, u32[]{:S(2)}, u32[]{:S(2)}) %collective-permute-start.34) | collective-permute-done | bytes 12320 | tf_op jit(solution)/shard_map/ppermute | solution.py:277
  100.5 1.0 collective-permute-done.36
  102.0 2.3 %collective-permute-start.37 = (f32[8,384]{1,0:T(8,128)S(1)}, f32[8,384]{1,0:T(8,128)S(1)}, u32[]{:S(2)}, u32[]{:S(2)}) collective-permute-start(f32[8,384]{1,0:T(8,128)S(1)} %select_select_fusion.2), channel_id=1, source_target_pairs={{0,4},{1,5},{2,6},{3,7},{4,8},{5,9},{6,10},{7,11},{8,12},{9,13},{1... | collective-permute-start | bytes 36872 | tf_op jit(solution)/shard_map/ppermute | solution.py:277
  104.3 1.7 %collective-permute-start.39 = (f32[8,384]{1,0:T(8,128)S(1)}, f32[8,384]{1,0:T(8,128)S(1)}, u32[]{:S(2)}, u32[]{:S(2)}) collective-permute-start(f32[8,384]{1,0:T(8,128)S(1)} %select_select_fusion.2), channel_id=1, source_target_pairs={{0,8},{1,9},{2,10},{3,11},{4,12},{5,13},{6,14},{7,15},{8,0},{9,1},... | collective-permute-start | bytes 36872 | tf_op jit(solution)/shard_map/ppermute | solution.py:281
  106.0 0.9 collective-permute-done.37
  106.9 2.6 %collective-permute-done.39 = f32[8,384]{1,0:T(8,128)S(1)} collective-permute-done((f32[8,384]{1,0:T(8,128)S(1)}, f32[8,384]{1,0:T(8,128)S(1)}, u32[]{:S(2)}, u32[]{:S(2)}) %collective-permute-start.39) | collective-permute-done | bytes 12320 | tf_op jit(solution)/shard_map/ppermute | solution.py:281
  110.1 2.3 %collective-permute-start.42 = (f32[8,384]{1,0:T(8,128)S(1)}, f32[8,384]{1,0:T(8,128)S(1)}, u32[]{:S(2)}, u32[]{:S(2)}) collective-permute-start(f32[8,384]{1,0:T(8,128)S(1)} %select_select_fusion.1), channel_id=1, source_target_pairs={{0,16},{1,17},{2,18},{3,19},{4,20},{5,21},{6,22},{7,23},{8,24},{9,... | collective-permute-start | bytes 36872 | tf_op jit(solution)/shard_map/ppermute | solution.py:281
  112.5 2.5 %collective-permute-done.40 = f32[8,384]{1,0:T(8,128)S(1)} collective-permute-done((f32[8,384]{1,0:T(8,128)S(1)}, f32[8,384]{1,0:T(8,128)S(1)}, u32[]{:S(2)}, u32[]{:S(2)}) %collective-permute-start.40) | collective-permute-done | bytes 12320 | tf_op jit(solution)/shard_map/ppermute | solution.py:277
  115.4 0.8 collective-permute-done.41
  116.5 1.3 copy-done.1
  117.8 5.1 %shard_map.87 = (bf16[384,768]{1,0:T(8,128)(2,1)S(1)}, bf16[192,3584]{1,0:T(8,128)(2,1)S(1)}, f32[192,3584]{1,0:T(8,128)S(1)}, f32[1,384]{1,0:T(1,128)S(1)}) custom-call(s32[1]{0:T(128)} %bitcast.refs_8_.at_ref, f32[384,768]{1,0:T(8,128)S(1)} %copy-done, f32[384,768]{1,0:T(8,128)S(1)} %copy-done.1, f32[8,384]{1,0:T(8,128)S(1)} %select_select_fusion.stats, ...), custom_call_target="tpu_custom_call" | custom-call | flops 2113929216 | bytes 4194304 | tf_op jit(solution)/shard_map/pallas_call | solution.py:248
  123.2 3.0 %collective-permute-done.43 = bf16[192,3584]{1,0:T(8,128)(2,1)S(1)} collective-permute-done((bf16[192,3584]{1,0:T(8,128)(2,1)S(1)}, bf16[192,3584]{1,0:T(8,128)(2,1)S(1)}, u32[]{:S(2)}, u32[]{:S(2)}) %collective-permute-start.43) | collective-permute-done | bytes 1376288 | tf_op jit(solution)/shard_map/ppermute | solution.py:40
  126.6 1.4 collective-permute-start.46
  128.1 2.4 %collective-permute-start.45 = (bf16[48,3584]{1,0:T(8,128)(2,1)S(1)}, bf16[48,3584]{1,0:T(8,128)(2,1)S(1)}, u32[]{:S(2)}, u32[]{:S(2)}) collective-permute-start(bf16[48,3584]{1,0:T(8,128)(2,1)S(1)} %get-tuple-element.58), channel_id=1, source_target_pairs={{0,16},{1,17},{2,18},{3,19},{4,20},{5,21},{6,22},{7,23},{8,24},{9,... | collective-permute-start | bytes 1032200 | tf_op jit(solution)/shard_map/ppermute | solution.py:45
  130.9 4.8 %convolution_convert_fusion = bf16[3584,768]{1,0:T(8,128)(2,1)} fusion(bf16[384,3584]{1,0:T(8,128)(2,1)S(1)} %copy-done.8, bf16[384,768]{1,0:T(8,128)(2,1)S(1)} %get-tuple-element.29), kind=kOutput, calls=%fused_computation | convolution fusion | flops 2116681728 | bytes 8847360 | tf_op jit(solution)/shard_map/dot_general | solution.py:368
  135.7 3.8 %collective-permute-done.45 = bf16[48,3584]{1,0:T(8,128)(2,1)S(1)} collective-permute-done((bf16[48,3584]{1,0:T(8,128)(2,1)S(1)}, bf16[48,3584]{1,0:T(8,128)(2,1)S(1)}, u32[]{:S(2)}, u32[]{:S(2)}) %collective-permute-start.45) | collective-permute-done | bytes 344096 | tf_op jit(solution)/shard_map/ppermute | solution.py:45
  140.0 1.6 %collective-permute-start.47 = (bf16[12,3584]{1,0:T(8,128)(2,1)S(1)}, bf16[12,3584]{1,0:T(8,128)(2,1)S(1)}, u32[]{:S(2)}, u32[]{:S(2)}) collective-permute-start(bf16[12,3584]{1,0:T(8,128)(2,1)S(1)} %get-tuple-element.60), channel_id=1, source_target_pairs={{0,12},{1,13},{2,14},{3,15},{4,0},{5,1},{6,2},{7,3},{8,4},{9,5},{1... | collective-permute-start | bytes 258056 | tf_op jit(solution)/shard_map/ppermute | solution.py:45
  141.6 0.5 collective-permute-start.49
  142.1 1.7 %collective-permute-start.48 = (bf16[12,3584]{1,0:T(8,128)(2,1)S(1)}, bf16[12,3584]{1,0:T(8,128)(2,1)S(1)}, u32[]{:S(2)}, u32[]{:S(2)}) collective-permute-start(bf16[12,3584]{1,0:T(8,128)(2,1)S(1)} %get-tuple-element.62), channel_id=1, source_target_pairs={{0,8},{1,9},{2,10},{3,11},{4,12},{5,13},{6,14},{7,15},{8,0},{9,1},... | collective-permute-start | bytes 258056 | tf_op jit(solution)/shard_map/ppermute | solution.py:45
  143.8 1.0 collective-permute-done.47
  144.9 4.0 %collective-permute-done.49 = bf16[12,3584]{1,0:T(8,128)(2,1)S(1)} collective-permute-done((bf16[12,3584]{1,0:T(8,128)(2,1)S(1)}, bf16[12,3584]{1,0:T(8,128)(2,1)S(1)}, u32[]{:S(2)}, u32[]{:S(2)}) %collective-permute-start.49) | collective-permute-done | bytes 86048 | tf_op jit(solution)/shard_map/ppermute | solution.py:45
  148.9 2.4 %collective-permute-start.50 = (bf16[3,3584]{1,0:T(4,128)(2,1)S(1)}, bf16[3,3584]{1,0:T(4,128)(2,1)S(1)}, u32[]{:S(2)}, u32[]{:S(2)}) collective-permute-start(bf16[3,3584]{1,0:T(4,128)(2,1)S(1)} %get-tuple-element.63), channel_id=1, source_target_pairs={{0,3},{1,0},{2,1},{3,2},{4,7},{5,4},{6,5},{7,6},{8,11},{9,8},{10,9... | collective-permute-start | bytes 64520 | tf_op jit(solution)/shard_map/ppermute | solution.py:45
  151.4 1.6 %collective-permute-start.51 = (bf16[3,3584]{1,0:T(4,128)(2,1)S(1)}, bf16[3,3584]{1,0:T(4,128)(2,1)S(1)}, u32[]{:S(2)}, u32[]{:S(2)}) collective-permute-start(bf16[3,3584]{1,0:T(4,128)(2,1)S(1)} %get-tuple-element.65), channel_id=1, source_target_pairs={{0,2},{1,3},{2,0},{3,1},{4,6},{5,7},{6,4},{7,5},{8,10},{9,11},{10,... | collective-permute-start | bytes 64520 | tf_op jit(solution)/shard_map/ppermute | solution.py:45
  153.0 0.6 dynamic-slice_bitcast_fusion
  153.6 2.9 %collective-permute-done.52 = bf16[3,3584]{1,0:T(4,128)(2,1)S(1)} collective-permute-done((bf16[3,3584]{1,0:T(4,128)(2,1)S(1)}, bf16[3,3584]{1,0:T(4,128)(2,1)S(1)}, u32[]{:S(2)}, u32[]{:S(2)}) %collective-permute-start.52) | collective-permute-done | bytes 21536 | tf_op jit(solution)/shard_map/ppermute | solution.py:45
  156.7 0.6 fusion
  (122 shorter events, 8.5 us)
Async XLA Ops:
  0.6 55.7 %copy-start.6 = (s32[384]{0:T(512)S(1)}, s32[384]{0:T(512)}, u32[]{:S(2)}) copy-start(s32[384]{0:T(512)} %param.11) | copy-start | bytes 4612
  0.6 5.8 %collective-permute-start.9 = (bf16[3,8192]{1,0:T(4,128)(2,1)}, bf16[3,8192]{1,0:T(4,128)(2,1)S(1)}, u32[]{:S(2)}, u32[]{:S(2)}) collective-permute-start(bf16[3,8192]{1,0:T(4,128)(2,1)} %param.6), channel_id=1, source_target_pairs={{0,1},{1,2},{2,3},{3,0},{4,5},{5,6},{6,7},{7,4},{8,9},{9,10},{10,1... | collective-permute-start | bytes 147464 | tf_op jit(solution)/shard_map/ppermute | solution.py:45
  2.4 4.5 %collective-permute-start.11 = (bf16[3,8192]{1,0:T(4,128)(2,1)}, bf16[3,8192]{1,0:T(4,128)(2,1)S(1)}, u32[]{:S(2)}, u32[]{:S(2)}) collective-permute-start(bf16[3,8192]{1,0:T(4,128)(2,1)} %param.6), channel_id=1, source_target_pairs={{0,3},{1,0},{2,1},{3,2},{4,7},{5,4},{6,5},{7,6},{8,11},{9,8},{10,9... | collective-permute-start | bytes 147464 | tf_op jit(solution)/shard_map/ppermute | solution.py:45
  3.9 6.0 %collective-permute-start.10 = (bf16[3,8192]{1,0:T(4,128)(2,1)}, bf16[3,8192]{1,0:T(4,128)(2,1)S(1)}, u32[]{:S(2)}, u32[]{:S(2)}) collective-permute-start(bf16[3,8192]{1,0:T(4,128)(2,1)} %param.6), channel_id=1, source_target_pairs={{0,2},{1,3},{2,0},{3,1},{4,6},{5,7},{6,4},{7,5},{8,10},{9,11},{10,... | collective-permute-start | bytes 147464 | tf_op jit(solution)/shard_map/ppermute | solution.py:45
  11.0 7.7 %collective-permute-start.12 = (bf16[12,8192]{1,0:T(8,128)(2,1)S(1)}, bf16[12,8192]{1,0:T(8,128)(2,1)S(1)}, u32[]{:S(2)}, u32[]{:S(2)}) collective-permute-start(bf16[12,8192]{1,0:T(8,128)(2,1)S(1)} %pad_maximum_fusion.3), channel_id=1, source_target_pairs={{0,4},{1,5},{2,6},{3,7},{4,8},{5,9},{6,10},{7,11},{8,12},{9,13},{1... | collective-permute-start | bytes 589832 | tf_op jit(solution)/shard_map/ppermute | solution.py:45
  12.6 18.1 %collective-permute-start = (bf16[3,3584]{1,0:T(4,128)(2,1)}, bf16[3,3584]{1,0:T(4,128)(2,1)S(1)}, u32[]{:S(2)}, u32[]{:S(2)}) collective-permute-start(bf16[3,3584]{1,0:T(4,128)(2,1)} %param.8), channel_id=1, source_target_pairs={{0,1},{1,2},{2,3},{3,0},{4,5},{5,6},{6,7},{7,4},{8,9},{9,10},{10,1... | collective-permute-start | bytes 64520 | tf_op jit(solution)/shard_map/ppermute | solution.py:45
  13.0 17.8 %collective-permute-start.2 = (bf16[3,3584]{1,0:T(4,128)(2,1)}, bf16[3,3584]{1,0:T(4,128)(2,1)S(1)}, u32[]{:S(2)}, u32[]{:S(2)}) collective-permute-start(bf16[3,3584]{1,0:T(4,128)(2,1)} %param.8), channel_id=1, source_target_pairs={{0,3},{1,0},{2,1},{3,2},{4,7},{5,4},{6,5},{7,6},{8,11},{9,8},{10,9... | collective-permute-start | bytes 64520 | tf_op jit(solution)/shard_map/ppermute | solution.py:45
  15.9 18.2 %collective-permute-start.1 = (bf16[3,3584]{1,0:T(4,128)(2,1)}, bf16[3,3584]{1,0:T(4,128)(2,1)S(1)}, u32[]{:S(2)}, u32[]{:S(2)}) collective-permute-start(bf16[3,3584]{1,0:T(4,128)(2,1)} %param.8), channel_id=1, source_target_pairs={{0,2},{1,3},{2,0},{3,1},{4,6},{5,7},{6,4},{7,5},{8,10},{9,11},{10,... | collective-permute-start | bytes 64520 | tf_op jit(solution)/shard_map/ppermute | solution.py:45
  16.7 8.5 %collective-permute-start.14 = (bf16[12,8192]{1,0:T(8,128)(2,1)S(1)}, bf16[12,8192]{1,0:T(8,128)(2,1)S(1)}, u32[]{:S(2)}, u32[]{:S(2)}) collective-permute-start(bf16[12,8192]{1,0:T(8,128)(2,1)S(1)} %pad_maximum_fusion.3), channel_id=1, source_target_pairs={{0,12},{1,13},{2,14},{3,15},{4,0},{5,1},{6,2},{7,3},{8,4},{9,5},{1... | collective-permute-start | bytes 589832 | tf_op jit(solution)/shard_map/ppermute | solution.py:45
  18.6 7.9 %collective-permute-start.13 = (bf16[12,8192]{1,0:T(8,128)(2,1)S(1)}, bf16[12,8192]{1,0:T(8,128)(2,1)S(1)}, u32[]{:S(2)}, u32[]{:S(2)}) collective-permute-start(bf16[12,8192]{1,0:T(8,128)(2,1)S(1)} %pad_maximum_fusion.3), channel_id=1, source_target_pairs={{0,8},{1,9},{2,10},{3,11},{4,12},{5,13},{6,14},{7,15},{8,0},{9,1},... | collective-permute-start | bytes 589832 | tf_op jit(solution)/shard_map/ppermute | solution.py:45
  25.1 27.1 %collective-permute-start.19 = (bf16[24,8192]{1,0:T(8,128)(2,1)S(1)}, bf16[24,8192]{1,0:T(8,128)(2,1)S(1)}, u32[]{:S(2)}, u32[]{:S(2)}) collective-permute-start(bf16[24,8192]{1,0:T(8,128)(2,1)S(1)} %pad_maximum_fusion.1.refs_0_), channel_id=1, source_target_pairs={{0,32},{1,33},{2,34},{3,35},{4,36},{5,37},{6,38},{7,39},{8,40},{9,... | collective-permute-start | bytes 1179656 | tf_op jit(solution)/shard_map/ppermute | solution.py:40
  26.5 25.9 %collective-permute-start.17 = (bf16[24,8192]{1,0:T(8,128)(2,1)S(1)}, bf16[24,8192]{1,0:T(8,128)(2,1)S(1)}, u32[]{:S(2)}, u32[]{:S(2)}) collective-permute-start(bf16[24,8192]{1,0:T(8,128)(2,1)S(1)} %pad_maximum_fusion.1.refs_0_), channel_id=1, source_target_pairs={{0,80},{1,81},{2,82},{3,83},{4,84},{5,85},{6,86},{7,87},{8,88},{9,... | collective-permute-start | bytes 1179656 | tf_op jit(solution)/shard_map/ppermute | solution.py:45
  30.8 22.1 %collective-permute-start.15 = (bf16[24,8192]{1,0:T(8,128)(2,1)S(1)}, bf16[24,8192]{1,0:T(8,128)(2,1)S(1)}, u32[]{:S(2)}, u32[]{:S(2)}) collective-permute-start(bf16[24,8192]{1,0:T(8,128)(2,1)S(1)} %pad_maximum_fusion.1.refs_0_), channel_id=1, source_target_pairs={{0,64},{1,65},{2,66},{3,67},{4,68},{5,69},{6,70},{7,71},{8,72},{9,... | collective-permute-start | bytes 1179656 | tf_op jit(solution)/shard_map/ppermute | solution.py:45
  30.9 22.1 %collective-permute-start.18 = (bf16[24,8192]{1,0:T(8,128)(2,1)S(1)}, bf16[24,8192]{1,0:T(8,128)(2,1)S(1)}, u32[]{:S(2)}, u32[]{:S(2)}) collective-permute-start(bf16[24,8192]{1,0:T(8,128)(2,1)S(1)} %pad_maximum_fusion.refs_1_), channel_id=1, source_target_pairs={{0,80},{1,81},{2,82},{3,83},{4,84},{5,85},{6,86},{7,87},{8,88},{9,... | collective-permute-start | bytes 1179656 | tf_op jit(solution)/shard_map/ppermute | solution.py:45
  34.9 18.1 %copy-start.2 = (bf16[12,3584]{1,0:T(8,128)(2,1)}, bf16[12,3584]{1,0:T(8,128)(2,1)S(1)}, u32[]{:S(2)}) copy-start(bf16[12,3584]{1,0:T(8,128)(2,1)S(1)} %pad_maximum_fusion.4) | copy-start | bytes 258052
  34.9 4.9 %collective-permute-start.5 = (bf16[12,3584]{1,0:T(8,128)(2,1)S(1)}, bf16[12,3584]{1,0:T(8,128)(2,1)S(1)}, u32[]{:S(2)}, u32[]{:S(2)}) collective-permute-start(bf16[12,3584]{1,0:T(8,128)(2,1)S(1)} %pad_maximum_fusion.4), channel_id=1, source_target_pairs={{0,12},{1,13},{2,14},{3,15},{4,0},{5,1},{6,2},{7,3},{8,4},{9,5},{1... | collective-permute-start | bytes 258056 | tf_op jit(solution)/shard_map/ppermute | solution.py:45
  39.8 16.3 %copy-start.3 = (bf16[12,3584]{1,0:T(8,128)(2,1)}, bf16[12,3584]{1,0:T(8,128)(2,1)S(1)}, u32[]{:S(2)}) copy-start(bf16[12,3584]{1,0:T(8,128)(2,1)S(1)} %collective-permute-done.5) | copy-start | bytes 258052
  39.8 6.3 %collective-permute-start.4 = (bf16[12,3584]{1,0:T(8,128)(2,1)S(1)}, bf16[12,3584]{1,0:T(8,128)(2,1)S(1)}, u32[]{:S(2)}, u32[]{:S(2)}) collective-permute-start(bf16[12,3584]{1,0:T(8,128)(2,1)S(1)} %pad_maximum_fusion.4), channel_id=1, source_target_pairs={{0,8},{1,9},{2,10},{3,11},{4,12},{5,13},{6,14},{7,15},{8,0},{9,1},... | collective-permute-start | bytes 258056 | tf_op jit(solution)/shard_map/ppermute | solution.py:45
  46.1 10.0 %copy-start.4 = (bf16[12,3584]{1,0:T(8,128)(2,1)}, bf16[12,3584]{1,0:T(8,128)(2,1)S(1)}, u32[]{:S(2)}) copy-start(bf16[12,3584]{1,0:T(8,128)(2,1)S(1)} %collective-permute-done.4) | copy-start | bytes 258052
  46.1 6.2 %collective-permute-start.3 = (bf16[12,3584]{1,0:T(8,128)(2,1)S(1)}, bf16[12,3584]{1,0:T(8,128)(2,1)S(1)}, u32[]{:S(2)}, u32[]{:S(2)}) collective-permute-start(bf16[12,3584]{1,0:T(8,128)(2,1)S(1)} %pad_maximum_fusion.4), channel_id=1, source_target_pairs={{0,4},{1,5},{2,6},{3,7},{4,8},{5,9},{6,10},{7,11},{8,12},{9,13},{1... | collective-permute-start | bytes 258056 | tf_op jit(solution)/shard_map/ppermute | solution.py:45
  52.3 3.9 %copy-start.5 = (bf16[12,3584]{1,0:T(8,128)(2,1)}, bf16[12,3584]{1,0:T(8,128)(2,1)S(1)}, u32[]{:S(2)}) copy-start(bf16[12,3584]{1,0:T(8,128)(2,1)S(1)} %collective-permute-done.3) | copy-start | bytes 258052
  52.3 4.2 %collective-permute-start.20 = (bf16[24,8192]{1,0:T(8,128)(2,1)S(1)}, bf16[24,8192]{1,0:T(8,128)(2,1)S(1)}, u32[]{:S(2)}, u32[]{:S(2)}) collective-permute-start(bf16[24,8192]{1,0:T(8,128)(2,1)S(1)} %pad_maximum_fusion.refs_1_), channel_id=1, source_target_pairs={{0,32},{1,33},{2,34},{3,35},{4,36},{5,37},{6,38},{7,39},{8,40},{9,... | collective-permute-start | bytes 1179656 | tf_op jit(solution)/shard_map/ppermute | solution.py:40
  52.3 9.1 %collective-permute-start.16 = (bf16[24,8192]{1,0:T(8,128)(2,1)S(1)}, bf16[24,8192]{1,0:T(8,128)(2,1)S(1)}, u32[]{:S(2)}, u32[]{:S(2)}) collective-permute-start(bf16[24,8192]{1,0:T(8,128)(2,1)S(1)} %pad_maximum_fusion.refs_1_), channel_id=1, source_target_pairs={{0,64},{1,65},{2,66},{3,67},{4,68},{5,69},{6,70},{7,71},{8,72},{9,... | collective-permute-start | bytes 1179656 | tf_op jit(solution)/shard_map/ppermute | solution.py:45
  52.4 8.9 %collective-permute-start.23 = (bf16[24,8192]{1,0:T(8,128)(2,1)S(1)}, bf16[24,8192]{1,0:T(8,128)(2,1)}, u32[]{:S(2)}, u32[]{:S(2)}) collective-permute-start(bf16[24,8192]{1,0:T(8,128)(2,1)S(1)} %collective-permute-done.17.refs_4_), channel_id=1, source_target_pairs={{0,32},{1,33},{2,34},{3,35},{4,36},{5,37},{6,38},{7,39},{8,40},{9,... | collective-permute-start | bytes 1179656 | tf_op jit(solution)/shard_map/ppermute | solution.py:40
  52.9 12.8 %collective-permute-start.25 = (bf16[24,8192]{1,0:T(8,128)(2,1)S(1)}, bf16[24,8192]{1,0:T(8,128)(2,1)}, u32[]{:S(2)}, u32[]{:S(2)}) collective-permute-start(bf16[24,8192]{1,0:T(8,128)(2,1)S(1)} %collective-permute-done.15.refs_2_), channel_id=1, source_target_pairs={{0,64},{1,65},{2,66},{3,67},{4,68},{5,69},{6,70},{7,71},{8,72},{9,... | collective-permute-start | bytes 1179656 | tf_op jit(solution)/shard_map/ppermute | solution.py:45
  53.0 12.7 %collective-permute-start.26 = (bf16[24,8192]{1,0:T(8,128)(2,1)S(1)}, bf16[24,8192]{1,0:T(8,128)(2,1)}, u32[]{:S(2)}, u32[]{:S(2)}) collective-permute-start(bf16[24,8192]{1,0:T(8,128)(2,1)S(1)} %collective-permute-done.18.refs_5_), channel_id=1, source_target_pairs={{0,80},{1,81},{2,82},{3,83},{4,84},{5,85},{6,86},{7,87},{8,88},{9,... | collective-permute-start | bytes 1179656 | tf_op jit(solution)/shard_map/ppermute | solution.py:45
  56.5 10.9 %collective-permute-start.21 = (bf16[24,8192]{1,0:T(8,128)(2,1)S(1)}, bf16[24,8192]{1,0:T(8,128)(2,1)S(1)}, u32[]{:S(2)}, u32[]{:S(2)}) collective-permute-start(bf16[24,8192]{1,0:T(8,128)(2,1)S(1)} %collective-permute-done.15.refs_2_), channel_id=1, source_target_pairs={{0,32},{1,33},{2,34},{3,35},{4,36},{5,37},{6,38},{7,39},{8,40},{9,... | collective-permute-start | bytes 1179656 | tf_op jit(solution)/shard_map/ppermute | solution.py:40
  61.3 6.1 %collective-permute-start.24 = (bf16[24,8192]{1,0:T(8,128)(2,1)S(1)}, bf16[24,8192]{1,0:T(8,128)(2,1)S(1)}, u32[]{:S(2)}, u32[]{:S(2)}) collective-permute-start(bf16[24,8192]{1,0:T(8,128)(2,1)S(1)} %collective-permute-done.18.refs_5_), channel_id=1, source_target_pairs={{0,32},{1,33},{2,34},{3,35},{4,36},{5,37},{6,38},{7,39},{8,40},{9,... | collective-permute-start | bytes 1179656 | tf_op jit(solution)/shard_map/ppermute | solution.py:40
  61.3 6.6 %collective-permute-start.22 = (bf16[24,8192]{1,0:T(8,128)(2,1)S(1)}, bf16[24,8192]{1,0:T(8,128)(2,1)S(1)}, u32[]{:S(2)}, u32[]{:S(2)}) collective-permute-start(bf16[24,8192]{1,0:T(8,128)(2,1)S(1)} %collective-permute-done.16.refs_3_), channel_id=1, source_target_pairs={{0,32},{1,33},{2,34},{3,35},{4,36},{5,37},{6,38},{7,39},{8,40},{9,... | collective-permute-start | bytes 1179656 | tf_op jit(solution)/shard_map/ppermute | solution.py:40
  65.6 3.3 %collective-permute-start.27 = (bf16[24,8192]{1,0:T(8,128)(2,1)}, bf16[24,8192]{1,0:T(8,128)(2,1)S(1)}, u32[]{:S(2)}, u32[]{:S(2)}) collective-permute-start(bf16[24,8192]{1,0:T(8,128)(2,1)} %collective-permute-done.25.refs_12_), channel_id=1, source_target_pairs={{0,32},{1,33},{2,34},{3,35},{4,36},{5,37},{6,38},{7,39},{8,40},{9,... | collective-permute-start | bytes 1179656 | tf_op jit(solution)/shard_map/ppermute | solution.py:40
  65.6 4.2 %collective-permute-start.28 = (bf16[24,8192]{1,0:T(8,128)(2,1)}, bf16[24,8192]{1,0:T(8,128)(2,1)S(1)}, u32[]{:S(2)}, u32[]{:S(2)}) collective-permute-start(bf16[24,8192]{1,0:T(8,128)(2,1)} %collective-permute-done.26.refs_13_), channel_id=1, source_target_pairs={{0,32},{1,33},{2,34},{3,35},{4,36},{5,37},{6,38},{7,39},{8,40},{9,... | collective-permute-start | bytes 1179656 | tf_op jit(solution)/shard_map/ppermute | solution.py:40
  67.3 16.7 %copy-start.7 = (s32[384]{0:T(512)S(1)}, s32[384]{0:T(512)}, u32[]{:S(2)}) copy-start(s32[384]{0:T(512)} %param.10) | copy-start | bytes 4612
  67.3 16.7 %collective-permute-start.29 = (bf16[48,3584]{1,0:T(8,128)(2,1)S(1)}, bf16[48,3584]{1,0:T(8,128)(2,1)}, u32[]{:S(2)}, u32[]{:S(2)}) collective-permute-start(bf16[48,3584]{1,0:T(8,128)(2,1)S(1)} %pad_maximum_fusion.2.refs_0_), channel_id=1, source_target_pairs={{0,32},{1,33},{2,34},{3,35},{4,36},{5,37},{6,38},{7,39},{8,40},{9,... | collective-permute-start | bytes 1032200 | tf_op jit(solution)/shard_map/ppermute | solution.py:40
  67.5 15.4 %collective-permute-start.8 = (bf16[48,3584]{1,0:T(8,128)(2,1)S(1)}, bf16[48,3584]{1,0:T(8,128)(2,1)}, u32[]{:S(2)}, u32[]{:S(2)}) collective-permute-start(bf16[48,3584]{1,0:T(8,128)(2,1)S(1)} %pad_maximum_fusion.2.refs_0_), channel_id=1, source_target_pairs={{0,80},{1,81},{2,82},{3,83},{4,84},{5,85},{6,86},{7,87},{8,88},{9,... | collective-permute-start | bytes 1032200 | tf_op jit(solution)/shard_map/ppermute | solution.py:45
  68.0 14.9 %collective-permute-start.7 = (bf16[48,3584]{1,0:T(8,128)(2,1)S(1)}, bf16[48,3584]{1,0:T(8,128)(2,1)}, u32[]{:S(2)}, u32[]{:S(2)}) collective-permute-start(bf16[48,3584]{1,0:T(8,128)(2,1)S(1)} %pad_maximum_fusion.2.refs_0_), channel_id=1, source_target_pairs={{0,16},{1,17},{2,18},{3,19},{4,20},{5,21},{6,22},{7,23},{8,24},{9,... | collective-permute-start | bytes 1032200 | tf_op jit(solution)/shard_map/ppermute | solution.py:45
  68.9 14.0 %collective-permute-start.6 = (bf16[48,3584]{1,0:T(8,128)(2,1)S(1)}, bf16[48,3584]{1,0:T(8,128)(2,1)}, u32[]{:S(2)}, u32[]{:S(2)}) collective-permute-start(bf16[48,3584]{1,0:T(8,128)(2,1)S(1)} %pad_maximum_fusion.2.refs_0_), channel_id=1, source_target_pairs={{0,64},{1,65},{2,66},{3,67},{4,68},{5,69},{6,70},{7,71},{8,72},{9,... | collective-permute-start | bytes 1032200 | tf_op jit(solution)/shard_map/ppermute | solution.py:45
  82.9 2.1 %collective-permute-start.30 = (bf16[48,3584]{1,0:T(8,128)(2,1)}, bf16[48,3584]{1,0:T(8,128)(2,1)S(1)}, u32[]{:S(2)}, u32[]{:S(2)}) collective-permute-start(bf16[48,3584]{1,0:T(8,128)(2,1)} %collective-permute-done.6.refs_1_), channel_id=1, source_target_pairs={{0,32},{1,33},{2,34},{3,35},{4,36},{5,37},{6,38},{7,39},{8,40},{9,... | collective-permute-start | bytes 1032200 | tf_op jit(solution)/shard_map/ppermute | solution.py:40
  83.5 2.0 %collective-permute-start.31 = (bf16[48,3584]{1,0:T(8,128)(2,1)}, bf16[48,3584]{1,0:T(8,128)(2,1)S(1)}, u32[]{:S(2)}, u32[]{:S(2)}) collective-permute-start(bf16[48,3584]{1,0:T(8,128)(2,1)} %collective-permute-done.7.refs_2_), channel_id=1, source_target_pairs={{0,32},{1,33},{2,34},{3,35},{4,36},{5,37},{6,38},{7,39},{8,40},{9,... | collective-permute-start | bytes 1032200 | tf_op jit(solution)/shard_map/ppermute | solution.py:40
  83.6 2.4 %collective-permute-start.32 = (bf16[48,3584]{1,0:T(8,128)(2,1)}, bf16[48,3584]{1,0:T(8,128)(2,1)S(1)}, u32[]{:S(2)}, u32[]{:S(2)}) collective-permute-start(bf16[48,3584]{1,0:T(8,128)(2,1)} %collective-permute-done.8.refs_3_), channel_id=1, source_target_pairs={{0,32},{1,33},{2,34},{3,35},{4,36},{5,37},{6,38},{7,39},{8,40},{9,... | collective-permute-start | bytes 1032200 | tf_op jit(solution)/shard_map/ppermute | solution.py:40
  86.0 30.6 %copy-start = (f32[384,768]{1,0:T(8,128)S(1)}, f32[384,768]{1,0:T(8,128)}, u32[]{:S(2)}) copy-start(f32[384,768]{1,0:T(8,128)} %shard_map.85.refs_9_.t_in) | copy-start | bytes 3538948
  94.0 1.3 collective-permute-start.33
  95.6 4.9 %collective-permute-start.34 = (f32[8,384]{1,0:T(8,128)S(1)}, f32[8,384]{1,0:T(8,128)S(1)}, u32[]{:S(2)}, u32[]{:S(2)}) collective-permute-start(f32[8,384]{1,0:T(8,128)S(1)} %select_select_fusion.3), channel_id=1, source_target_pairs={{0,1},{1,2},{2,3},{3,0},{4,5},{5,6},{6,7},{7,4},{8,9},{9,10},{10,1... | collective-permute-start | bytes 36872 | tf_op jit(solution)/shard_map/ppermute | solution.py:277
  96.2 5.2 %collective-permute-start.36 = (f32[8,384]{1,0:T(8,128)S(1)}, f32[8,384]{1,0:T(8,128)S(1)}, u32[]{:S(2)}, u32[]{:S(2)}) collective-permute-start(f32[8,384]{1,0:T(8,128)S(1)} %select_select_fusion.3), channel_id=1, source_target_pairs={{0,2},{1,3},{2,0},{3,1},{4,6},{5,7},{6,4},{7,5},{8,10},{9,11},{10,... | collective-permute-start | bytes 36872 | tf_op jit(solution)/shard_map/ppermute | solution.py:281
  100.5 1.2 collective-permute-start.35
  102.0 4.9 %collective-permute-start.37 = (f32[8,384]{1,0:T(8,128)S(1)}, f32[8,384]{1,0:T(8,128)S(1)}, u32[]{:S(2)}, u32[]{:S(2)}) collective-permute-start(f32[8,384]{1,0:T(8,128)S(1)} %select_select_fusion.2), channel_id=1, source_target_pairs={{0,4},{1,5},{2,6},{3,7},{4,8},{5,9},{6,10},{7,11},{8,12},{9,13},{1... | collective-permute-start | bytes 36872 | tf_op jit(solution)/shard_map/ppermute | solution.py:277
  104.3 5.2 %collective-permute-start.39 = (f32[8,384]{1,0:T(8,128)S(1)}, f32[8,384]{1,0:T(8,128)S(1)}, u32[]{:S(2)}, u32[]{:S(2)}) collective-permute-start(f32[8,384]{1,0:T(8,128)S(1)} %select_select_fusion.2), channel_id=1, source_target_pairs={{0,8},{1,9},{2,10},{3,11},{4,12},{5,13},{6,14},{7,15},{8,0},{9,1},... | collective-permute-start | bytes 36872 | tf_op jit(solution)/shard_map/ppermute | solution.py:281
  106.9 2.6 %collective-permute-start.38 = (f32[8,384]{1,0:T(8,128)S(1)}, f32[8,384]{1,0:T(8,128)S(1)}, u32[]{:S(2)}, u32[]{:S(2)}) collective-permute-start(f32[8,384]{1,0:T(8,128)S(1)} %collective-permute-done.37), channel_id=1, source_target_pairs={{0,32},{1,33},{2,34},{3,35},{4,36},{5,37},{6,38},{7,39},{8,40},{9,... | collective-permute-start | bytes 36872 | tf_op jit(solution)/shard_map/ppermute | solution.py:40
  109.8 5.1 %collective-permute-start.40 = (f32[8,384]{1,0:T(8,128)S(1)}, f32[8,384]{1,0:T(8,128)S(1)}, u32[]{:S(2)}, u32[]{:S(2)}) collective-permute-start(f32[8,384]{1,0:T(8,128)S(1)} %select_select_fusion.1), channel_id=1, source_target_pairs={{0,64},{1,65},{2,66},{3,67},{4,68},{5,69},{6,70},{7,71},{8,72},{9,... | collective-permute-start | bytes 36872 | tf_op jit(solution)/shard_map/ppermute | solution.py:277
  110.1 5.2 %collective-permute-start.42 = (f32[8,384]{1,0:T(8,128)S(1)}, f32[8,384]{1,0:T(8,128)S(1)}, u32[]{:S(2)}, u32[]{:S(2)}) collective-permute-start(f32[8,384]{1,0:T(8,128)S(1)} %select_select_fusion.1), channel_id=1, source_target_pairs={{0,16},{1,17},{2,18},{3,19},{4,20},{5,21},{6,22},{7,23},{8,24},{9,... | collective-permute-start | bytes 36872 | tf_op jit(solution)/shard_map/ppermute | solution.py:281
  115.0 1.2 collective-permute-start.41
  116.5 1.3 copy-start.1
  122.9 3.2 %collective-permute-start.43 = (bf16[192,3584]{1,0:T(8,128)(2,1)S(1)}, bf16[192,3584]{1,0:T(8,128)(2,1)S(1)}, u32[]{:S(2)}, u32[]{:S(2)}) collective-permute-start(bf16[192,3584]{1,0:T(8,128)(2,1)S(1)} %get-tuple-element.27), channel_id=1, source_target_pairs={{0,32},{1,33},{2,34},{3,35},{4,36},{5,37},{6,38},{7,39},{8,40},{9,... | collective-permute-start | bytes 4128776 | tf_op jit(solution)/shard_map/ppermute | solution.py:40
  126.2 4.7 %copy-start.8 = (bf16[384,3584]{1,0:T(8,128)(2,1)S(1)}, bf16[384,3584]{1,0:T(8,128)(2,1)}, u32[]{:S(2)}) copy-start(bf16[384,3584]{1,0:T(8,128)(2,1)} %get-tuple-element.28) | copy-start | bytes 8257540
  126.6 9.0 %collective-permute-start.46 = (bf16[48,3584]{1,0:T(8,128)(2,1)S(1)}, bf16[48,3584]{1,0:T(8,128)(2,1)S(1)}, u32[]{:S(2)}, u32[]{:S(2)}) collective-permute-start(bf16[48,3584]{1,0:T(8,128)(2,1)S(1)} %get-tuple-element.57), channel_id=1, source_target_pairs={{0,64},{1,65},{2,66},{3,67},{4,68},{5,69},{6,70},{7,71},{8,72},{9,... | collective-permute-start | bytes 1032200 | tf_op jit(solution)/shard_map/ppermute | solution.py:45
  128.1 11.3 %collective-permute-start.45 = (bf16[48,3584]{1,0:T(8,128)(2,1)S(1)}, bf16[48,3584]{1,0:T(8,128)(2,1)S(1)}, u32[]{:S(2)}, u32[]{:S(2)}) collective-permute-start(bf16[48,3584]{1,0:T(8,128)(2,1)S(1)} %get-tuple-element.58), channel_id=1, source_target_pairs={{0,16},{1,17},{2,18},{3,19},{4,20},{5,21},{6,22},{7,23},{8,24},{9,... | collective-permute-start | bytes 1032200 | tf_op jit(solution)/shard_map/ppermute | solution.py:45
  130.5 9.2 %collective-permute-start.44 = (bf16[48,3584]{1,0:T(8,128)(2,1)S(1)}, bf16[48,3584]{1,0:T(8,128)(2,1)S(1)}, u32[]{:S(2)}, u32[]{:S(2)}) collective-permute-start(bf16[48,3584]{1,0:T(8,128)(2,1)S(1)} %get-tuple-element.59), channel_id=1, source_target_pairs={{0,80},{1,81},{2,82},{3,83},{4,84},{5,85},{6,86},{7,87},{8,88},{9,... | collective-permute-start | bytes 1032200 | tf_op jit(solution)/shard_map/ppermute | solution.py:45
  140.0 4.9 %collective-permute-start.47 = (bf16[12,3584]{1,0:T(8,128)(2,1)S(1)}, bf16[12,3584]{1,0:T(8,128)(2,1)S(1)}, u32[]{:S(2)}, u32[]{:S(2)}) collective-permute-start(bf16[12,3584]{1,0:T(8,128)(2,1)S(1)} %get-tuple-element.60), channel_id=1, source_target_pairs={{0,12},{1,13},{2,14},{3,15},{4,0},{5,1},{6,2},{7,3},{8,4},{9,5},{1... | collective-permute-start | bytes 258056 | tf_op jit(solution)/shard_map/ppermute | solution.py:45
  141.6 7.2 %collective-permute-start.49 = (bf16[12,3584]{1,0:T(8,128)(2,1)S(1)}, bf16[12,3584]{1,0:T(8,128)(2,1)S(1)}, u32[]{:S(2)}, u32[]{:S(2)}) collective-permute-start(bf16[12,3584]{1,0:T(8,128)(2,1)S(1)} %get-tuple-element.61), channel_id=1, source_target_pairs={{0,4},{1,5},{2,6},{3,7},{4,8},{5,9},{6,10},{7,11},{8,12},{9,13},{1... | collective-permute-start | bytes 258056 | tf_op jit(solution)/shard_map/ppermute | solution.py:45
  142.1 6.7 %collective-permute-start.48 = (bf16[12,3584]{1,0:T(8,128)(2,1)S(1)}, bf16[12,3584]{1,0:T(8,128)(2,1)S(1)}, u32[]{:S(2)}, u32[]{:S(2)}) collective-permute-start(bf16[12,3584]{1,0:T(8,128)(2,1)S(1)} %get-tuple-element.62), channel_id=1, source_target_pairs={{0,8},{1,9},{2,10},{3,11},{4,12},{5,13},{6,14},{7,15},{8,0},{9,1},... | collective-permute-start | bytes 258056 | tf_op jit(solution)/shard_map/ppermute | solution.py:45
  148.9 4.6 %collective-permute-start.50 = (bf16[3,3584]{1,0:T(4,128)(2,1)S(1)}, bf16[3,3584]{1,0:T(4,128)(2,1)S(1)}, u32[]{:S(2)}, u32[]{:S(2)}) collective-permute-start(bf16[3,3584]{1,0:T(4,128)(2,1)S(1)} %get-tuple-element.63), channel_id=1, source_target_pairs={{0,3},{1,0},{2,1},{3,2},{4,7},{5,4},{6,5},{7,6},{8,11},{9,8},{10,9... | collective-permute-start | bytes 64520 | tf_op jit(solution)/shard_map/ppermute | solution.py:45
  151.4 5.1 %collective-permute-start.52 = (bf16[3,3584]{1,0:T(4,128)(2,1)S(1)}, bf16[3,3584]{1,0:T(4,128)(2,1)S(1)}, u32[]{:S(2)}, u32[]{:S(2)}) collective-permute-start(bf16[3,3584]{1,0:T(4,128)(2,1)S(1)} %get-tuple-element.64), channel_id=1, source_target_pairs={{0,1},{1,2},{2,3},{3,0},{4,5},{5,6},{6,7},{7,4},{8,9},{9,10},{10,1... | collective-permute-start | bytes 64520 | tf_op jit(solution)/shard_map/ppermute | solution.py:45
  151.4 5.4 %collective-permute-start.51 = (bf16[3,3584]{1,0:T(4,128)(2,1)S(1)}, bf16[3,3584]{1,0:T(4,128)(2,1)S(1)}, u32[]{:S(2)}, u32[]{:S(2)}) collective-permute-start(bf16[3,3584]{1,0:T(4,128)(2,1)S(1)} %get-tuple-element.65), channel_id=1, source_target_pairs={{0,2},{1,3},{2,0},{3,1},{4,6},{5,7},{6,4},{7,5},{8,10},{9,11},{10,... | collective-permute-start | bytes 64520 | tf_op jit(solution)/shard_map/ppermute | solution.py:45
